TPU v7x, 512 devices: a whole 4x8x8 slice. The times are simulated.
512 devices in a mesh: slab: 16 (over z_hi, y), dom: 32 (over z_lo, x, core).
Axes of the slice: x: 4, y: 8, z: 8 (z_hi: 2, z_lo: 4; z = z_hi * 4 + z_lo), core: 2. Of those that a mesh axis runs over, the one named last changes fastest.
Arguments:
- velocity: float32 [3, 343, 65536], P(None, None, ('slab', 'dom')), may hold values from -17 to 17
- slot_map: int32 [16, 32, 128], P('slab', 'dom'), may hold values from 0 to 127, each once within a row
- class_index: int32 [16, 32, 128], P('slab', 'dom'), may hold values from 0 to 15, as said below
- schur_blocks: float32 [16, 218, 218], replicated, may hold values from -1.21 to 8.75, as said below
Outputs:
- pressure: float32 [218, 65536], P(None, ('slab', 'dom'))
- residual: float32 [218, 65536], P(None, ('slab', 'dom'))
Inputs may be any that keep to these rules, and one draw needn't show every extreme that they name: On each device the entries of slot_map are a permutation of the brick positions (bx * 8 + by) * 16 + bz: every position holds one element. `class_index`: on every device each of the 16 classes holds exactly 8 of its elements. `schur_blocks`: every block is symmetric and positive definite.
All inputs are finite; a program needn't handle non-finite values.
Results may differ from a plain program's by a relative error of at most 0.0003.
Values sent between devices are 32-bit elements; how exact they have to be, the bound alone decides.
No kernel may reach another device: no remote copies, remote signals or barrier semaphores. Data moves between devices by JAX's collectives and lax.ppermute only.
A program may use at most 64 MiB of HBM per device.

v0:
```python
import jax
import jax.numpy as jnp
import numpy as np
from jax import lax
from jax.sharding import PartitionSpec as P

BX = 1
BY = 8
BZ = 16
CLASSES = 16
ITERS = 2


DELTA_T = 0.05
EINSUM_FORMS = ("pa,kabcm->kpbcm", "pb,kabcm->kapcm", "pc,kabcm->kabpm")


def padded_2(shard, sides, width):
    for axis, dim in sides:
        count, length = (lax.axis_size(axis), shard.shape[dim])
        up = [(i, (i + 1) % count) for i in range(count)]
        down = [(j, i) for i, j in up]
        last = lax.slice_in_dim(shard, length - width, length, axis=dim)
        leading = lax.slice_in_dim(shard, 0, width, axis=dim)
        before = lax.ppermute(last, axis, up)
        after = lax.ppermute(leading, axis, down)
        shard = jnp.concatenate([before, shard, after], axis=dim)
    return shard


def gll_tables():
    degree = 6
    outer_point = 0.830223896278567
    inner_point = 0.46884879347071423
    points = np.array([-1.0, -outer_point, -inner_point, 0.0, inner_point, outer_point, 1.0])
    values = (231.0 * points**6 - 315.0 * points**4 + 105.0 * points**2 - 5.0) / 16.0
    weights = 2.0 / (degree * (degree + 1) * values**2)
    derivative = np.zeros((7, 7))
    for target in range(7):
        for source in range(7):
            if target != source:
                derivative[target, source] = values[target] / (
                    values[source] * (points[target] - points[source])
                )
    derivative[0, 0] = -degree * (degree + 1) / 4.0
    derivative[6, 6] = degree * (degree + 1) / 4.0
    return (derivative, weights)


def shell_tables():
    surface = np.array(
        [
            index
            for index in range(343)
            if index // 49 in (0, 6) or index // 7 % 7 in (0, 6) or index % 7 in (0, 6)
        ]
    )
    factor = np.where((np.arange(7) == 0) | (np.arange(7) == 6), 2.0, 1.0)
    multiple = (factor[:, None, None] * factor[None, :, None] * factor[None, None, :]).reshape(-1)
    return (surface, 1.0 / multiple)


def cube_weights(weights_np):
    return (
        weights_np[:, None, None] * weights_np[None, :, None] * weights_np[None, None, :]
    ).reshape(-1)


def derive(derivative, nodal_cube, axis_index):
    return jnp.einsum(
        EINSUM_FORMS[axis_index], derivative, nodal_cube, precision=lax.Precision.HIGHEST
    )


def to_lines(nodal_field):
    components = nodal_field.shape[0]
    cube_view = nodal_field.reshape(components, 7, 7, 7, BX, BY, BZ)
    return cube_view.transpose(0, 4, 1, 5, 2, 6, 3).reshape(components, 7 * BX, 7 * BY, 7 * BZ)


def from_lines(line_field):
    components = line_field.shape[0]
    cube_view = line_field.reshape(components, BX, 7, BY, 7, BZ, 7)
    return cube_view.transpose(0, 2, 4, 6, 1, 3, 5).reshape(components, 343, BX * BY * BZ)


def join_along(extended, axis_index):
    length = extended.shape[axis_index] - 2
    middle = lax.slice_in_dim(extended, 1, length + 1, axis=axis_index)
    lower_side = lax.slice_in_dim(extended, 0, length, axis=axis_index)
    upper_side = lax.slice_in_dim(extended, 2, length + 2, axis=axis_index)
    node_spot = jnp.arange(length) % 7
    dims_shape = [1] * extended.ndim
    dims_shape[axis_index] = length
    at_start = (node_spot == 0).astype(jnp.float32).reshape(dims_shape)
    at_end = (node_spot == 6).astype(jnp.float32).reshape(dims_shape)
    return middle + at_start * lower_side + at_end * upper_side


def assemble(nodal_field):
    line_field = to_lines(nodal_field)
    extended = padded_2(line_field, (("slab", 1),), 1)
    joined = join_along(extended, 1)
    extended = padded_2(joined, (("dom", 2),), 1)
    joined = join_along(extended, 2)
    wrapped = jnp.concatenate([joined[..., -1:], joined, joined[..., :1]], axis=3)
    return from_lines(join_along(wrapped, 3))


def per_device(velocity, slot_map, class_index, schur_blocks):
    derivative_np, weights_np = gll_tables()
    surface, inverse_np = shell_tables()
    derivative = jnp.asarray(derivative_np, jnp.float32)
    quadrature = jnp.asarray(cube_weights(weights_np), jnp.float32)
    full_weight = jnp.asarray(inverse_np, jnp.float32)
    shell_weight = jnp.asarray(inverse_np[surface], jnp.float32)
    elements = velocity.shape[2]
    mode_count = surface.shape[0]
    positions = jnp.arange(elements, dtype=jnp.int32)
    placed = slot_map.reshape(elements)
    arrival = jnp.zeros((elements,), jnp.int32).at[placed].set(positions)
    brick_vel = jnp.take(velocity, arrival, axis=2)
    brick_class = jnp.take(class_index.reshape(elements), arrival)
    grouping = jnp.argsort(brick_class, stable=True)
    ungroup = jnp.zeros((elements,), jnp.int32).at[grouping].set(positions)
    nodal_cube = brick_vel.reshape(3, 7, 7, 7, elements)
    advect = (
        nodal_cube[0] * derive(derivative, nodal_cube, 0)
        + nodal_cube[1] * derive(derivative, nodal_cube, 1)
        + nodal_cube[2] * derive(derivative, nodal_cube, 2)
    )
    averaged = assemble(advect.reshape(3, 343, elements)) * full_weight[:, None]
    intermediate = (brick_vel - DELTA_T * averaged).reshape(3, 7, 7, 7, elements)
    diverge = (
        derive(derivative, intermediate[0:1], 0)
        + derive(derivative, intermediate[1:2], 1)
        + derive(derivative, intermediate[2:3], 2)
    )
    source = -1.0 / DELTA_T * quadrature[:, None] * diverge.reshape(343, elements)
    pressure_load = jnp.take(assemble(source[None])[0], surface, axis=0)

    def weighted(first_vec, second_vec):
        return jnp.sum(first_vec * second_vec * shell_weight[:, None])

    def squares(vector):
        return lax.psum(weighted(vector, vector), ("slab", "dom"))

    solution = jnp.zeros_like(pressure_load)
    residual = pressure_load
    direction = pressure_load
    current = squares(residual)
    for iteration in range(ITERS):
        grouped = jnp.take(direction, grouping, axis=1).reshape(
            mode_count, CLASSES, elements // CLASSES
        )
        product = jnp.einsum("cij,jcn->icn", schur_blocks, grouped, precision=lax.Precision.HIGHEST)
        element_out = jnp.take(product.reshape(mode_count, elements), ungroup, axis=1)
        padded = jnp.zeros((1, 343, elements), jnp.float32).at[0, surface].set(element_out)
        applied = jnp.take(assemble(padded)[0], surface, axis=0)
        step_size = current / lax.psum(weighted(direction, applied), ("slab", "dom"))
        solution = solution + step_size * direction
        residual = residual - step_size * applied
        if iteration + 1 < ITERS:
            following = squares(residual)
            direction = residual + following / current * direction
            current = following
    return (jnp.take(solution, placed, axis=1), jnp.take(residual, placed, axis=1))


def solution(mesh):
    return jax.shard_map(
        per_device,
        mesh=mesh,
        in_specs=(
            P(None, None, ("slab", "dom")),
            P("slab", "dom", None),
            P("slab", "dom", None),
            P(),
        ),
        out_specs=(P(None, ("slab", "dom")), P(None, ("slab", "dom"))),
        check_vma=False,
    )
```

profile of v0, /device:TPU:1, one launch (start us, length us, event | category | flops | bytes accessed | tf_op | source)
XLA Modules:
  0.0 550.9 jit_solution(15374606545472765554)
XLA Ops:
  1.3 1.0 scatter_custom_fusion
  2.3 1.2 gather_fusion.1
  3.6 1.4 copy.68
  5.0 1.1 gather_fusion
  9.5 0.9 mul.331
  11.4 1.9 fusion.6
  13.3 3.4 reshape_reshape.3
  16.7 11.3 %copy.80 = f32[3,7,7,7,1,8,16]{3,6,2,5,1,0,4:T(8,128)} copy(f32[3,7,7,7,1,8,16]{6,5,1,3,2,0,4:T(8,128)} %reshape_reshape.3) | data formatting | bytes 1053696 | tf_op jit(solution)/shard_map/reshape;reshape | solution.py:77
  28.0 7.2 %reshape.188 = f32[3,7,56,112]{3,2,1,0:T(8,128)S(1)} reshape(f32[3,1,7,8,7,16,7]{6,5,4,3,2,0,1:T(8,128)} %bitcast.135) | data formatting | bytes 1053696 | tf_op jit(solution)/shard_map/reshape | solution.py:78
  35.2 4.0 collective-permute-start
  39.3 12.3 %collective-permute-start.1 = (f32[3,1,56,112]{3,2,1,0:T(8,128)S(1)}, f32[3,1,56,112]{3,2,1,0:T(8,128)S(1)}, u32[]{:S(2)}, u32[]{:S(2)}) collective-permute-start(f32[3,1,56,112]{3,2,1,0:T(8,128)S(1)} %get-tuple-element.29), channel_id=1, source_target_pairs={{32,0},{64,32},{96,64},{128,96},{160,128},{192,160},{224,192},{256... | collective-permute-start | bytes 225800 | tf_op jit(solution)/shard_map/ppermute | solution.py:26
  51.6 2.5 sort.17
  54.1 1.0 scatter_custom_fusion.1
  55.4 4.0 collective-permute-start.2
  59.4 2.8 collective-permute-start.3
  62.2 2.5 collective-permute-done.3
  65.7 7.0 %reshape.189 = f32[3,1,7,8,7,16,7]{6,5,4,3,2,0,1:T(8,128)} reshape(f32[3,7,56,112]{3,2,1,0:T(8,128)S(1)} %fusion.17) | data formatting | bytes 1053696 | tf_op jit(solution)/shard_map/reshape | solution.py:83
  72.7 12.1 %copy.81 = f32[3,7,7,7,1,8,16]{6,5,3,2,1,0,4:T(8,128)} copy(f32[3,7,7,7,1,8,16]{3,6,2,5,1,0,4:T(8,128)} %bitcast.136) | data formatting | bytes 1053696 | tf_op jit(solution)/shard_map/transpose | solution.py:84
  84.9 3.0 reshape.190
  91.1 1.5 multiply_bitcast_fusion
  92.6 4.2 copy.91
  96.8 1.6 reshape.195
  98.4 1.9 collective-permute-start.4
  100.4 10.1 %collective-permute-start.5 = (f32[1,1,56,112]{3,2,1,0:T(8,128)S(1)}, f32[1,1,56,112]{3,2,1,0:T(8,128)S(1)}, u32[]{:S(2)}, u32[]{:S(2)}) collective-permute-start(f32[1,1,56,112]{3,2,1,0:T(8,128)S(1)} %get-tuple-element.47), channel_id=1, source_target_pairs={{32,0},{64,32},{96,64},{128,96},{160,128},{192,160},{224,192},{256... | collective-permute-start | bytes 75272 | tf_op jit(solution)/shard_map/ppermute | solution.py:26
  110.5 0.9 collective-permute-done.5
  111.5 2.5 collective-permute-start.6
  114.0 6.0 %collective-permute-start.7 = (f32[1,7,1,112]{3,2,1,0:T(1,128)S(1)}, f32[1,7,1,112]{3,2,1,0:T(1,128)S(1)}, u32[]{:S(2)}, u32[]{:S(2)}) collective-permute-start(f32[1,7,1,112]{3,2,1,0:T(1,128)S(1)} %get-tuple-element.45), channel_id=1, source_target_pairs={{1,0},{2,1},{3,2},{4,3},{5,4},{6,5},{7,6},{8,7},{9,8},{10,9},{11,1... | collective-permute-start | bytes 9416 | tf_op jit(solution)/shard_map/ppermute | solution.py:26
  121.1 1.7 reshape.196
  122.9 4.3 copy.92
  127.2 1.7 squeeze_reshape.9
  130.5 6.9 %fusion.10 = f32[218,128]{0,1:T(8,128)S(1)} fusion(f32[16,218,218]{2,0,1:T(8,128)} %param.18, f32[128,218]{1,0:T(8,128)S(1)} %gather_fusion.3, pred[128]{0:T(512)(128)(4,1)S(1)} %compare_and_fusion.2), kind=kOutput, calls=%fused_computation.28 | convolution fusion | flops 73024768 | bytes 3264896 | tf_op jit(solution)/shard_map/cij,jcn->icn/dot_general | solution.py:156
  138.3 1.1 scatter_custom_fusion.2
  139.4 1.5 reshape.200
  141.0 4.2 copy.96
  145.2 1.6 reshape.201
  146.8 1.9 collective-permute-start.8
  148.7 10.0 %collective-permute-start.9 = (f32[1,1,56,112]{3,2,1,0:T(8,128)S(1)}, f32[1,1,56,112]{3,2,1,0:T(8,128)S(1)}, u32[]{:S(2)}, u32[]{:S(2)}) collective-permute-start(f32[1,1,56,112]{3,2,1,0:T(8,128)S(1)} %get-tuple-element.41), channel_id=1, source_target_pairs={{32,0},{64,32},{96,64},{128,96},{160,128},{192,160},{224,192},{256... | collective-permute-start | bytes 75272 | tf_op jit(solution)/shard_map/ppermute | solution.py:26
  158.7 1.0 collective-permute-done.9
  159.7 1.9 collective-permute-start.10
  161.7 9.1 %collective-permute-start.11 = (f32[1,7,1,112]{3,2,1,0:T(1,128)S(1)}, f32[1,7,1,112]{3,2,1,0:T(1,128)S(1)}, u32[]{:S(2)}, u32[]{:S(2)}) collective-permute-start(f32[1,7,1,112]{3,2,1,0:T(1,128)S(1)} %get-tuple-element.39), channel_id=1, source_target_pairs={{1,0},{2,1},{3,2},{4,3},{5,4},{6,5},{7,6},{8,7},{9,8},{10,9},{11,1... | collective-permute-start | bytes 9416 | tf_op jit(solution)/shard_map/ppermute | solution.py:26
  171.9 1.7 reshape.202
  173.6 4.3 copy.97
  177.9 1.7 squeeze_reshape.10
  181.1 107.9 %all-reduce.2 = (f32[]{:T(128)}, f32[]{:T(128)}) all-reduce(f32[]{:T(128)} %get-tuple-element.13, f32[]{:T(128)} %get-tuple-element.12), channel_id=1, replica_groups=mesh['slab'=16,'dom'=32] {'slab','dom'}, use_global_device_ids=true, to_apply=%region_2.4 | all-reduce | flops 2 | bytes 16 | tf_op jit(solution)/shard_map/psum | solution.py:146
  291.1 93.4 %psum.30 = f32[]{:T(128)} all-reduce(f32[]{:T(128)} %multiply_reduce_fusion.1), channel_id=1, replica_groups=mesh['slab'=16,'dom'=32] {'slab','dom'}, use_global_device_ids=true, to_apply=%region_9.12 | all-reduce | flops 1 | bytes 8 | tf_op jit(solution)/shard_map/psum | solution.py:146
  386.8 6.9 %fusion.13 = f32[218,128]{0,1:T(8,128)S(1)} fusion(f32[16,218,218]{2,0,1:T(8,128)} %param.18, f32[128,218]{1,0:T(8,128)S(1)} %gather_fusion.6, pred[128]{0:T(512)(128)(4,1)S(1)} %copy-done.12), kind=kOutput, calls=%fused_computation.29 | convolution fusion | flops 73024768 | bytes 3264896 | tf_op jit(solution)/shard_map/cij,jcn->icn/dot_general | solution.py:156
  394.8 1.5 scatter_custom_fusion.3
  396.3 1.5 reshape.205
  397.8 4.2 copy.101
  402.0 2.2 reshape.206
  405.0 2.1 collective-permute-start.12
  407.1 9.2 %collective-permute-start.13 = (f32[1,1,56,112]{3,2,1,0:T(8,128)S(1)}, f32[1,1,56,112]{3,2,1,0:T(8,128)S(1)}, u32[]{:S(2)}, u32[]{:S(2)}) collective-permute-start(f32[1,1,56,112]{3,2,1,0:T(8,128)S(1)} %get-tuple-element.35), channel_id=1, source_target_pairs={{32,0},{64,32},{96,64},{128,96},{160,128},{192,160},{224,192},{256... | collective-permute-start | bytes 75272 | tf_op jit(solution)/shard_map/ppermute | solution.py:26
  416.3 0.9 collective-permute-done.13
  417.2 1.2 fusion.40
  418.4 5.4 collective-permute-start.14
  423.8 1.9 collective-permute-start.15
  425.8 3.0 collective-permute-done.15
  429.0 0.9 fusion.32
  429.9 2.7 reshape.207
  432.6 4.3 copy.102
  436.9 1.7 squeeze_reshape.11
  439.3 1.6 multiply_reduce_fusion
  440.9 104.0 %psum.31 = f32[]{:T(128)} all-reduce(f32[]{:T(128)} %multiply_reduce_fusion), channel_id=1, replica_groups=mesh['slab'=16,'dom'=32] {'slab','dom'}, use_global_device_ids=true, to_apply=%region_12.15 | all-reduce | flops 1 | bytes 8 | tf_op jit(solution)/shard_map/psum | solution.py:160
  546.2 0.9 multiply_subtract_fusion.1
  (141 shorter events, 23.5 us)
Async XLA Ops:
  0.6 1.7 copy-start
  2.3 4.1 copy-start.4
  35.2 20.0 %collective-permute-start = (f32[3,1,56,112]{3,2,1,0:T(8,128)S(1)}, f32[3,1,56,112]{3,2,1,0:T(8,128)S(1)}, u32[]{:S(2)}, u32[]{:S(2)}) collective-permute-start(f32[3,1,56,112]{3,2,1,0:T(8,128)S(1)} %get-tuple-element.28), channel_id=1, source_target_pairs={{0,32},{32,64},{64,96},{96,128},{128,160},{160,192},{192,224},{224... | collective-permute-start | bytes 225800 | tf_op jit(solution)/shard_map/ppermute | solution.py:25
  39.3 15.9 %collective-permute-start.1 = (f32[3,1,56,112]{3,2,1,0:T(8,128)S(1)}, f32[3,1,56,112]{3,2,1,0:T(8,128)S(1)}, u32[]{:S(2)}, u32[]{:S(2)}) collective-permute-start(f32[3,1,56,112]{3,2,1,0:T(8,128)S(1)} %get-tuple-element.29), channel_id=1, source_target_pairs={{32,0},{64,32},{96,64},{128,96},{160,128},{192,160},{224,192},{256... | collective-permute-start | bytes 225800 | tf_op jit(solution)/shard_map/ppermute | solution.py:26
  54.1 76.4 %copy-start.11 = (pred[128]{0:T(512)(128)(4,1)}, pred[128]{0:T(512)(128)(4,1)S(1)}, u32[]{:S(2)}) copy-start(pred[128]{0:T(512)(128)(4,1)S(1)} %compare_and_fusion.2) | copy-start | bytes 388
  54.1 75.6 %copy-start.9 = (s32[1024]{0:T(1024)}, s32[1024]{0:T(1024)S(1)}, u32[]{:S(2)}) copy-start(s32[1024]{0:T(1024)S(1)} %pad_clamp_fusion.2) | copy-start | bytes 12292
  55.2 83.0 %copy-start.13 = (pred[128]{0:T(512)(128)(4,1)}, pred[128]{0:T(512)(128)(4,1)S(1)}, u32[]{:S(2)}) copy-start(pred[128]{0:T(512)(128)(4,1)S(1)} %compare_and_fusion.1) | copy-start | bytes 388
  55.4 6.8 %collective-permute-start.2 = (f32[3,7,1,112]{3,2,1,0:T(1,128)S(1)}, f32[3,7,1,112]{3,2,1,0:T(1,128)S(1)}, u32[]{:S(2)}, u32[]{:S(2)}) collective-permute-start(f32[3,7,1,112]{3,2,1,0:T(1,128)S(1)} %get-tuple-element.26), channel_id=1, source_target_pairs={{0,1},{1,2},{2,3},{3,4},{4,5},{5,6},{6,7},{7,8},{8,9},{9,10},{10,1... | collective-permute-start | bytes 28232 | tf_op jit(solution)/shard_map/ppermute | solution.py:25
  59.4 5.3 collective-permute-start.3
  62.2 58.7 %copy-start.7 = (f32[112]{0:T(128)}, f32[112]{0:T(128)S(1)}, u32[]{:S(2)}) copy-start(f32[112]{0:T(128)S(1)} %get-tuple-element.57) | copy-start | bytes 1348
  84.9 3.4 copy-start.15
  87.9 1.5 copy-start.3
  89.1 2.0 copy-start.5
  92.6 17.8 %copy-start.16 = (s32[218]{0:T(256)S(1)}, s32[218]{0:T(256)}, u32[]{:S(2)}) copy-start(s32[218]{0:T(256)} %constant.135.clone) | copy-start | bytes 2620
  98.4 12.0 %collective-permute-start.4 = (f32[1,1,56,112]{3,2,1,0:T(8,128)S(1)}, f32[1,1,56,112]{3,2,1,0:T(8,128)S(1)}, u32[]{:S(2)}, u32[]{:S(2)}) collective-permute-start(f32[1,1,56,112]{3,2,1,0:T(8,128)S(1)} %get-tuple-element.46), channel_id=1, source_target_pairs={{0,32},{32,64},{64,96},{96,128},{128,160},{160,192},{192,224},{224... | collective-permute-start | bytes 75272 | tf_op jit(solution)/shard_map/ppermute | solution.py:25
  100.4 11.0 %collective-permute-start.5 = (f32[1,1,56,112]{3,2,1,0:T(8,128)S(1)}, f32[1,1,56,112]{3,2,1,0:T(8,128)S(1)}, u32[]{:S(2)}, u32[]{:S(2)}) collective-permute-start(f32[1,1,56,112]{3,2,1,0:T(8,128)S(1)} %get-tuple-element.47), channel_id=1, source_target_pairs={{32,0},{64,32},{96,64},{128,96},{160,128},{192,160},{224,192},{256... | collective-permute-start | bytes 75272 | tf_op jit(solution)/shard_map/ppermute | solution.py:26
  111.5 8.5 %collective-permute-start.6 = (f32[1,7,1,112]{3,2,1,0:T(1,128)S(1)}, f32[1,7,1,112]{3,2,1,0:T(1,128)S(1)}, u32[]{:S(2)}, u32[]{:S(2)}) collective-permute-start(f32[1,7,1,112]{3,2,1,0:T(1,128)S(1)} %get-tuple-element.44), channel_id=1, source_target_pairs={{0,1},{1,2},{2,3},{3,4},{4,5},{5,6},{6,7},{7,8},{8,9},{9,10},{10,1... | collective-permute-start | bytes 9416 | tf_op jit(solution)/shard_map/ppermute | solution.py:25
  114.0 6.6 %collective-permute-start.7 = (f32[1,7,1,112]{3,2,1,0:T(1,128)S(1)}, f32[1,7,1,112]{3,2,1,0:T(1,128)S(1)}, u32[]{:S(2)}, u32[]{:S(2)}) collective-permute-start(f32[1,7,1,112]{3,2,1,0:T(1,128)S(1)} %get-tuple-element.45), channel_id=1, source_target_pairs={{1,0},{2,1},{3,2},{4,3},{5,4},{6,5},{7,6},{8,7},{9,8},{10,9},{11,1... | collective-permute-start | bytes 9416 | tf_op jit(solution)/shard_map/ppermute | solution.py:26
  120.0 17.3 %copy-start.10 = (s32[1024]{0:T(1024)}, s32[1024]{0:T(1024)S(1)}, u32[]{:S(2)}) copy-start(s32[1024]{0:T(1024)S(1)} %pad_clamp_fusion.1) | copy-start | bytes 12292
  145.2 26.5 %copy-start.8 = (f32[112]{0:T(128)S(1)}, f32[112]{0:T(128)}, u32[]{:S(2)}) copy-start(f32[112]{0:T(128)} %copy-done.7) | copy-start | bytes 1348
  146.8 11.9 %collective-permute-start.8 = (f32[1,1,56,112]{3,2,1,0:T(8,128)S(1)}, f32[1,1,56,112]{3,2,1,0:T(8,128)S(1)}, u32[]{:S(2)}, u32[]{:S(2)}) collective-permute-start(f32[1,1,56,112]{3,2,1,0:T(8,128)S(1)} %get-tuple-element.40), channel_id=1, source_target_pairs={{0,32},{32,64},{64,96},{96,128},{128,160},{160,192},{192,224},{224... | collective-permute-start | bytes 75272 | tf_op jit(solution)/shard_map/ppermute | solution.py:25
  148.7 10.9 %collective-permute-start.9 = (f32[1,1,56,112]{3,2,1,0:T(8,128)S(1)}, f32[1,1,56,112]{3,2,1,0:T(8,128)S(1)}, u32[]{:S(2)}, u32[]{:S(2)}) collective-permute-start(f32[1,1,56,112]{3,2,1,0:T(8,128)S(1)} %get-tuple-element.41), channel_id=1, source_target_pairs={{32,0},{64,32},{96,64},{128,96},{160,128},{192,160},{224,192},{256... | collective-permute-start | bytes 75272 | tf_op jit(solution)/shard_map/ppermute | solution.py:26
  159.7 11.1 %collective-permute-start.10 = (f32[1,7,1,112]{3,2,1,0:T(1,128)S(1)}, f32[1,7,1,112]{3,2,1,0:T(1,128)S(1)}, u32[]{:S(2)}, u32[]{:S(2)}) collective-permute-start(f32[1,7,1,112]{3,2,1,0:T(1,128)S(1)} %get-tuple-element.38), channel_id=1, source_target_pairs={{0,1},{1,2},{2,3},{3,4},{4,5},{5,6},{6,7},{7,8},{8,9},{9,10},{10,1... | collective-permute-start | bytes 9416 | tf_op jit(solution)/shard_map/ppermute | solution.py:25
  161.7 9.7 %collective-permute-start.11 = (f32[1,7,1,112]{3,2,1,0:T(1,128)S(1)}, f32[1,7,1,112]{3,2,1,0:T(1,128)S(1)}, u32[]{:S(2)}, u32[]{:S(2)}) collective-permute-start(f32[1,7,1,112]{3,2,1,0:T(1,128)S(1)} %get-tuple-element.39), channel_id=1, source_target_pairs={{1,0},{2,1},{3,2},{4,3},{5,4},{6,5},{7,6},{8,7},{9,8},{10,9},{11,1... | collective-permute-start | bytes 9416 | tf_op jit(solution)/shard_map/ppermute | solution.py:26
  173.6 6.8 %copy-start.6 = (f32[218]{0:T(256)S(1)}, f32[218]{0:T(256)}, u32[]{:S(2)}) copy-start(f32[218]{0:T(256)} %constant.134.clone) | copy-start | bytes 2620
  177.9 208.9 %copy-start.12 = (pred[128]{0:T(512)(128)(4,1)S(1)}, pred[128]{0:T(512)(128)(4,1)}, u32[]{:S(2)}) copy-start(pred[128]{0:T(512)(128)(4,1)} %copy-done.11) | copy-start | bytes 388
  385.8 8.8 %copy-start.14 = (pred[128]{0:T(512)(128)(4,1)S(1)}, pred[128]{0:T(512)(128)(4,1)}, u32[]{:S(2)}) copy-start(pred[128]{0:T(512)(128)(4,1)} %copy-done.13) | copy-start | bytes 388
  385.8 8.9 %copy-start.2 = (f32[218,128]{1,0:T(8,128)}, f32[218,128]{1,0:T(8,128)S(1)}, u32[]{:S(2)}) copy-start(f32[218,128]{1,0:T(8,128)S(1)} %multiply_add_fusion.1) | copy-start | bytes 334852
  397.8 18.5 %copy-start.17 = (s32[1,1,128]{2,1,0:T(1,128)S(1)}, s32[1,1,128]{2,1,0:T(1,128)}, u32[]{:S(2)}) copy-start(s32[1,1,128]{2,1,0:T(1,128)} %param.16) | copy-start | bytes 1540
  405.0 11.3 %collective-permute-start.12 = (f32[1,1,56,112]{3,2,1,0:T(8,128)S(1)}, f32[1,1,56,112]{3,2,1,0:T(8,128)S(1)}, u32[]{:S(2)}, u32[]{:S(2)}) collective-permute-start(f32[1,1,56,112]{3,2,1,0:T(8,128)S(1)} %get-tuple-element.34), channel_id=1, source_target_pairs={{0,32},{32,64},{64,96},{96,128},{128,160},{160,192},{192,224},{224... | collective-permute-start | bytes 75272 | tf_op jit(solution)/shard_map/ppermute | solution.py:25
  407.1 10.1 %collective-permute-start.13 = (f32[1,1,56,112]{3,2,1,0:T(8,128)S(1)}, f32[1,1,56,112]{3,2,1,0:T(8,128)S(1)}, u32[]{:S(2)}, u32[]{:S(2)}) collective-permute-start(f32[1,1,56,112]{3,2,1,0:T(8,128)S(1)} %get-tuple-element.35), channel_id=1, source_target_pairs={{32,0},{64,32},{96,64},{128,96},{160,128},{192,160},{224,192},{256... | collective-permute-start | bytes 75272 | tf_op jit(solution)/shard_map/ppermute | solution.py:26
  418.4 7.3 %collective-permute-start.14 = (f32[1,7,1,112]{3,2,1,0:T(1,128)S(1)}, f32[1,7,1,112]{3,2,1,0:T(1,128)S(1)}, u32[]{:S(2)}, u32[]{:S(2)}) collective-permute-start(f32[1,7,1,112]{3,2,1,0:T(1,128)S(1)} %get-tuple-element.32), channel_id=1, source_target_pairs={{0,1},{1,2},{2,3},{3,4},{4,5},{5,6},{6,7},{7,8},{8,9},{9,10},{10,1... | collective-permute-start | bytes 9416 | tf_op jit(solution)/shard_map/ppermute | solution.py:25
  423.8 4.9 collective-permute-start.15
  432.6 117.9 %copy-start.1 = (s32[1,1,128]{2,1,0:T(1,128)S(1)}, s32[1,1,128]{2,1,0:T(1,128)}, u32[]{:S(2)}) copy-start(s32[1,1,128]{2,1,0:T(1,128)} %param.17) | copy-start | bytes 1540
where the time goes:
time: 560 us; the launch traced here: 551 us
  blocking collectives  305 us (54%)
  local copies, waits for them, and re-layouts  113 us (20%)
  starting transfers between devices  85 us (15%)
  matrix products  17.9 us (3%)
  other arithmetic  13.9 us (2%)
  waiting for transfers between devices  9.44 us (2%)
  between operations  6.09 us (1%)
    psum x2, blocking collectives, squares(): return lax.psum(weighted(vector, vector), ('slab', 'dom'))  201 us
    psum x1, blocking collectives, per_device(): lax.psum(weighted(direction, applied), ('slab', 'dom'))  104 us
    ppermute x8, starting transfers between devices, padded_2(): after = lax.ppermute(leading, axis, down)  61.3 us
    transpose x4, local copies, waits for them, and re-layouts, from_lines(): cube_view.transpose(0, 2, 4, 6, 1, 3, 5)  25 us
    ppermute x8, starting transfers between devices, padded_2(): before = lax.ppermute(last, axis, up)  23.7 us
    another operation x2, local copies, waits for them, and re-layouts, to_lines(): cube_view = nodal_field.reshape(components, 7, 7, 7, BX, BY, BZ)  14.7 us
    dot_general x2, matrix products, per_device(): jnp.einsum('cij,jcn->icn', schur_blocks, grouped, precision=lax.Precision...  13.7 us
    reshape x4, local copies, waits for them, and re-layouts, from_lines(): cube_view = line_field.reshape(components, BX, 7, BY, 7, BZ, 7)  13.1 us
  transfers between devices with their start and end apart: 16, of which 7 were waited for; matrix products, arithmetic and copies ran while one was open for 1% of the time, Pallas kernels for 0%

commit v1 on v0

v1 whole, which is shorter than its diff:
```python
import functools

import jax
import jax.numpy as jnp
import numpy as np
from jax import lax
from jax.experimental import pallas as pl
from jax.experimental.pallas import tpu as pltpu
from jax.sharding import PartitionSpec as P

CLASSES = 16
MODES = 218
NODES = 343
LANES = 128
BZ = 16
BY = 8
DELTA_T = 0.05
HIGH = lax.Precision.HIGHEST
F32 = jnp.float32


def gll_tables():
    degree = 6
    outer_point = 0.830223896278567
    inner_point = 0.46884879347071423
    points = np.array([-1.0, -outer_point, -inner_point, 0.0, inner_point, outer_point, 1.0])
    values = (231.0 * points**6 - 315.0 * points**4 + 105.0 * points**2 - 5.0) / 16.0
    weights = 2.0 / (degree * (degree + 1) * values**2)
    derivative = np.zeros((7, 7))
    for target in range(7):
        for source in range(7):
            if target != source:
                derivative[target, source] = values[target] / (
                    values[source] * (points[target] - points[source])
                )
    derivative[0, 0] = -degree * (degree + 1) / 4.0
    derivative[6, 6] = degree * (degree + 1) / 4.0
    return derivative, weights


DERIV, WEIGHTS = gll_tables()
FACTOR = np.where((np.arange(7) == 0) | (np.arange(7) == 6), 2.0, 1.0)


def shell_runs():
    runs, offset = [], 0
    for a in range(7):
        for b in range(7):
            base = 8 * (7 * a + b)
            if a in (0, 6) or b in (0, 6):
                runs.append((offset, base, 7))
                offset += 7
            else:
                runs.append((offset, base, 1))
                runs.append((offset + 1, base + 6, 1))
                offset += 2
    return runs


RUNS = shell_runs()


def constant_tables():
    rolls = np.zeros((8, 8, LANES))
    for shift in range(8):
        for target in range(7):
            source = (target - shift) % 8
            if source < 7:
                rolls[shift, target] = DERIV[target, source]
    span = np.zeros((2, 8, LANES))
    span[0, :7] = WEIGHTS[:, None]
    span[1, :7] = 1.0 / FACTOR[:, None]
    multiple = (FACTOR[:, None, None] * FACTOR[None, :, None] * FACTOR[None, None, :]).reshape(-1)
    surface = [
        i for i in range(NODES) if i // 49 in (0, 6) or i // 7 % 7 in (0, 6) or i % 7 in (0, 6)
    ]
    shell = np.zeros((224, LANES))
    shell[:MODES] = (1.0 / multiple[surface])[:, None]
    return rolls.astype(np.float32), span.astype(np.float32), shell.astype(np.float32)


ROLLS, SPAN, SHELL = constant_tables()


def iotas(shape):
    lane = lax.broadcasted_iota(jnp.int32, shape, len(shape) - 1)
    node = lax.broadcasted_iota(jnp.int32, shape, len(shape) - 2)
    return lane % BZ, lane // BZ, node


def join_local(sheet):
    bz, by, node = iotas(sheet.shape)
    low = pltpu.roll(sheet, 2, 1)
    low = jnp.where(bz == 0, pltpu.roll(low, LANES - 15, 2), pltpu.roll(low, 1, 2))
    high = pltpu.roll(sheet, 6, 1)
    high = jnp.where(bz == BZ - 1, pltpu.roll(high, 15, 2), pltpu.roll(high, LANES - 1, 2))
    sheet = sheet + jnp.where(node == 0, low, jnp.where(node == 6, high, 0.0))
    first, last = sheet[0], sheet[6]
    first_by = by[0]
    new_first = first + jnp.where(first_by > 0, pltpu.roll(last, BZ, 1), 0.0)
    new_last = last + jnp.where(first_by < BY - 1, pltpu.roll(first, LANES - BZ, 1), 0.0)
    return jnp.concatenate([new_first[None], sheet[1:6], new_last[None]], axis=0)


def add_received(a, sheet, low_x, high_x, low_y, high_y):
    if a == 0:
        sheet = sheet + low_x
    if a == 6:
        sheet = sheet + high_x
    _, by, _ = iotas(sheet.shape[1:])
    first = sheet[0] + jnp.where(by == 0, low_y, 0.0)
    last = sheet[6] + jnp.where(by == BY - 1, high_y, 0.0)
    return jnp.concatenate([first[None], sheet[1:6], last[None]], axis=0)


def derive_sheets(sheets, target):
    total = float(DERIV[target, 0]) * sheets[0]
    for source in range(1, 7):
        total = total + float(DERIV[target, source]) * sheets[source]
    return total


def derive_span(rolls_ref, sheet):
    total = rolls_ref[0] * sheet
    for shift in range(1, 8):
        total = total + rolls_ref[shift] * pltpu.roll(sheet, shift, 1)
    return total


def permutation(slot_ref):
    position = lax.broadcasted_iota(jnp.int32, (LANES, LANES), 0)
    return jnp.where(position == slot_ref[...], 1.0, 0.0).astype(F32)


def emit_faces(part_ref, up_ref, down_ref, index):
    up_ref[index] = part_ref[index, 6]
    down_ref[index] = part_ref[index, 0]


def advect_kernel(vel_ref, slot_ref, class_ref, rolls_ref, brick_ref, part_ref, up_ref, down_ref, class_out):
    one_hot = permutation(slot_ref)
    nt = (((1,), (1,)), ((), ()))
    class_out[...] = lax.dot_general(
        jnp.broadcast_to(class_ref[...].astype(F32), (8, LANES)), one_hot, nt, precision=HIGH
    )
    for i in range(3):
        moved = lax.dot_general(vel_ref[i], one_hot, nt, precision=HIGH, preferred_element_type=F32)
        brick_ref[i] = jnp.zeros((7, 7, 8, LANES), F32)
        for a in range(7):
            for b in range(7):
                row = 7 * (7 * a + b)
                brick_ref[i, a, b, 0:7, :] = moved[row : row + 7]

    def component(i, carry):
        sheets = [brick_ref[i, a] for a in range(7)]
        for a in range(7):
            along_a = derive_sheets(sheets, a)
            sheet = sheets[a]
            along_b = jnp.stack(
                [derive_sheets([sheet[b] for b in range(7)], target) for target in range(7)], axis=0
            )
            along_c = derive_span(rolls_ref, sheet)
            advect = (
                brick_ref[0, a] * along_a + brick_ref[1, a] * along_b + brick_ref[2, a] * along_c
            )
            part_ref[i, a] = join_local(advect)
        emit_faces(part_ref, up_ref, down_ref, i)
        return carry

    lax.fori_loop(0, 3, component, 0)


def side_kernel(part_ref, low_x_ref, high_x_ref, up_ref, down_ref):
    for i in range(part_ref.shape[0]):
        for a in range(7):
            first, last = part_ref[i, a, 0], part_ref[i, a, 6]
            if a == 0:
                first, last = first + low_x_ref[i, 0], last + low_x_ref[i, 6]
            if a == 6:
                first, last = first + high_x_ref[i, 0], last + high_x_ref[i, 6]
            up_ref[i, a] = pltpu.roll(last, BZ, 1)
            down_ref[i, a] = pltpu.roll(first, LANES - BZ, 1)


def source_kernel(
    part_ref, low_x_ref, high_x_ref, low_y_ref, high_y_ref, brick_ref, rolls_ref, span_ref,
    out_ref, up_ref, down_ref, middle_ref,
):
    for i in range(3):
        for a in range(7):
            sheet = add_received(
                a, part_ref[i, a], low_x_ref[i], high_x_ref[i], low_y_ref[i, a], high_y_ref[i, a]
            )
            scaled = [
                sheet[b] * (span_ref[1] * float(DELTA_T / (FACTOR[a] * FACTOR[b]))) for b in range(7)
            ]
            middle_ref[i, a] = brick_ref[i, a] - jnp.stack(scaled, axis=0)
    sheets = [middle_ref[0, a] for a in range(7)]
    for a in range(7):
        along_a = derive_sheets(sheets, a)
        second = middle_ref[1, a]
        along_b = jnp.stack(
            [derive_sheets([second[b] for b in range(7)], target) for target in range(7)], axis=0
        )
        diverge = along_a + along_b + derive_span(rolls_ref, middle_ref[2, a])
        source = [
            diverge[b] * (span_ref[0] * float(-1.0 / DELTA_T * WEIGHTS[a] * WEIGHTS[b]))
            for b in range(7)
        ]
        out_ref[0, a] = join_local(jnp.stack(source, axis=0))
    emit_faces(out_ref, up_ref, down_ref, 0)


def gather_modes(part_ref, low_x_ref, high_x_ref, low_y_ref, high_y_ref, full_ref, modes_ref):
    for a in range(7):
        sheet = add_received(
            a, part_ref[0, a], low_x_ref[0], high_x_ref[0], low_y_ref[0, a], high_y_ref[0, a]
        )
        full_ref[56 * a : 56 * a + 56] = sheet.reshape(56, LANES)
    modes_ref[216:224] = jnp.zeros((8, LANES), F32)
    for compact, padded, rows in RUNS:
        modes_ref[compact : compact + rows] = full_ref[padded : padded + rows]


def multiply_blocks(schur_ref, class_ref, modes_ref, image_ref):
    mine = class_ref[0:1, :]
    modes = modes_ref[0:MODES]
    total = jnp.zeros((MODES, LANES), F32)
    for c in range(CLASSES):
        chosen = jnp.where(jnp.abs(mine - float(c)) < 0.5, modes, 0.0)
        total = total + jnp.dot(schur_ref[c], chosen, precision=HIGH, preferred_element_type=F32)
    image_ref[0:MODES] = total
    image_ref[MODES:224] = jnp.zeros((224 - MODES, LANES), F32)


def scatter_modes(image_ref, full_ref, out_ref, up_ref, down_ref):
    full_ref[...] = jnp.zeros((392, LANES), F32)
    for compact, padded, rows in RUNS:
        full_ref[padded : padded + rows] = image_ref[compact : compact + rows]
    for a in range(7):
        out_ref[0, a] = join_local(full_ref[56 * a : 56 * a + 56].reshape(7, 8, LANES))
    emit_faces(out_ref, up_ref, down_ref, 0)


def total_of(values):
    return jnp.sum(jnp.sum(values, axis=0, keepdims=True), axis=1, keepdims=True)


def first_apply_kernel(
    part_ref, low_x_ref, high_x_ref, low_y_ref, high_y_ref, schur_ref, class_ref,
    load_ref, image_ref, out_ref, up_ref, down_ref, full_ref,
):
    gather_modes(part_ref, low_x_ref, high_x_ref, low_y_ref, high_y_ref, full_ref, load_ref)
    multiply_blocks(schur_ref, class_ref, load_ref, image_ref)
    scatter_modes(image_ref, full_ref, out_ref, up_ref, down_ref)


def second_apply_kernel(
    part_ref, low_x_ref, high_x_ref, low_y_ref, high_y_ref, schur_ref, class_ref, load_ref,
    first_ref, shell_ref, power_ref, dots_ref, out_ref, up_ref, down_ref, image_ref, full_ref,
):
    gather_modes(part_ref, low_x_ref, high_x_ref, low_y_ref, high_y_ref, full_ref, power_ref)
    multiply_blocks(schur_ref, class_ref, power_ref, image_ref)
    scatter_modes(image_ref, full_ref, out_ref, up_ref, down_ref)
    load, power, shell = load_ref[...], power_ref[...], shell_ref[...]
    first, image = first_ref[...], image_ref[...]
    lane = lax.broadcasted_iota(jnp.int32, (1, LANES), 1)
    dots = jnp.zeros((1, LANES), F32)
    values = (
        load * load * shell, load * first, power * power * shell, load * image, power * image
    )
    for k, value in enumerate(values):
        dots = dots + jnp.where(lane == k, total_of(value), 0.0)
    dots_ref[...] = dots


def finish_kernel(
    part_ref, low_x_ref, high_x_ref, low_y_ref, high_y_ref, load_ref, power_ref, dots_ref, slot_ref,
    pressure_ref, residual_ref, full_ref, modes_ref,
):
    gather_modes(part_ref, low_x_ref, high_x_ref, low_y_ref, high_y_ref, full_ref, modes_ref)
    dots = jnp.sum(dots_ref[...], axis=0)
    square, energy, power_square, cross, power_energy = (dots[:, k : k + 1] for k in range(5))
    step = square / energy
    fresh = square - 2.0 * step * energy + step * step * power_square
    ratio = fresh / square
    grow = 1.0 + ratio
    curvature = (
        grow * grow * energy
        - step * grow * (cross + power_square)
        + step * step * power_energy
    )
    second = fresh / curvature
    load, power, twice = load_ref[...], power_ref[...], modes_ref[...]
    pressure = step * load + second * (grow * load - step * power)
    residual = load - step * power - second * (grow * power - step * twice)
    one_hot = permutation(slot_ref)
    pressure_ref[...] = jnp.dot(pressure, one_hot, precision=HIGH, preferred_element_type=F32)[:MODES]
    residual_ref[...] = jnp.dot(residual, one_hot, precision=HIGH, preferred_element_type=F32)[:MODES]


def call(kernel, outs, args, scratch=(), name=None):
    vmem = pl.BlockSpec(memory_space=pltpu.VMEM)
    return pl.pallas_call(
        kernel,
        out_shape=tuple(jax.ShapeDtypeStruct(shape, F32) for shape in outs),
        in_specs=[vmem] * len(args),
        out_specs=tuple([vmem] * len(outs)),
        scratch_shapes=[pltpu.VMEM(shape, F32) for shape in scratch],
        compiler_params=pltpu.CompilerParams(vmem_limit_bytes=48 << 20),
        name=name,
    )(*args)


def ring(axis, upward, downward):
    count = lax.axis_size(axis)
    up = [(i, (i + 1) % count) for i in range(count)]
    down = [(j, i) for i, j in up]
    return lax.ppermute(upward, axis, up), lax.ppermute(downward, axis, down)


def exchange(part, upward, downward):
    low_x, high_x = ring("slab", upward, downward)
    k = part.shape[0]
    up, down = call(
        side_kernel, [(k, 7, 8, LANES)] * 2, (part, low_x, high_x), name="side"
    )
    low_y, high_y = ring("dom", up, down)
    return part, low_x, high_x, low_y, high_y


def gather_sum(row, axis):
    count = lax.axis_size(axis)
    return lax.all_to_all(jnp.broadcast_to(row[None], (count, 1, LANES)), axis, 0, 0)


def per_device(velocity, slot_map, class_index, schur_blocks):
    slots = slot_map.reshape(1, LANES)
    rolls, span, shell = jnp.asarray(ROLLS), jnp.asarray(SPAN), jnp.asarray(SHELL)
    face = (7, 8, LANES)
    whole = (7, 7, 8, LANES)
    modes = (224, LANES)
    brick, part, up, down, classes = call(
        advect_kernel,
        [(3, *whole), (3, *whole), (3, *face), (3, *face), (8, LANES)],
        (velocity, slots, class_index.reshape(1, LANES), rolls),
        name="advect",
    )
    part, up, down = call(
        source_kernel,
        [(1, *whole), (1, *face), (1, *face)],
        (*exchange(part, up, down), brick, rolls, span),
        [(3, *whole)],
        name="source",
    )
    load, first, part, up, down = call(
        first_apply_kernel,
        [modes, modes, (1, *whole), (1, *face), (1, *face)],
        (*exchange(part, up, down), schur_blocks, classes),
        [(392, LANES)],
        name="first",
    )
    power, dots, part, up, down = call(
        second_apply_kernel,
        [modes, (1, LANES), (1, *whole), (1, *face), (1, *face)],
        (*exchange(part, up, down), schur_blocks, classes, load, first, shell),
        [modes, (392, LANES)],
        name="second",
    )
    dots = gather_sum(dots, "dom").sum(axis=0)
    dots = gather_sum(dots, "slab")
    return call(
        finish_kernel,
        [(MODES, LANES), (MODES, LANES)],
        (*exchange(part, up, down), load, power, dots, slots),
        [(392, LANES), modes],
        name="finish",
    )


def solution(mesh):
    return jax.shard_map(
        per_device,
        mesh=mesh,
        in_specs=(
            P(None, None, ("slab", "dom")),
            P("slab", "dom", None),
            P("slab", "dom", None),
            P(),
        ),
        out_specs=(P(None, ("slab", "dom")), P(None, ("slab", "dom"))),
        check_vma=False,
    )
```

time: 560 us -> 147 us (0.26); the launches traced: 551 us -> 145 us
  blocking collectives: 305 us -> 17 us
  local copies, waits for them, and re-layouts: 113 us -> 8.52 us
  matrix products: 17.9 us -> 0 us
  other arithmetic: 13.9 us -> 0.02 us
  Pallas kernels: 0 us -> 12.2 us
  starting transfers between devices: 85 us -> 96.6 us
    psum x3 -> x0, blocking collectives: 305 us -> none  [the longest x2 201 us: squares(): return lax.psum(weighted(vector, vector), ('slab', 'dom'))]
    transpose x7 -> x0, local copies, waits for them, and re-layouts: 37.7 us -> none  [the longest x4 25 us: from_lines(): cube_view.transpose(0, 2, 4, 6, 1, 3, 5)]
    reshape x13 -> x0, local copies, waits for them, and re-layouts: 32.5 us -> none  [the longest x4 13.1 us: from_lines(): cube_view = line_field.reshape(components, BX, 7, BY, 7, BZ, 7)]
    another operation x8 -> x0, local copies, waits for them, and re-layouts: 20 us -> none  [the longest x2 14.7 us: to_lines(): cube_view = nodal_field.reshape(components, 7, 7, 7, BX, BY, BZ)]
    dot_general x8 -> x0, matrix products: 17.9 us -> none  [the longest x2 13.7 us: per_device(): jnp.einsum('cij,jcn->icn', schur_blocks, grouped, precision=lax.Precision...]
    all_to_all x0 -> x1, blocking collectives: none -> 17 us  [gather_sum(): lax.all_to_all(jnp.broadcast_to(row[None], (count, 1, LANES)), axis, 0, 0)]
    all_to_all x0 -> x1, starting transfers between devices: none -> 13.4 us  [gather_sum(): lax.all_to_all(jnp.broadcast_to(row[None], (count, 1, LANES)), axis, 0, 0)]
    pallas_call x0 -> x9, Pallas kernels: none -> 12.2 us  [call(): pl.pallas_call(kernel, out_shape=tuple((jax.ShapeDtypeStruct(shape, F32)...]
  transfers between devices with their start and end apart: 16 -> 17, of which waited for: 7 -> 7; matrix products, arithmetic and copies ran while one was open for 1% -> 3% of each run, Pallas kernels for 0% -> 0%
where the time goes in v1:
time: 147 us; the launch traced here: 145 us
  starting transfers between devices  96.6 us (66%)
  blocking collectives  17 us (12%)
  Pallas kernels  12.2 us (8%)
  waiting for transfers between devices  9.85 us (7%)
  local copies, waits for them, and re-layouts  8.52 us (6%)
    ppermute x16, starting transfers between devices, ring(): return (lax.ppermute(upward, axis, up), lax.ppermute(downward, axis, down))  83.2 us
    all_to_all x1, blocking collectives, gather_sum(): lax.all_to_all(jnp.broadcast_to(row[None], (count, 1, LANES)), axis, 0, 0)  17 us
    all_to_all x1, starting transfers between devices, gather_sum(): lax.all_to_all(jnp.broadcast_to(row[None], (count, 1, LANES)), axis, 0, 0)  13.4 us
    pallas_call x9, Pallas kernels, call(): pl.pallas_call(kernel, out_shape=tuple((jax.ShapeDtypeStruct(shape, F32)...  12.2 us
    ppermute x16, waiting for transfers between devices, ring(): return (lax.ppermute(upward, axis, up), lax.ppermute(downward, axis, down))  8.2 us
    unnamed x15, local copies, waits for them, and re-layouts  7.9 us
  transfers between devices with their start and end apart: 17, of which 7 were waited for; matrix products, arithmetic and copies ran while one was open for 3% of the time, Pallas kernels for 0%

profile of v1, /device:TPU:1, one launch (start us, length us, event | category | flops | bytes accessed | tf_op | source)
XLA Modules:
  0.0 145.0 jit_solution(14804766246834463917)
XLA Ops:
  0.6 0.0 copy-start
  0.6 1.0 copy-done
  1.7 0.0 copy-start.1
  1.7 0.8 copy-done.1
  2.4 0.0 copy-start.4
  2.4 0.7 copy-done.4
  3.1 0.0 copy-start.6
  3.1 0.7 copy-done.6
  3.7 2.8 %advect.1 = (f32[3,7,7,8,128]{4,3,2,1,0:T(8,128)S(1)}, f32[3,7,7,8,128]{4,3,2,1,0:T(8,128)S(1)}, f32[3,7,8,128]{3,2,1,0:T(8,128)S(1)}, f32[3,7,8,128]{3,2,1,0:T(8,128)S(1)}, f32[8,128]{1,0:T(8,128)S(1)}) custom-call(f32[3,343,128]{2,1,0:T(8,128)S(1)} %copy-done, s32[1,128]{1,0:T(1,128)S(1)} %bitcast.4, s32[1,128]{1,0:T(1,128)S(1)} %bitcast.7, ...), custom_call_target="tpu_custom_call" | custom-call | tf_op jit(solution)/shard_map/advect/pallas_call | solution.py:304
  6.6 4.0 %collective-permute-start = (f32[3,7,8,128]{3,2,1,0:T(8,128)S(1)}, f32[3,7,8,128]{3,2,1,0:T(8,128)S(1)}, u32[]{:S(2)}, u32[]{:S(2)}) collective-permute-start(f32[3,7,8,128]{3,2,1,0:T(8,128)S(1)} %get-tuple-element.29), channel_id=1, source_target_pairs={{0,32},{32,64},{64,96},{96,128},{128,160},{160,192},{192,224},{224... | collective-permute-start | bytes 258056 | tf_op jit(solution)/shard_map/ppermute | solution.py:319
  10.6 12.3 %collective-permute-start.1 = (f32[3,7,8,128]{3,2,1,0:T(8,128)S(1)}, f32[3,7,8,128]{3,2,1,0:T(8,128)S(1)}, u32[]{:S(2)}, u32[]{:S(2)}) collective-permute-start(f32[3,7,8,128]{3,2,1,0:T(8,128)S(1)} %get-tuple-element.30), channel_id=1, source_target_pairs={{32,0},{64,32},{96,64},{128,96},{160,128},{192,160},{224,192},{256... | collective-permute-start | bytes 258056 | tf_op jit(solution)/shard_map/ppermute | solution.py:319
  22.9 0.8 collective-permute-done.low_x_ref
  23.7 0.7 collective-permute-done.1.high_x_ref
  24.4 0.1 side.4
  24.5 4.9 %collective-permute-start.2 = (f32[3,7,8,128]{3,2,1,0:T(8,128)S(1)}, f32[3,7,8,128]{3,2,1,0:T(8,128)S(1)}, u32[]{:S(2)}, u32[]{:S(2)}) collective-permute-start(f32[3,7,8,128]{3,2,1,0:T(8,128)S(1)} %get-tuple-element.31), channel_id=1, source_target_pairs={{0,1},{1,2},{2,3},{3,4},{4,5},{5,6},{6,7},{7,8},{8,9},{9,10},{10,1... | collective-permute-start | bytes 258056 | tf_op jit(solution)/shard_map/ppermute | solution.py:319
  29.4 2.0 %collective-permute-start.3 = (f32[3,7,8,128]{3,2,1,0:T(8,128)S(1)}, f32[3,7,8,128]{3,2,1,0:T(8,128)S(1)}, u32[]{:S(2)}, u32[]{:S(2)}) collective-permute-start(f32[3,7,8,128]{3,2,1,0:T(8,128)S(1)} %get-tuple-element.32), channel_id=1, source_target_pairs={{1,0},{2,1},{3,2},{4,3},{5,4},{6,5},{7,6},{8,7},{9,8},{10,9},{11,1... | collective-permute-start | bytes 258056 | tf_op jit(solution)/shard_map/ppermute | solution.py:319
  31.4 0.0 collective-permute-done.2.low_y_ref
  31.4 4.1 %collective-permute-done.3.high_y_ref = f32[3,7,8,128]{3,2,1,0:T(8,128)S(1)} collective-permute-done((f32[3,7,8,128]{3,2,1,0:T(8,128)S(1)}, f32[3,7,8,128]{3,2,1,0:T(8,128)S(1)}, u32[]{:S(2)}, u32[]{:S(2)}) %collective-permute-start.3) | collective-permute-done | bytes 86048 | tf_op jit(solution)/shard_map/ppermute | solution.py:319
  35.5 0.0 copy-start.3
  35.5 0.7 copy-done.3
  36.2 0.6 source.1
  36.8 1.9 %collective-permute-start.4 = (f32[1,7,8,128]{3,2,1,0:T(8,128)S(1)}, f32[1,7,8,128]{3,2,1,0:T(8,128)S(1)}, u32[]{:S(2)}, u32[]{:S(2)}) collective-permute-start(f32[1,7,8,128]{3,2,1,0:T(8,128)S(1)} %get-tuple-element.35), channel_id=1, source_target_pairs={{0,32},{32,64},{64,96},{96,128},{128,160},{160,192},{192,224},{224... | collective-permute-start | bytes 86024 | tf_op jit(solution)/shard_map/ppermute | solution.py:319
  38.7 11.3 %collective-permute-start.5 = (f32[1,7,8,128]{3,2,1,0:T(8,128)S(1)}, f32[1,7,8,128]{3,2,1,0:T(8,128)S(1)}, u32[]{:S(2)}, u32[]{:S(2)}) collective-permute-start(f32[1,7,8,128]{3,2,1,0:T(8,128)S(1)} %get-tuple-element.36), channel_id=1, source_target_pairs={{32,0},{64,32},{96,64},{128,96},{160,128},{192,160},{224,192},{256... | collective-permute-start | bytes 86024 | tf_op jit(solution)/shard_map/ppermute | solution.py:319
  50.1 0.0 collective-permute-done.4.low_x_ref
  50.1 1.0 collective-permute-done.5.high_x_ref
  51.0 0.1 side.5
  51.1 2.4 %collective-permute-start.6 = (f32[1,7,8,128]{3,2,1,0:T(8,128)S(1)}, f32[1,7,8,128]{3,2,1,0:T(8,128)S(1)}, u32[]{:S(2)}, u32[]{:S(2)}) collective-permute-start(f32[1,7,8,128]{3,2,1,0:T(8,128)S(1)} %get-tuple-element.37), channel_id=1, source_target_pairs={{0,1},{1,2},{2,3},{3,4},{4,5},{5,6},{6,7},{7,8},{8,9},{9,10},{10,1... | collective-permute-start | bytes 86024 | tf_op jit(solution)/shard_map/ppermute | solution.py:319
  53.5 4.7 %collective-permute-start.7 = (f32[1,7,8,128]{3,2,1,0:T(8,128)S(1)}, f32[1,7,8,128]{3,2,1,0:T(8,128)S(1)}, u32[]{:S(2)}, u32[]{:S(2)}) collective-permute-start(f32[1,7,8,128]{3,2,1,0:T(8,128)S(1)} %get-tuple-element.38), channel_id=1, source_target_pairs={{1,0},{2,1},{3,2},{4,3},{5,4},{6,5},{7,6},{8,7},{9,8},{10,9},{11,1... | collective-permute-start | bytes 86024 | tf_op jit(solution)/shard_map/ppermute | solution.py:319
  58.3 4.1 %copy.13.schur_ref = f32[16,218,218]{2,1,0:T(8,128)S(1)} copy(f32[16,218,218]{2,0,1:T(8,128)} %param.10) | data formatting | bytes 6083072 | tf_op args[3]
  62.3 0.0 copy-start.2
  62.4 0.0 collective-permute-done.6.low_y_ref
  62.4 0.0 collective-permute-done.7.high_y_ref
  62.4 0.0 copy-start.5
  62.4 3.6 %first.1 = (f32[224,128]{1,0:T(8,128)S(1)}, f32[224,128]{1,0:T(8,128)S(1)}, f32[1,7,7,8,128]{4,3,2,1,0:T(8,128)S(1)}, f32[1,7,8,128]{3,2,1,0:T(8,128)S(1)}, f32[1,7,8,128]{3,2,1,0:T(8,128)S(1)}) custom-call(f32[1,7,7,8,128]{4,3,2,1,0:T(8,128)S(1)} %get-tuple-element.34.part_ref, f32[1,7,8,128]{3,2,1,0:T(8,128)S(1)} %collective-permute-done.4.low_x_ref, ...), custom_call_target="tpu_custom_call" | custom-call | tf_op jit(solution)/shard_map/first/pallas_call | solution.py:304
  66.0 1.9 %collective-permute-start.8 = (f32[1,7,8,128]{3,2,1,0:T(8,128)S(1)}, f32[1,7,8,128]{3,2,1,0:T(8,128)S(1)}, u32[]{:S(2)}, u32[]{:S(2)}) collective-permute-start(f32[1,7,8,128]{3,2,1,0:T(8,128)S(1)} %get-tuple-element.41), channel_id=1, source_target_pairs={{0,32},{32,64},{64,96},{96,128},{128,160},{160,192},{192,224},{224... | collective-permute-start | bytes 86024 | tf_op jit(solution)/shard_map/ppermute | solution.py:319
  67.9 10.0 %collective-permute-start.9 = (f32[1,7,8,128]{3,2,1,0:T(8,128)S(1)}, f32[1,7,8,128]{3,2,1,0:T(8,128)S(1)}, u32[]{:S(2)}, u32[]{:S(2)}) collective-permute-start(f32[1,7,8,128]{3,2,1,0:T(8,128)S(1)} %get-tuple-element.42), channel_id=1, source_target_pairs={{32,0},{64,32},{96,64},{128,96},{160,128},{192,160},{224,192},{256... | collective-permute-start | bytes 86024 | tf_op jit(solution)/shard_map/ppermute | solution.py:319
  77.8 0.0 collective-permute-done.8.low_x_ref
  77.9 1.0 collective-permute-done.9.high_x_ref
  78.8 0.1 side.6
  78.9 1.9 %collective-permute-start.10 = (f32[1,7,8,128]{3,2,1,0:T(8,128)S(1)}, f32[1,7,8,128]{3,2,1,0:T(8,128)S(1)}, u32[]{:S(2)}, u32[]{:S(2)}) collective-permute-start(f32[1,7,8,128]{3,2,1,0:T(8,128)S(1)} %get-tuple-element.43), channel_id=1, source_target_pairs={{0,1},{1,2},{2,3},{3,4},{4,5},{5,6},{6,7},{7,8},{8,9},{9,10},{10,1... | collective-permute-start | bytes 86024 | tf_op jit(solution)/shard_map/ppermute | solution.py:319
  80.8 8.6 %collective-permute-start.11 = (f32[1,7,8,128]{3,2,1,0:T(8,128)S(1)}, f32[1,7,8,128]{3,2,1,0:T(8,128)S(1)}, u32[]{:S(2)}, u32[]{:S(2)}) collective-permute-start(f32[1,7,8,128]{3,2,1,0:T(8,128)S(1)} %get-tuple-element.44), channel_id=1, source_target_pairs={{1,0},{2,1},{3,2},{4,3},{5,4},{6,5},{7,6},{8,7},{9,8},{10,9},{11,1... | collective-permute-start | bytes 86024 | tf_op jit(solution)/shard_map/ppermute | solution.py:319
  89.4 0.0 collective-permute-done.10.low_y_ref
  89.4 0.6 collective-permute-done.11.high_y_ref
  90.1 0.0 copy-done.2
  90.1 3.6 %second.1 = (f32[224,128]{1,0:T(8,128)S(1)}, f32[1,128]{1,0:T(1,128)S(1)}, f32[1,7,7,8,128]{4,3,2,1,0:T(8,128)S(1)}, f32[1,7,8,128]{3,2,1,0:T(8,128)S(1)}, f32[1,7,8,128]{3,2,1,0:T(8,128)S(1)}) custom-call(f32[1,7,7,8,128]{4,3,2,1,0:T(8,128)S(1)} %get-tuple-element.40.part_ref, f32[1,7,8,128]{3,2,1,0:T(8,128)S(1)} %collective-permute-done.8.low_x_ref, ...), custom_call_target="tpu_custom_call" | custom-call | tf_op jit(solution)/shard_map/second/pallas_call | solution.py:304
  93.6 1.9 %collective-permute-start.12 = (f32[1,7,8,128]{3,2,1,0:T(8,128)S(1)}, f32[1,7,8,128]{3,2,1,0:T(8,128)S(1)}, u32[]{:S(2)}, u32[]{:S(2)}) collective-permute-start(f32[1,7,8,128]{3,2,1,0:T(8,128)S(1)} %get-tuple-element.48), channel_id=1, source_target_pairs={{0,32},{32,64},{64,96},{96,128},{128,160},{160,192},{192,224},{224... | collective-permute-start | bytes 86024 | tf_op jit(solution)/shard_map/ppermute | solution.py:319
  95.6 10.0 %collective-permute-start.13 = (f32[1,7,8,128]{3,2,1,0:T(8,128)S(1)}, f32[1,7,8,128]{3,2,1,0:T(8,128)S(1)}, u32[]{:S(2)}, u32[]{:S(2)}) collective-permute-start(f32[1,7,8,128]{3,2,1,0:T(8,128)S(1)} %get-tuple-element.49), channel_id=1, source_target_pairs={{32,0},{64,32},{96,64},{128,96},{160,128},{192,160},{224,192},{256... | collective-permute-start | bytes 86024 | tf_op jit(solution)/shard_map/ppermute | solution.py:319
  105.5 0.6 broadcast_in_dim.7
  106.2 13.4 %all-to-all-start = ((f32[32,1,128]{2,1,0:T(1,128)}), f32[32,1,128]{2,1,0:T(1,128)S(1)}, u32[]{:S(2)}, u32[]{:S(2)}) async-start(f32[32,1,128]{2,1,0:T(1,128)} %broadcast_in_dim.7), calls=%async_computation | async-start | bytes 32768 | tf_op jit(solution)/shard_map/all_to_all | solution.py:334
  119.6 0.0 collective-permute-done.12.low_x_ref
  119.6 0.0 collective-permute-done.13.high_x_ref
  119.6 0.1 side.7
  119.7 3.5 %collective-permute-start.14 = (f32[1,7,8,128]{3,2,1,0:T(8,128)S(1)}, f32[1,7,8,128]{3,2,1,0:T(8,128)S(1)}, u32[]{:S(2)}, u32[]{:S(2)}) collective-permute-start(f32[1,7,8,128]{3,2,1,0:T(8,128)S(1)} %get-tuple-element.50), channel_id=1, source_target_pairs={{0,1},{1,2},{2,3},{3,4},{4,5},{5,6},{6,7},{7,8},{8,9},{9,10},{10,1... | collective-permute-start | bytes 86024 | tf_op jit(solution)/shard_map/ppermute | solution.py:319
  123.2 1.9 %collective-permute-start.15 = (f32[1,7,8,128]{3,2,1,0:T(8,128)S(1)}, f32[1,7,8,128]{3,2,1,0:T(8,128)S(1)}, u32[]{:S(2)}, u32[]{:S(2)}) collective-permute-start(f32[1,7,8,128]{3,2,1,0:T(8,128)S(1)} %get-tuple-element.51), channel_id=1, source_target_pairs={{1,0},{2,1},{3,2},{4,3},{5,4},{6,5},{7,6},{8,7},{9,8},{10,9},{11,1... | collective-permute-start | bytes 86024 | tf_op jit(solution)/shard_map/ppermute | solution.py:319
  125.2 1.7 %all-to-all-done = f32[32,1,128]{2,1,0:T(1,128)S(1)} async-done(((f32[32,1,128]{2,1,0:T(1,128)}), f32[32,1,128]{2,1,0:T(1,128)S(1)}, u32[]{:S(2)}, u32[]{:S(2)}) %all-to-all-start) | async-done | bytes 16416 | tf_op jit(solution)/shard_map/all_to_all | solution.py:334
  126.8 17.0 %all_to_all.10.dots_ref = f32[16,1,128]{2,1,0:T(1,128)S(1)} all-to-all(f32[16,1,128]{2,1,0:T(1,128)S(1)} %broadcast_in_dim.16), channel_id=1, replica_groups=mesh['slab'=16,'dom'=32] {'slab'}, dimensions={0} | all-to-all | bytes 16384 | tf_op jit(solution)/shard_map/all_to_all | solution.py:334
  143.8 0.0 collective-permute-done.14.low_y_ref
  143.8 0.0 collective-permute-done.15.high_y_ref
  143.8 0.0 copy-done.5
  143.8 1.2 finish.1
  (2 shorter events, 0.0 us)
Async XLA Ops:
  0.6 1.0 copy-start
  1.7 0.8 copy-start.1
  2.4 0.7 copy-start.4
  3.1 0.7 copy-start.6
  6.6 17.1 %collective-permute-start = (f32[3,7,8,128]{3,2,1,0:T(8,128)S(1)}, f32[3,7,8,128]{3,2,1,0:T(8,128)S(1)}, u32[]{:S(2)}, u32[]{:S(2)}) collective-permute-start(f32[3,7,8,128]{3,2,1,0:T(8,128)S(1)} %get-tuple-element.29), channel_id=1, source_target_pairs={{0,32},{32,64},{64,96},{96,128},{128,160},{160,192},{192,224},{224... | collective-permute-start | bytes 258056 | tf_op jit(solution)/shard_map/ppermute | solution.py:319
  10.6 13.8 %collective-permute-start.1 = (f32[3,7,8,128]{3,2,1,0:T(8,128)S(1)}, f32[3,7,8,128]{3,2,1,0:T(8,128)S(1)}, u32[]{:S(2)}, u32[]{:S(2)}) collective-permute-start(f32[3,7,8,128]{3,2,1,0:T(8,128)S(1)} %get-tuple-element.30), channel_id=1, source_target_pairs={{32,0},{64,32},{96,64},{128,96},{160,128},{192,160},{224,192},{256... | collective-permute-start | bytes 258056 | tf_op jit(solution)/shard_map/ppermute | solution.py:319
  24.5 6.9 %collective-permute-start.2 = (f32[3,7,8,128]{3,2,1,0:T(8,128)S(1)}, f32[3,7,8,128]{3,2,1,0:T(8,128)S(1)}, u32[]{:S(2)}, u32[]{:S(2)}) collective-permute-start(f32[3,7,8,128]{3,2,1,0:T(8,128)S(1)} %get-tuple-element.31), channel_id=1, source_target_pairs={{0,1},{1,2},{2,3},{3,4},{4,5},{5,6},{6,7},{7,8},{8,9},{9,10},{10,1... | collective-permute-start | bytes 258056 | tf_op jit(solution)/shard_map/ppermute | solution.py:319
  29.4 6.1 %collective-permute-start.3 = (f32[3,7,8,128]{3,2,1,0:T(8,128)S(1)}, f32[3,7,8,128]{3,2,1,0:T(8,128)S(1)}, u32[]{:S(2)}, u32[]{:S(2)}) collective-permute-start(f32[3,7,8,128]{3,2,1,0:T(8,128)S(1)} %get-tuple-element.32), channel_id=1, source_target_pairs={{1,0},{2,1},{3,2},{4,3},{5,4},{6,5},{7,6},{8,7},{9,8},{10,9},{11,1... | collective-permute-start | bytes 258056 | tf_op jit(solution)/shard_map/ppermute | solution.py:319
  35.5 0.7 copy-start.3
  36.8 13.2 %collective-permute-start.4 = (f32[1,7,8,128]{3,2,1,0:T(8,128)S(1)}, f32[1,7,8,128]{3,2,1,0:T(8,128)S(1)}, u32[]{:S(2)}, u32[]{:S(2)}) collective-permute-start(f32[1,7,8,128]{3,2,1,0:T(8,128)S(1)} %get-tuple-element.35), channel_id=1, source_target_pairs={{0,32},{32,64},{64,96},{96,128},{128,160},{160,192},{192,224},{224... | collective-permute-start | bytes 86024 | tf_op jit(solution)/shard_map/ppermute | solution.py:319
  38.7 12.3 %collective-permute-start.5 = (f32[1,7,8,128]{3,2,1,0:T(8,128)S(1)}, f32[1,7,8,128]{3,2,1,0:T(8,128)S(1)}, u32[]{:S(2)}, u32[]{:S(2)}) collective-permute-start(f32[1,7,8,128]{3,2,1,0:T(8,128)S(1)} %get-tuple-element.36), channel_id=1, source_target_pairs={{32,0},{64,32},{96,64},{128,96},{160,128},{192,160},{224,192},{256... | collective-permute-start | bytes 86024 | tf_op jit(solution)/shard_map/ppermute | solution.py:319
  51.1 11.3 %collective-permute-start.6 = (f32[1,7,8,128]{3,2,1,0:T(8,128)S(1)}, f32[1,7,8,128]{3,2,1,0:T(8,128)S(1)}, u32[]{:S(2)}, u32[]{:S(2)}) collective-permute-start(f32[1,7,8,128]{3,2,1,0:T(8,128)S(1)} %get-tuple-element.37), channel_id=1, source_target_pairs={{0,1},{1,2},{2,3},{3,4},{4,5},{5,6},{6,7},{7,8},{8,9},{9,10},{10,1... | collective-permute-start | bytes 86024 | tf_op jit(solution)/shard_map/ppermute | solution.py:319
  53.5 8.9 %collective-permute-start.7 = (f32[1,7,8,128]{3,2,1,0:T(8,128)S(1)}, f32[1,7,8,128]{3,2,1,0:T(8,128)S(1)}, u32[]{:S(2)}, u32[]{:S(2)}) collective-permute-start(f32[1,7,8,128]{3,2,1,0:T(8,128)S(1)} %get-tuple-element.38), channel_id=1, source_target_pairs={{1,0},{2,1},{3,2},{4,3},{5,4},{6,5},{7,6},{8,7},{9,8},{10,9},{11,1... | collective-permute-start | bytes 86024 | tf_op jit(solution)/shard_map/ppermute | solution.py:319
  62.3 27.7 %copy-start.2 = (f32[224,128]{1,0:T(8,128)S(1)}, f32[224,128]{1,0:T(8,128)}, u32[]{:S(2)}) copy-start(f32[224,128]{1,0:T(8,128)} %constant.10.clone.shell_ref) | copy-start | bytes 344068
  62.4 81.4 %copy-start.5 = (s32[1,1,128]{2,1,0:T(1,128)S(1)}, s32[1,1,128]{2,1,0:T(1,128)}, u32[]{:S(2)}) copy-start(s32[1,1,128]{2,1,0:T(1,128)} %param.8) | copy-start | bytes 1540
  66.0 11.9 %collective-permute-start.8 = (f32[1,7,8,128]{3,2,1,0:T(8,128)S(1)}, f32[1,7,8,128]{3,2,1,0:T(8,128)S(1)}, u32[]{:S(2)}, u32[]{:S(2)}) collective-permute-start(f32[1,7,8,128]{3,2,1,0:T(8,128)S(1)} %get-tuple-element.41), channel_id=1, source_target_pairs={{0,32},{32,64},{64,96},{96,128},{128,160},{160,192},{192,224},{224... | collective-permute-start | bytes 86024 | tf_op jit(solution)/shard_map/ppermute | solution.py:319
  67.9 10.9 %collective-permute-start.9 = (f32[1,7,8,128]{3,2,1,0:T(8,128)S(1)}, f32[1,7,8,128]{3,2,1,0:T(8,128)S(1)}, u32[]{:S(2)}, u32[]{:S(2)}) collective-permute-start(f32[1,7,8,128]{3,2,1,0:T(8,128)S(1)} %get-tuple-element.42), channel_id=1, source_target_pairs={{32,0},{64,32},{96,64},{128,96},{160,128},{192,160},{224,192},{256... | collective-permute-start | bytes 86024 | tf_op jit(solution)/shard_map/ppermute | solution.py:319
  78.9 10.5 %collective-permute-start.10 = (f32[1,7,8,128]{3,2,1,0:T(8,128)S(1)}, f32[1,7,8,128]{3,2,1,0:T(8,128)S(1)}, u32[]{:S(2)}, u32[]{:S(2)}) collective-permute-start(f32[1,7,8,128]{3,2,1,0:T(8,128)S(1)} %get-tuple-element.43), channel_id=1, source_target_pairs={{0,1},{1,2},{2,3},{3,4},{4,5},{5,6},{6,7},{7,8},{8,9},{9,10},{10,1... | collective-permute-start | bytes 86024 | tf_op jit(solution)/shard_map/ppermute | solution.py:319
  80.8 9.2 %collective-permute-start.11 = (f32[1,7,8,128]{3,2,1,0:T(8,128)S(1)}, f32[1,7,8,128]{3,2,1,0:T(8,128)S(1)}, u32[]{:S(2)}, u32[]{:S(2)}) collective-permute-start(f32[1,7,8,128]{3,2,1,0:T(8,128)S(1)} %get-tuple-element.44), channel_id=1, source_target_pairs={{1,0},{2,1},{3,2},{4,3},{5,4},{6,5},{7,6},{8,7},{9,8},{10,9},{11,1... | collective-permute-start | bytes 86024 | tf_op jit(solution)/shard_map/ppermute | solution.py:319
  93.6 25.9 %collective-permute-start.12 = (f32[1,7,8,128]{3,2,1,0:T(8,128)S(1)}, f32[1,7,8,128]{3,2,1,0:T(8,128)S(1)}, u32[]{:S(2)}, u32[]{:S(2)}) collective-permute-start(f32[1,7,8,128]{3,2,1,0:T(8,128)S(1)} %get-tuple-element.48), channel_id=1, source_target_pairs={{0,32},{32,64},{64,96},{96,128},{128,160},{160,192},{192,224},{224... | collective-permute-start | bytes 86024 | tf_op jit(solution)/shard_map/ppermute | solution.py:319
  95.6 24.0 %collective-permute-start.13 = (f32[1,7,8,128]{3,2,1,0:T(8,128)S(1)}, f32[1,7,8,128]{3,2,1,0:T(8,128)S(1)}, u32[]{:S(2)}, u32[]{:S(2)}) collective-permute-start(f32[1,7,8,128]{3,2,1,0:T(8,128)S(1)} %get-tuple-element.49), channel_id=1, source_target_pairs={{32,0},{64,32},{96,64},{128,96},{160,128},{192,160},{224,192},{256... | collective-permute-start | bytes 86024 | tf_op jit(solution)/shard_map/ppermute | solution.py:319
  106.2 20.7 %all-to-all-start = ((f32[32,1,128]{2,1,0:T(1,128)}), f32[32,1,128]{2,1,0:T(1,128)S(1)}, u32[]{:S(2)}, u32[]{:S(2)}) async-start(f32[32,1,128]{2,1,0:T(1,128)} %broadcast_in_dim.7), calls=%async_computation | async-start | bytes 32768 | tf_op jit(solution)/shard_map/all_to_all | solution.py:334
  119.7 24.1 %collective-permute-start.14 = (f32[1,7,8,128]{3,2,1,0:T(8,128)S(1)}, f32[1,7,8,128]{3,2,1,0:T(8,128)S(1)}, u32[]{:S(2)}, u32[]{:S(2)}) collective-permute-start(f32[1,7,8,128]{3,2,1,0:T(8,128)S(1)} %get-tuple-element.50), channel_id=1, source_target_pairs={{0,1},{1,2},{2,3},{3,4},{4,5},{5,6},{6,7},{7,8},{8,9},{9,10},{10,1... | collective-permute-start | bytes 86024 | tf_op jit(solution)/shard_map/ppermute | solution.py:319
  123.2 20.6 %collective-permute-start.15 = (f32[1,7,8,128]{3,2,1,0:T(8,128)S(1)}, f32[1,7,8,128]{3,2,1,0:T(8,128)S(1)}, u32[]{:S(2)}, u32[]{:S(2)}) collective-permute-start(f32[1,7,8,128]{3,2,1,0:T(8,128)S(1)} %get-tuple-element.51), channel_id=1, source_target_pairs={{1,0},{2,1},{3,2},{4,3},{5,4},{6,5},{7,6},{8,7},{9,8},{10,9},{11,1... | collective-permute-start | bytes 86024 | tf_op jit(solution)/shard_map/ppermute | solution.py:319

commit v2 on v1

v2 whole, which is shorter than its diff:
```python
import jax
import jax.numpy as jnp
import numpy as np
from jax import lax
from jax.experimental import pallas as pl
from jax.experimental.pallas import tpu as pltpu
from jax.sharding import PartitionSpec as P

CLASSES = 16
MODES = 218
NODES = 343
LANES = 128
BZ = 16
BY = 8
DELTA_T = 0.05
HIGH = lax.Precision.HIGHEST
F32 = jnp.float32


def gll_tables():
    degree = 6
    outer_point = 0.830223896278567
    inner_point = 0.46884879347071423
    points = np.array([-1.0, -outer_point, -inner_point, 0.0, inner_point, outer_point, 1.0])
    values = (231.0 * points**6 - 315.0 * points**4 + 105.0 * points**2 - 5.0) / 16.0
    weights = 2.0 / (degree * (degree + 1) * values**2)
    derivative = np.zeros((7, 7))
    for target in range(7):
        for source in range(7):
            if target != source:
                derivative[target, source] = values[target] / (
                    values[source] * (points[target] - points[source])
                )
    derivative[0, 0] = -degree * (degree + 1) / 4.0
    derivative[6, 6] = degree * (degree + 1) / 4.0
    return derivative, weights


DERIV, WEIGHTS = gll_tables()
FACTOR = np.where((np.arange(7) == 0) | (np.arange(7) == 6), 2.0, 1.0)


def shell_runs():
    runs, offset = [], 0
    for a in range(7):
        for b in range(7):
            base = 8 * (7 * a + b)
            if a in (0, 6) or b in (0, 6):
                runs.append((offset, base, 7))
                offset += 7
            else:
                runs.append((offset, base, 1))
                runs.append((offset + 1, base + 6, 1))
                offset += 2
    return runs


RUNS = shell_runs()


def shell_table():
    multiple = (FACTOR[:, None, None] * FACTOR[None, :, None] * FACTOR[None, None, :]).reshape(-1)
    surface = [
        i for i in range(NODES) if i // 49 in (0, 6) or i // 7 % 7 in (0, 6) or i % 7 in (0, 6)
    ]
    shell = np.zeros((224, LANES))
    shell[:MODES] = (1.0 / multiple[surface])[:, None]
    return shell.astype(np.float32)


SHELL = shell_table()


def span_vector(values):
    node = lax.broadcasted_iota(jnp.int32, (8, LANES), 0)
    table = jnp.zeros((8, LANES), F32)
    for c in range(7):
        table = jnp.where(node == c, float(values[c]), table)
    return table


def span_rolls():
    tables = []
    for shift in range(8):
        sources = [(target - shift) % 8 for target in range(7)]
        tables.append(
            span_vector([DERIV[t, c] if c < 7 else 0.0 for t, c in zip(range(7), sources)])
        )
    return tables


def even_place(axis, like):
    return jnp.full(like.shape, lax.axis_index(axis) % 2, jnp.int32) == 0


def lower_upper(axis, near, far):
    even = even_place(axis, near)
    return jnp.where(even, far, near), jnp.where(even, near, far)


def iotas(shape):
    lane = lax.broadcasted_iota(jnp.int32, shape, len(shape) - 1)
    node = lax.broadcasted_iota(jnp.int32, shape, len(shape) - 2)
    return lane % BZ, lane // BZ, node


def join_local(sheet):
    bz, by, node = iotas(sheet.shape)
    low = pltpu.roll(sheet, 2, 1)
    low = jnp.where(bz == 0, pltpu.roll(low, LANES - 15, 2), pltpu.roll(low, 1, 2))
    high = pltpu.roll(sheet, 6, 1)
    high = jnp.where(bz == BZ - 1, pltpu.roll(high, 15, 2), pltpu.roll(high, LANES - 1, 2))
    sheet = sheet + jnp.where(node == 0, low, jnp.where(node == 6, high, 0.0))
    first, last = sheet[0], sheet[6]
    first_by = by[0]
    new_first = first + jnp.where(first_by > 0, pltpu.roll(last, BZ, 1), 0.0)
    new_last = last + jnp.where(first_by < BY - 1, pltpu.roll(first, LANES - BZ, 1), 0.0)
    return jnp.concatenate([new_first[None], sheet[1:6], new_last[None]], axis=0)


def add_received(a, sheet, far_x, near_x, far_y, near_y):
    if a == 0:
        sheet = sheet + lower_upper("slab", near_x, far_x)[0]
    if a == 6:
        sheet = sheet + lower_upper("slab", near_x, far_x)[1]
    low_y, high_y = lower_upper("dom", near_y, far_y)
    _, by, _ = iotas(sheet.shape[1:])
    first = sheet[0] + jnp.where(by == 0, low_y, 0.0)
    last = sheet[6] + jnp.where(by == BY - 1, high_y, 0.0)
    return jnp.concatenate([first[None], sheet[1:6], last[None]], axis=0)


def derive_sheets(sheets, target):
    total = float(DERIV[target, 0]) * sheets[0]
    for source in range(1, 7):
        total = total + float(DERIV[target, source]) * sheets[source]
    return total


def derive_span(rolls, sheet):
    total = rolls[0] * sheet
    for shift in range(1, 8):
        total = total + rolls[shift] * pltpu.roll(sheet, shift, 1)
    return total


def permutation(slot_ref):
    position = lax.broadcasted_iota(jnp.int32, (LANES, LANES), 0)
    return jnp.where(position == slot_ref[...], 1.0, 0.0).astype(F32)


def emit_faces(part_ref, far_ref, near_ref, index):
    low, high = part_ref[index, 0], part_ref[index, 6]
    even = even_place("slab", low)
    far_ref[index] = jnp.where(even, low, high)
    near_ref[index] = jnp.where(even, high, low)


def advect_kernel(
    vel_hbm, slot_hbm, class_hbm,
    brick_ref, part_ref, far_ref, near_ref, class_out,
    vel_ref, slot_ref, class_ref, sems,
):
    copies = [
        pltpu.make_async_copy(src, dst, sems.at[k])
        for k, (src, dst) in enumerate(
            ((slot_hbm, slot_ref), (class_hbm, class_ref), (vel_hbm, vel_ref))
        )
    ]
    for copy in copies:
        copy.start()
    rolls = span_rolls()
    brick_ref[:, :, :, 7:8, :] = jnp.zeros((3, 7, 7, 1, LANES), F32)
    copies[0].wait()
    copies[1].wait()
    one_hot = permutation(slot_ref)
    nt = (((1,), (1,)), ((), ()))
    class_out[...] = lax.dot_general(
        jnp.broadcast_to(class_ref[...].astype(F32), (8, LANES)), one_hot, nt, precision=HIGH
    )
    copies[2].wait()
    for i in range(3):
        moved = lax.dot_general(vel_ref[i], one_hot, nt, precision=HIGH, preferred_element_type=F32)
        for a in range(7):
            for b in range(7):
                row = 7 * (7 * a + b)
                brick_ref[i, a, b, 0:7, :] = moved[row : row + 7]

    def component(i, carry):
        sheets = [brick_ref[i, a] for a in range(7)]
        for a in range(7):
            along_a = derive_sheets(sheets, a)
            sheet = sheets[a]
            along_b = jnp.stack(
                [derive_sheets([sheet[b] for b in range(7)], target) for target in range(7)], axis=0
            )
            along_c = derive_span(rolls, sheet)
            advect = (
                brick_ref[0, a] * along_a + brick_ref[1, a] * along_b + brick_ref[2, a] * along_c
            )
            part_ref[i, a] = join_local(advect)
        emit_faces(part_ref, far_ref, near_ref, i)
        return carry

    lax.fori_loop(0, 3, component, 0)


def side_kernel(part_ref, far_x_ref, near_x_ref, far_ref, near_ref):
    for i in range(part_ref.shape[0]):
        low_x, high_x = lower_upper("slab", near_x_ref[i], far_x_ref[i])
        for a in range(7):
            first, last = part_ref[i, a, 0], part_ref[i, a, 6]
            if a == 0:
                first, last = first + low_x[0], last + low_x[6]
            if a == 6:
                first, last = first + high_x[0], last + high_x[6]
            down, up = pltpu.roll(first, LANES - BZ, 1), pltpu.roll(last, BZ, 1)
            even = even_place("dom", up)
            far_ref[i, a] = jnp.where(even, down, up)
            near_ref[i, a] = jnp.where(even, up, down)


def source_kernel(
    part_ref, far_x_ref, near_x_ref, far_y_ref, near_y_ref, brick_ref,
    out_ref, far_ref, near_ref, middle_ref,
):
    rolls = span_rolls()
    weights = span_vector(WEIGHTS)
    inverse = span_vector(1.0 / FACTOR)
    for i in range(3):
        for a in range(7):
            sheet = add_received(
                a, part_ref[i, a], far_x_ref[i], near_x_ref[i], far_y_ref[i, a], near_y_ref[i, a]
            )
            scaled = [
                sheet[b] * (inverse * float(DELTA_T / (FACTOR[a] * FACTOR[b]))) for b in range(7)
            ]
            middle_ref[i, a] = brick_ref[i, a] - jnp.stack(scaled, axis=0)
    sheets = [middle_ref[0, a] for a in range(7)]
    for a in range(7):
        along_a = derive_sheets(sheets, a)
        second = middle_ref[1, a]
        along_b = jnp.stack(
            [derive_sheets([second[b] for b in range(7)], target) for target in range(7)], axis=0
        )
        diverge = along_a + along_b + derive_span(rolls, middle_ref[2, a])
        source = [
            diverge[b] * (weights * float(-1.0 / DELTA_T * WEIGHTS[a] * WEIGHTS[b]))
            for b in range(7)
        ]
        out_ref[0, a] = join_local(jnp.stack(source, axis=0))
    emit_faces(out_ref, far_ref, near_ref, 0)


def gather_modes(part_ref, far_x_ref, near_x_ref, far_y_ref, near_y_ref, full_ref, modes_ref):
    for a in range(7):
        sheet = add_received(
            a, part_ref[0, a], far_x_ref[0], near_x_ref[0], far_y_ref[0, a], near_y_ref[0, a]
        )
        full_ref[56 * a : 56 * a + 56] = sheet.reshape(56, LANES)
    modes_ref[216:224] = jnp.zeros((8, LANES), F32)
    for compact, padded, rows in RUNS:
        modes_ref[compact : compact + rows] = full_ref[padded : padded + rows]


STARTS = tuple(range(0, MODES, 32))


def block_copy(schur_hbm, schur_ref, sems, start):
    rows = pl.ds(CLASSES * start, CLASSES * min(32, MODES - start))
    return pltpu.make_async_copy(schur_hbm.at[rows], schur_ref.at[rows], sems.at[start // 32])


def start_blocks(schur_hbm, schur_ref, sems):
    for start in STARTS:
        block_copy(schur_hbm, schur_ref, sems, start).start()


def multiply_blocks(schur_hbm, schur_ref, sems, class_ref, modes_ref, image_ref):
    modes = modes_ref[0:MODES]
    row = lax.broadcasted_iota(jnp.int32, (CLASSES, LANES), 0).astype(F32)
    mine = jnp.where(jnp.abs(class_ref[0:1, :] - row) < 0.5, 1.0, 0.0)
    image_ref[216:224] = jnp.zeros((8, LANES), F32)
    for start in STARTS:
        count = min(32, MODES - start)
        block_copy(schur_hbm, schur_ref, sems, start).wait()
        block = schur_ref[CLASSES * start : CLASSES * (start + count)]
        every = jnp.dot(block, modes, precision=HIGH, preferred_element_type=F32)
        every = every.reshape(count, 2, 8, LANES) * mine.reshape(2, 8, LANES)
        image_ref[start : start + count] = jnp.sum(every[:, 0] + every[:, 1], axis=1)


def scatter_modes(image_ref, full_ref, out_ref, far_ref, near_ref):
    full_ref[...] = jnp.zeros((392, LANES), F32)
    for compact, padded, rows in RUNS:
        full_ref[padded : padded + rows] = image_ref[compact : compact + rows]
    for a in range(7):
        out_ref[0, a] = join_local(full_ref[56 * a : 56 * a + 56].reshape(7, 8, LANES))
    emit_faces(out_ref, far_ref, near_ref, 0)


def total_of(values):
    return jnp.sum(jnp.sum(values, axis=0, keepdims=True), axis=1, keepdims=True)


def first_apply_kernel(
    part_ref, far_x_ref, near_x_ref, far_y_ref, near_y_ref, schur_hbm, class_ref,
    load_ref, image_ref, out_ref, far_ref, near_ref, full_ref, schur_ref, sems,
):
    start_blocks(schur_hbm, schur_ref, sems)
    gather_modes(part_ref, far_x_ref, near_x_ref, far_y_ref, near_y_ref, full_ref, load_ref)
    multiply_blocks(schur_hbm, schur_ref, sems, class_ref, load_ref, image_ref)
    scatter_modes(image_ref, full_ref, out_ref, far_ref, near_ref)


def second_apply_kernel(
    part_ref, far_x_ref, near_x_ref, far_y_ref, near_y_ref, schur_hbm, class_ref, load_ref,
    first_ref, shell_ref, power_ref, dots_ref, out_ref, far_ref, near_ref, image_ref, full_ref, schur_ref,
    sems,
):
    start_blocks(schur_hbm, schur_ref, sems)
    gather_modes(part_ref, far_x_ref, near_x_ref, far_y_ref, near_y_ref, full_ref, power_ref)
    multiply_blocks(schur_hbm, schur_ref, sems, class_ref, power_ref, image_ref)
    scatter_modes(image_ref, full_ref, out_ref, far_ref, near_ref)
    load, power, shell = load_ref[...], power_ref[...], shell_ref[...]
    first, image = first_ref[...], image_ref[...]
    lane = lax.broadcasted_iota(jnp.int32, (1, LANES), 1)
    dots = jnp.zeros((1, LANES), F32)
    values = (
        load * load * shell, load * first, power * power * shell, load * image, power * image
    )
    for k, value in enumerate(values):
        dots = dots + jnp.where(lane == k, total_of(value), 0.0)
    dots_ref[...] = dots


def finish_kernel(
    part_ref, far_x_ref, near_x_ref, far_y_ref, near_y_ref, load_ref, power_ref, dots_ref, slot_ref,
    pressure_ref, residual_ref, full_ref, modes_ref,
):
    gather_modes(part_ref, far_x_ref, near_x_ref, far_y_ref, near_y_ref, full_ref, modes_ref)
    dots = jnp.sum(dots_ref[...], axis=0, keepdims=True)
    square, energy, power_square, cross, power_energy = (dots[:, k : k + 1] for k in range(5))
    step = square / energy
    fresh = square - 2.0 * step * energy + step * step * power_square
    ratio = fresh / square
    grow = 1.0 + ratio
    curvature = (
        grow * grow * energy
        - step * grow * (cross + power_square)
        + step * step * power_energy
    )
    second = fresh / curvature
    load, power, twice = load_ref[...], power_ref[...], modes_ref[...]
    pressure = step * load + second * (grow * load - step * power)
    residual = load - step * power - second * (grow * power - step * twice)
    one_hot = permutation(slot_ref)
    pressure_ref[...] = jnp.dot(pressure, one_hot, precision=HIGH, preferred_element_type=F32)[:MODES]
    residual_ref[...] = jnp.dot(residual, one_hot, precision=HIGH, preferred_element_type=F32)[:MODES]


def call(kernel, outs, args, scratch=(), name=None, hbm=()):
    vmem = pl.BlockSpec(memory_space=pltpu.VMEM)
    places = [pl.BlockSpec(memory_space=pltpu.HBM) if k in hbm else vmem for k in range(len(args))]
    args = [
        pltpu.with_memory_space_constraint(x, pltpu.HBM) if k in hbm else x
        for k, x in enumerate(args)
    ]
    return pl.pallas_call(
        kernel,
        out_shape=tuple(jax.ShapeDtypeStruct(shape, F32) for shape in outs),
        in_specs=places,
        out_specs=tuple([vmem] * len(outs)),
        scratch_shapes=[pltpu.VMEM(s, F32) if isinstance(s, tuple) else s for s in scratch],
        compiler_params=pltpu.CompilerParams(vmem_limit_bytes=48 << 20),
        name=name,
    )(*args)


def partners(axis):
    count = lax.axis_size(axis)
    far = [(i, (i + 1) % count if i % 2 else (i - 1) % count) for i in range(count)]
    near = [(i, i ^ 1) for i in range(count)]
    return far, near


def swap(axis, far, near):
    far_pairs, near_pairs = partners(axis)
    return lax.ppermute(far, axis, far_pairs), lax.ppermute(near, axis, near_pairs)


def exchange(part, far, near, dots=None):
    far_x, near_x = swap("slab", far, near)
    k = part.shape[0]
    if dots is not None:
        inner, outer = reduction_groups()
        rows = gather_parts(dots, inner)
        far_x, near_x, rows = lax.optimization_barrier((far_x, near_x, rows))
        rows = gather_parts(rows.sum(axis=0), outer).reshape(-1, LANES)
    far, near = call(side_kernel, [(k, 7, 8, LANES)] * 2, (part, far_x, near_x), name="side")
    received = part, far_x, near_x, *swap("dom", far, near)
    return received if dots is None else (received, rows)


def gather_parts(row, groups):
    count = len(groups[0])
    spread = jnp.broadcast_to(row.reshape(1, 1, LANES), (count, 1, LANES))
    return lax.all_to_all(spread, ("slab", "dom"), 0, 0, axis_index_groups=groups)


def reduction_groups():
    slabs, doms = lax.axis_size("slab"), lax.axis_size("dom")
    run = min(8, doms)
    total = slabs * doms
    inner = [list(range(i, i + run)) for i in range(0, total, run)]
    outer = [list(range(k, total, run)) for k in range(run)]
    return inner, outer


def per_device(velocity, slot_map, class_index, schur_blocks):
    slots = slot_map.reshape(1, LANES)
    shell = jnp.asarray(SHELL)
    schur = schur_blocks.transpose(1, 0, 2).reshape(MODES * CLASSES, MODES)
    face = (7, 8, LANES)
    whole = (7, 7, 8, LANES)
    modes = (224, LANES)
    blocks = [(MODES * CLASSES, MODES), pltpu.SemaphoreType.DMA((len(STARTS),))]
    brick, part, far, near, classes = call(
        advect_kernel,
        [(3, *whole), (3, *whole), (3, *face), (3, *face), (8, LANES)],
        (velocity, slots, class_index.reshape(1, LANES)),
        [
            (3, NODES, LANES),
            pltpu.VMEM((1, LANES), jnp.int32),
            pltpu.VMEM((1, LANES), jnp.int32),
            pltpu.SemaphoreType.DMA((3,)),
        ],
        name="advect",
        hbm=(0, 1, 2),
    )
    part, far, near = call(
        source_kernel,
        [(1, *whole), (1, *face), (1, *face)],
        (*exchange(part, far, near), brick),
        [(3, *whole)],
        name="source",
    )
    load, first, part, far, near = call(
        first_apply_kernel,
        [modes, modes, (1, *whole), (1, *face), (1, *face)],
        (*exchange(part, far, near), schur, classes),
        [(392, LANES), *blocks],
        name="first",
        hbm=(5,),
    )
    power, dots, part, far, near = call(
        second_apply_kernel,
        [modes, (1, LANES), (1, *whole), (1, *face), (1, *face)],
        (*exchange(part, far, near), schur, classes, load, first, shell),
        [modes, (392, LANES), *blocks],
        name="second",
        hbm=(5,),
    )
    received, rows = exchange(part, far, near, dots)
    return call(
        finish_kernel,
        [(MODES, LANES), (MODES, LANES)],
        (*received, load, power, rows, slots),
        [(392, LANES), modes],
        name="finish",
    )


def solution(mesh):
    return jax.shard_map(
        per_device,
        mesh=mesh,
        in_specs=(
            P(None, None, ("slab", "dom")),
            P("slab", "dom", None),
            P("slab", "dom", None),
            P(),
        ),
        out_specs=(P(None, ("slab", "dom")), P(None, ("slab", "dom"))),
        check_vma=False,
    )
```

time: 147 us -> 131 us (0.89); the launches traced: 145 us -> 131 us
  starting transfers between devices: 96.6 us -> 81.8 us
  Pallas kernels: 12.2 us -> 21.4 us
  local copies, waits for them, and re-layouts: 8.52 us -> 0.65 us
  blocking collectives: 17 us -> 11.2 us
  waiting for transfers between devices: 9.85 us -> 14.7 us
    pallas_call x9, Pallas kernels: 12.2 us -> 21.4 us  [call(): pl.pallas_call(kernel, out_shape=tuple((jax.ShapeDtypeStruct(shape, F32)...]
    ppermute x16, starting transfers between devices: 83.2 us -> 74.4 us  [the longest x8 45.8 us: swap(): lax.ppermute(far, axis, far_pairs)]
    unnamed x15 -> x4, local copies, waits for them, and re-layouts: 7.9 us -> 0.01 us
    all_to_all x1, starting transfers between devices: 13.4 us -> 7.39 us  [gather_parts(): lax.all_to_all(spread, ('slab', 'dom'), 0, 0, axis_index_groups=groups)]
    all_to_all x1, blocking collectives: 17 us -> 11.2 us  [gather_parts(): lax.all_to_all(spread, ('slab', 'dom'), 0, 0, axis_index_groups=groups)]
    ppermute x16, waiting for transfers between devices: 8.2 us -> 12.4 us  [the longest x8 6.53 us: swap(): lax.ppermute(far, axis, far_pairs)]
  transfers between devices with their start and end apart: 17 -> 17, of which waited for: 7 -> 10; matrix products, arithmetic and copies ran while one was open for 3% -> 0% of each run, Pallas kernels for 0% -> 0%
where the time goes in v2:
time: 131 us
  starting transfers between devices  81.8 us (62%)
  Pallas kernels  21.4 us (16%)
  waiting for transfers between devices  14.7 us (11%)
  blocking collectives  11.2 us (9%)
    ppermute x8, starting transfers between devices, swap(): lax.ppermute(far, axis, far_pairs)  45.8 us
    ppermute x8, starting transfers between devices, swap(): lax.ppermute(near, axis, near_pairs)  28.6 us
    pallas_call x9, Pallas kernels, call(): pl.pallas_call(kernel, out_shape=tuple((jax.ShapeDtypeStruct(shape, F32)...  21.4 us
    all_to_all x1, blocking collectives, gather_parts(): lax.all_to_all(spread, ('slab', 'dom'), 0, 0, axis_index_groups=groups)  11.2 us
    all_to_all x1, starting transfers between devices, gather_parts(): lax.all_to_all(spread, ('slab', 'dom'), 0, 0, axis_index_groups=groups)  7.39 us
    ppermute x8, waiting for transfers between devices, swap(): lax.ppermute(far, axis, far_pairs)  6.53 us
    ppermute x8, waiting for transfers between devices, swap(): lax.ppermute(near, axis, near_pairs)  5.85 us
  transfers between devices with their start and end apart: 17, of which 10 were waited for; matrix products, arithmetic and copies ran while one was open for 0% of the time, Pallas kernels for 0%

profile of v2, /device:TPU:1, one launch (start us, length us, event | category | flops | bytes accessed | tf_op | source)
XLA Modules:
  0.0 130.7 jit_solution(5657734061458455277)
XLA Ops:
  0.6 0.0 copy-start
  0.6 4.0 %advect.1 = (f32[3,7,7,8,128]{4,3,2,1,0:T(8,128)S(1)}, f32[3,7,7,8,128]{4,3,2,1,0:T(8,128)S(1)}, f32[3,7,8,128]{3,2,1,0:T(8,128)S(1)}, f32[3,7,8,128]{3,2,1,0:T(8,128)S(1)}, f32[8,128]{1,0:T(8,128)S(1)}) custom-call(f32[3,343,128]{2,1,0:T(8,128)} %vel_hbm.1, s32[1,128]{1,0:T(1,128)} %bitcast.8, s32[1,128]{1,0:T(1,128)} %bitcast.13), custom_call_target="tpu_custom_call" | custom-call | tf_op jit(solution)/shard_map/advect/pallas_call | solution.py:369
  4.6 14.4 %collective-permute-start = (f32[3,7,8,128]{3,2,1,0:T(8,128)S(1)}, f32[3,7,8,128]{3,2,1,0:T(8,128)S(1)}, u32[]{:S(2)}, u32[]{:S(2)}) collective-permute-start(f32[3,7,8,128]{3,2,1,0:T(8,128)S(1)} %get-tuple-element.32), channel_id=1, source_target_pairs={{0,480},{32,64},{64,32},{96,128},{128,96},{160,192},{192,160},{224... | collective-permute-start | bytes 258056 | tf_op jit(solution)/shard_map/ppermute | solution.py:389
  19.0 1.9 %collective-permute-start.1 = (f32[3,7,8,128]{3,2,1,0:T(8,128)S(1)}, f32[3,7,8,128]{3,2,1,0:T(8,128)S(1)}, u32[]{:S(2)}, u32[]{:S(2)}) collective-permute-start(f32[3,7,8,128]{3,2,1,0:T(8,128)S(1)} %get-tuple-element.33), channel_id=1, source_target_pairs={{0,32},{32,0},{64,96},{96,64},{128,160},{160,128},{192,224},{224,1... | collective-permute-start | bytes 258056 | tf_op jit(solution)/shard_map/ppermute | solution.py:389
  20.9 0.8 collective-permute-done.far_x_ref
  21.8 2.5 %collective-permute-done.1.near_x_ref = f32[3,7,8,128]{3,2,1,0:T(8,128)S(1)} collective-permute-done((f32[3,7,8,128]{3,2,1,0:T(8,128)S(1)}, f32[3,7,8,128]{3,2,1,0:T(8,128)S(1)}, u32[]{:S(2)}, u32[]{:S(2)}) %collective-permute-start.1) | collective-permute-done | bytes 86048 | tf_op jit(solution)/shard_map/ppermute | solution.py:389
  24.2 0.1 side.4
  24.3 5.1 %collective-permute-start.2 = (f32[3,7,8,128]{3,2,1,0:T(8,128)S(1)}, f32[3,7,8,128]{3,2,1,0:T(8,128)S(1)}, u32[]{:S(2)}, u32[]{:S(2)}) collective-permute-start(f32[3,7,8,128]{3,2,1,0:T(8,128)S(1)} %get-tuple-element.34), channel_id=1, source_target_pairs={{0,31},{1,2},{2,1},{3,4},{4,3},{5,6},{6,5},{7,8},{8,7},{9,10},{10,... | collective-permute-start | bytes 258056 | tf_op jit(solution)/shard_map/ppermute | solution.py:389
  29.5 4.3 %collective-permute-start.3 = (f32[3,7,8,128]{3,2,1,0:T(8,128)S(1)}, f32[3,7,8,128]{3,2,1,0:T(8,128)S(1)}, u32[]{:S(2)}, u32[]{:S(2)}) collective-permute-start(f32[3,7,8,128]{3,2,1,0:T(8,128)S(1)} %get-tuple-element.35), channel_id=1, source_target_pairs={{0,1},{1,0},{2,3},{3,2},{4,5},{5,4},{6,7},{7,6},{8,9},{9,8},{10,11... | collective-permute-start | bytes 258056 | tf_op jit(solution)/shard_map/ppermute | solution.py:389
  33.8 0.0 collective-permute-done.2.far_y_ref
  33.8 0.9 collective-permute-done.3.near_y_ref
  34.7 0.6 source.1
  35.3 6.3 %collective-permute-start.4 = (f32[1,7,8,128]{3,2,1,0:T(8,128)S(1)}, f32[1,7,8,128]{3,2,1,0:T(8,128)S(1)}, u32[]{:S(2)}, u32[]{:S(2)}) collective-permute-start(f32[1,7,8,128]{3,2,1,0:T(8,128)S(1)} %get-tuple-element.38), channel_id=1, source_target_pairs={{0,480},{32,64},{64,32},{96,128},{128,96},{160,192},{192,160},{224... | collective-permute-start | bytes 86024 | tf_op jit(solution)/shard_map/ppermute | solution.py:389
  41.6 1.9 %collective-permute-start.5 = (f32[1,7,8,128]{3,2,1,0:T(8,128)S(1)}, f32[1,7,8,128]{3,2,1,0:T(8,128)S(1)}, u32[]{:S(2)}, u32[]{:S(2)}) collective-permute-start(f32[1,7,8,128]{3,2,1,0:T(8,128)S(1)} %get-tuple-element.39), channel_id=1, source_target_pairs={{0,32},{32,0},{64,96},{96,64},{128,160},{160,128},{192,224},{224,1... | collective-permute-start | bytes 86024 | tf_op jit(solution)/shard_map/ppermute | solution.py:389
  43.5 2.8 %collective-permute-done.4.far_x_ref = f32[1,7,8,128]{3,2,1,0:T(8,128)S(1)} collective-permute-done((f32[1,7,8,128]{3,2,1,0:T(8,128)S(1)}, f32[1,7,8,128]{3,2,1,0:T(8,128)S(1)}, u32[]{:S(2)}, u32[]{:S(2)}) %collective-permute-start.4) | collective-permute-done | bytes 28704 | tf_op jit(solution)/shard_map/ppermute | solution.py:389
  46.3 0.2 collective-permute-done.5.near_x_ref
  46.5 0.1 side.5
  46.6 3.4 %collective-permute-start.6 = (f32[1,7,8,128]{3,2,1,0:T(8,128)S(1)}, f32[1,7,8,128]{3,2,1,0:T(8,128)S(1)}, u32[]{:S(2)}, u32[]{:S(2)}) collective-permute-start(f32[1,7,8,128]{3,2,1,0:T(8,128)S(1)} %get-tuple-element.40), channel_id=1, source_target_pairs={{0,31},{1,2},{2,1},{3,4},{4,3},{5,6},{6,5},{7,8},{8,7},{9,10},{10,... | collective-permute-start | bytes 86024 | tf_op jit(solution)/shard_map/ppermute | solution.py:389
  50.0 5.1 %collective-permute-start.7 = (f32[1,7,8,128]{3,2,1,0:T(8,128)S(1)}, f32[1,7,8,128]{3,2,1,0:T(8,128)S(1)}, u32[]{:S(2)}, u32[]{:S(2)}) collective-permute-start(f32[1,7,8,128]{3,2,1,0:T(8,128)S(1)} %get-tuple-element.41), channel_id=1, source_target_pairs={{0,1},{1,0},{2,3},{3,2},{4,5},{5,4},{6,7},{7,6},{8,9},{9,8},{10,11... | collective-permute-start | bytes 86024 | tf_op jit(solution)/shard_map/ppermute | solution.py:389
  55.1 0.0 collective-permute-done.6.far_y_ref
  55.1 0.8 collective-permute-done.7.near_y_ref
  55.9 0.0 copy-start.1
  55.9 7.6 %first.1 = (f32[224,128]{1,0:T(8,128)S(1)}, f32[224,128]{1,0:T(8,128)S(1)}, f32[1,7,7,8,128]{4,3,2,1,0:T(8,128)S(1)}, f32[1,7,8,128]{3,2,1,0:T(8,128)S(1)}, f32[1,7,8,128]{3,2,1,0:T(8,128)S(1)}) custom-call(f32[1,7,7,8,128]{4,3,2,1,0:T(8,128)S(1)} %get-tuple-element.37.part_ref, f32[1,7,8,128]{3,2,1,0:T(8,128)S(1)} %collective-permute-done.4.far_x_ref, ...), custom_call_target="tpu_custom_call" | custom-call | tf_op jit(solution)/shard_map/first/pallas_call | solution.py:369
  63.5 6.0 %collective-permute-start.8 = (f32[1,7,8,128]{3,2,1,0:T(8,128)S(1)}, f32[1,7,8,128]{3,2,1,0:T(8,128)S(1)}, u32[]{:S(2)}, u32[]{:S(2)}) collective-permute-start(f32[1,7,8,128]{3,2,1,0:T(8,128)S(1)} %get-tuple-element.44), channel_id=1, source_target_pairs={{0,480},{32,64},{64,32},{96,128},{128,96},{160,192},{192,160},{224... | collective-permute-start | bytes 86024 | tf_op jit(solution)/shard_map/ppermute | solution.py:389
  69.6 1.9 %collective-permute-start.9 = (f32[1,7,8,128]{3,2,1,0:T(8,128)S(1)}, f32[1,7,8,128]{3,2,1,0:T(8,128)S(1)}, u32[]{:S(2)}, u32[]{:S(2)}) collective-permute-start(f32[1,7,8,128]{3,2,1,0:T(8,128)S(1)} %get-tuple-element.45), channel_id=1, source_target_pairs={{0,32},{32,0},{64,96},{96,64},{128,160},{160,128},{192,224},{224,1... | collective-permute-start | bytes 86024 | tf_op jit(solution)/shard_map/ppermute | solution.py:389
  71.5 2.9 %collective-permute-done.8.far_x_ref = f32[1,7,8,128]{3,2,1,0:T(8,128)S(1)} collective-permute-done((f32[1,7,8,128]{3,2,1,0:T(8,128)S(1)}, f32[1,7,8,128]{3,2,1,0:T(8,128)S(1)}, u32[]{:S(2)}, u32[]{:S(2)}) %collective-permute-start.8) | collective-permute-done | bytes 28704 | tf_op jit(solution)/shard_map/ppermute | solution.py:389
  74.4 0.0 collective-permute-done.9.near_x_ref
  74.4 0.1 side.6
  74.5 1.9 %collective-permute-start.10 = (f32[1,7,8,128]{3,2,1,0:T(8,128)S(1)}, f32[1,7,8,128]{3,2,1,0:T(8,128)S(1)}, u32[]{:S(2)}, u32[]{:S(2)}) collective-permute-start(f32[1,7,8,128]{3,2,1,0:T(8,128)S(1)} %get-tuple-element.46), channel_id=1, source_target_pairs={{0,31},{1,2},{2,1},{3,4},{4,3},{5,6},{6,5},{7,8},{8,7},{9,10},{10,... | collective-permute-start | bytes 86024 | tf_op jit(solution)/shard_map/ppermute | solution.py:389
  76.4 6.9 %collective-permute-start.11 = (f32[1,7,8,128]{3,2,1,0:T(8,128)S(1)}, f32[1,7,8,128]{3,2,1,0:T(8,128)S(1)}, u32[]{:S(2)}, u32[]{:S(2)}) collective-permute-start(f32[1,7,8,128]{3,2,1,0:T(8,128)S(1)} %get-tuple-element.47), channel_id=1, source_target_pairs={{0,1},{1,0},{2,3},{3,2},{4,5},{5,4},{6,7},{7,6},{8,9},{9,8},{10,11... | collective-permute-start | bytes 86024 | tf_op jit(solution)/shard_map/ppermute | solution.py:389
  83.4 0.0 collective-permute-done.10.far_y_ref
  83.4 0.6 collective-permute-done.11.near_y_ref
  84.0 0.0 copy-done
  84.0 7.6 %second.1 = (f32[224,128]{1,0:T(8,128)S(1)}, f32[1,128]{1,0:T(1,128)S(1)}, f32[1,7,7,8,128]{4,3,2,1,0:T(8,128)S(1)}, f32[1,7,8,128]{3,2,1,0:T(8,128)S(1)}, f32[1,7,8,128]{3,2,1,0:T(8,128)S(1)}) custom-call(f32[1,7,7,8,128]{4,3,2,1,0:T(8,128)S(1)} %get-tuple-element.43.part_ref, f32[1,7,8,128]{3,2,1,0:T(8,128)S(1)} %collective-permute-done.8.far_x_ref, ...), custom_call_target="tpu_custom_call" | custom-call | tf_op jit(solution)/shard_map/second/pallas_call | solution.py:369
  91.6 5.7 %collective-permute-start.12 = (f32[1,7,8,128]{3,2,1,0:T(8,128)S(1)}, f32[1,7,8,128]{3,2,1,0:T(8,128)S(1)}, u32[]{:S(2)}, u32[]{:S(2)}) collective-permute-start(f32[1,7,8,128]{3,2,1,0:T(8,128)S(1)} %get-tuple-element.51), channel_id=1, source_target_pairs={{0,480},{32,64},{64,32},{96,128},{128,96},{160,192},{192,160},{224... | collective-permute-start | bytes 86024 | tf_op jit(solution)/shard_map/ppermute | solution.py:389
  97.3 1.9 %collective-permute-start.13 = (f32[1,7,8,128]{3,2,1,0:T(8,128)S(1)}, f32[1,7,8,128]{3,2,1,0:T(8,128)S(1)}, u32[]{:S(2)}, u32[]{:S(2)}) collective-permute-start(f32[1,7,8,128]{3,2,1,0:T(8,128)S(1)} %get-tuple-element.52), channel_id=1, source_target_pairs={{0,32},{32,0},{64,96},{96,64},{128,160},{160,128},{192,224},{224,1... | collective-permute-start | bytes 86024 | tf_op jit(solution)/shard_map/ppermute | solution.py:389
  99.3 11.2 %all_to_all.10 = f32[8,1,128]{2,1,0:T(1,128)S(1)} all-to-all(f32[8,1,128]{2,1,0:T(1,128)S(1)} %broadcast_in_dim.13), channel_id=1, replica_groups={{0,1,2,3,4,5,6,7},{8,9,10,11,12,13,14,15},{16,17,18,19,20,21,22,23},{24..., dimensions={0} | all-to-all | bytes 8192 | tf_op jit(solution)/shard_map/all_to_all | solution.py:408
  110.5 0.0 collective-permute-done.12.far_x_ref
  110.5 0.0 collective-permute-done.13.near_x_ref
  110.5 0.6 broadcast_in_dim.14
  111.2 7.4 %all-to-all-start.1 = ((f32[64,1,128]{2,1,0:T(1,128)}), f32[64,1,128]{2,1,0:T(1,128)S(1)}, u32[]{:S(2)}, u32[]{:S(2)}) async-start(f32[64,1,128]{2,1,0:T(1,128)} %broadcast_in_dim.14), calls=%async_computation.1 | async-start | bytes 65536 | tf_op jit(solution)/shard_map/all_to_all | solution.py:408
  118.6 0.1 side.7
  118.7 3.1 %collective-permute-start.14 = (f32[1,7,8,128]{3,2,1,0:T(8,128)S(1)}, f32[1,7,8,128]{3,2,1,0:T(8,128)S(1)}, u32[]{:S(2)}, u32[]{:S(2)}) collective-permute-start(f32[1,7,8,128]{3,2,1,0:T(8,128)S(1)} %get-tuple-element.56), channel_id=1, source_target_pairs={{0,31},{1,2},{2,1},{3,4},{4,3},{5,6},{6,5},{7,8},{8,7},{9,10},{10,... | collective-permute-start | bytes 86024 | tf_op jit(solution)/shard_map/ppermute | solution.py:389
  121.7 4.6 %collective-permute-start.15 = (f32[1,7,8,128]{3,2,1,0:T(8,128)S(1)}, f32[1,7,8,128]{3,2,1,0:T(8,128)S(1)}, u32[]{:S(2)}, u32[]{:S(2)}) collective-permute-start(f32[1,7,8,128]{3,2,1,0:T(8,128)S(1)} %get-tuple-element.57), channel_id=1, source_target_pairs={{0,1},{1,0},{2,3},{3,2},{4,5},{5,4},{6,7},{7,6},{8,9},{9,8},{10,11... | collective-permute-start | bytes 86024 | tf_op jit(solution)/shard_map/ppermute | solution.py:389
  126.3 0.0 collective-permute-done.14.far_y_ref
  126.3 0.8 collective-permute-done.15.near_y_ref
  127.1 2.3 %all-to-all-done.1 = f32[64,1,128]{2,1,0:T(1,128)S(1)} async-done(((f32[64,1,128]{2,1,0:T(1,128)}), f32[64,1,128]{2,1,0:T(1,128)S(1)}, u32[]{:S(2)}, u32[]{:S(2)}) %all-to-all-start.1) | async-done | bytes 32800 | tf_op jit(solution)/shard_map/all_to_all | solution.py:408
  129.5 0.0 copy-done.1
  129.5 1.2 finish.1
  (2 shorter events, 0.0 us)
Async XLA Ops:
  0.6 83.4 %copy-start = (f32[224,128]{1,0:T(8,128)S(1)}, f32[224,128]{1,0:T(8,128)}, u32[]{:S(2)}) copy-start(f32[224,128]{1,0:T(8,128)} %constant.4.clone.shell_ref) | copy-start | bytes 344068
  4.6 17.1 %collective-permute-start = (f32[3,7,8,128]{3,2,1,0:T(8,128)S(1)}, f32[3,7,8,128]{3,2,1,0:T(8,128)S(1)}, u32[]{:S(2)}, u32[]{:S(2)}) collective-permute-start(f32[3,7,8,128]{3,2,1,0:T(8,128)S(1)} %get-tuple-element.32), channel_id=1, source_target_pairs={{0,480},{32,64},{64,32},{96,128},{128,96},{160,192},{192,160},{224... | collective-permute-start | bytes 258056 | tf_op jit(solution)/shard_map/ppermute | solution.py:389
  19.0 5.2 %collective-permute-start.1 = (f32[3,7,8,128]{3,2,1,0:T(8,128)S(1)}, f32[3,7,8,128]{3,2,1,0:T(8,128)S(1)}, u32[]{:S(2)}, u32[]{:S(2)}) collective-permute-start(f32[3,7,8,128]{3,2,1,0:T(8,128)S(1)} %get-tuple-element.33), channel_id=1, source_target_pairs={{0,32},{32,0},{64,96},{96,64},{128,160},{160,128},{192,224},{224,1... | collective-permute-start | bytes 258056 | tf_op jit(solution)/shard_map/ppermute | solution.py:389
  24.3 9.4 %collective-permute-start.2 = (f32[3,7,8,128]{3,2,1,0:T(8,128)S(1)}, f32[3,7,8,128]{3,2,1,0:T(8,128)S(1)}, u32[]{:S(2)}, u32[]{:S(2)}) collective-permute-start(f32[3,7,8,128]{3,2,1,0:T(8,128)S(1)} %get-tuple-element.34), channel_id=1, source_target_pairs={{0,31},{1,2},{2,1},{3,4},{4,3},{5,6},{6,5},{7,8},{8,7},{9,10},{10,... | collective-permute-start | bytes 258056 | tf_op jit(solution)/shard_map/ppermute | solution.py:389
  29.5 5.2 %collective-permute-start.3 = (f32[3,7,8,128]{3,2,1,0:T(8,128)S(1)}, f32[3,7,8,128]{3,2,1,0:T(8,128)S(1)}, u32[]{:S(2)}, u32[]{:S(2)}) collective-permute-start(f32[3,7,8,128]{3,2,1,0:T(8,128)S(1)} %get-tuple-element.35), channel_id=1, source_target_pairs={{0,1},{1,0},{2,3},{3,2},{4,5},{5,4},{6,7},{7,6},{8,9},{9,8},{10,11... | collective-permute-start | bytes 258056 | tf_op jit(solution)/shard_map/ppermute | solution.py:389
  35.3 11.0 %collective-permute-start.4 = (f32[1,7,8,128]{3,2,1,0:T(8,128)S(1)}, f32[1,7,8,128]{3,2,1,0:T(8,128)S(1)}, u32[]{:S(2)}, u32[]{:S(2)}) collective-permute-start(f32[1,7,8,128]{3,2,1,0:T(8,128)S(1)} %get-tuple-element.38), channel_id=1, source_target_pairs={{0,480},{32,64},{64,32},{96,128},{128,96},{160,192},{192,160},{224... | collective-permute-start | bytes 86024 | tf_op jit(solution)/shard_map/ppermute | solution.py:389
  41.6 4.9 %collective-permute-start.5 = (f32[1,7,8,128]{3,2,1,0:T(8,128)S(1)}, f32[1,7,8,128]{3,2,1,0:T(8,128)S(1)}, u32[]{:S(2)}, u32[]{:S(2)}) collective-permute-start(f32[1,7,8,128]{3,2,1,0:T(8,128)S(1)} %get-tuple-element.39), channel_id=1, source_target_pairs={{0,32},{32,0},{64,96},{96,64},{128,160},{160,128},{192,224},{224,1... | collective-permute-start | bytes 86024 | tf_op jit(solution)/shard_map/ppermute | solution.py:389
  46.6 8.5 %collective-permute-start.6 = (f32[1,7,8,128]{3,2,1,0:T(8,128)S(1)}, f32[1,7,8,128]{3,2,1,0:T(8,128)S(1)}, u32[]{:S(2)}, u32[]{:S(2)}) collective-permute-start(f32[1,7,8,128]{3,2,1,0:T(8,128)S(1)} %get-tuple-element.40), channel_id=1, source_target_pairs={{0,31},{1,2},{2,1},{3,4},{4,3},{5,6},{6,5},{7,8},{8,7},{9,10},{10,... | collective-permute-start | bytes 86024 | tf_op jit(solution)/shard_map/ppermute | solution.py:389
  50.0 6.0 %collective-permute-start.7 = (f32[1,7,8,128]{3,2,1,0:T(8,128)S(1)}, f32[1,7,8,128]{3,2,1,0:T(8,128)S(1)}, u32[]{:S(2)}, u32[]{:S(2)}) collective-permute-start(f32[1,7,8,128]{3,2,1,0:T(8,128)S(1)} %get-tuple-element.41), channel_id=1, source_target_pairs={{0,1},{1,0},{2,3},{3,2},{4,5},{5,4},{6,7},{7,6},{8,9},{9,8},{10,11... | collective-permute-start | bytes 86024 | tf_op jit(solution)/shard_map/ppermute | solution.py:389
  55.9 73.5 %copy-start.1 = (s32[1,1,128]{2,1,0:T(1,128)S(1)}, s32[1,1,128]{2,1,0:T(1,128)}, u32[]{:S(2)}) copy-start(s32[1,1,128]{2,1,0:T(1,128)} %param.6) | copy-start | bytes 1540
  63.5 10.9 %collective-permute-start.8 = (f32[1,7,8,128]{3,2,1,0:T(8,128)S(1)}, f32[1,7,8,128]{3,2,1,0:T(8,128)S(1)}, u32[]{:S(2)}, u32[]{:S(2)}) collective-permute-start(f32[1,7,8,128]{3,2,1,0:T(8,128)S(1)} %get-tuple-element.44), channel_id=1, source_target_pairs={{0,480},{32,64},{64,32},{96,128},{128,96},{160,192},{192,160},{224... | collective-permute-start | bytes 86024 | tf_op jit(solution)/shard_map/ppermute | solution.py:389
  69.6 4.8 %collective-permute-start.9 = (f32[1,7,8,128]{3,2,1,0:T(8,128)S(1)}, f32[1,7,8,128]{3,2,1,0:T(8,128)S(1)}, u32[]{:S(2)}, u32[]{:S(2)}) collective-permute-start(f32[1,7,8,128]{3,2,1,0:T(8,128)S(1)} %get-tuple-element.45), channel_id=1, source_target_pairs={{0,32},{32,0},{64,96},{96,64},{128,160},{160,128},{192,224},{224,1... | collective-permute-start | bytes 86024 | tf_op jit(solution)/shard_map/ppermute | solution.py:389
  74.5 8.9 %collective-permute-start.10 = (f32[1,7,8,128]{3,2,1,0:T(8,128)S(1)}, f32[1,7,8,128]{3,2,1,0:T(8,128)S(1)}, u32[]{:S(2)}, u32[]{:S(2)}) collective-permute-start(f32[1,7,8,128]{3,2,1,0:T(8,128)S(1)} %get-tuple-element.46), channel_id=1, source_target_pairs={{0,31},{1,2},{2,1},{3,4},{4,3},{5,6},{6,5},{7,8},{8,7},{9,10},{10,... | collective-permute-start | bytes 86024 | tf_op jit(solution)/shard_map/ppermute | solution.py:389
  76.4 7.6 %collective-permute-start.11 = (f32[1,7,8,128]{3,2,1,0:T(8,128)S(1)}, f32[1,7,8,128]{3,2,1,0:T(8,128)S(1)}, u32[]{:S(2)}, u32[]{:S(2)}) collective-permute-start(f32[1,7,8,128]{3,2,1,0:T(8,128)S(1)} %get-tuple-element.47), channel_id=1, source_target_pairs={{0,1},{1,0},{2,3},{3,2},{4,5},{5,4},{6,7},{7,6},{8,9},{9,8},{10,11... | collective-permute-start | bytes 86024 | tf_op jit(solution)/shard_map/ppermute | solution.py:389
  91.6 18.9 %collective-permute-start.12 = (f32[1,7,8,128]{3,2,1,0:T(8,128)S(1)}, f32[1,7,8,128]{3,2,1,0:T(8,128)S(1)}, u32[]{:S(2)}, u32[]{:S(2)}) collective-permute-start(f32[1,7,8,128]{3,2,1,0:T(8,128)S(1)} %get-tuple-element.51), channel_id=1, source_target_pairs={{0,480},{32,64},{64,32},{96,128},{128,96},{160,192},{192,160},{224... | collective-permute-start | bytes 86024 | tf_op jit(solution)/shard_map/ppermute | solution.py:389
  97.3 13.2 %collective-permute-start.13 = (f32[1,7,8,128]{3,2,1,0:T(8,128)S(1)}, f32[1,7,8,128]{3,2,1,0:T(8,128)S(1)}, u32[]{:S(2)}, u32[]{:S(2)}) collective-permute-start(f32[1,7,8,128]{3,2,1,0:T(8,128)S(1)} %get-tuple-element.52), channel_id=1, source_target_pairs={{0,32},{32,0},{64,96},{96,64},{128,160},{160,128},{192,224},{224,1... | collective-permute-start | bytes 86024 | tf_op jit(solution)/shard_map/ppermute | solution.py:389
  111.2 18.3 %all-to-all-start.1 = ((f32[64,1,128]{2,1,0:T(1,128)}), f32[64,1,128]{2,1,0:T(1,128)S(1)}, u32[]{:S(2)}, u32[]{:S(2)}) async-start(f32[64,1,128]{2,1,0:T(1,128)} %broadcast_in_dim.14), calls=%async_computation.1 | async-start | bytes 65536 | tf_op jit(solution)/shard_map/all_to_all | solution.py:408
  118.7 7.6 %collective-permute-start.14 = (f32[1,7,8,128]{3,2,1,0:T(8,128)S(1)}, f32[1,7,8,128]{3,2,1,0:T(8,128)S(1)}, u32[]{:S(2)}, u32[]{:S(2)}) collective-permute-start(f32[1,7,8,128]{3,2,1,0:T(8,128)S(1)} %get-tuple-element.56), channel_id=1, source_target_pairs={{0,31},{1,2},{2,1},{3,4},{4,3},{5,6},{6,5},{7,8},{8,7},{9,10},{10,... | collective-permute-start | bytes 86024 | tf_op jit(solution)/shard_map/ppermute | solution.py:389
  121.7 5.4 %collective-permute-start.15 = (f32[1,7,8,128]{3,2,1,0:T(8,128)S(1)}, f32[1,7,8,128]{3,2,1,0:T(8,128)S(1)}, u32[]{:S(2)}, u32[]{:S(2)}) collective-permute-start(f32[1,7,8,128]{3,2,1,0:T(8,128)S(1)} %get-tuple-element.57), channel_id=1, source_target_pairs={{0,1},{1,0},{2,3},{3,2},{4,5},{5,4},{6,7},{7,6},{8,9},{9,8},{10,11... | collective-permute-start | bytes 86024 | tf_op jit(solution)/shard_map/ppermute | solution.py:389

commit v3 on v2

--- a/solution.py
+++ b/solution.py
@@ -13,8 +13,8 @@
 BZ = 16
 BY = 8
 DELTA_T = 0.05
-HIGH = lax.Precision.HIGHEST
 F32 = jnp.float32
+BF16 = jnp.bfloat16
 
 
 def gll_tables():
@@ -146,7 +146,18 @@
 
 def permutation(slot_ref):
     position = lax.broadcasted_iota(jnp.int32, (LANES, LANES), 0)
-    return jnp.where(position == slot_ref[...], 1.0, 0.0).astype(F32)
+    return jnp.where(position == slot_ref[...], 1.0, 0.0).astype(BF16)
+
+
+def moved(values, one_hot, dims):
+    return sum(
+        lax.dot_general(term, one_hot, (dims, ((), ())), preferred_element_type=F32)
+        for term in terms(values)
+    )
+
+
+TO_BRICK = ((1,), (1,))
+TO_STORED = ((1,), (0,))
 
 
 def emit_faces(part_ref, far_ref, near_ref, index):
@@ -164,7 +175,10 @@
     copies = [
         pltpu.make_async_copy(src, dst, sems.at[k])
         for k, (src, dst) in enumerate(
-            ((slot_hbm, slot_ref), (class_hbm, class_ref), (vel_hbm, vel_ref))
+            (
+                (slot_hbm, slot_ref), (class_hbm, class_ref),
+                *((vel_hbm.at[i], vel_ref.at[i]) for i in range(3)),
+            )
         )
     ]
     for copy in copies:
@@ -174,17 +188,16 @@
     copies[0].wait()
     copies[1].wait()
     one_hot = permutation(slot_ref)
-    nt = (((1,), (1,)), ((), ()))
-    class_out[...] = lax.dot_general(
-        jnp.broadcast_to(class_ref[...].astype(F32), (8, LANES)), one_hot, nt, precision=HIGH
-    )
-    copies[2].wait()
+    class_out[...] = moved(
+        jnp.broadcast_to(class_ref[...].astype(F32), (8, LANES)), one_hot, TO_BRICK
+    )
     for i in range(3):
-        moved = lax.dot_general(vel_ref[i], one_hot, nt, precision=HIGH, preferred_element_type=F32)
+        copies[2 + i].wait()
+        stored = moved(vel_ref[i], one_hot, TO_BRICK)
         for a in range(7):
             for b in range(7):
                 row = 7 * (7 * a + b)
-                brick_ref[i, a, b, 0:7, :] = moved[row : row + 7]
+                brick_ref[i, a, b, 0:7, :] = stored[row : row + 7]
 
     def component(i, carry):
         sheets = [brick_ref[i, a] for a in range(7)]
@@ -263,31 +276,54 @@
         modes_ref[compact : compact + rows] = full_ref[padded : padded + rows]
 
 
-STARTS = tuple(range(0, MODES, 32))
-
-
-def block_copy(schur_hbm, schur_ref, sems, start):
-    rows = pl.ds(CLASSES * start, CLASSES * min(32, MODES - start))
-    return pltpu.make_async_copy(schur_hbm.at[rows], schur_ref.at[rows], sems.at[start // 32])
-
-
-def start_blocks(schur_hbm, schur_ref, sems):
-    for start in STARTS:
-        block_copy(schur_hbm, schur_ref, sems, start).start()
-
-
-def multiply_blocks(schur_hbm, schur_ref, sems, class_ref, modes_ref, image_ref):
-    modes = modes_ref[0:MODES]
-    row = lax.broadcasted_iota(jnp.int32, (CLASSES, LANES), 0).astype(F32)
-    mine = jnp.where(jnp.abs(class_ref[0:1, :] - row) < 0.5, 1.0, 0.0)
-    image_ref[216:224] = jnp.zeros((8, LANES), F32)
-    for start in STARTS:
-        count = min(32, MODES - start)
-        block_copy(schur_hbm, schur_ref, sems, start).wait()
-        block = schur_ref[CLASSES * start : CLASSES * (start + count)]
-        every = jnp.dot(block, modes, precision=HIGH, preferred_element_type=F32)
-        every = every.reshape(count, 2, 8, LANES) * mine.reshape(2, 8, LANES)
-        image_ref[start : start + count] = jnp.sum(every[:, 0] + every[:, 1], axis=1)
+def terms(values):
+    high = values.astype(BF16)
+    rest = values - high.astype(F32)
+    middle = rest.astype(BF16)
+    return high, middle, (rest - middle.astype(F32)).astype(BF16)
+
+
+def split_kernel(schur_hbm, split_ref, schur_ref, left_ref, right_ref, sems):
+    parts = 2
+    size = MODES * CLASSES // parts
+    copies = [
+        pltpu.make_async_copy(
+            schur_hbm.at[pl.ds(size * k, size)], schur_ref.at[pl.ds(size * k, size)], sems.at[k]
+        )
+        for k in range(parts)
+    ]
+    for copy in copies:
+        copy.start()
+    for k in range(3):
+        split_ref[224 * k + 208 : 224 * k + 224] = jnp.zeros((16, 256 * CLASSES), BF16)
+    right_ref[...] = jnp.zeros(right_ref.shape, F32)
+    for copy in copies:
+        copy.wait()
+    left_ref[...] = schur_ref[:, :LANES]
+    right_ref[:, : MODES - LANES] = schur_ref[:, LANES:]
+    for c in range(CLASSES):
+        for half, half_ref in enumerate((left_ref, right_ref)):
+            block = half_ref[pl.ds(c, MODES, stride=CLASSES), :]
+            place = LANES * (2 * c + half)
+            for k, term in enumerate(terms(block)):
+                split_ref[224 * k : 224 * k + MODES, place : place + LANES] = term
+
+
+def multiply_blocks(split_ref, class_ref, modes_ref, image_ref, right_ref, last_ref):
+    high, middle, low = terms(modes_ref[...])
+    pair = jnp.concatenate([high, middle], axis=1)
+    zeros = jnp.zeros((32, 2 * LANES), BF16)
+    mine = class_ref[0:1, :]
+    for c in range(CLASSES):
+        chosen = jnp.where(jnp.abs(mine - float(c)) < 0.5, 1.0, 0.0).astype(BF16)
+        right_ref[256 * c : 256 * c + 224] = pair * jnp.concatenate([chosen, chosen], axis=1)
+        right_ref[256 * c + 224 : 256 * c + 256] = zeros
+        last_ref[256 * c : 256 * c + 224] = low * chosen
+        last_ref[256 * c + 224 : 256 * c + 256] = zeros[:, :LANES]
+    total = jnp.dot(split_ref[...], right_ref[...], preferred_element_type=F32)
+    total = total[:, :LANES] + total[:, LANES:]
+    small = jnp.dot(split_ref[0:224], last_ref[...], preferred_element_type=F32)
+    image_ref[...] = total[0:224] + (total[224:448] + (total[448:672] + small))
 
 
 def scatter_modes(image_ref, full_ref, out_ref, far_ref, near_ref):
@@ -304,23 +340,21 @@
 
 
 def first_apply_kernel(
-    part_ref, far_x_ref, near_x_ref, far_y_ref, near_y_ref, schur_hbm, class_ref,
-    load_ref, image_ref, out_ref, far_ref, near_ref, full_ref, schur_ref, sems,
+    part_ref, far_x_ref, near_x_ref, far_y_ref, near_y_ref, split_ref, class_ref,
+    load_ref, image_ref, out_ref, far_ref, near_ref, full_ref, right_ref, last_ref,
 ):
-    start_blocks(schur_hbm, schur_ref, sems)
     gather_modes(part_ref, far_x_ref, near_x_ref, far_y_ref, near_y_ref, full_ref, load_ref)
-    multiply_blocks(schur_hbm, schur_ref, sems, class_ref, load_ref, image_ref)
+    multiply_blocks(split_ref, class_ref, load_ref, image_ref, right_ref, last_ref)
     scatter_modes(image_ref, full_ref, out_ref, far_ref, near_ref)
 
 
 def second_apply_kernel(
-    part_ref, far_x_ref, near_x_ref, far_y_ref, near_y_ref, schur_hbm, class_ref, load_ref,
-    first_ref, shell_ref, power_ref, dots_ref, out_ref, far_ref, near_ref, image_ref, full_ref, schur_ref,
-    sems,
+    part_ref, far_x_ref, near_x_ref, far_y_ref, near_y_ref, split_ref, class_ref, load_ref,
+    first_ref, shell_ref, power_ref, dots_ref, out_ref, far_ref, near_ref, image_ref, full_ref, right_ref,
+    last_ref,
 ):
-    start_blocks(schur_hbm, schur_ref, sems)
     gather_modes(part_ref, far_x_ref, near_x_ref, far_y_ref, near_y_ref, full_ref, power_ref)
-    multiply_blocks(schur_hbm, schur_ref, sems, class_ref, power_ref, image_ref)
+    multiply_blocks(split_ref, class_ref, power_ref, image_ref, right_ref, last_ref)
     scatter_modes(image_ref, full_ref, out_ref, far_ref, near_ref)
     load, power, shell = load_ref[...], power_ref[...], shell_ref[...]
     first, image = first_ref[...], image_ref[...]
@@ -355,8 +389,8 @@
     pressure = step * load + second * (grow * load - step * power)
     residual = load - step * power - second * (grow * power - step * twice)
     one_hot = permutation(slot_ref)
-    pressure_ref[...] = jnp.dot(pressure, one_hot, precision=HIGH, preferred_element_type=F32)[:MODES]
-    residual_ref[...] = jnp.dot(residual, one_hot, precision=HIGH, preferred_element_type=F32)[:MODES]
+    pressure_ref[...] = moved(pressure, one_hot, TO_STORED)[:MODES]
+    residual_ref[...] = moved(residual, one_hot, TO_STORED)[:MODES]
 
 
 def call(kernel, outs, args, scratch=(), name=None, hbm=()):
@@ -368,11 +402,13 @@
     ]
     return pl.pallas_call(
         kernel,
-        out_shape=tuple(jax.ShapeDtypeStruct(shape, F32) for shape in outs),
+        out_shape=tuple(
+            jax.ShapeDtypeStruct(*(o if isinstance(o[0], tuple) else (o, F32))) for o in outs
+        ),
         in_specs=places,
         out_specs=tuple([vmem] * len(outs)),
         scratch_shapes=[pltpu.VMEM(s, F32) if isinstance(s, tuple) else s for s in scratch],
-        compiler_params=pltpu.CompilerParams(vmem_limit_bytes=48 << 20),
+        compiler_params=pltpu.CompilerParams(vmem_limit_bytes=24 << 20),
         name=name,
     )(*args)
 
@@ -389,16 +425,19 @@
     return lax.ppermute(far, axis, far_pairs), lax.ppermute(near, axis, near_pairs)
 
 
-def exchange(part, far, near, dots=None):
+def exchange(part, far, near, dots=None, beside=None):
     far_x, near_x = swap("slab", far, near)
     k = part.shape[0]
+    if beside is not None:
+        part, beside = lax.optimization_barrier((part, beside))
     if dots is not None:
-        inner, outer = reduction_groups()
-        rows = gather_parts(dots, inner)
-        far_x, near_x, rows = lax.optimization_barrier((far_x, near_x, rows))
-        rows = gather_parts(rows.sum(axis=0), outer).reshape(-1, LANES)
+        cores, chips = reduction_groups()
+        dots = lax.psum(dots, ("slab", "dom"), axis_index_groups=cores)
+        rows = gather_parts(dots, chips).reshape(-1, LANES)
     far, near = call(side_kernel, [(k, 7, 8, LANES)] * 2, (part, far_x, near_x), name="side")
     received = part, far_x, near_x, *swap("dom", far, near)
+    if beside is not None:
+        return received, beside
     return received if dots is None else (received, rows)
 
 
@@ -409,12 +448,9 @@
 
 
 def reduction_groups():
-    slabs, doms = lax.axis_size("slab"), lax.axis_size("dom")
-    run = min(8, doms)
-    total = slabs * doms
-    inner = [list(range(i, i + run)) for i in range(0, total, run)]
-    outer = [list(range(k, total, run)) for k in range(run)]
-    return inner, outer
+    total = lax.axis_size("slab") * lax.axis_size("dom")
+    pairs = [[i, i + 1] for i in range(0, total, 2)]
+    return pairs, [list(range(k, total, 2)) for k in range(2)]
 
 
 def per_device(velocity, slot_map, class_index, schur_blocks):
@@ -424,7 +460,7 @@
     face = (7, 8, LANES)
     whole = (7, 7, 8, LANES)
     modes = (224, LANES)
-    blocks = [(MODES * CLASSES, MODES), pltpu.SemaphoreType.DMA((len(STARTS),))]
+    rights = [pltpu.VMEM((256 * CLASSES, n), BF16) for n in (2 * LANES, LANES)]
     brick, part, far, near, classes = call(
         advect_kernel,
         [(3, *whole), (3, *whole), (3, *face), (3, *face), (8, LANES)],
@@ -433,33 +469,40 @@
             (3, NODES, LANES),
             pltpu.VMEM((1, LANES), jnp.int32),
             pltpu.VMEM((1, LANES), jnp.int32),
-            pltpu.SemaphoreType.DMA((3,)),
+            pltpu.SemaphoreType.DMA((5,)),
         ],
         name="advect",
         hbm=(0, 1, 2),
     )
+    split = call(
+        split_kernel,
+        [((672, 256 * CLASSES), BF16)],
+        (schur,),
+        [(MODES * CLASSES, MODES), *[(MODES * CLASSES, LANES)] * 2, pltpu.SemaphoreType.DMA((2,))],
+        name="split",
+        hbm=(0,),
+    )[0]
+    received, split = exchange(part, far, near, beside=split)
     part, far, near = call(
         source_kernel,
         [(1, *whole), (1, *face), (1, *face)],
-        (*exchange(part, far, near), brick),
+        (*received, brick),
         [(3, *whole)],
         name="source",
     )
     load, first, part, far, near = call(
         first_apply_kernel,
         [modes, modes, (1, *whole), (1, *face), (1, *face)],
-        (*exchange(part, far, near), schur, classes),
-        [(392, LANES), *blocks],
+        (*exchange(part, far, near), split, classes),
+        [(392, LANES), *rights],
         name="first",
-        hbm=(5,),
     )
     power, dots, part, far, near = call(
         second_apply_kernel,
         [modes, (1, LANES), (1, *whole), (1, *face), (1, *face)],
-        (*exchange(part, far, near), schur, classes, load, first, shell),
-        [modes, (392, LANES), *blocks],
+        (*exchange(part, far, near), split, classes, load, first, shell),
+        [modes, (392, LANES), *rights],
         name="second",
-        hbm=(5,),
     )
     received, rows = exchange(part, far, near, dots)
     return call(

time: 131 us -> 122 us (0.931)
  blocking collectives: 11.2 us -> 4.6 us
  Pallas kernels: 21.4 us -> 16.4 us
  starting transfers between devices: 81.8 us -> 83.8 us
    all_to_all x1 -> x0, blocking collectives: 11.2 us -> none  [gather_parts(): lax.all_to_all(spread, ('slab', 'dom'), 0, 0, axis_index_groups=groups)]
    pallas_call x9 -> x10, Pallas kernels: 21.4 us -> 16.4 us  [call(): pl.pallas_call(kernel, out_shape=tuple((jax.ShapeDtypeStruct(*(o if isins...]
    psum x0 -> x1, blocking collectives: none -> 4.6 us  [exchange(): dots = lax.psum(dots, ('slab', 'dom'), axis_index_groups=cores)]
    all_to_all x1, starting transfers between devices: 7.39 us -> 9.71 us  [gather_parts(): lax.all_to_all(spread, ('slab', 'dom'), 0, 0, axis_index_groups=groups)]
    all_to_all x1, waiting for transfers between devices: 2.32 us -> 0.01 us  [gather_parts(): lax.all_to_all(spread, ('slab', 'dom'), 0, 0, axis_index_groups=groups)]
    ppermute x8, waiting for transfers between devices: 6.53 us -> 8.1 us  [swap(): lax.ppermute(far, axis, far_pairs)]
  transfers between devices with their start and end apart: 17 -> 17, of which waited for: 10 -> 7; matrix products, arithmetic and copies ran while one was open for 0% -> 0% of each run, Pallas kernels for 0% -> 5%
where the time goes in v3:
time: 122 us; the launch traced here: 121 us
  starting transfers between devices  83.8 us (69%)
  Pallas kernels  16.4 us (13%)
  waiting for transfers between devices  14.6 us (12%)
  blocking collectives  4.6 us (4%)
    ppermute x8, starting transfers between devices, swap(): lax.ppermute(far, axis, far_pairs)  45.9 us
    ppermute x8, starting transfers between devices, swap(): lax.ppermute(near, axis, near_pairs)  28.3 us
    pallas_call x10, Pallas kernels, call(): pl.pallas_call(kernel, out_shape=tuple((jax.ShapeDtypeStruct(*(o if isins...  16.4 us
    all_to_all x1, starting transfers between devices, gather_parts(): lax.all_to_all(spread, ('slab', 'dom'), 0, 0, axis_index_groups=groups)  9.71 us
    ppermute x8, waiting for transfers between devices, swap(): lax.ppermute(far, axis, far_pairs)  8.1 us
    ppermute x8, waiting for transfers between devices, swap(): lax.ppermute(near, axis, near_pairs)  6.47 us
    psum x1, blocking collectives, exchange(): dots = lax.psum(dots, ('slab', 'dom'), axis_index_groups=cores)  4.6 us
  transfers between devices with their start and end apart: 17, of which 7 were waited for; matrix products, arithmetic and copies ran while one was open for 0% of the time, Pallas kernels for 5%

profile of v3, /device:TPU:1, one launch (start us, length us, event | category | flops | bytes accessed | tf_op | source)
XLA Modules:
  0.0 121.0 jit_solution(2575495235576002128)
XLA Ops:
  0.6 3.6 %advect.1 = (f32[3,7,7,8,128]{4,3,2,1,0:T(8,128)S(1)}, f32[3,7,7,8,128]{4,3,2,1,0:T(8,128)S(1)}, f32[3,7,8,128]{3,2,1,0:T(8,128)S(1)}, f32[3,7,8,128]{3,2,1,0:T(8,128)S(1)}, f32[8,128]{1,0:T(8,128)S(1)}) custom-call(f32[3,343,128]{2,1,0:T(8,128)} %vel_hbm.1, s32[1,128]{1,0:T(1,128)} %bitcast.8, s32[1,128]{1,0:T(1,128)} %bitcast.12), custom_call_target="tpu_custom_call" | custom-call | tf_op jit(solution)/shard_map/advect/pallas_call | solution.py:403
  4.2 14.4 %collective-permute-start = (f32[3,7,8,128]{3,2,1,0:T(8,128)S(1)}, f32[3,7,8,128]{3,2,1,0:T(8,128)S(1)}, u32[]{:S(2)}, u32[]{:S(2)}) collective-permute-start(f32[3,7,8,128]{3,2,1,0:T(8,128)S(1)} %get-tuple-element.32), channel_id=1, source_target_pairs={{0,480},{32,64},{64,32},{96,128},{128,96},{160,192},{192,160},{224... | collective-permute-start | bytes 258056 | tf_op jit(solution)/shard_map/ppermute | solution.py:425
  18.6 1.9 %collective-permute-start.1 = (f32[3,7,8,128]{3,2,1,0:T(8,128)S(1)}, f32[3,7,8,128]{3,2,1,0:T(8,128)S(1)}, u32[]{:S(2)}, u32[]{:S(2)}) collective-permute-start(f32[3,7,8,128]{3,2,1,0:T(8,128)S(1)} %get-tuple-element.33), channel_id=1, source_target_pairs={{0,32},{32,0},{64,96},{96,64},{128,160},{160,128},{192,224},{224,1... | collective-permute-start | bytes 258056 | tf_op jit(solution)/shard_map/ppermute | solution.py:425
  20.5 5.7 %split.1.split_ref = bf16[672,4096]{1,0:T(8,128)(2,1)S(1)} custom-call(f32[3488,218]{1,0:T(8,128)} %bitcast.11), custom_call_target="tpu_custom_call" | custom-call | tf_op jit(solution)/shard_map/split/pallas_call | solution.py:403
  26.2 0.0 copy-start
  26.2 0.0 collective-permute-done.far_x_ref
  26.2 0.0 collective-permute-done.1.near_x_ref
  26.2 0.1 side.4
  26.4 4.0 %collective-permute-start.2 = (f32[3,7,8,128]{3,2,1,0:T(8,128)S(1)}, f32[3,7,8,128]{3,2,1,0:T(8,128)S(1)}, u32[]{:S(2)}, u32[]{:S(2)}) collective-permute-start(f32[3,7,8,128]{3,2,1,0:T(8,128)S(1)} %get-tuple-element.34), channel_id=1, source_target_pairs={{0,31},{1,2},{2,1},{3,4},{4,3},{5,6},{6,5},{7,8},{8,7},{9,10},{10,... | collective-permute-start | bytes 258056 | tf_op jit(solution)/shard_map/ppermute | solution.py:425
  30.3 5.5 %collective-permute-start.3 = (f32[3,7,8,128]{3,2,1,0:T(8,128)S(1)}, f32[3,7,8,128]{3,2,1,0:T(8,128)S(1)}, u32[]{:S(2)}, u32[]{:S(2)}) collective-permute-start(f32[3,7,8,128]{3,2,1,0:T(8,128)S(1)} %get-tuple-element.35), channel_id=1, source_target_pairs={{0,1},{1,0},{2,3},{3,2},{4,5},{5,4},{6,7},{7,6},{8,9},{9,8},{10,11... | collective-permute-start | bytes 258056 | tf_op jit(solution)/shard_map/ppermute | solution.py:425
  35.8 0.0 collective-permute-done.2.far_y_ref
  35.8 0.9 collective-permute-done.3.near_y_ref
  36.7 0.6 source.1
  37.4 4.0 %collective-permute-start.4 = (f32[1,7,8,128]{3,2,1,0:T(8,128)S(1)}, f32[1,7,8,128]{3,2,1,0:T(8,128)S(1)}, u32[]{:S(2)}, u32[]{:S(2)}) collective-permute-start(f32[1,7,8,128]{3,2,1,0:T(8,128)S(1)} %get-tuple-element.38), channel_id=1, source_target_pairs={{0,480},{32,64},{64,32},{96,128},{128,96},{160,192},{192,160},{224... | collective-permute-start | bytes 86024 | tf_op jit(solution)/shard_map/ppermute | solution.py:425
  41.4 1.9 %collective-permute-start.5 = (f32[1,7,8,128]{3,2,1,0:T(8,128)S(1)}, f32[1,7,8,128]{3,2,1,0:T(8,128)S(1)}, u32[]{:S(2)}, u32[]{:S(2)}) collective-permute-start(f32[1,7,8,128]{3,2,1,0:T(8,128)S(1)} %get-tuple-element.39), channel_id=1, source_target_pairs={{0,32},{32,0},{64,96},{96,64},{128,160},{160,128},{192,224},{224,1... | collective-permute-start | bytes 86024 | tf_op jit(solution)/shard_map/ppermute | solution.py:425
  43.3 4.7 %collective-permute-done.4.far_x_ref = f32[1,7,8,128]{3,2,1,0:T(8,128)S(1)} collective-permute-done((f32[1,7,8,128]{3,2,1,0:T(8,128)S(1)}, f32[1,7,8,128]{3,2,1,0:T(8,128)S(1)}, u32[]{:S(2)}, u32[]{:S(2)}) %collective-permute-start.4) | collective-permute-done | bytes 28704 | tf_op jit(solution)/shard_map/ppermute | solution.py:425
  48.0 0.0 collective-permute-done.5.near_x_ref
  48.0 0.1 side.5
  48.1 1.9 %collective-permute-start.6 = (f32[1,7,8,128]{3,2,1,0:T(8,128)S(1)}, f32[1,7,8,128]{3,2,1,0:T(8,128)S(1)}, u32[]{:S(2)}, u32[]{:S(2)}) collective-permute-start(f32[1,7,8,128]{3,2,1,0:T(8,128)S(1)} %get-tuple-element.40), channel_id=1, source_target_pairs={{0,31},{1,2},{2,1},{3,4},{4,3},{5,6},{6,5},{7,8},{8,7},{9,10},{10,... | collective-permute-start | bytes 86024 | tf_op jit(solution)/shard_map/ppermute | solution.py:425
  50.0 6.9 %collective-permute-start.7 = (f32[1,7,8,128]{3,2,1,0:T(8,128)S(1)}, f32[1,7,8,128]{3,2,1,0:T(8,128)S(1)}, u32[]{:S(2)}, u32[]{:S(2)}) collective-permute-start(f32[1,7,8,128]{3,2,1,0:T(8,128)S(1)} %get-tuple-element.41), channel_id=1, source_target_pairs={{0,1},{1,0},{2,3},{3,2},{4,5},{5,4},{6,7},{7,6},{8,9},{9,8},{10,11... | collective-permute-start | bytes 86024 | tf_op jit(solution)/shard_map/ppermute | solution.py:425
  56.9 0.0 collective-permute-done.6.far_y_ref
  56.9 0.8 collective-permute-done.7.near_y_ref
  57.7 0.0 copy-start.1
  57.7 2.5 %first.1 = (f32[224,128]{1,0:T(8,128)S(1)}, f32[224,128]{1,0:T(8,128)S(1)}, f32[1,7,7,8,128]{4,3,2,1,0:T(8,128)S(1)}, f32[1,7,8,128]{3,2,1,0:T(8,128)S(1)}, f32[1,7,8,128]{3,2,1,0:T(8,128)S(1)}) custom-call(f32[1,7,7,8,128]{4,3,2,1,0:T(8,128)S(1)} %get-tuple-element.37.part_ref, f32[1,7,8,128]{3,2,1,0:T(8,128)S(1)} %collective-permute-done.4.far_x_ref, ...), custom_call_target="tpu_custom_call" | custom-call | tf_op jit(solution)/shard_map/first/pallas_call | solution.py:403
  60.2 5.3 %collective-permute-start.8 = (f32[1,7,8,128]{3,2,1,0:T(8,128)S(1)}, f32[1,7,8,128]{3,2,1,0:T(8,128)S(1)}, u32[]{:S(2)}, u32[]{:S(2)}) collective-permute-start(f32[1,7,8,128]{3,2,1,0:T(8,128)S(1)} %get-tuple-element.45), channel_id=1, source_target_pairs={{0,480},{32,64},{64,32},{96,128},{128,96},{160,192},{192,160},{224... | collective-permute-start | bytes 86024 | tf_op jit(solution)/shard_map/ppermute | solution.py:425
  65.5 1.9 %collective-permute-start.9 = (f32[1,7,8,128]{3,2,1,0:T(8,128)S(1)}, f32[1,7,8,128]{3,2,1,0:T(8,128)S(1)}, u32[]{:S(2)}, u32[]{:S(2)}) collective-permute-start(f32[1,7,8,128]{3,2,1,0:T(8,128)S(1)} %get-tuple-element.46), channel_id=1, source_target_pairs={{0,32},{32,0},{64,96},{96,64},{128,160},{160,128},{192,224},{224,1... | collective-permute-start | bytes 86024 | tf_op jit(solution)/shard_map/ppermute | solution.py:425
  67.4 3.4 %collective-permute-done.8.far_x_ref = f32[1,7,8,128]{3,2,1,0:T(8,128)S(1)} collective-permute-done((f32[1,7,8,128]{3,2,1,0:T(8,128)S(1)}, f32[1,7,8,128]{3,2,1,0:T(8,128)S(1)}, u32[]{:S(2)}, u32[]{:S(2)}) %collective-permute-start.8) | collective-permute-done | bytes 28704 | tf_op jit(solution)/shard_map/ppermute | solution.py:425
  70.8 0.0 collective-permute-done.9.near_x_ref
  70.8 0.1 side.6
  70.9 1.9 %collective-permute-start.10 = (f32[1,7,8,128]{3,2,1,0:T(8,128)S(1)}, f32[1,7,8,128]{3,2,1,0:T(8,128)S(1)}, u32[]{:S(2)}, u32[]{:S(2)}) collective-permute-start(f32[1,7,8,128]{3,2,1,0:T(8,128)S(1)} %get-tuple-element.47), channel_id=1, source_target_pairs={{0,31},{1,2},{2,1},{3,4},{4,3},{5,6},{6,5},{7,8},{8,7},{9,10},{10,... | collective-permute-start | bytes 86024 | tf_op jit(solution)/shard_map/ppermute | solution.py:425
  72.9 6.3 %collective-permute-start.11 = (f32[1,7,8,128]{3,2,1,0:T(8,128)S(1)}, f32[1,7,8,128]{3,2,1,0:T(8,128)S(1)}, u32[]{:S(2)}, u32[]{:S(2)}) collective-permute-start(f32[1,7,8,128]{3,2,1,0:T(8,128)S(1)} %get-tuple-element.48), channel_id=1, source_target_pairs={{0,1},{1,0},{2,3},{3,2},{4,5},{5,4},{6,7},{7,6},{8,9},{9,8},{10,11... | collective-permute-start | bytes 86024 | tf_op jit(solution)/shard_map/ppermute | solution.py:425
  79.2 0.0 collective-permute-done.10.far_y_ref
  79.2 0.8 collective-permute-done.11.near_y_ref
  80.0 0.0 copy-done
  80.0 2.5 %second.1 = (f32[224,128]{1,0:T(8,128)S(1)}, f32[1,128]{1,0:T(1,128)S(1)}, f32[1,7,7,8,128]{4,3,2,1,0:T(8,128)S(1)}, f32[1,7,8,128]{3,2,1,0:T(8,128)S(1)}, f32[1,7,8,128]{3,2,1,0:T(8,128)S(1)}) custom-call(f32[1,7,7,8,128]{4,3,2,1,0:T(8,128)S(1)} %get-tuple-element.44.part_ref, f32[1,7,8,128]{3,2,1,0:T(8,128)S(1)} %collective-permute-done.8.far_x_ref, ...), custom_call_target="tpu_custom_call" | custom-call | tf_op jit(solution)/shard_map/second/pallas_call | solution.py:403
  82.5 4.6 %psum.7 = f32[128]{0:T(128)S(1)} all-reduce(f32[128]{0:T(128)S(1)} %bitcast.10), channel_id=1, replica_groups={{0,1},{2,3},{4,5},{6,7},{8,9},{10,11},{12,13},{14,15},{16,17},{18,19},{..., use_global_device_ids=true, to_apply=%region_0.0 | all-reduce | flops 128 | bytes 1024 | tf_op jit(solution)/shard_map/psum | solution.py:435
  87.1 0.7 broadcast_in_dim.8
  87.8 9.7 %all-to-all-start = ((f32[256,1,128]{2,1,0:T(1,128)}), f32[256,1,128]{2,1,0:T(1,128)S(1)}, u32[]{:S(2)}, u32[]{:S(2)}) async-start(f32[256,1,128]{2,1,0:T(1,128)} %broadcast_in_dim.8), calls=%async_computation | async-start | bytes 262144 | tf_op jit(solution)/shard_map/all_to_all | solution.py:447
  97.6 9.1 %collective-permute-start.12 = (f32[1,7,8,128]{3,2,1,0:T(8,128)S(1)}, f32[1,7,8,128]{3,2,1,0:T(8,128)S(1)}, u32[]{:S(2)}, u32[]{:S(2)}) collective-permute-start(f32[1,7,8,128]{3,2,1,0:T(8,128)S(1)} %get-tuple-element.52), channel_id=1, source_target_pairs={{0,480},{32,64},{64,32},{96,128},{128,96},{160,192},{192,160},{224... | collective-permute-start | bytes 86024 | tf_op jit(solution)/shard_map/ppermute | solution.py:425
  106.7 1.9 %collective-permute-start.13 = (f32[1,7,8,128]{3,2,1,0:T(8,128)S(1)}, f32[1,7,8,128]{3,2,1,0:T(8,128)S(1)}, u32[]{:S(2)}, u32[]{:S(2)}) collective-permute-start(f32[1,7,8,128]{3,2,1,0:T(8,128)S(1)} %get-tuple-element.53), channel_id=1, source_target_pairs={{0,32},{32,0},{64,96},{96,64},{128,160},{160,128},{192,224},{224,1... | collective-permute-start | bytes 86024 | tf_op jit(solution)/shard_map/ppermute | solution.py:425
  108.7 0.0 collective-permute-done.12.far_x_ref
  108.7 2.8 %collective-permute-done.13.near_x_ref = f32[1,7,8,128]{3,2,1,0:T(8,128)S(1)} collective-permute-done((f32[1,7,8,128]{3,2,1,0:T(8,128)S(1)}, f32[1,7,8,128]{3,2,1,0:T(8,128)S(1)}, u32[]{:S(2)}, u32[]{:S(2)}) %collective-permute-start.13) | collective-permute-done | bytes 28704 | tf_op jit(solution)/shard_map/ppermute | solution.py:425
  111.4 0.1 side.7
  111.5 5.2 %collective-permute-start.14 = (f32[1,7,8,128]{3,2,1,0:T(8,128)S(1)}, f32[1,7,8,128]{3,2,1,0:T(8,128)S(1)}, u32[]{:S(2)}, u32[]{:S(2)}) collective-permute-start(f32[1,7,8,128]{3,2,1,0:T(8,128)S(1)} %get-tuple-element.54), channel_id=1, source_target_pairs={{0,31},{1,2},{2,1},{3,4},{4,3},{5,6},{6,5},{7,8},{8,7},{9,10},{10,... | collective-permute-start | bytes 86024 | tf_op jit(solution)/shard_map/ppermute | solution.py:425
  116.7 1.9 %collective-permute-start.15 = (f32[1,7,8,128]{3,2,1,0:T(8,128)S(1)}, f32[1,7,8,128]{3,2,1,0:T(8,128)S(1)}, u32[]{:S(2)}, u32[]{:S(2)}) collective-permute-start(f32[1,7,8,128]{3,2,1,0:T(8,128)S(1)} %get-tuple-element.55), channel_id=1, source_target_pairs={{0,1},{1,0},{2,3},{3,2},{4,5},{5,4},{6,7},{7,6},{8,9},{9,8},{10,11... | collective-permute-start | bytes 86024 | tf_op jit(solution)/shard_map/ppermute | solution.py:425
  118.7 0.0 collective-permute-done.14.far_y_ref
  118.7 1.2 collective-permute-done.15.near_y_ref
  119.8 0.0 all-to-all-done
  119.8 0.0 copy-done.1
  119.8 1.1 finish.1
Async XLA Ops:
  4.2 22.0 %collective-permute-start = (f32[3,7,8,128]{3,2,1,0:T(8,128)S(1)}, f32[3,7,8,128]{3,2,1,0:T(8,128)S(1)}, u32[]{:S(2)}, u32[]{:S(2)}) collective-permute-start(f32[3,7,8,128]{3,2,1,0:T(8,128)S(1)} %get-tuple-element.32), channel_id=1, source_target_pairs={{0,480},{32,64},{64,32},{96,128},{128,96},{160,192},{192,160},{224... | collective-permute-start | bytes 258056 | tf_op jit(solution)/shard_map/ppermute | solution.py:425
  18.6 7.6 %collective-permute-start.1 = (f32[3,7,8,128]{3,2,1,0:T(8,128)S(1)}, f32[3,7,8,128]{3,2,1,0:T(8,128)S(1)}, u32[]{:S(2)}, u32[]{:S(2)}) collective-permute-start(f32[3,7,8,128]{3,2,1,0:T(8,128)S(1)} %get-tuple-element.33), channel_id=1, source_target_pairs={{0,32},{32,0},{64,96},{96,64},{128,160},{160,128},{192,224},{224,1... | collective-permute-start | bytes 258056 | tf_op jit(solution)/shard_map/ppermute | solution.py:425
  26.2 53.8 %copy-start = (f32[224,128]{1,0:T(8,128)S(1)}, f32[224,128]{1,0:T(8,128)}, u32[]{:S(2)}) copy-start(f32[224,128]{1,0:T(8,128)} %constant.2.clone.shell_ref) | copy-start | bytes 344068
  26.4 9.4 %collective-permute-start.2 = (f32[3,7,8,128]{3,2,1,0:T(8,128)S(1)}, f32[3,7,8,128]{3,2,1,0:T(8,128)S(1)}, u32[]{:S(2)}, u32[]{:S(2)}) collective-permute-start(f32[3,7,8,128]{3,2,1,0:T(8,128)S(1)} %get-tuple-element.34), channel_id=1, source_target_pairs={{0,31},{1,2},{2,1},{3,4},{4,3},{5,6},{6,5},{7,8},{8,7},{9,10},{10,... | collective-permute-start | bytes 258056 | tf_op jit(solution)/shard_map/ppermute | solution.py:425
  30.3 6.4 %collective-permute-start.3 = (f32[3,7,8,128]{3,2,1,0:T(8,128)S(1)}, f32[3,7,8,128]{3,2,1,0:T(8,128)S(1)}, u32[]{:S(2)}, u32[]{:S(2)}) collective-permute-start(f32[3,7,8,128]{3,2,1,0:T(8,128)S(1)} %get-tuple-element.35), channel_id=1, source_target_pairs={{0,1},{1,0},{2,3},{3,2},{4,5},{5,4},{6,7},{7,6},{8,9},{9,8},{10,11... | collective-permute-start | bytes 258056 | tf_op jit(solution)/shard_map/ppermute | solution.py:425
  37.4 10.6 %collective-permute-start.4 = (f32[1,7,8,128]{3,2,1,0:T(8,128)S(1)}, f32[1,7,8,128]{3,2,1,0:T(8,128)S(1)}, u32[]{:S(2)}, u32[]{:S(2)}) collective-permute-start(f32[1,7,8,128]{3,2,1,0:T(8,128)S(1)} %get-tuple-element.38), channel_id=1, source_target_pairs={{0,480},{32,64},{64,32},{96,128},{128,96},{160,192},{192,160},{224... | collective-permute-start | bytes 86024 | tf_op jit(solution)/shard_map/ppermute | solution.py:425
  41.4 6.6 %collective-permute-start.5 = (f32[1,7,8,128]{3,2,1,0:T(8,128)S(1)}, f32[1,7,8,128]{3,2,1,0:T(8,128)S(1)}, u32[]{:S(2)}, u32[]{:S(2)}) collective-permute-start(f32[1,7,8,128]{3,2,1,0:T(8,128)S(1)} %get-tuple-element.39), channel_id=1, source_target_pairs={{0,32},{32,0},{64,96},{96,64},{128,160},{160,128},{192,224},{224,1... | collective-permute-start | bytes 86024 | tf_op jit(solution)/shard_map/ppermute | solution.py:425
  48.1 8.8 %collective-permute-start.6 = (f32[1,7,8,128]{3,2,1,0:T(8,128)S(1)}, f32[1,7,8,128]{3,2,1,0:T(8,128)S(1)}, u32[]{:S(2)}, u32[]{:S(2)}) collective-permute-start(f32[1,7,8,128]{3,2,1,0:T(8,128)S(1)} %get-tuple-element.40), channel_id=1, source_target_pairs={{0,31},{1,2},{2,1},{3,4},{4,3},{5,6},{6,5},{7,8},{8,7},{9,10},{10,... | collective-permute-start | bytes 86024 | tf_op jit(solution)/shard_map/ppermute | solution.py:425
  50.0 7.7 %collective-permute-start.7 = (f32[1,7,8,128]{3,2,1,0:T(8,128)S(1)}, f32[1,7,8,128]{3,2,1,0:T(8,128)S(1)}, u32[]{:S(2)}, u32[]{:S(2)}) collective-permute-start(f32[1,7,8,128]{3,2,1,0:T(8,128)S(1)} %get-tuple-element.41), channel_id=1, source_target_pairs={{0,1},{1,0},{2,3},{3,2},{4,5},{5,4},{6,7},{7,6},{8,9},{9,8},{10,11... | collective-permute-start | bytes 86024 | tf_op jit(solution)/shard_map/ppermute | solution.py:425
  57.7 62.1 %copy-start.1 = (s32[1,1,128]{2,1,0:T(1,128)S(1)}, s32[1,1,128]{2,1,0:T(1,128)}, u32[]{:S(2)}) copy-start(s32[1,1,128]{2,1,0:T(1,128)} %param.6) | copy-start | bytes 1540
  60.2 10.6 %collective-permute-start.8 = (f32[1,7,8,128]{3,2,1,0:T(8,128)S(1)}, f32[1,7,8,128]{3,2,1,0:T(8,128)S(1)}, u32[]{:S(2)}, u32[]{:S(2)}) collective-permute-start(f32[1,7,8,128]{3,2,1,0:T(8,128)S(1)} %get-tuple-element.45), channel_id=1, source_target_pairs={{0,480},{32,64},{64,32},{96,128},{128,96},{160,192},{192,160},{224... | collective-permute-start | bytes 86024 | tf_op jit(solution)/shard_map/ppermute | solution.py:425
  65.5 5.3 %collective-permute-start.9 = (f32[1,7,8,128]{3,2,1,0:T(8,128)S(1)}, f32[1,7,8,128]{3,2,1,0:T(8,128)S(1)}, u32[]{:S(2)}, u32[]{:S(2)}) collective-permute-start(f32[1,7,8,128]{3,2,1,0:T(8,128)S(1)} %get-tuple-element.46), channel_id=1, source_target_pairs={{0,32},{32,0},{64,96},{96,64},{128,160},{160,128},{192,224},{224,1... | collective-permute-start | bytes 86024 | tf_op jit(solution)/shard_map/ppermute | solution.py:425
  70.9 8.3 %collective-permute-start.10 = (f32[1,7,8,128]{3,2,1,0:T(8,128)S(1)}, f32[1,7,8,128]{3,2,1,0:T(8,128)S(1)}, u32[]{:S(2)}, u32[]{:S(2)}) collective-permute-start(f32[1,7,8,128]{3,2,1,0:T(8,128)S(1)} %get-tuple-element.47), channel_id=1, source_target_pairs={{0,31},{1,2},{2,1},{3,4},{4,3},{5,6},{6,5},{7,8},{8,7},{9,10},{10,... | collective-permute-start | bytes 86024 | tf_op jit(solution)/shard_map/ppermute | solution.py:425
  72.9 7.2 %collective-permute-start.11 = (f32[1,7,8,128]{3,2,1,0:T(8,128)S(1)}, f32[1,7,8,128]{3,2,1,0:T(8,128)S(1)}, u32[]{:S(2)}, u32[]{:S(2)}) collective-permute-start(f32[1,7,8,128]{3,2,1,0:T(8,128)S(1)} %get-tuple-element.48), channel_id=1, source_target_pairs={{0,1},{1,0},{2,3},{3,2},{4,5},{5,4},{6,7},{7,6},{8,9},{9,8},{10,11... | collective-permute-start | bytes 86024 | tf_op jit(solution)/shard_map/ppermute | solution.py:425
  87.8 32.0 %all-to-all-start = ((f32[256,1,128]{2,1,0:T(1,128)}), f32[256,1,128]{2,1,0:T(1,128)S(1)}, u32[]{:S(2)}, u32[]{:S(2)}) async-start(f32[256,1,128]{2,1,0:T(1,128)} %broadcast_in_dim.8), calls=%async_computation | async-start | bytes 262144 | tf_op jit(solution)/shard_map/all_to_all | solution.py:447
  97.6 11.1 %collective-permute-start.12 = (f32[1,7,8,128]{3,2,1,0:T(8,128)S(1)}, f32[1,7,8,128]{3,2,1,0:T(8,128)S(1)}, u32[]{:S(2)}, u32[]{:S(2)}) collective-permute-start(f32[1,7,8,128]{3,2,1,0:T(8,128)S(1)} %get-tuple-element.52), channel_id=1, source_target_pairs={{0,480},{32,64},{64,32},{96,128},{128,96},{160,192},{192,160},{224... | collective-permute-start | bytes 86024 | tf_op jit(solution)/shard_map/ppermute | solution.py:425
  106.7 4.7 %collective-permute-start.13 = (f32[1,7,8,128]{3,2,1,0:T(8,128)S(1)}, f32[1,7,8,128]{3,2,1,0:T(8,128)S(1)}, u32[]{:S(2)}, u32[]{:S(2)}) collective-permute-start(f32[1,7,8,128]{3,2,1,0:T(8,128)S(1)} %get-tuple-element.53), channel_id=1, source_target_pairs={{0,32},{32,0},{64,96},{96,64},{128,160},{160,128},{192,224},{224,1... | collective-permute-start | bytes 86024 | tf_op jit(solution)/shard_map/ppermute | solution.py:425
  111.5 7.2 %collective-permute-start.14 = (f32[1,7,8,128]{3,2,1,0:T(8,128)S(1)}, f32[1,7,8,128]{3,2,1,0:T(8,128)S(1)}, u32[]{:S(2)}, u32[]{:S(2)}) collective-permute-start(f32[1,7,8,128]{3,2,1,0:T(8,128)S(1)} %get-tuple-element.54), channel_id=1, source_target_pairs={{0,31},{1,2},{2,1},{3,4},{4,3},{5,6},{6,5},{7,8},{8,7},{9,10},{10,... | collective-permute-start | bytes 86024 | tf_op jit(solution)/shard_map/ppermute | solution.py:425
  116.7 3.1 %collective-permute-start.15 = (f32[1,7,8,128]{3,2,1,0:T(8,128)S(1)}, f32[1,7,8,128]{3,2,1,0:T(8,128)S(1)}, u32[]{:S(2)}, u32[]{:S(2)}) collective-permute-start(f32[1,7,8,128]{3,2,1,0:T(8,128)S(1)} %get-tuple-element.55), channel_id=1, source_target_pairs={{0,1},{1,0},{2,3},{3,2},{4,5},{5,4},{6,7},{7,6},{8,9},{9,8},{10,11... | collective-permute-start | bytes 86024 | tf_op jit(solution)/shard_map/ppermute | solution.py:425

commit v4 on v3

--- a/solution.py
+++ b/solution.py
@@ -1,3 +1,5 @@
+import functools
+
 import jax
 import jax.numpy as jnp
 import numpy as np
@@ -283,33 +285,51 @@
     return high, middle, (rest - middle.astype(F32)).astype(BF16)
 
 
-def split_kernel(schur_hbm, split_ref, schur_ref, left_ref, right_ref, sems):
-    parts = 2
-    size = MODES * CLASSES // parts
+HALF = 8
+
+
+def split_kernel(half, schur_hbm, split_ref, schur_ref, left_ref, right_ref, sems):
     copies = [
         pltpu.make_async_copy(
-            schur_hbm.at[pl.ds(size * k, size)], schur_ref.at[pl.ds(size * k, size)], sems.at[k]
+            schur_hbm.at[pl.ds(109 * k, 109), pl.ds(HALF * half, HALF)],
+            schur_ref.at[pl.ds(109 * k, 109)],
+            sems.at[k],
         )
-        for k in range(parts)
+        for k in range(2)
     ]
     for copy in copies:
         copy.start()
     for k in range(3):
-        split_ref[224 * k + 208 : 224 * k + 224] = jnp.zeros((16, 256 * CLASSES), BF16)
+        split_ref[224 * k + 208 : 224 * k + 224] = jnp.zeros((16, 256 * HALF), BF16)
     right_ref[...] = jnp.zeros(right_ref.shape, F32)
     for copy in copies:
         copy.wait()
-    left_ref[...] = schur_ref[:, :LANES]
-    right_ref[:, : MODES - LANES] = schur_ref[:, LANES:]
-    for c in range(CLASSES):
-        for half, half_ref in enumerate((left_ref, right_ref)):
-            block = half_ref[pl.ds(c, MODES, stride=CLASSES), :]
-            place = LANES * (2 * c + half)
+    left_ref[...] = schur_ref[:, :, :LANES].reshape(MODES * HALF, LANES)
+    right_ref[:, : MODES - LANES] = schur_ref[:, :, LANES:].reshape(MODES * HALF, MODES - LANES)
+    for c in range(HALF):
+        for side, side_ref in enumerate((left_ref, right_ref)):
+            block = side_ref[pl.ds(c, MODES, stride=HALF), :]
+            place = LANES * (2 * c + side)
             for k, term in enumerate(terms(block)):
                 split_ref[224 * k : 224 * k + MODES, place : place + LANES] = term
 
 
-def multiply_blocks(split_ref, class_ref, modes_ref, image_ref, right_ref, last_ref):
+def split_half(schur, half):
+    return call(
+        functools.partial(split_kernel, half),
+        [((672, 256 * HALF), BF16)],
+        (schur,),
+        [
+            (MODES, HALF, MODES),
+            *[(MODES * HALF, LANES)] * 2,
+            pltpu.SemaphoreType.DMA((2,)),
+        ],
+        name="split",
+        hbm=(0,),
+    )[0]
+
+
+def multiply_blocks(split_refs, class_ref, modes_ref, image_ref, right_ref, last_ref):
     high, middle, low = terms(modes_ref[...])
     pair = jnp.concatenate([high, middle], axis=1)
     zeros = jnp.zeros((32, 2 * LANES), BF16)
@@ -320,9 +340,12 @@
         right_ref[256 * c + 224 : 256 * c + 256] = zeros
         last_ref[256 * c : 256 * c + 224] = low * chosen
         last_ref[256 * c + 224 : 256 * c + 256] = zeros[:, :LANES]
-    total = jnp.dot(split_ref[...], right_ref[...], preferred_element_type=F32)
+    total, small = 0.0, 0.0
+    for half, split_ref in enumerate(split_refs):
+        rows = pl.ds(256 * HALF * half, 256 * HALF)
+        total = total + jnp.dot(split_ref[...], right_ref[rows], preferred_element_type=F32)
+        small = small + jnp.dot(split_ref[0:224], last_ref[rows], preferred_element_type=F32)
     total = total[:, :LANES] + total[:, LANES:]
-    small = jnp.dot(split_ref[0:224], last_ref[...], preferred_element_type=F32)
     image_ref[...] = total[0:224] + (total[224:448] + (total[448:672] + small))
 
 
@@ -340,21 +363,21 @@
 
 
 def first_apply_kernel(
-    part_ref, far_x_ref, near_x_ref, far_y_ref, near_y_ref, split_ref, class_ref,
+    part_ref, far_x_ref, near_x_ref, far_y_ref, near_y_ref, split_0, split_1, class_ref,
     load_ref, image_ref, out_ref, far_ref, near_ref, full_ref, right_ref, last_ref,
 ):
     gather_modes(part_ref, far_x_ref, near_x_ref, far_y_ref, near_y_ref, full_ref, load_ref)
-    multiply_blocks(split_ref, class_ref, load_ref, image_ref, right_ref, last_ref)
+    multiply_blocks((split_0, split_1), class_ref, load_ref, image_ref, right_ref, last_ref)
     scatter_modes(image_ref, full_ref, out_ref, far_ref, near_ref)
 
 
 def second_apply_kernel(
-    part_ref, far_x_ref, near_x_ref, far_y_ref, near_y_ref, split_ref, class_ref, load_ref,
+    part_ref, far_x_ref, near_x_ref, far_y_ref, near_y_ref, split_0, split_1, class_ref, load_ref,
     first_ref, shell_ref, power_ref, dots_ref, out_ref, far_ref, near_ref, image_ref, full_ref, right_ref,
     last_ref,
 ):
     gather_modes(part_ref, far_x_ref, near_x_ref, far_y_ref, near_y_ref, full_ref, power_ref)
-    multiply_blocks(split_ref, class_ref, power_ref, image_ref, right_ref, last_ref)
+    multiply_blocks((split_0, split_1), class_ref, power_ref, image_ref, right_ref, last_ref)
     scatter_modes(image_ref, full_ref, out_ref, far_ref, near_ref)
     load, power, shell = load_ref[...], power_ref[...], shell_ref[...]
     first, image = first_ref[...], image_ref[...]
@@ -373,7 +396,7 @@
     pressure_ref, residual_ref, full_ref, modes_ref,
 ):
     gather_modes(part_ref, far_x_ref, near_x_ref, far_y_ref, near_y_ref, full_ref, modes_ref)
-    dots = jnp.sum(dots_ref[...], axis=0, keepdims=True)
+    dots = jnp.sum(dots_ref[...], axis=0)[0:1]
     square, energy, power_square, cross, power_energy = (dots[:, k : k + 1] for k in range(5))
     step = square / energy
     fresh = square - 2.0 * step * energy + step * step * power_square
@@ -431,9 +454,9 @@
     if beside is not None:
         part, beside = lax.optimization_barrier((part, beside))
     if dots is not None:
-        cores, chips = reduction_groups()
-        dots = lax.psum(dots, ("slab", "dom"), axis_index_groups=cores)
-        rows = gather_parts(dots, chips).reshape(-1, LANES)
+        rows = gather_parts(dots, "dom")
+        far_x, near_x, rows = lax.optimization_barrier((far_x, near_x, rows))
+        rows = gather_parts(rows.sum(axis=0), "slab", 4)
     far, near = call(side_kernel, [(k, 7, 8, LANES)] * 2, (part, far_x, near_x), name="side")
     received = part, far_x, near_x, *swap("dom", far, near)
     if beside is not None:
@@ -441,22 +464,15 @@
     return received if dots is None else (received, rows)
 
 
-def gather_parts(row, groups):
-    count = len(groups[0])
-    spread = jnp.broadcast_to(row.reshape(1, 1, LANES), (count, 1, LANES))
-    return lax.all_to_all(spread, ("slab", "dom"), 0, 0, axis_index_groups=groups)
-
-
-def reduction_groups():
-    total = lax.axis_size("slab") * lax.axis_size("dom")
-    pairs = [[i, i + 1] for i in range(0, total, 2)]
-    return pairs, [list(range(k, total, 2)) for k in range(2)]
+def gather_parts(row, axis, copies=1):
+    spread = jnp.broadcast_to(row[None], (lax.axis_size(axis), copies, LANES))
+    return lax.all_to_all(spread, axis, 0, 0)
 
 
 def per_device(velocity, slot_map, class_index, schur_blocks):
     slots = slot_map.reshape(1, LANES)
     shell = jnp.asarray(SHELL)
-    schur = schur_blocks.transpose(1, 0, 2).reshape(MODES * CLASSES, MODES)
+    schur = schur_blocks.transpose(1, 0, 2)
     face = (7, 8, LANES)
     whole = (7, 7, 8, LANES)
     modes = (224, LANES)
@@ -474,15 +490,7 @@
         name="advect",
         hbm=(0, 1, 2),
     )
-    split = call(
-        split_kernel,
-        [((672, 256 * CLASSES), BF16)],
-        (schur,),
-        [(MODES * CLASSES, MODES), *[(MODES * CLASSES, LANES)] * 2, pltpu.SemaphoreType.DMA((2,))],
-        name="split",
-        hbm=(0,),
-    )[0]
-    received, split = exchange(part, far, near, beside=split)
+    received, split_0 = exchange(part, far, near, beside=split_half(schur, 0))
     part, far, near = call(
         source_kernel,
         [(1, *whole), (1, *face), (1, *face)],
@@ -490,17 +498,18 @@
         [(3, *whole)],
         name="source",
     )
+    received, split_1 = exchange(part, far, near, beside=split_half(schur, 1))
     load, first, part, far, near = call(
         first_apply_kernel,
         [modes, modes, (1, *whole), (1, *face), (1, *face)],
-        (*exchange(part, far, near), split, classes),
+        (*received, split_0, split_1, classes),
         [(392, LANES), *rights],
         name="first",
     )
     power, dots, part, far, near = call(
         second_apply_kernel,
         [modes, (1, LANES), (1, *whole), (1, *face), (1, *face)],
-        (*exchange(part, far, near), split, classes, load, first, shell),
+        (*exchange(part, far, near), split_0, split_1, classes, load, first, shell),
         [modes, (392, LANES), *rights],
         name="second",
     )

time: 122 us -> 121 us (level)
  the two profiles are of different devices: /device:TPU:1 before, /device:TPU:2 now
where the time goes in v4:
time: 121 us; the launch traced here: 120 us
  starting transfers between devices  81.1 us (67%)
  waiting for transfers between devices  20.3 us (17%)
  Pallas kernels  16.4 us (14%)
  local copies, waits for them, and re-layouts  1.25 us (1%)
    ppermute x8, starting transfers between devices, swap(): lax.ppermute(far, axis, far_pairs)  44.3 us
    ppermute x8, starting transfers between devices, swap(): lax.ppermute(near, axis, near_pairs)  19.5 us
    all_to_all x2, starting transfers between devices, gather_parts(): return lax.all_to_all(spread, axis, 0, 0)  17.2 us
    pallas_call x11, Pallas kernels, call(): pl.pallas_call(kernel, out_shape=tuple((jax.ShapeDtypeStruct(*(o if isins...  16.4 us
    ppermute x8, waiting for transfers between devices, swap(): lax.ppermute(far, axis, far_pairs)  8.45 us
    all_to_all x2, waiting for transfers between devices, gather_parts(): return lax.all_to_all(spread, axis, 0, 0)  6.06 us
    ppermute x8, waiting for transfers between devices, swap(): lax.ppermute(near, axis, near_pairs)  5.8 us
  transfers between devices with their start and end apart: 18, of which 10 were waited for; matrix products, arithmetic and copies ran while one was open for 0% of the time, Pallas kernels for 5%

profile of v4, /device:TPU:2, one launch (start us, length us, event | category | flops | bytes accessed | tf_op | source)
XLA Modules:
  0.0 120.0 jit_solution(10822618808218784740)
XLA Ops:
  0.6 3.6 %advect.1 = (f32[3,7,7,8,128]{4,3,2,1,0:T(8,128)S(1)}, f32[3,7,7,8,128]{4,3,2,1,0:T(8,128)S(1)}, f32[3,7,8,128]{3,2,1,0:T(8,128)S(1)}, f32[3,7,8,128]{3,2,1,0:T(8,128)S(1)}, f32[8,128]{1,0:T(8,128)S(1)}) custom-call(f32[3,343,128]{2,1,0:T(8,128)} %vel_hbm.1, s32[1,128]{1,0:T(1,128)} %bitcast.4, s32[1,128]{1,0:T(1,128)} %bitcast.9), custom_call_target="tpu_custom_call" | custom-call | tf_op jit(solution)/shard_map/advect/pallas_call | solution.py:426
  4.2 13.8 %collective-permute-start = (f32[3,7,8,128]{3,2,1,0:T(8,128)S(1)}, f32[3,7,8,128]{3,2,1,0:T(8,128)S(1)}, u32[]{:S(2)}, u32[]{:S(2)}) collective-permute-start(f32[3,7,8,128]{3,2,1,0:T(8,128)S(1)} %get-tuple-element.37), channel_id=1, source_target_pairs={{0,480},{32,64},{64,32},{96,128},{128,96},{160,192},{192,160},{224... | collective-permute-start | bytes 258056 | tf_op jit(solution)/shard_map/ppermute | solution.py:448
  18.1 1.9 %collective-permute-start.1 = (f32[3,7,8,128]{3,2,1,0:T(8,128)S(1)}, f32[3,7,8,128]{3,2,1,0:T(8,128)S(1)}, u32[]{:S(2)}, u32[]{:S(2)}) collective-permute-start(f32[3,7,8,128]{3,2,1,0:T(8,128)S(1)} %get-tuple-element.38), channel_id=1, source_target_pairs={{0,32},{32,0},{64,96},{96,64},{128,160},{160,128},{192,224},{224,1... | collective-permute-start | bytes 258056 | tf_op jit(solution)/shard_map/ppermute | solution.py:448
  20.0 2.9 %split.2.split_0 = bf16[672,2048]{1,0:T(8,128)(2,1)S(1)} custom-call(f32[218,16,218]{2,1,0:T(8,128)} %bitcast.7), custom_call_target="tpu_custom_call" | custom-call | tf_op jit(solution)/shard_map/split/pallas_call | solution.py:426
  22.9 0.0 collective-permute-done.far_x_ref
  22.9 1.6 %collective-permute-done.1.near_x_ref = f32[3,7,8,128]{3,2,1,0:T(8,128)S(1)} collective-permute-done((f32[3,7,8,128]{3,2,1,0:T(8,128)S(1)}, f32[3,7,8,128]{3,2,1,0:T(8,128)S(1)}, u32[]{:S(2)}, u32[]{:S(2)}) %collective-permute-start.1) | collective-permute-done | bytes 86048 | tf_op jit(solution)/shard_map/ppermute | solution.py:448
  24.4 0.1 side.4
  24.6 1.9 %collective-permute-start.2 = (f32[3,7,8,128]{3,2,1,0:T(8,128)S(1)}, f32[3,7,8,128]{3,2,1,0:T(8,128)S(1)}, u32[]{:S(2)}, u32[]{:S(2)}) collective-permute-start(f32[3,7,8,128]{3,2,1,0:T(8,128)S(1)} %get-tuple-element.39), channel_id=1, source_target_pairs={{0,31},{1,2},{2,1},{3,4},{4,3},{5,6},{6,5},{7,8},{8,7},{9,10},{10,... | collective-permute-start | bytes 258056 | tf_op jit(solution)/shard_map/ppermute | solution.py:448
  26.5 3.5 %collective-permute-start.3 = (f32[3,7,8,128]{3,2,1,0:T(8,128)S(1)}, f32[3,7,8,128]{3,2,1,0:T(8,128)S(1)}, u32[]{:S(2)}, u32[]{:S(2)}) collective-permute-start(f32[3,7,8,128]{3,2,1,0:T(8,128)S(1)} %get-tuple-element.40), channel_id=1, source_target_pairs={{0,1},{1,0},{2,3},{3,2},{4,5},{5,4},{6,7},{7,6},{8,9},{9,8},{10,11... | collective-permute-start | bytes 258056 | tf_op jit(solution)/shard_map/ppermute | solution.py:448
  30.0 0.4 collective-permute-done.2.far_y_ref
  30.4 0.5 collective-permute-done.3.near_y_ref
  30.9 0.6 source.1
  31.6 7.7 %collective-permute-start.4 = (f32[1,7,8,128]{3,2,1,0:T(8,128)S(1)}, f32[1,7,8,128]{3,2,1,0:T(8,128)S(1)}, u32[]{:S(2)}, u32[]{:S(2)}) collective-permute-start(f32[1,7,8,128]{3,2,1,0:T(8,128)S(1)} %get-tuple-element.44), channel_id=1, source_target_pairs={{0,480},{32,64},{64,32},{96,128},{128,96},{160,192},{192,160},{224... | collective-permute-start | bytes 86024 | tf_op jit(solution)/shard_map/ppermute | solution.py:448
  39.2 1.9 %collective-permute-start.5 = (f32[1,7,8,128]{3,2,1,0:T(8,128)S(1)}, f32[1,7,8,128]{3,2,1,0:T(8,128)S(1)}, u32[]{:S(2)}, u32[]{:S(2)}) collective-permute-start(f32[1,7,8,128]{3,2,1,0:T(8,128)S(1)} %get-tuple-element.45), channel_id=1, source_target_pairs={{0,32},{32,0},{64,96},{96,64},{128,160},{160,128},{192,224},{224,1... | collective-permute-start | bytes 86024 | tf_op jit(solution)/shard_map/ppermute | solution.py:448
  41.1 2.9 %split.3.split_1 = bf16[672,2048]{1,0:T(8,128)(2,1)S(1)} custom-call(f32[218,16,218]{2,1,0:T(8,128)} %bitcast.8), custom_call_target="tpu_custom_call" | custom-call | tf_op jit(solution)/shard_map/split/pallas_call | solution.py:426
  44.0 0.0 collective-permute-done.4.far_x_ref
  44.0 0.9 collective-permute-done.5.near_x_ref
  45.0 0.1 side.5
  45.1 2.2 %collective-permute-start.6 = (f32[1,7,8,128]{3,2,1,0:T(8,128)S(1)}, f32[1,7,8,128]{3,2,1,0:T(8,128)S(1)}, u32[]{:S(2)}, u32[]{:S(2)}) collective-permute-start(f32[1,7,8,128]{3,2,1,0:T(8,128)S(1)} %get-tuple-element.46), channel_id=1, source_target_pairs={{0,31},{1,2},{2,1},{3,4},{4,3},{5,6},{6,5},{7,8},{8,7},{9,10},{10,... | collective-permute-start | bytes 86024 | tf_op jit(solution)/shard_map/ppermute | solution.py:448
  47.3 2.9 %collective-permute-start.7 = (f32[1,7,8,128]{3,2,1,0:T(8,128)S(1)}, f32[1,7,8,128]{3,2,1,0:T(8,128)S(1)}, u32[]{:S(2)}, u32[]{:S(2)}) collective-permute-start(f32[1,7,8,128]{3,2,1,0:T(8,128)S(1)} %get-tuple-element.47), channel_id=1, source_target_pairs={{0,1},{1,0},{2,3},{3,2},{4,5},{5,4},{6,7},{7,6},{8,9},{9,8},{10,11... | collective-permute-start | bytes 86024 | tf_op jit(solution)/shard_map/ppermute | solution.py:448
  50.2 0.0 collective-permute-done.6.far_y_ref
  50.3 0.8 collective-permute-done.7.near_y_ref
  51.1 0.0 copy-start
  51.1 2.5 %first.1 = (f32[224,128]{1,0:T(8,128)S(1)}, f32[224,128]{1,0:T(8,128)S(1)}, f32[1,7,7,8,128]{4,3,2,1,0:T(8,128)S(1)}, f32[1,7,8,128]{3,2,1,0:T(8,128)S(1)}, f32[1,7,8,128]{3,2,1,0:T(8,128)S(1)}) custom-call(f32[1,7,7,8,128]{4,3,2,1,0:T(8,128)S(1)} %get-tuple-element.43.part_ref, f32[1,7,8,128]{3,2,1,0:T(8,128)S(1)} %collective-permute-done.4.far_x_ref, ...), custom_call_target="tpu_custom_call" | custom-call | tf_op jit(solution)/shard_map/first/pallas_call | solution.py:426
  53.5 6.0 %collective-permute-start.8 = (f32[1,7,8,128]{3,2,1,0:T(8,128)S(1)}, f32[1,7,8,128]{3,2,1,0:T(8,128)S(1)}, u32[]{:S(2)}, u32[]{:S(2)}) collective-permute-start(f32[1,7,8,128]{3,2,1,0:T(8,128)S(1)} %get-tuple-element.52), channel_id=1, source_target_pairs={{0,480},{32,64},{64,32},{96,128},{128,96},{160,192},{192,160},{224... | collective-permute-start | bytes 86024 | tf_op jit(solution)/shard_map/ppermute | solution.py:448
  59.6 1.9 %collective-permute-start.9 = (f32[1,7,8,128]{3,2,1,0:T(8,128)S(1)}, f32[1,7,8,128]{3,2,1,0:T(8,128)S(1)}, u32[]{:S(2)}, u32[]{:S(2)}) collective-permute-start(f32[1,7,8,128]{3,2,1,0:T(8,128)S(1)} %get-tuple-element.53), channel_id=1, source_target_pairs={{0,32},{32,0},{64,96},{96,64},{128,160},{160,128},{192,224},{224,1... | collective-permute-start | bytes 86024 | tf_op jit(solution)/shard_map/ppermute | solution.py:448
  61.5 3.8 %collective-permute-done.8.far_x_ref = f32[1,7,8,128]{3,2,1,0:T(8,128)S(1)} collective-permute-done((f32[1,7,8,128]{3,2,1,0:T(8,128)S(1)}, f32[1,7,8,128]{3,2,1,0:T(8,128)S(1)}, u32[]{:S(2)}, u32[]{:S(2)}) %collective-permute-start.8) | collective-permute-done | bytes 28704 | tf_op jit(solution)/shard_map/ppermute | solution.py:448
  65.3 0.0 collective-permute-done.9.near_x_ref
  65.3 0.1 side.6
  65.4 4.8 %collective-permute-start.10 = (f32[1,7,8,128]{3,2,1,0:T(8,128)S(1)}, f32[1,7,8,128]{3,2,1,0:T(8,128)S(1)}, u32[]{:S(2)}, u32[]{:S(2)}) collective-permute-start(f32[1,7,8,128]{3,2,1,0:T(8,128)S(1)} %get-tuple-element.54), channel_id=1, source_target_pairs={{0,31},{1,2},{2,1},{3,4},{4,3},{5,6},{6,5},{7,8},{8,7},{9,10},{10,... | collective-permute-start | bytes 86024 | tf_op jit(solution)/shard_map/ppermute | solution.py:448
  70.2 1.9 %collective-permute-start.11 = (f32[1,7,8,128]{3,2,1,0:T(8,128)S(1)}, f32[1,7,8,128]{3,2,1,0:T(8,128)S(1)}, u32[]{:S(2)}, u32[]{:S(2)}) collective-permute-start(f32[1,7,8,128]{3,2,1,0:T(8,128)S(1)} %get-tuple-element.55), channel_id=1, source_target_pairs={{0,1},{1,0},{2,3},{3,2},{4,5},{5,4},{6,7},{7,6},{8,9},{9,8},{10,11... | collective-permute-start | bytes 86024 | tf_op jit(solution)/shard_map/ppermute | solution.py:448
  72.1 0.0 collective-permute-done.10.far_y_ref
  72.1 1.2 collective-permute-done.11.near_y_ref
  73.3 0.0 copy-done
  73.3 0.0 copy-start.1
  73.3 2.5 %second.1 = (f32[224,128]{1,0:T(8,128)S(1)}, f32[1,128]{1,0:T(1,128)S(1)}, f32[1,7,7,8,128]{4,3,2,1,0:T(8,128)S(1)}, f32[1,7,8,128]{3,2,1,0:T(8,128)S(1)}, f32[1,7,8,128]{3,2,1,0:T(8,128)S(1)}) custom-call(f32[1,7,7,8,128]{4,3,2,1,0:T(8,128)S(1)} %get-tuple-element.51.part_ref, f32[1,7,8,128]{3,2,1,0:T(8,128)S(1)} %collective-permute-done.8.far_x_ref, ...), custom_call_target="tpu_custom_call" | custom-call | tf_op jit(solution)/shard_map/second/pallas_call | solution.py:426
  75.8 0.6 broadcast_in_dim.7
  76.4 11.7 %all-to-all-start = ((f32[32,1,128]{2,1,0:T(1,128)}), f32[32,1,128]{2,1,0:T(1,128)S(1)}, u32[]{:S(2)}, u32[]{:S(2)}) async-start(f32[32,1,128]{2,1,0:T(1,128)} %broadcast_in_dim.7), calls=%async_computation | async-start | bytes 32768 | tf_op jit(solution)/shard_map/all_to_all | solution.py:469
  88.2 6.0 %collective-permute-start.12 = (f32[1,7,8,128]{3,2,1,0:T(8,128)S(1)}, f32[1,7,8,128]{3,2,1,0:T(8,128)S(1)}, u32[]{:S(2)}, u32[]{:S(2)}) collective-permute-start(f32[1,7,8,128]{3,2,1,0:T(8,128)S(1)} %get-tuple-element.59), channel_id=1, source_target_pairs={{0,480},{32,64},{64,32},{96,128},{128,96},{160,192},{192,160},{224... | collective-permute-start | bytes 86024 | tf_op jit(solution)/shard_map/ppermute | solution.py:448
  94.2 1.9 %collective-permute-start.13 = (f32[1,7,8,128]{3,2,1,0:T(8,128)S(1)}, f32[1,7,8,128]{3,2,1,0:T(8,128)S(1)}, u32[]{:S(2)}, u32[]{:S(2)}) collective-permute-start(f32[1,7,8,128]{3,2,1,0:T(8,128)S(1)} %get-tuple-element.60), channel_id=1, source_target_pairs={{0,32},{32,0},{64,96},{96,64},{128,160},{160,128},{192,224},{224,1... | collective-permute-start | bytes 86024 | tf_op jit(solution)/shard_map/ppermute | solution.py:448
  96.1 4.2 %collective-permute-done.12.far_x_ref = f32[1,7,8,128]{3,2,1,0:T(8,128)S(1)} collective-permute-done((f32[1,7,8,128]{3,2,1,0:T(8,128)S(1)}, f32[1,7,8,128]{3,2,1,0:T(8,128)S(1)}, u32[]{:S(2)}, u32[]{:S(2)}) %collective-permute-start.12) | collective-permute-done | bytes 28704 | tf_op jit(solution)/shard_map/ppermute | solution.py:448
  100.3 0.0 collective-permute-done.13.near_x_ref
  100.3 0.0 all-to-all-done
  100.3 0.1 reduce_sum.9
  100.4 0.6 broadcast_in_dim.16
  101.0 5.5 %all-to-all-start.1 = ((f32[16,4,128]{2,1,0:T(4,128)}), f32[16,4,128]{2,1,0:T(4,128)S(1)}, u32[]{:S(2)}, u32[]{:S(2)}) async-start(f32[16,4,128]{2,1,0:T(4,128)} %broadcast_in_dim.16), calls=%async_computation.1 | async-start | bytes 65536 | tf_op jit(solution)/shard_map/all_to_all | solution.py:469
  106.5 0.1 side.7
  106.5 1.9 %collective-permute-start.14 = (f32[1,7,8,128]{3,2,1,0:T(8,128)S(1)}, f32[1,7,8,128]{3,2,1,0:T(8,128)S(1)}, u32[]{:S(2)}, u32[]{:S(2)}) collective-permute-start(f32[1,7,8,128]{3,2,1,0:T(8,128)S(1)} %get-tuple-element.64), channel_id=1, source_target_pairs={{0,31},{1,2},{2,1},{3,4},{4,3},{5,6},{6,5},{7,8},{8,7},{9,10},{10,... | collective-permute-start | bytes 86024 | tf_op jit(solution)/shard_map/ppermute | solution.py:448
  108.5 3.5 %collective-permute-start.15 = (f32[1,7,8,128]{3,2,1,0:T(8,128)S(1)}, f32[1,7,8,128]{3,2,1,0:T(8,128)S(1)}, u32[]{:S(2)}, u32[]{:S(2)}) collective-permute-start(f32[1,7,8,128]{3,2,1,0:T(8,128)S(1)} %get-tuple-element.65), channel_id=1, source_target_pairs={{0,1},{1,0},{2,3},{3,2},{4,5},{5,4},{6,7},{7,6},{8,9},{9,8},{10,11... | collective-permute-start | bytes 86024 | tf_op jit(solution)/shard_map/ppermute | solution.py:448
  112.0 0.0 collective-permute-done.14.far_y_ref
  112.0 0.8 collective-permute-done.15.near_y_ref
  112.8 6.1 %all-to-all-done.1.dots_ref = f32[16,4,128]{2,1,0:T(4,128)S(1)} async-done(((f32[16,4,128]{2,1,0:T(4,128)}), f32[16,4,128]{2,1,0:T(4,128)S(1)}, u32[]{:S(2)}, u32[]{:S(2)}) %all-to-all-start.1) | async-done | bytes 32800 | tf_op jit(solution)/shard_map/all_to_all | solution.py:469
  118.9 0.0 copy-done.1
  118.9 1.1 finish.1
Async XLA Ops:
  4.2 18.6 %collective-permute-start = (f32[3,7,8,128]{3,2,1,0:T(8,128)S(1)}, f32[3,7,8,128]{3,2,1,0:T(8,128)S(1)}, u32[]{:S(2)}, u32[]{:S(2)}) collective-permute-start(f32[3,7,8,128]{3,2,1,0:T(8,128)S(1)} %get-tuple-element.37), channel_id=1, source_target_pairs={{0,480},{32,64},{64,32},{96,128},{128,96},{160,192},{192,160},{224... | collective-permute-start | bytes 258056 | tf_op jit(solution)/shard_map/ppermute | solution.py:448
  18.1 6.4 %collective-permute-start.1 = (f32[3,7,8,128]{3,2,1,0:T(8,128)S(1)}, f32[3,7,8,128]{3,2,1,0:T(8,128)S(1)}, u32[]{:S(2)}, u32[]{:S(2)}) collective-permute-start(f32[3,7,8,128]{3,2,1,0:T(8,128)S(1)} %get-tuple-element.38), channel_id=1, source_target_pairs={{0,32},{32,0},{64,96},{96,64},{128,160},{160,128},{192,224},{224,1... | collective-permute-start | bytes 258056 | tf_op jit(solution)/shard_map/ppermute | solution.py:448
  24.6 5.8 %collective-permute-start.2 = (f32[3,7,8,128]{3,2,1,0:T(8,128)S(1)}, f32[3,7,8,128]{3,2,1,0:T(8,128)S(1)}, u32[]{:S(2)}, u32[]{:S(2)}) collective-permute-start(f32[3,7,8,128]{3,2,1,0:T(8,128)S(1)} %get-tuple-element.39), channel_id=1, source_target_pairs={{0,31},{1,2},{2,1},{3,4},{4,3},{5,6},{6,5},{7,8},{8,7},{9,10},{10,... | collective-permute-start | bytes 258056 | tf_op jit(solution)/shard_map/ppermute | solution.py:448
  26.5 4.4 %collective-permute-start.3 = (f32[3,7,8,128]{3,2,1,0:T(8,128)S(1)}, f32[3,7,8,128]{3,2,1,0:T(8,128)S(1)}, u32[]{:S(2)}, u32[]{:S(2)}) collective-permute-start(f32[3,7,8,128]{3,2,1,0:T(8,128)S(1)} %get-tuple-element.40), channel_id=1, source_target_pairs={{0,1},{1,0},{2,3},{3,2},{4,5},{5,4},{6,7},{7,6},{8,9},{9,8},{10,11... | collective-permute-start | bytes 258056 | tf_op jit(solution)/shard_map/ppermute | solution.py:448
  31.6 12.5 %collective-permute-start.4 = (f32[1,7,8,128]{3,2,1,0:T(8,128)S(1)}, f32[1,7,8,128]{3,2,1,0:T(8,128)S(1)}, u32[]{:S(2)}, u32[]{:S(2)}) collective-permute-start(f32[1,7,8,128]{3,2,1,0:T(8,128)S(1)} %get-tuple-element.44), channel_id=1, source_target_pairs={{0,480},{32,64},{64,32},{96,128},{128,96},{160,192},{192,160},{224... | collective-permute-start | bytes 86024 | tf_op jit(solution)/shard_map/ppermute | solution.py:448
  39.2 5.8 %collective-permute-start.5 = (f32[1,7,8,128]{3,2,1,0:T(8,128)S(1)}, f32[1,7,8,128]{3,2,1,0:T(8,128)S(1)}, u32[]{:S(2)}, u32[]{:S(2)}) collective-permute-start(f32[1,7,8,128]{3,2,1,0:T(8,128)S(1)} %get-tuple-element.45), channel_id=1, source_target_pairs={{0,32},{32,0},{64,96},{96,64},{128,160},{160,128},{192,224},{224,1... | collective-permute-start | bytes 86024 | tf_op jit(solution)/shard_map/ppermute | solution.py:448
  45.1 5.2 %collective-permute-start.6 = (f32[1,7,8,128]{3,2,1,0:T(8,128)S(1)}, f32[1,7,8,128]{3,2,1,0:T(8,128)S(1)}, u32[]{:S(2)}, u32[]{:S(2)}) collective-permute-start(f32[1,7,8,128]{3,2,1,0:T(8,128)S(1)} %get-tuple-element.46), channel_id=1, source_target_pairs={{0,31},{1,2},{2,1},{3,4},{4,3},{5,6},{6,5},{7,8},{8,7},{9,10},{10,... | collective-permute-start | bytes 86024 | tf_op jit(solution)/shard_map/ppermute | solution.py:448
  47.3 3.8 %collective-permute-start.7 = (f32[1,7,8,128]{3,2,1,0:T(8,128)S(1)}, f32[1,7,8,128]{3,2,1,0:T(8,128)S(1)}, u32[]{:S(2)}, u32[]{:S(2)}) collective-permute-start(f32[1,7,8,128]{3,2,1,0:T(8,128)S(1)} %get-tuple-element.47), channel_id=1, source_target_pairs={{0,1},{1,0},{2,3},{3,2},{4,5},{5,4},{6,7},{7,6},{8,9},{9,8},{10,11... | collective-permute-start | bytes 86024 | tf_op jit(solution)/shard_map/ppermute | solution.py:448
  51.1 22.2 %copy-start = (f32[224,128]{1,0:T(8,128)S(1)}, f32[224,128]{1,0:T(8,128)}, u32[]{:S(2)}) copy-start(f32[224,128]{1,0:T(8,128)} %constant.4.clone.shell_ref) | copy-start | bytes 344068
  53.5 11.8 %collective-permute-start.8 = (f32[1,7,8,128]{3,2,1,0:T(8,128)S(1)}, f32[1,7,8,128]{3,2,1,0:T(8,128)S(1)}, u32[]{:S(2)}, u32[]{:S(2)}) collective-permute-start(f32[1,7,8,128]{3,2,1,0:T(8,128)S(1)} %get-tuple-element.52), channel_id=1, source_target_pairs={{0,480},{32,64},{64,32},{96,128},{128,96},{160,192},{192,160},{224... | collective-permute-start | bytes 86024 | tf_op jit(solution)/shard_map/ppermute | solution.py:448
  59.6 5.8 %collective-permute-start.9 = (f32[1,7,8,128]{3,2,1,0:T(8,128)S(1)}, f32[1,7,8,128]{3,2,1,0:T(8,128)S(1)}, u32[]{:S(2)}, u32[]{:S(2)}) collective-permute-start(f32[1,7,8,128]{3,2,1,0:T(8,128)S(1)} %get-tuple-element.53), channel_id=1, source_target_pairs={{0,32},{32,0},{64,96},{96,64},{128,160},{160,128},{192,224},{224,1... | collective-permute-start | bytes 86024 | tf_op jit(solution)/shard_map/ppermute | solution.py:448
  65.4 6.7 %collective-permute-start.10 = (f32[1,7,8,128]{3,2,1,0:T(8,128)S(1)}, f32[1,7,8,128]{3,2,1,0:T(8,128)S(1)}, u32[]{:S(2)}, u32[]{:S(2)}) collective-permute-start(f32[1,7,8,128]{3,2,1,0:T(8,128)S(1)} %get-tuple-element.54), channel_id=1, source_target_pairs={{0,31},{1,2},{2,1},{3,4},{4,3},{5,6},{6,5},{7,8},{8,7},{9,10},{10,... | collective-permute-start | bytes 86024 | tf_op jit(solution)/shard_map/ppermute | solution.py:448
  70.2 3.1 %collective-permute-start.11 = (f32[1,7,8,128]{3,2,1,0:T(8,128)S(1)}, f32[1,7,8,128]{3,2,1,0:T(8,128)S(1)}, u32[]{:S(2)}, u32[]{:S(2)}) collective-permute-start(f32[1,7,8,128]{3,2,1,0:T(8,128)S(1)} %get-tuple-element.55), channel_id=1, source_target_pairs={{0,1},{1,0},{2,3},{3,2},{4,5},{5,4},{6,7},{7,6},{8,9},{9,8},{10,11... | collective-permute-start | bytes 86024 | tf_op jit(solution)/shard_map/ppermute | solution.py:448
  73.3 45.6 %copy-start.1 = (s32[1,1,128]{2,1,0:T(1,128)S(1)}, s32[1,1,128]{2,1,0:T(1,128)}, u32[]{:S(2)}) copy-start(s32[1,1,128]{2,1,0:T(1,128)} %param.6) | copy-start | bytes 1540
  76.4 23.9 %all-to-all-start = ((f32[32,1,128]{2,1,0:T(1,128)}), f32[32,1,128]{2,1,0:T(1,128)S(1)}, u32[]{:S(2)}, u32[]{:S(2)}) async-start(f32[32,1,128]{2,1,0:T(1,128)} %broadcast_in_dim.7), calls=%async_computation | async-start | bytes 32768 | tf_op jit(solution)/shard_map/all_to_all | solution.py:469
  88.2 12.1 %collective-permute-start.12 = (f32[1,7,8,128]{3,2,1,0:T(8,128)S(1)}, f32[1,7,8,128]{3,2,1,0:T(8,128)S(1)}, u32[]{:S(2)}, u32[]{:S(2)}) collective-permute-start(f32[1,7,8,128]{3,2,1,0:T(8,128)S(1)} %get-tuple-element.59), channel_id=1, source_target_pairs={{0,480},{32,64},{64,32},{96,128},{128,96},{160,192},{192,160},{224... | collective-permute-start | bytes 86024 | tf_op jit(solution)/shard_map/ppermute | solution.py:448
  94.2 6.1 %collective-permute-start.13 = (f32[1,7,8,128]{3,2,1,0:T(8,128)S(1)}, f32[1,7,8,128]{3,2,1,0:T(8,128)S(1)}, u32[]{:S(2)}, u32[]{:S(2)}) collective-permute-start(f32[1,7,8,128]{3,2,1,0:T(8,128)S(1)} %get-tuple-element.60), channel_id=1, source_target_pairs={{0,32},{32,0},{64,96},{96,64},{128,160},{160,128},{192,224},{224,1... | collective-permute-start | bytes 86024 | tf_op jit(solution)/shard_map/ppermute | solution.py:448
  101.0 17.9 %all-to-all-start.1 = ((f32[16,4,128]{2,1,0:T(4,128)}), f32[16,4,128]{2,1,0:T(4,128)S(1)}, u32[]{:S(2)}, u32[]{:S(2)}) async-start(f32[16,4,128]{2,1,0:T(4,128)} %broadcast_in_dim.16), calls=%async_computation.1 | async-start | bytes 65536 | tf_op jit(solution)/shard_map/all_to_all | solution.py:469
  106.5 5.4 %collective-permute-start.14 = (f32[1,7,8,128]{3,2,1,0:T(8,128)S(1)}, f32[1,7,8,128]{3,2,1,0:T(8,128)S(1)}, u32[]{:S(2)}, u32[]{:S(2)}) collective-permute-start(f32[1,7,8,128]{3,2,1,0:T(8,128)S(1)} %get-tuple-element.64), channel_id=1, source_target_pairs={{0,31},{1,2},{2,1},{3,4},{4,3},{5,6},{6,5},{7,8},{8,7},{9,10},{10,... | collective-permute-start | bytes 86024 | tf_op jit(solution)/shard_map/ppermute | solution.py:448
  108.5 4.3 %collective-permute-start.15 = (f32[1,7,8,128]{3,2,1,0:T(8,128)S(1)}, f32[1,7,8,128]{3,2,1,0:T(8,128)S(1)}, u32[]{:S(2)}, u32[]{:S(2)}) collective-permute-start(f32[1,7,8,128]{3,2,1,0:T(8,128)S(1)} %get-tuple-element.65), channel_id=1, source_target_pairs={{0,1},{1,0},{2,3},{3,2},{4,5},{5,4},{6,7},{7,6},{8,9},{9,8},{10,11... | collective-permute-start | bytes 86024 | tf_op jit(solution)/shard_map/ppermute | solution.py:448

commit v5 on v4

--- a/solution.py
+++ b/solution.py
@@ -58,6 +58,7 @@
 
 
 RUNS = shell_runs()
+FACE_ROWS = {padded // 8: compact for compact, padded, rows in RUNS if rows == 7}
 
 
 def shell_table():
@@ -106,30 +107,51 @@
     return lane % BZ, lane // BZ, node
 
 
-def join_local(sheet):
-    bz, by, node = iotas(sheet.shape)
+def join_span(sheet):
+    bz, _, node = iotas(sheet.shape)
     low = pltpu.roll(sheet, 2, 1)
     low = jnp.where(bz == 0, pltpu.roll(low, LANES - 15, 2), pltpu.roll(low, 1, 2))
     high = pltpu.roll(sheet, 6, 1)
     high = jnp.where(bz == BZ - 1, pltpu.roll(high, 15, 2), pltpu.roll(high, LANES - 1, 2))
-    sheet = sheet + jnp.where(node == 0, low, jnp.where(node == 6, high, 0.0))
+    return sheet + jnp.where(node == 0, low, jnp.where(node == 6, high, 0.0))
+
+
+def join_local(sheet):
+    sheet = join_span(sheet)
+    _, by, _ = iotas(sheet.shape[1:])
     first, last = sheet[0], sheet[6]
-    first_by = by[0]
-    new_first = first + jnp.where(first_by > 0, pltpu.roll(last, BZ, 1), 0.0)
-    new_last = last + jnp.where(first_by < BY - 1, pltpu.roll(first, LANES - BZ, 1), 0.0)
+    new_first = first + jnp.where(by > 0, pltpu.roll(last, BZ, 1), 0.0)
+    new_last = last + jnp.where(by < BY - 1, pltpu.roll(first, LANES - BZ, 1), 0.0)
     return jnp.concatenate([new_first[None], sheet[1:6], new_last[None]], axis=0)
 
 
-def add_received(a, sheet, far_x, near_x, far_y, near_y):
+def add_streamwise(a, sheet, far_x, near_x):
     if a == 0:
         sheet = sheet + lower_upper("slab", near_x, far_x)[0]
     if a == 6:
         sheet = sheet + lower_upper("slab", near_x, far_x)[1]
-    low_y, high_y = lower_upper("dom", near_y, far_y)
+    return sheet
+
+
+def add_second(sheet, low_y, high_y):
     _, by, _ = iotas(sheet.shape[1:])
     first = sheet[0] + jnp.where(by == 0, low_y, 0.0)
     last = sheet[6] + jnp.where(by == BY - 1, high_y, 0.0)
     return jnp.concatenate([first[None], sheet[1:6], last[None]], axis=0)
+
+
+def pack_groups(blocks, start):
+    _, group, _ = iotas(blocks[0].shape)
+    total = jnp.zeros(blocks[0].shape, F32)
+    for k, block in enumerate(blocks):
+        shift = (BZ * k - start) % LANES
+        total = jnp.where(group == k, pltpu.roll(block, shift, 1) if shift else block, total)
+    return total
+
+
+def lanes_from(packed, group, start):
+    shift = (start - BZ * group) % LANES
+    return pltpu.roll(packed, shift, 1) if shift else packed
 
 
 def derive_sheets(sheets, target):
@@ -235,6 +257,17 @@
             near_ref[i, a] = jnp.where(even, up, down)
 
 
+def row_kernel(part_ref, far_x_ref, near_x_ref, class_ref, far_ref, near_ref):
+    classes = class_ref[...]
+    for a in range(7):
+        sheet = add_streamwise(a, part_ref[0, a], far_x_ref[0], near_x_ref[0])
+        blocks = [*(sheet[b] for b in range(7)), classes]
+        down, up = pack_groups(blocks, 0), pack_groups(blocks, LANES - BZ)
+        even = even_place("dom", up)
+        far_ref[0, a] = jnp.where(even, down, up)
+        near_ref[0, a] = jnp.where(even, up, down)
+
+
 def source_kernel(
     part_ref, far_x_ref, near_x_ref, far_y_ref, near_y_ref, brick_ref,
     out_ref, far_ref, near_ref, middle_ref,
@@ -244,9 +277,8 @@
     inverse = span_vector(1.0 / FACTOR)
     for i in range(3):
         for a in range(7):
-            sheet = add_received(
-                a, part_ref[i, a], far_x_ref[i], near_x_ref[i], far_y_ref[i, a], near_y_ref[i, a]
-            )
+            sheet = add_streamwise(a, part_ref[i, a], far_x_ref[i], near_x_ref[i])
+            sheet = add_second(sheet, *lower_upper("dom", near_y_ref[i, a], far_y_ref[i, a]))
             scaled = [
                 sheet[b] * (inverse * float(DELTA_T / (FACTOR[a] * FACTOR[b]))) for b in range(7)
             ]
@@ -267,12 +299,7 @@
     emit_faces(out_ref, far_ref, near_ref, 0)
 
 
-def gather_modes(part_ref, far_x_ref, near_x_ref, far_y_ref, near_y_ref, full_ref, modes_ref):
-    for a in range(7):
-        sheet = add_received(
-            a, part_ref[0, a], far_x_ref[0], near_x_ref[0], far_y_ref[0, a], near_y_ref[0, a]
-        )
-        full_ref[56 * a : 56 * a + 56] = sheet.reshape(56, LANES)
+def gather_modes(full_ref, modes_ref):
     modes_ref[216:224] = jnp.zeros((8, LANES), F32)
     for compact, padded, rows in RUNS:
         modes_ref[compact : compact + rows] = full_ref[padded : padded + rows]
@@ -329,33 +356,51 @@
     )[0]
 
 
-def multiply_blocks(split_refs, class_ref, modes_ref, image_ref, right_ref, last_ref):
+def multiply_blocks(splits, class_ref, modes_ref, image_ref, right_ref, last_ref, ghost=None):
     high, middle, low = terms(modes_ref[...])
     pair = jnp.concatenate([high, middle], axis=1)
+    mine = class_ref[0:1, :]
+    both, last_both, rows = jnp.concatenate([mine, mine], axis=1), mine, 224
+    if ghost is not None:
+        modes, classes = (
+            x + pltpu.roll(x, 32, 1) + pltpu.roll(x, 64, 1) for x in (ghost[0], ghost[1])
+        )
+        lane = lax.broadcasted_iota(jnp.int32, modes.shape, 1)
+        three = [
+            jnp.where((lane >= 32 * k) & (lane < 32 * k + 32), term.astype(F32), 0.0)
+            for k, term in enumerate(terms(modes))
+        ]
+        low = jnp.concatenate([low, (three[0] + three[1] + three[2]).astype(BF16)], axis=1)
+        last_both, rows = jnp.concatenate([mine, classes[0:1]], axis=1), 672
     zeros = jnp.zeros((32, 2 * LANES), BF16)
-    mine = class_ref[0:1, :]
     for c in range(CLASSES):
-        chosen = jnp.where(jnp.abs(mine - float(c)) < 0.5, 1.0, 0.0).astype(BF16)
-        right_ref[256 * c : 256 * c + 224] = pair * jnp.concatenate([chosen, chosen], axis=1)
+        chosen, last_chosen = (
+            jnp.where(jnp.abs(x - float(c)) < 0.5, 1.0, 0.0).astype(BF16) for x in (both, last_both)
+        )
+        right_ref[256 * c : 256 * c + 224] = pair * chosen
         right_ref[256 * c + 224 : 256 * c + 256] = zeros
-        last_ref[256 * c : 256 * c + 224] = low * chosen
-        last_ref[256 * c + 224 : 256 * c + 256] = zeros[:, :LANES]
+        last_ref[256 * c : 256 * c + 224] = low * last_chosen
+        last_ref[256 * c + 224 : 256 * c + 256] = zeros[:, : low.shape[1]]
     total, small = 0.0, 0.0
-    for half, split_ref in enumerate(split_refs):
-        rows = pl.ds(256 * HALF * half, 256 * HALF)
-        total = total + jnp.dot(split_ref[...], right_ref[rows], preferred_element_type=F32)
-        small = small + jnp.dot(split_ref[0:224], last_ref[rows], preferred_element_type=F32)
+    for half, split_ref in enumerate(splits):
+        part = pl.ds(256 * HALF * half, 256 * HALF)
+        total = total + jnp.dot(split_ref[...], right_ref[part], preferred_element_type=F32)
+        small = small + jnp.dot(split_ref[0:rows], last_ref[part], preferred_element_type=F32)
     total = total[:, :LANES] + total[:, LANES:]
-    image_ref[...] = total[0:224] + (total[224:448] + (total[448:672] + small))
-
-
-def scatter_modes(image_ref, full_ref, out_ref, far_ref, near_ref):
+    image_ref[...] = total[0:224] + (total[224:448] + (total[448:672] + small[0:224, :LANES]))
+    if ghost is None:
+        return None
+    extra = small[:, LANES:]
+    extra = extra[0:224] + (extra[224:448] + extra[448:672])
+    return extra + (pltpu.roll(extra, LANES - 32, 1) + pltpu.roll(extra, LANES - 64, 1))
+
+
+def scatter_modes(image_ref, full_ref, out_ref):
     full_ref[...] = jnp.zeros((392, LANES), F32)
     for compact, padded, rows in RUNS:
         full_ref[padded : padded + rows] = image_ref[compact : compact + rows]
     for a in range(7):
         out_ref[0, a] = join_local(full_ref[56 * a : 56 * a + 56].reshape(7, 8, LANES))
-    emit_faces(out_ref, far_ref, near_ref, 0)
 
 
 def total_of(values):
@@ -364,21 +409,56 @@
 
 def first_apply_kernel(
     part_ref, far_x_ref, near_x_ref, far_y_ref, near_y_ref, split_0, split_1, class_ref,
-    load_ref, image_ref, out_ref, far_ref, near_ref, full_ref, right_ref, last_ref,
+    load_ref, image_ref, out_ref, far_ref, near_ref,
+    full_ref, ghost_ref, ghost_modes_ref, side_ref, right_ref, last_ref,
 ):
-    gather_modes(part_ref, far_x_ref, near_x_ref, far_y_ref, near_y_ref, full_ref, load_ref)
-    multiply_blocks((split_0, split_1), class_ref, load_ref, image_ref, right_ref, last_ref)
-    scatter_modes(image_ref, full_ref, out_ref, far_ref, near_ref)
+    _, by, _ = iotas((8, LANES))
+    for a in range(7):
+        sheet = add_streamwise(a, part_ref[0, a], far_x_ref[0], near_x_ref[0])
+        low, high = lower_upper("dom", near_y_ref[0, a], far_y_ref[0, a])
+        for b in range(7):
+            block = jnp.where(by == 0, lanes_from(low, b, 0), 0.0)
+            block = jnp.where(by == 1, lanes_from(high, b, BZ), block)
+            if b == 6:
+                block = block + jnp.where(by == 0, sheet[0], 0.0)
+            if b == 0:
+                block = block + jnp.where(by == 1, pltpu.roll(sheet[6], 2 * BZ, 1), 0.0)
+            ghost_ref[56 * a + 8 * b : 56 * a + 8 * b + 8] = block
+        sheet = add_second(sheet, lanes_from(low, 6, 0), lanes_from(high, 0, LANES - BZ))
+        full_ref[56 * a : 56 * a + 56] = sheet.reshape(56, LANES)
+    low, high = lower_upper("dom", near_y_ref[0, 0], far_y_ref[0, 0])
+    ghost_class = jnp.where(by == 0, lanes_from(low, 7, 0), 0.0)
+    ghost_class = jnp.where(by == 1, lanes_from(high, 7, BZ), ghost_class)
+    gather_modes(full_ref, load_ref)
+    gather_modes(ghost_ref, ghost_modes_ref)
+    ghost_image = multiply_blocks(
+        (split_0, split_1), class_ref, load_ref, image_ref, right_ref, last_ref,
+        (ghost_modes_ref[...], ghost_class),
+    )
+    scatter_modes(image_ref, full_ref, out_ref)
+    ghost_modes_ref[...] = ghost_image
+    side_ref[...] = jnp.zeros(side_ref.shape, F32)
+    for k, b in enumerate((6, 0)):
+        for a in range(7):
+            row = FACE_ROWS[7 * a + b]
+            side_ref[k, a, 0:7] = ghost_modes_ref[row : row + 7]
+    below, above = join_span(side_ref[0]), join_span(side_ref[1])
+    for a in range(7):
+        out_ref[0, a, 0] += jnp.where(by == 0, below[a], 0.0)
+        out_ref[0, a, 6] += jnp.where(by == BY - 1, pltpu.roll(above[a], LANES - 2 * BZ, 1), 0.0)
+    emit_faces(out_ref, far_ref, near_ref, 0)
 
 
 def second_apply_kernel(
-    part_ref, far_x_ref, near_x_ref, far_y_ref, near_y_ref, split_0, split_1, class_ref, load_ref,
-    first_ref, shell_ref, power_ref, dots_ref, out_ref, far_ref, near_ref, image_ref, full_ref, right_ref,
-    last_ref,
+    part_ref, far_x_ref, near_x_ref, split_0, split_1, class_ref, load_ref, first_ref, shell_ref,
+    power_ref, send_ref, out_ref, image_ref, full_ref, right_ref, last_ref,
 ):
-    gather_modes(part_ref, far_x_ref, near_x_ref, far_y_ref, near_y_ref, full_ref, power_ref)
+    for a in range(7):
+        sheet = add_streamwise(a, part_ref[0, a], far_x_ref[0], near_x_ref[0])
+        full_ref[56 * a : 56 * a + 56] = sheet.reshape(56, LANES)
+    gather_modes(full_ref, power_ref)
     multiply_blocks((split_0, split_1), class_ref, power_ref, image_ref, right_ref, last_ref)
-    scatter_modes(image_ref, full_ref, out_ref, far_ref, near_ref)
+    scatter_modes(image_ref, full_ref, out_ref)
     load, power, shell = load_ref[...], power_ref[...], shell_ref[...]
     first, image = first_ref[...], image_ref[...]
     lane = lax.broadcasted_iota(jnp.int32, (1, LANES), 1)
@@ -388,14 +468,44 @@
     )
     for k, value in enumerate(values):
         dots = dots + jnp.where(lane == k, total_of(value), 0.0)
-    dots_ref[...] = dots
+    node = lax.broadcasted_iota(jnp.int32, (8, LANES), 0)
+    count = send_ref.shape[0]
+    mine = lax.axis_index("dom")
+    alone = jnp.where(node == 7, dots, 0.0)
+    send_ref[...] = jnp.broadcast_to(alone[None], send_ref.shape)
+    up = pack_groups([out_ref[0, a, 6] for a in range(7)], LANES - BZ)
+    down = pack_groups([out_ref[0, a, 0] for a in range(7)], 0)
+    send_ref[lax.rem(mine + 1, count)] = jnp.where(node == 7, dots, up)
+    send_ref[lax.rem(mine + count - 1, count)] = jnp.where(node == 7, dots, down)
+
+
+def middle_kernel(part_ref, got_ref, far_ref, near_ref, low_ref, high_ref, sums_ref):
+    node = lax.broadcasted_iota(jnp.int32, (8, LANES), 0)
+    count = got_ref.shape[0]
+    mine = lax.axis_index("dom")
+    low = jnp.where(node < 7, got_ref[lax.rem(mine + count - 1, count)], 0.0)
+    high = jnp.where(node < 7, got_ref[lax.rem(mine + 1, count)], 0.0)
+    faces = []
+    for a in range(7):
+        low_ref[a], high_ref[a] = lanes_from(low, a, 0), lanes_from(high, a, LANES - BZ)
+        if a in (0, 6):
+            faces.append(add_second(part_ref[0, a], low_ref[a], high_ref[a]))
+    even = even_place("slab", faces[0])
+    far_ref[0] = jnp.where(even, faces[0], faces[1])
+    near_ref[0] = jnp.where(even, faces[1], faces[0])
+    total = jnp.sum(got_ref[...], axis=0)[7:8]
+    sums_ref[...] = jnp.broadcast_to(total[None], sums_ref.shape)
 
 
 def finish_kernel(
-    part_ref, far_x_ref, near_x_ref, far_y_ref, near_y_ref, load_ref, power_ref, dots_ref, slot_ref,
+    part_ref, far_x_ref, near_x_ref, low_ref, high_ref, load_ref, power_ref, dots_ref, slot_ref,
     pressure_ref, residual_ref, full_ref, modes_ref,
 ):
-    gather_modes(part_ref, far_x_ref, near_x_ref, far_y_ref, near_y_ref, full_ref, modes_ref)
+    for a in range(7):
+        sheet = add_streamwise(a, part_ref[0, a], far_x_ref[0], near_x_ref[0])
+        sheet = add_second(sheet, low_ref[a], high_ref[a])
+        full_ref[56 * a : 56 * a + 56] = sheet.reshape(56, LANES)
+    gather_modes(full_ref, modes_ref)
     dots = jnp.sum(dots_ref[...], axis=0)[0:1]
     square, energy, power_square, cross, power_energy = (dots[:, k : k + 1] for k in range(5))
     step = square / energy
@@ -448,25 +558,16 @@
     return lax.ppermute(far, axis, far_pairs), lax.ppermute(near, axis, near_pairs)
 
 
-def exchange(part, far, near, dots=None, beside=None):
+def exchange(part, far, near, beside, rows=None):
     far_x, near_x = swap("slab", far, near)
-    k = part.shape[0]
-    if beside is not None:
-        part, beside = lax.optimization_barrier((part, beside))
-    if dots is not None:
-        rows = gather_parts(dots, "dom")
-        far_x, near_x, rows = lax.optimization_barrier((far_x, near_x, rows))
-        rows = gather_parts(rows.sum(axis=0), "slab", 4)
-    far, near = call(side_kernel, [(k, 7, 8, LANES)] * 2, (part, far_x, near_x), name="side")
-    received = part, far_x, near_x, *swap("dom", far, near)
-    if beside is not None:
-        return received, beside
-    return received if dots is None else (received, rows)
-
-
-def gather_parts(row, axis, copies=1):
-    spread = jnp.broadcast_to(row[None], (lax.axis_size(axis), copies, LANES))
-    return lax.all_to_all(spread, axis, 0, 0)
+    part, beside = lax.optimization_barrier((part, beside))
+    outs = [(part.shape[0], 7, 8, LANES)] * 2
+    args = (part, far_x, near_x)
+    if rows is None:
+        far, near = call(side_kernel, outs, args, name="side")
+    else:
+        far, near = call(row_kernel, outs, (*args, rows), name="rows")
+    return (part, far_x, near_x, *swap("dom", far, near)), beside
 
 
 def per_device(velocity, slot_map, class_index, schur_blocks):
@@ -490,7 +591,7 @@
         name="advect",
         hbm=(0, 1, 2),
     )
-    received, split_0 = exchange(part, far, near, beside=split_half(schur, 0))
+    received, split_0 = exchange(part, far, near, split_half(schur, 0))
     part, far, near = call(
         source_kernel,
         [(1, *whole), (1, *face), (1, *face)],
@@ -498,26 +599,33 @@
         [(3, *whole)],
         name="source",
     )
-    received, split_1 = exchange(part, far, near, beside=split_half(schur, 1))
+    received, split_1 = exchange(part, far, near, split_half(schur, 1), classes)
     load, first, part, far, near = call(
         first_apply_kernel,
         [modes, modes, (1, *whole), (1, *face), (1, *face)],
         (*received, split_0, split_1, classes),
-        [(392, LANES), *rights],
+        [(392, LANES), (392, LANES), modes, (2, *face), rights[0], rights[0]],
         name="first",
     )
-    power, dots, part, far, near = call(
+    slabs, doms = lax.axis_size("slab"), lax.axis_size("dom")
+    power, send, part = call(
         second_apply_kernel,
-        [modes, (1, LANES), (1, *whole), (1, *face), (1, *face)],
-        (*exchange(part, far, near), split_0, split_1, classes, load, first, shell),
+        [modes, (doms, 8, LANES), (1, *whole)],
+        (part, *swap("slab", far, near), split_0, split_1, classes, load, first, shell),
         [modes, (392, LANES), *rights],
         name="second",
     )
-    received, rows = exchange(part, far, near, dots)
+    far, near, low, high, sums = call(
+        middle_kernel,
+        [(1, *face), (1, *face), face, face, (slabs, 4, LANES)],
+        (part, lax.all_to_all(send, "dom", 0, 0)),
+        name="middle",
+    )
+    dots = lax.all_to_all(sums, "slab", 0, 0)
     return call(
         finish_kernel,
         [(MODES, LANES), (MODES, LANES)],
-        (*received, load, power, rows, slots),
+        (part, *swap("slab", far, near), low, high, load, power, dots, slots),
         [(392, LANES), modes],
         name="finish",
     )

time: 121 us -> 110 us (0.909)
  the two profiles are of different devices: /device:TPU:2 before, /device:TPU:1 now
where the time goes in v5:
time: 110 us
  starting transfers between devices  66.9 us (61%)
  Pallas kernels  18.3 us (17%)
  blocking collectives  15.8 us (14%)
  waiting for transfers between devices  7.82 us (7%)
    ppermute x6, starting transfers between devices, swap(): lax.ppermute(far, axis, far_pairs)  44.2 us
    pallas_call x10, Pallas kernels, call(): pl.pallas_call(kernel, out_shape=tuple((jax.ShapeDtypeStruct(*(o if isins...  18.3 us
    ppermute x6, starting transfers between devices, swap(): lax.ppermute(near, axis, near_pairs)  17.5 us
    all_to_all x1, blocking collectives, per_device(): lax.all_to_all(send, 'dom', 0, 0)  15.8 us
    all_to_all x1, starting transfers between devices, per_device(): dots = lax.all_to_all(sums, 'slab', 0, 0)  5.21 us
    ppermute x6, waiting for transfers between devices, swap(): lax.ppermute(near, axis, near_pairs)  4.87 us
    ppermute x6, waiting for transfers between devices, swap(): lax.ppermute(far, axis, far_pairs)  2.94 us
  transfers between devices with their start and end apart: 13, of which 6 were waited for; matrix products, arithmetic and copies ran while one was open for 0% of the time, Pallas kernels for 5%

profile of v5, /device:TPU:1, one launch (start us, length us, event | category | flops | bytes accessed | tf_op | source)
XLA Modules:
  0.0 109.6 jit_solution(15350496871289890822)
XLA Ops:
  0.6 3.6 %advect.1 = (f32[3,7,7,8,128]{4,3,2,1,0:T(8,128)S(1)}, f32[3,7,7,8,128]{4,3,2,1,0:T(8,128)S(1)}, f32[3,7,8,128]{3,2,1,0:T(8,128)S(1)}, f32[3,7,8,128]{3,2,1,0:T(8,128)S(1)}, f32[8,128]{1,0:T(8,128)S(1)}) custom-call(f32[3,343,128]{2,1,0:T(8,128)} %vel_hbm.1, s32[1,128]{1,0:T(1,128)} %bitcast.3, s32[1,128]{1,0:T(1,128)} %bitcast.7), custom_call_target="tpu_custom_call" | custom-call | tf_op jit(solution)/shard_map/advect/pallas_call | solution.py:536
  4.2 14.4 %collective-permute-start = (f32[3,7,8,128]{3,2,1,0:T(8,128)S(1)}, f32[3,7,8,128]{3,2,1,0:T(8,128)S(1)}, u32[]{:S(2)}, u32[]{:S(2)}) collective-permute-start(f32[3,7,8,128]{3,2,1,0:T(8,128)S(1)} %get-tuple-element.33), channel_id=1, source_target_pairs={{0,480},{32,64},{64,32},{96,128},{128,96},{160,192},{192,160},{224... | collective-permute-start | bytes 258056 | tf_op jit(solution)/shard_map/ppermute | solution.py:558
  18.6 1.9 %collective-permute-start.1 = (f32[3,7,8,128]{3,2,1,0:T(8,128)S(1)}, f32[3,7,8,128]{3,2,1,0:T(8,128)S(1)}, u32[]{:S(2)}, u32[]{:S(2)}) collective-permute-start(f32[3,7,8,128]{3,2,1,0:T(8,128)S(1)} %get-tuple-element.34), channel_id=1, source_target_pairs={{0,32},{32,0},{64,96},{96,64},{128,160},{160,128},{192,224},{224,1... | collective-permute-start | bytes 258056 | tf_op jit(solution)/shard_map/ppermute | solution.py:558
  20.5 2.9 %split.2.split_0 = bf16[672,2048]{1,0:T(8,128)(2,1)S(1)} custom-call(f32[218,16,218]{2,1,0:T(8,128)} %bitcast.5), custom_call_target="tpu_custom_call" | custom-call | tf_op jit(solution)/shard_map/split/pallas_call | solution.py:536
  23.4 0.0 collective-permute-done.far_x_ref
  23.4 0.4 collective-permute-done.1.near_x_ref
  23.8 0.1 side.1
  24.0 5.1 %collective-permute-start.2 = (f32[3,7,8,128]{3,2,1,0:T(8,128)S(1)}, f32[3,7,8,128]{3,2,1,0:T(8,128)S(1)}, u32[]{:S(2)}, u32[]{:S(2)}) collective-permute-start(f32[3,7,8,128]{3,2,1,0:T(8,128)S(1)} %get-tuple-element.35), channel_id=1, source_target_pairs={{0,31},{1,2},{2,1},{3,4},{4,3},{5,6},{6,5},{7,8},{8,7},{9,10},{10,... | collective-permute-start | bytes 258056 | tf_op jit(solution)/shard_map/ppermute | solution.py:558
  29.1 4.3 %collective-permute-start.3 = (f32[3,7,8,128]{3,2,1,0:T(8,128)S(1)}, f32[3,7,8,128]{3,2,1,0:T(8,128)S(1)}, u32[]{:S(2)}, u32[]{:S(2)}) collective-permute-start(f32[3,7,8,128]{3,2,1,0:T(8,128)S(1)} %get-tuple-element.36), channel_id=1, source_target_pairs={{0,1},{1,0},{2,3},{3,2},{4,5},{5,4},{6,7},{7,6},{8,9},{9,8},{10,11... | collective-permute-start | bytes 258056 | tf_op jit(solution)/shard_map/ppermute | solution.py:558
  33.4 0.0 collective-permute-done.2.far_y_ref
  33.4 0.9 collective-permute-done.3.near_y_ref
  34.3 0.6 source.1
  34.9 6.3 %collective-permute-start.4 = (f32[1,7,8,128]{3,2,1,0:T(8,128)S(1)}, f32[1,7,8,128]{3,2,1,0:T(8,128)S(1)}, u32[]{:S(2)}, u32[]{:S(2)}) collective-permute-start(f32[1,7,8,128]{3,2,1,0:T(8,128)S(1)} %get-tuple-element.40), channel_id=1, source_target_pairs={{0,480},{32,64},{64,32},{96,128},{128,96},{160,192},{192,160},{224... | collective-permute-start | bytes 86024 | tf_op jit(solution)/shard_map/ppermute | solution.py:558
  41.2 1.9 %collective-permute-start.5 = (f32[1,7,8,128]{3,2,1,0:T(8,128)S(1)}, f32[1,7,8,128]{3,2,1,0:T(8,128)S(1)}, u32[]{:S(2)}, u32[]{:S(2)}) collective-permute-start(f32[1,7,8,128]{3,2,1,0:T(8,128)S(1)} %get-tuple-element.41), channel_id=1, source_target_pairs={{0,32},{32,0},{64,96},{96,64},{128,160},{160,128},{192,224},{224,1... | collective-permute-start | bytes 86024 | tf_op jit(solution)/shard_map/ppermute | solution.py:558
  43.1 2.9 %split.3.split_1 = bf16[672,2048]{1,0:T(8,128)(2,1)S(1)} custom-call(f32[218,16,218]{2,1,0:T(8,128)} %bitcast.6), custom_call_target="tpu_custom_call" | custom-call | tf_op jit(solution)/shard_map/split/pallas_call | solution.py:536
  46.0 0.0 collective-permute-done.4.far_x_ref
  46.0 0.1 collective-permute-done.5.near_x_ref
  46.1 0.2 rows.1
  46.3 3.4 %collective-permute-start.6 = (f32[1,7,8,128]{3,2,1,0:T(8,128)S(1)}, f32[1,7,8,128]{3,2,1,0:T(8,128)S(1)}, u32[]{:S(2)}, u32[]{:S(2)}) collective-permute-start(f32[1,7,8,128]{3,2,1,0:T(8,128)S(1)} %get-tuple-element.43), channel_id=1, source_target_pairs={{0,31},{1,2},{2,1},{3,4},{4,3},{5,6},{6,5},{7,8},{8,7},{9,10},{10,... | collective-permute-start | bytes 86024 | tf_op jit(solution)/shard_map/ppermute | solution.py:558
  49.7 0.0 copy-start
  49.7 5.5 %collective-permute-start.7 = (f32[1,7,8,128]{3,2,1,0:T(8,128)S(1)}, f32[1,7,8,128]{3,2,1,0:T(8,128)S(1)}, u32[]{:S(2)}, u32[]{:S(2)}) collective-permute-start(f32[1,7,8,128]{3,2,1,0:T(8,128)S(1)} %get-tuple-element.44), channel_id=1, source_target_pairs={{0,1},{1,0},{2,3},{3,2},{4,5},{5,4},{6,7},{7,6},{8,9},{9,8},{10,11... | collective-permute-start | bytes 86024 | tf_op jit(solution)/shard_map/ppermute | solution.py:558
  55.2 0.0 collective-permute-done.6.far_y_ref
  55.2 0.8 collective-permute-done.7.near_y_ref
  56.0 3.7 %first.1 = (f32[224,128]{1,0:T(8,128)S(1)}, f32[224,128]{1,0:T(8,128)S(1)}, f32[1,7,7,8,128]{4,3,2,1,0:T(8,128)S(1)}, f32[1,7,8,128]{3,2,1,0:T(8,128)S(1)}, f32[1,7,8,128]{3,2,1,0:T(8,128)S(1)}) custom-call(f32[1,7,7,8,128]{4,3,2,1,0:T(8,128)S(1)} %get-tuple-element.39.part_ref, f32[1,7,8,128]{3,2,1,0:T(8,128)S(1)} %collective-permute-done.4.far_x_ref, ...), custom_call_target="tpu_custom_call" | custom-call | tf_op jit(solution)/shard_map/first/pallas_call | solution.py:536
  59.7 5.8 %collective-permute-start.8 = (f32[1,7,8,128]{3,2,1,0:T(8,128)S(1)}, f32[1,7,8,128]{3,2,1,0:T(8,128)S(1)}, u32[]{:S(2)}, u32[]{:S(2)}) collective-permute-start(f32[1,7,8,128]{3,2,1,0:T(8,128)S(1)} %get-tuple-element.48), channel_id=1, source_target_pairs={{0,480},{32,64},{64,32},{96,128},{128,96},{160,192},{192,160},{224... | collective-permute-start | bytes 86024 | tf_op jit(solution)/shard_map/ppermute | solution.py:558
  65.5 1.9 %collective-permute-start.9 = (f32[1,7,8,128]{3,2,1,0:T(8,128)S(1)}, f32[1,7,8,128]{3,2,1,0:T(8,128)S(1)}, u32[]{:S(2)}, u32[]{:S(2)}) collective-permute-start(f32[1,7,8,128]{3,2,1,0:T(8,128)S(1)} %get-tuple-element.49), channel_id=1, source_target_pairs={{0,32},{32,0},{64,96},{96,64},{128,160},{160,128},{192,224},{224,1... | collective-permute-start | bytes 86024 | tf_op jit(solution)/shard_map/ppermute | solution.py:558
  67.4 2.9 %collective-permute-done.8.far_x_ref = f32[1,7,8,128]{3,2,1,0:T(8,128)S(1)} collective-permute-done((f32[1,7,8,128]{3,2,1,0:T(8,128)S(1)}, f32[1,7,8,128]{3,2,1,0:T(8,128)S(1)}, u32[]{:S(2)}, u32[]{:S(2)}) %collective-permute-start.8) | collective-permute-done | bytes 28704 | tf_op jit(solution)/shard_map/ppermute | solution.py:558
  70.4 0.0 collective-permute-done.9.near_x_ref
  70.4 0.0 copy-done
  70.4 0.0 copy-start.1
  70.4 2.6 %second.1 = (f32[224,128]{1,0:T(8,128)S(1)}, f32[32,8,128]{2,1,0:T(8,128)S(1)}, f32[1,7,7,8,128]{4,3,2,1,0:T(8,128)S(1)}) custom-call(f32[1,7,7,8,128]{4,3,2,1,0:T(8,128)S(1)} %get-tuple-element.47.part_ref, f32[1,7,8,128]{3,2,1,0:T(8,128)S(1)} %collective-permute-done.8.far_x_ref, f32[1,7,8,128]{3,2,1,0:T(8,128)S(1)} %collective-permute-done.9.near_x_ref, ...), custom_call_target="tpu_custom_call" | custom-call | tf_op jit(solution)/shard_map/second/pallas_call | solution.py:536
  72.9 15.8 %all_to_all.10.got_ref = f32[32,8,128]{2,1,0:T(8,128)S(1)} all-to-all(f32[32,8,128]{2,1,0:T(8,128)S(1)} %get-tuple-element.53), channel_id=1, replica_groups=mesh['slab'=16,'dom'=32] {'dom'}, dimensions={0} | all-to-all | bytes 262144 | tf_op jit(solution)/shard_map/all_to_all | solution.py:621
  88.7 0.7 middle.1
  89.4 5.2 %all-to-all-start.1 = ((f32[16,4,128]{2,1,0:T(4,128)}), f32[16,4,128]{2,1,0:T(4,128)S(1)}, u32[]{:S(2)}, u32[]{:S(2)}) async-start(f32[16,4,128]{2,1,0:T(4,128)} %get-tuple-element.59), calls=%async_computation.1 | async-start | bytes 65536 | tf_op jit(solution)/shard_map/all_to_all | solution.py:624
  94.6 9.3 %collective-permute-start.10 = (f32[1,7,8,128]{3,2,1,0:T(8,128)S(1)}, f32[1,7,8,128]{3,2,1,0:T(8,128)S(1)}, u32[]{:S(2)}, u32[]{:S(2)}) collective-permute-start(f32[1,7,8,128]{3,2,1,0:T(8,128)S(1)} %get-tuple-element.54), channel_id=1, source_target_pairs={{0,480},{32,64},{64,32},{96,128},{128,96},{160,192},{192,160},{224... | collective-permute-start | bytes 86024 | tf_op jit(solution)/shard_map/ppermute | solution.py:558
  103.9 1.9 %collective-permute-start.11 = (f32[1,7,8,128]{3,2,1,0:T(8,128)S(1)}, f32[1,7,8,128]{3,2,1,0:T(8,128)S(1)}, u32[]{:S(2)}, u32[]{:S(2)}) collective-permute-start(f32[1,7,8,128]{3,2,1,0:T(8,128)S(1)} %get-tuple-element.55), channel_id=1, source_target_pairs={{0,32},{32,0},{64,96},{96,64},{128,160},{160,128},{192,224},{224,1... | collective-permute-start | bytes 86024 | tf_op jit(solution)/shard_map/ppermute | solution.py:558
  105.8 0.0 collective-permute-done.10.far_x_ref
  105.8 2.7 %collective-permute-done.11.near_x_ref = f32[1,7,8,128]{3,2,1,0:T(8,128)S(1)} collective-permute-done((f32[1,7,8,128]{3,2,1,0:T(8,128)S(1)}, f32[1,7,8,128]{3,2,1,0:T(8,128)S(1)}, u32[]{:S(2)}, u32[]{:S(2)}) %collective-permute-start.11) | collective-permute-done | bytes 28704 | tf_op jit(solution)/shard_map/ppermute | solution.py:558
  108.5 0.0 all-to-all-done.1.dots_ref
  108.5 0.0 copy-done.1
  108.5 1.1 %finish.1 = (f32[218,128]{1,0:T(8,128)}, f32[218,128]{1,0:T(8,128)}) custom-call(f32[1,7,7,8,128]{4,3,2,1,0:T(8,128)S(1)} %get-tuple-element.52.part_ref, f32[1,7,8,128]{3,2,1,0:T(8,128)S(1)} %collective-permute-done.10.far_x_ref, f32[1,7,8,128]{3,2,1,0:T(8,128)S(1)} %collective-permute-done.11.near_x_ref, f32[7,8,128]{2,1,0:T(8,128)S(1)} %get-tuple-element.56.low_ref, ...), custom_call_target="tpu_custom_call" | custom-call | tf_op jit(solution)/shard_map/finish/pallas_call | solution.py:536
Async XLA Ops:
  4.2 19.2 %collective-permute-start = (f32[3,7,8,128]{3,2,1,0:T(8,128)S(1)}, f32[3,7,8,128]{3,2,1,0:T(8,128)S(1)}, u32[]{:S(2)}, u32[]{:S(2)}) collective-permute-start(f32[3,7,8,128]{3,2,1,0:T(8,128)S(1)} %get-tuple-element.33), channel_id=1, source_target_pairs={{0,480},{32,64},{64,32},{96,128},{128,96},{160,192},{192,160},{224... | collective-permute-start | bytes 258056 | tf_op jit(solution)/shard_map/ppermute | solution.py:558
  18.6 5.2 %collective-permute-start.1 = (f32[3,7,8,128]{3,2,1,0:T(8,128)S(1)}, f32[3,7,8,128]{3,2,1,0:T(8,128)S(1)}, u32[]{:S(2)}, u32[]{:S(2)}) collective-permute-start(f32[3,7,8,128]{3,2,1,0:T(8,128)S(1)} %get-tuple-element.34), channel_id=1, source_target_pairs={{0,32},{32,0},{64,96},{96,64},{128,160},{160,128},{192,224},{224,1... | collective-permute-start | bytes 258056 | tf_op jit(solution)/shard_map/ppermute | solution.py:558
  24.0 9.4 %collective-permute-start.2 = (f32[3,7,8,128]{3,2,1,0:T(8,128)S(1)}, f32[3,7,8,128]{3,2,1,0:T(8,128)S(1)}, u32[]{:S(2)}, u32[]{:S(2)}) collective-permute-start(f32[3,7,8,128]{3,2,1,0:T(8,128)S(1)} %get-tuple-element.35), channel_id=1, source_target_pairs={{0,31},{1,2},{2,1},{3,4},{4,3},{5,6},{6,5},{7,8},{8,7},{9,10},{10,... | collective-permute-start | bytes 258056 | tf_op jit(solution)/shard_map/ppermute | solution.py:558
  29.1 5.2 %collective-permute-start.3 = (f32[3,7,8,128]{3,2,1,0:T(8,128)S(1)}, f32[3,7,8,128]{3,2,1,0:T(8,128)S(1)}, u32[]{:S(2)}, u32[]{:S(2)}) collective-permute-start(f32[3,7,8,128]{3,2,1,0:T(8,128)S(1)} %get-tuple-element.36), channel_id=1, source_target_pairs={{0,1},{1,0},{2,3},{3,2},{4,5},{5,4},{6,7},{7,6},{8,9},{9,8},{10,11... | collective-permute-start | bytes 258056 | tf_op jit(solution)/shard_map/ppermute | solution.py:558
  34.9 11.1 %collective-permute-start.4 = (f32[1,7,8,128]{3,2,1,0:T(8,128)S(1)}, f32[1,7,8,128]{3,2,1,0:T(8,128)S(1)}, u32[]{:S(2)}, u32[]{:S(2)}) collective-permute-start(f32[1,7,8,128]{3,2,1,0:T(8,128)S(1)} %get-tuple-element.40), channel_id=1, source_target_pairs={{0,480},{32,64},{64,32},{96,128},{128,96},{160,192},{192,160},{224... | collective-permute-start | bytes 86024 | tf_op jit(solution)/shard_map/ppermute | solution.py:558
  41.2 4.9 %collective-permute-start.5 = (f32[1,7,8,128]{3,2,1,0:T(8,128)S(1)}, f32[1,7,8,128]{3,2,1,0:T(8,128)S(1)}, u32[]{:S(2)}, u32[]{:S(2)}) collective-permute-start(f32[1,7,8,128]{3,2,1,0:T(8,128)S(1)} %get-tuple-element.41), channel_id=1, source_target_pairs={{0,32},{32,0},{64,96},{96,64},{128,160},{160,128},{192,224},{224,1... | collective-permute-start | bytes 86024 | tf_op jit(solution)/shard_map/ppermute | solution.py:558
  46.3 8.9 %collective-permute-start.6 = (f32[1,7,8,128]{3,2,1,0:T(8,128)S(1)}, f32[1,7,8,128]{3,2,1,0:T(8,128)S(1)}, u32[]{:S(2)}, u32[]{:S(2)}) collective-permute-start(f32[1,7,8,128]{3,2,1,0:T(8,128)S(1)} %get-tuple-element.43), channel_id=1, source_target_pairs={{0,31},{1,2},{2,1},{3,4},{4,3},{5,6},{6,5},{7,8},{8,7},{9,10},{10,... | collective-permute-start | bytes 86024 | tf_op jit(solution)/shard_map/ppermute | solution.py:558
  49.7 20.7 %copy-start = (f32[224,128]{1,0:T(8,128)S(1)}, f32[224,128]{1,0:T(8,128)}, u32[]{:S(2)}) copy-start(f32[224,128]{1,0:T(8,128)} %constant.2.clone.shell_ref) | copy-start | bytes 344068
  49.7 6.3 %collective-permute-start.7 = (f32[1,7,8,128]{3,2,1,0:T(8,128)S(1)}, f32[1,7,8,128]{3,2,1,0:T(8,128)S(1)}, u32[]{:S(2)}, u32[]{:S(2)}) collective-permute-start(f32[1,7,8,128]{3,2,1,0:T(8,128)S(1)} %get-tuple-element.44), channel_id=1, source_target_pairs={{0,1},{1,0},{2,3},{3,2},{4,5},{5,4},{6,7},{7,6},{8,9},{9,8},{10,11... | collective-permute-start | bytes 86024 | tf_op jit(solution)/shard_map/ppermute | solution.py:558
  59.7 10.6 %collective-permute-start.8 = (f32[1,7,8,128]{3,2,1,0:T(8,128)S(1)}, f32[1,7,8,128]{3,2,1,0:T(8,128)S(1)}, u32[]{:S(2)}, u32[]{:S(2)}) collective-permute-start(f32[1,7,8,128]{3,2,1,0:T(8,128)S(1)} %get-tuple-element.48), channel_id=1, source_target_pairs={{0,480},{32,64},{64,32},{96,128},{128,96},{160,192},{192,160},{224... | collective-permute-start | bytes 86024 | tf_op jit(solution)/shard_map/ppermute | solution.py:558
  65.5 4.9 %collective-permute-start.9 = (f32[1,7,8,128]{3,2,1,0:T(8,128)S(1)}, f32[1,7,8,128]{3,2,1,0:T(8,128)S(1)}, u32[]{:S(2)}, u32[]{:S(2)}) collective-permute-start(f32[1,7,8,128]{3,2,1,0:T(8,128)S(1)} %get-tuple-element.49), channel_id=1, source_target_pairs={{0,32},{32,0},{64,96},{96,64},{128,160},{160,128},{192,224},{224,1... | collective-permute-start | bytes 86024 | tf_op jit(solution)/shard_map/ppermute | solution.py:558
  70.4 38.1 %copy-start.1 = (s32[1,1,128]{2,1,0:T(1,128)S(1)}, s32[1,1,128]{2,1,0:T(1,128)}, u32[]{:S(2)}) copy-start(s32[1,1,128]{2,1,0:T(1,128)} %param.6) | copy-start | bytes 1540
  89.4 19.1 %all-to-all-start.1 = ((f32[16,4,128]{2,1,0:T(4,128)}), f32[16,4,128]{2,1,0:T(4,128)S(1)}, u32[]{:S(2)}, u32[]{:S(2)}) async-start(f32[16,4,128]{2,1,0:T(4,128)} %get-tuple-element.59), calls=%async_computation.1 | async-start | bytes 65536 | tf_op jit(solution)/shard_map/all_to_all | solution.py:624
  94.6 11.2 %collective-permute-start.10 = (f32[1,7,8,128]{3,2,1,0:T(8,128)S(1)}, f32[1,7,8,128]{3,2,1,0:T(8,128)S(1)}, u32[]{:S(2)}, u32[]{:S(2)}) collective-permute-start(f32[1,7,8,128]{3,2,1,0:T(8,128)S(1)} %get-tuple-element.54), channel_id=1, source_target_pairs={{0,480},{32,64},{64,32},{96,128},{128,96},{160,192},{192,160},{224... | collective-permute-start | bytes 86024 | tf_op jit(solution)/shard_map/ppermute | solution.py:558
  103.9 4.6 %collective-permute-start.11 = (f32[1,7,8,128]{3,2,1,0:T(8,128)S(1)}, f32[1,7,8,128]{3,2,1,0:T(8,128)S(1)}, u32[]{:S(2)}, u32[]{:S(2)}) collective-permute-start(f32[1,7,8,128]{3,2,1,0:T(8,128)S(1)} %get-tuple-element.55), channel_id=1, source_target_pairs={{0,32},{32,0},{64,96},{96,64},{128,160},{160,128},{192,224},{224,1... | collective-permute-start | bytes 86024 | tf_op jit(solution)/shard_map/ppermute | solution.py:558

commit v6 on v5

--- a/solution.py
+++ b/solution.py
@@ -242,35 +242,9 @@
     lax.fori_loop(0, 3, component, 0)
 
 
-def side_kernel(part_ref, far_x_ref, near_x_ref, far_ref, near_ref):
-    for i in range(part_ref.shape[0]):
-        low_x, high_x = lower_upper("slab", near_x_ref[i], far_x_ref[i])
-        for a in range(7):
-            first, last = part_ref[i, a, 0], part_ref[i, a, 6]
-            if a == 0:
-                first, last = first + low_x[0], last + low_x[6]
-            if a == 6:
-                first, last = first + high_x[0], last + high_x[6]
-            down, up = pltpu.roll(first, LANES - BZ, 1), pltpu.roll(last, BZ, 1)
-            even = even_place("dom", up)
-            far_ref[i, a] = jnp.where(even, down, up)
-            near_ref[i, a] = jnp.where(even, up, down)
-
-
-def row_kernel(part_ref, far_x_ref, near_x_ref, class_ref, far_ref, near_ref):
-    classes = class_ref[...]
-    for a in range(7):
-        sheet = add_streamwise(a, part_ref[0, a], far_x_ref[0], near_x_ref[0])
-        blocks = [*(sheet[b] for b in range(7)), classes]
-        down, up = pack_groups(blocks, 0), pack_groups(blocks, LANES - BZ)
-        even = even_place("dom", up)
-        far_ref[0, a] = jnp.where(even, down, up)
-        near_ref[0, a] = jnp.where(even, up, down)
-
-
 def source_kernel(
-    part_ref, far_x_ref, near_x_ref, far_y_ref, near_y_ref, brick_ref,
-    out_ref, far_ref, near_ref, middle_ref,
+    part_ref, far_x_ref, near_x_ref, brick_ref, class_ref,
+    out_ref, far_ref, near_ref, first_ref, last_ref, middle_ref,
 ):
     rolls = span_rolls()
     weights = span_vector(WEIGHTS)
@@ -278,7 +252,7 @@
     for i in range(3):
         for a in range(7):
             sheet = add_streamwise(a, part_ref[i, a], far_x_ref[i], near_x_ref[i])
-            sheet = add_second(sheet, *lower_upper("dom", near_y_ref[i, a], far_y_ref[i, a]))
+            first_ref[i, a], last_ref[i, a] = sheet[0], sheet[6]
             scaled = [
                 sheet[b] * (inverse * float(DELTA_T / (FACTOR[a] * FACTOR[b]))) for b in range(7)
             ]
@@ -296,7 +270,89 @@
             for b in range(7)
         ]
         out_ref[0, a] = join_local(jnp.stack(source, axis=0))
-    emit_faces(out_ref, far_ref, near_ref, 0)
+    classes = class_ref[...]
+    even = even_place("dom", classes)
+    for a in range(7):
+        rows = [*(out_ref[0, a, b] for b in range(7)), classes]
+        pairs = (
+            (pack_groups(rows, 0), pack_groups(rows, LANES - BZ)),
+            (
+                pack_groups([first_ref[i, a] for i in range(3)], 0),
+                pack_groups([last_ref[i, a] for i in range(3)], LANES - BZ),
+            ),
+        )
+        for k, (down, up) in enumerate(pairs):
+            far_ref[k, a] = jnp.where(even, down, up)
+            near_ref[k, a] = jnp.where(even, up, down)
+
+
+def face_source(rolls, weights, inverse, low, high):
+    across = []
+    for face in (low, high):
+        for i in range(3):
+            for a in range(7):
+                face[i][a] = face[i][a] * (inverse * float(-DELTA_T / (2.0 * FACTOR[a])))
+        across.append(
+            [derive_sheets(face[0], a) + derive_span(rolls, face[2][a][None])[0] for a in range(7)]
+        )
+    sheets = []
+    for a in range(7):
+        rows = []
+        for b in range(7):
+            total = float(DERIV[b, 0]) * low[1][a] + float(DERIV[b, 6]) * high[1][a]
+            if b == 0:
+                total = total + across[0][a]
+            if b == 6:
+                total = total + across[1][a]
+            rows.append(total * (weights * float(-1.0 / DELTA_T * WEIGHTS[a] * WEIGHTS[b])))
+        sheets.append(jnp.stack(rows, axis=0))
+    return sheets
+
+
+def correct_kernel(
+    part_ref, far_y_ref, near_y_ref, first_ref, last_ref, out_ref, far_ref, near_ref, class_out
+):
+    rolls = span_rolls()
+    weights = span_vector(WEIGHTS)
+    inverse = span_vector(1.0 / FACTOR)
+    _, by, _ = iotas((8, LANES))
+    received = [
+        [lower_upper("dom", near_y_ref[k, a], far_y_ref[k, a]) for a in range(7)] for k in range(2)
+    ]
+
+    def chosen(place, values):
+        return jnp.where(by == place, values, 0.0)
+
+    each = [(i, range(7)) for i in range(3)]
+    own = face_source(
+        rolls, weights, inverse,
+        [[chosen(0, lanes_from(received[1][a][0], i, 0)) for a in r] for i, r in each],
+        [[chosen(BY - 1, lanes_from(received[1][a][1], i, LANES - BZ)) for a in r] for i, r in each],
+    )
+    other = face_source(
+        rolls, weights, inverse,
+        [[chosen(1, pltpu.roll(last_ref[i, a], 2 * BZ, 1)) for a in r] for i, r in each],
+        [[chosen(0, first_ref[i, a]) for a in r] for i, r in each],
+    )
+    for a in range(7):
+        mine = part_ref[0, a] + join_local(own[a])
+        low, high = received[0][a]
+        theirs = join_span(other[a]) + jnp.stack(
+            [
+                chosen(0, lanes_from(low, b, 0)) + chosen(1, lanes_from(high, b, BZ))
+                for b in range(7)
+            ],
+            axis=0,
+        )
+        out_ref[0, a], out_ref[1, a] = mine, theirs
+        out_ref[0, a, 0] = mine[0] + chosen(0, theirs[6])
+        out_ref[0, a, 6] = mine[6] + chosen(BY - 1, pltpu.roll(theirs[0], LANES - 2 * BZ, 1))
+        out_ref[1, a, 6] = theirs[6] + chosen(0, mine[0])
+        out_ref[1, a, 0] = theirs[0] + chosen(1, pltpu.roll(mine[6], 2 * BZ, 1))
+    for k in range(2):
+        emit_faces(out_ref, far_ref, near_ref, k)
+    low, high = received[0][0]
+    class_out[...] = chosen(0, lanes_from(low, 7, 0)) + chosen(1, lanes_from(high, 7, BZ))
 
 
 def gather_modes(full_ref, modes_ref):
@@ -408,32 +464,20 @@
 
 
 def first_apply_kernel(
-    part_ref, far_x_ref, near_x_ref, far_y_ref, near_y_ref, split_0, split_1, class_ref,
+    part_ref, far_x_ref, near_x_ref, split_0, split_1, class_ref, ghost_class_ref,
     load_ref, image_ref, out_ref, far_ref, near_ref,
     full_ref, ghost_ref, ghost_modes_ref, side_ref, right_ref, last_ref,
 ):
     _, by, _ = iotas((8, LANES))
-    for a in range(7):
-        sheet = add_streamwise(a, part_ref[0, a], far_x_ref[0], near_x_ref[0])
-        low, high = lower_upper("dom", near_y_ref[0, a], far_y_ref[0, a])
-        for b in range(7):
-            block = jnp.where(by == 0, lanes_from(low, b, 0), 0.0)
-            block = jnp.where(by == 1, lanes_from(high, b, BZ), block)
-            if b == 6:
-                block = block + jnp.where(by == 0, sheet[0], 0.0)
-            if b == 0:
-                block = block + jnp.where(by == 1, pltpu.roll(sheet[6], 2 * BZ, 1), 0.0)
-            ghost_ref[56 * a + 8 * b : 56 * a + 8 * b + 8] = block
-        sheet = add_second(sheet, lanes_from(low, 6, 0), lanes_from(high, 0, LANES - BZ))
-        full_ref[56 * a : 56 * a + 56] = sheet.reshape(56, LANES)
-    low, high = lower_upper("dom", near_y_ref[0, 0], far_y_ref[0, 0])
-    ghost_class = jnp.where(by == 0, lanes_from(low, 7, 0), 0.0)
-    ghost_class = jnp.where(by == 1, lanes_from(high, 7, BZ), ghost_class)
+    for k, padded_ref in enumerate((full_ref, ghost_ref)):
+        for a in range(7):
+            sheet = add_streamwise(a, part_ref[k, a], far_x_ref[k], near_x_ref[k])
+            padded_ref[56 * a : 56 * a + 56] = sheet.reshape(56, LANES)
     gather_modes(full_ref, load_ref)
     gather_modes(ghost_ref, ghost_modes_ref)
     ghost_image = multiply_blocks(
         (split_0, split_1), class_ref, load_ref, image_ref, right_ref, last_ref,
-        (ghost_modes_ref[...], ghost_class),
+        (ghost_modes_ref[...], ghost_class_ref[...]),
     )
     scatter_modes(image_ref, full_ref, out_ref)
     ghost_modes_ref[...] = ghost_image
@@ -556,18 +600,6 @@
 def swap(axis, far, near):
     far_pairs, near_pairs = partners(axis)
     return lax.ppermute(far, axis, far_pairs), lax.ppermute(near, axis, near_pairs)
-
-
-def exchange(part, far, near, beside, rows=None):
-    far_x, near_x = swap("slab", far, near)
-    part, beside = lax.optimization_barrier((part, beside))
-    outs = [(part.shape[0], 7, 8, LANES)] * 2
-    args = (part, far_x, near_x)
-    if rows is None:
-        far, near = call(side_kernel, outs, args, name="side")
-    else:
-        far, near = call(row_kernel, outs, (*args, rows), name="rows")
-    return (part, far_x, near_x, *swap("dom", far, near)), beside
 
 
 def per_device(velocity, slot_map, class_index, schur_blocks):
@@ -591,19 +623,27 @@
         name="advect",
         hbm=(0, 1, 2),
     )
-    received, split_0 = exchange(part, far, near, split_half(schur, 0))
-    part, far, near = call(
+    swapped = swap("slab", far, near)
+    part, split_0 = lax.optimization_barrier((part, split_half(schur, 0)))
+    part, far, near, first_side, last_side = call(
         source_kernel,
-        [(1, *whole), (1, *face), (1, *face)],
-        (*received, brick),
+        [(1, *whole), (2, *face), (2, *face), (3, *face), (3, *face)],
+        (part, *swapped, brick, classes),
         [(3, *whole)],
         name="source",
     )
-    received, split_1 = exchange(part, far, near, split_half(schur, 1), classes)
+    part, far, near, ghost_classes = call(
+        correct_kernel,
+        [(2, *whole), (2, *face), (2, *face), (8, LANES)],
+        (part, *swap("dom", far, near), first_side, last_side),
+        name="correct",
+    )
+    swapped = swap("slab", far, near)
+    part, split_1 = lax.optimization_barrier((part, split_half(schur, 1)))
     load, first, part, far, near = call(
         first_apply_kernel,
         [modes, modes, (1, *whole), (1, *face), (1, *face)],
-        (*received, split_0, split_1, classes),
+        (part, *swapped, split_0, split_1, classes, ghost_classes),
         [(392, LANES), (392, LANES), modes, (2, *face), rights[0], rights[0]],
         name="first",
     )

time: 110 us -> 102 us (0.927)
  starting transfers between devices: 66.9 us -> 58.4 us
  Pallas kernels: 18.3 us -> 19.5 us
    ppermute x6 -> x5, starting transfers between devices: 17.5 us -> 12 us  [swap(): lax.ppermute(near, axis, near_pairs)]
    ppermute x6 -> x5, starting transfers between devices: 44.2 us -> 41.2 us  [swap(): lax.ppermute(far, axis, far_pairs)]
    pallas_call x10 -> x9, Pallas kernels: 18.3 us -> 19.5 us  [call(): pl.pallas_call(kernel, out_shape=tuple((jax.ShapeDtypeStruct(*(o if isins...]
    ppermute x6 -> x5, waiting for transfers between devices: 4.87 us -> 3.94 us  [swap(): lax.ppermute(near, axis, near_pairs)]
    ppermute x6 -> x5, waiting for transfers between devices: 2.94 us -> 3.18 us  [swap(): lax.ppermute(far, axis, far_pairs)]
  transfers between devices with their start and end apart: 13 -> 11, of which waited for: 6 -> 5; matrix products, arithmetic and copies ran while one was open for 0% -> 0% of each run, Pallas kernels for 5% -> 6%
where the time goes in v6:
time: 102 us
  starting transfers between devices  58.4 us (57%)
  Pallas kernels  19.5 us (19%)
  blocking collectives  15.9 us (16%)
  waiting for transfers between devices  7.12 us (7%)
    ppermute x5, starting transfers between devices, swap(): lax.ppermute(far, axis, far_pairs)  41.2 us
    pallas_call x9, Pallas kernels, call(): pl.pallas_call(kernel, out_shape=tuple((jax.ShapeDtypeStruct(*(o if isins...  19.5 us
    all_to_all x1, blocking collectives, per_device(): lax.all_to_all(send, 'dom', 0, 0)  15.9 us
    ppermute x5, starting transfers between devices, swap(): lax.ppermute(near, axis, near_pairs)  12 us
    all_to_all x1, starting transfers between devices, per_device(): dots = lax.all_to_all(sums, 'slab', 0, 0)  5.19 us
    ppermute x5, waiting for transfers between devices, swap(): lax.ppermute(near, axis, near_pairs)  3.94 us
    ppermute x5, waiting for transfers between devices, swap(): lax.ppermute(far, axis, far_pairs)  3.18 us
  transfers between devices with their start and end apart: 11, of which 5 were waited for; matrix products, arithmetic and copies ran while one was open for 0% of the time, Pallas kernels for 6%

profile of v6, /device:TPU:1, one launch (start us, length us, event | category | flops | bytes accessed | tf_op | source)
XLA Modules:
  0.0 101.7 jit_solution(15201042364922411789)
XLA Ops:
  0.6 3.6 %advect.1 = (f32[3,7,7,8,128]{4,3,2,1,0:T(8,128)S(1)}, f32[3,7,7,8,128]{4,3,2,1,0:T(8,128)S(1)}, f32[3,7,8,128]{3,2,1,0:T(8,128)S(1)}, f32[3,7,8,128]{3,2,1,0:T(8,128)S(1)}, f32[8,128]{1,0:T(8,128)S(1)}) custom-call(f32[3,343,128]{2,1,0:T(8,128)} %vel_hbm.1, s32[1,128]{1,0:T(1,128)} %bitcast.3, s32[1,128]{1,0:T(1,128)} %bitcast.7), custom_call_target="tpu_custom_call" | custom-call | tf_op jit(solution)/shard_map/advect/pallas_call | solution.py:580
  4.2 14.4 %collective-permute-start = (f32[3,7,8,128]{3,2,1,0:T(8,128)S(1)}, f32[3,7,8,128]{3,2,1,0:T(8,128)S(1)}, u32[]{:S(2)}, u32[]{:S(2)}) collective-permute-start(f32[3,7,8,128]{3,2,1,0:T(8,128)S(1)} %get-tuple-element.35), channel_id=1, source_target_pairs={{0,480},{32,64},{64,32},{96,128},{128,96},{160,192},{192,160},{224... | collective-permute-start | bytes 258056 | tf_op jit(solution)/shard_map/ppermute | solution.py:602
  18.6 1.9 %collective-permute-start.1 = (f32[3,7,8,128]{3,2,1,0:T(8,128)S(1)}, f32[3,7,8,128]{3,2,1,0:T(8,128)S(1)}, u32[]{:S(2)}, u32[]{:S(2)}) collective-permute-start(f32[3,7,8,128]{3,2,1,0:T(8,128)S(1)} %get-tuple-element.36), channel_id=1, source_target_pairs={{0,32},{32,0},{64,96},{96,64},{128,160},{160,128},{192,224},{224,1... | collective-permute-start | bytes 258056 | tf_op jit(solution)/shard_map/ppermute | solution.py:602
  20.5 2.9 %split.2.split_0 = bf16[672,2048]{1,0:T(8,128)(2,1)S(1)} custom-call(f32[218,16,218]{2,1,0:T(8,128)} %bitcast.5), custom_call_target="tpu_custom_call" | custom-call | tf_op jit(solution)/shard_map/split/pallas_call | solution.py:580
  23.4 0.0 collective-permute-done.far_x_ref
  23.4 0.4 collective-permute-done.1.near_x_ref
  23.8 0.9 source.1
  24.7 5.1 %collective-permute-start.2 = (f32[2,7,8,128]{3,2,1,0:T(8,128)S(1)}, f32[2,7,8,128]{3,2,1,0:T(8,128)S(1)}, u32[]{:S(2)}, u32[]{:S(2)}) collective-permute-start(f32[2,7,8,128]{3,2,1,0:T(8,128)S(1)} %get-tuple-element.40), channel_id=1, source_target_pairs={{0,31},{1,2},{2,1},{3,4},{4,3},{5,6},{6,5},{7,8},{8,7},{9,10},{10,... | collective-permute-start | bytes 172040 | tf_op jit(solution)/shard_map/ppermute | solution.py:602
  29.8 4.3 %collective-permute-start.3 = (f32[2,7,8,128]{3,2,1,0:T(8,128)S(1)}, f32[2,7,8,128]{3,2,1,0:T(8,128)S(1)}, u32[]{:S(2)}, u32[]{:S(2)}) collective-permute-start(f32[2,7,8,128]{3,2,1,0:T(8,128)S(1)} %get-tuple-element.41), channel_id=1, source_target_pairs={{0,1},{1,0},{2,3},{3,2},{4,5},{5,4},{6,7},{7,6},{8,9},{9,8},{10,11... | collective-permute-start | bytes 172040 | tf_op jit(solution)/shard_map/ppermute | solution.py:602
  34.2 0.0 collective-permute-done.2.far_y_ref
  34.2 0.9 collective-permute-done.3.near_y_ref
  35.0 1.3 %correct.1 = (f32[2,7,7,8,128]{4,3,2,1,0:T(8,128)S(1)}, f32[2,7,8,128]{3,2,1,0:T(8,128)S(1)}, f32[2,7,8,128]{3,2,1,0:T(8,128)S(1)}, f32[8,128]{1,0:T(8,128)S(1)}) custom-call(f32[1,7,7,8,128]{4,3,2,1,0:T(8,128)S(1)} %get-tuple-element.39.part_ref, f32[2,7,8,128]{3,2,1,0:T(8,128)S(1)} %collective-permute-done.2.far_y_ref, ...), custom_call_target="tpu_custom_call" | custom-call | tf_op jit(solution)/shard_map/correct/pallas_call | solution.py:580
  36.4 6.3 %collective-permute-start.4 = (f32[2,7,8,128]{3,2,1,0:T(8,128)S(1)}, f32[2,7,8,128]{3,2,1,0:T(8,128)S(1)}, u32[]{:S(2)}, u32[]{:S(2)}) collective-permute-start(f32[2,7,8,128]{3,2,1,0:T(8,128)S(1)} %get-tuple-element.46), channel_id=1, source_target_pairs={{0,480},{32,64},{64,32},{96,128},{128,96},{160,192},{192,160},{224... | collective-permute-start | bytes 172040 | tf_op jit(solution)/shard_map/ppermute | solution.py:602
  42.6 1.9 %collective-permute-start.5 = (f32[2,7,8,128]{3,2,1,0:T(8,128)S(1)}, f32[2,7,8,128]{3,2,1,0:T(8,128)S(1)}, u32[]{:S(2)}, u32[]{:S(2)}) collective-permute-start(f32[2,7,8,128]{3,2,1,0:T(8,128)S(1)} %get-tuple-element.47), channel_id=1, source_target_pairs={{0,32},{32,0},{64,96},{96,64},{128,160},{160,128},{192,224},{224,1... | collective-permute-start | bytes 172040 | tf_op jit(solution)/shard_map/ppermute | solution.py:602
  44.5 2.9 %split.3.split_1 = bf16[672,2048]{1,0:T(8,128)(2,1)S(1)} custom-call(f32[218,16,218]{2,1,0:T(8,128)} %bitcast.6), custom_call_target="tpu_custom_call" | custom-call | tf_op jit(solution)/shard_map/split/pallas_call | solution.py:580
  47.4 0.4 collective-permute-done.4.far_x_ref
  47.8 0.0 collective-permute-done.5.near_x_ref
  47.8 0.0 copy-start
  47.8 3.6 %first.1 = (f32[224,128]{1,0:T(8,128)S(1)}, f32[224,128]{1,0:T(8,128)S(1)}, f32[1,7,7,8,128]{4,3,2,1,0:T(8,128)S(1)}, f32[1,7,8,128]{3,2,1,0:T(8,128)S(1)}, f32[1,7,8,128]{3,2,1,0:T(8,128)S(1)}) custom-call(f32[2,7,7,8,128]{4,3,2,1,0:T(8,128)S(1)} %get-tuple-element.45.part_ref, f32[2,7,8,128]{3,2,1,0:T(8,128)S(1)} %collective-permute-done.4.far_x_ref, ...), custom_call_target="tpu_custom_call" | custom-call | tf_op jit(solution)/shard_map/first/pallas_call | solution.py:580
  51.4 6.2 %collective-permute-start.6 = (f32[1,7,8,128]{3,2,1,0:T(8,128)S(1)}, f32[1,7,8,128]{3,2,1,0:T(8,128)S(1)}, u32[]{:S(2)}, u32[]{:S(2)}) collective-permute-start(f32[1,7,8,128]{3,2,1,0:T(8,128)S(1)} %get-tuple-element.52), channel_id=1, source_target_pairs={{0,480},{32,64},{64,32},{96,128},{128,96},{160,192},{192,160},{224... | collective-permute-start | bytes 86024 | tf_op jit(solution)/shard_map/ppermute | solution.py:602
  57.6 1.9 %collective-permute-start.7 = (f32[1,7,8,128]{3,2,1,0:T(8,128)S(1)}, f32[1,7,8,128]{3,2,1,0:T(8,128)S(1)}, u32[]{:S(2)}, u32[]{:S(2)}) collective-permute-start(f32[1,7,8,128]{3,2,1,0:T(8,128)S(1)} %get-tuple-element.53), channel_id=1, source_target_pairs={{0,32},{32,0},{64,96},{96,64},{128,160},{160,128},{192,224},{224,1... | collective-permute-start | bytes 86024 | tf_op jit(solution)/shard_map/ppermute | solution.py:602
  59.5 2.8 %collective-permute-done.6.far_x_ref = f32[1,7,8,128]{3,2,1,0:T(8,128)S(1)} collective-permute-done((f32[1,7,8,128]{3,2,1,0:T(8,128)S(1)}, f32[1,7,8,128]{3,2,1,0:T(8,128)S(1)}, u32[]{:S(2)}, u32[]{:S(2)}) %collective-permute-start.6) | collective-permute-done | bytes 28704 | tf_op jit(solution)/shard_map/ppermute | solution.py:602
  62.3 0.0 collective-permute-done.7.near_x_ref
  62.3 0.0 copy-done
  62.3 0.0 copy-start.1
  62.3 2.6 %second.1 = (f32[224,128]{1,0:T(8,128)S(1)}, f32[32,8,128]{2,1,0:T(8,128)S(1)}, f32[1,7,7,8,128]{4,3,2,1,0:T(8,128)S(1)}) custom-call(f32[1,7,7,8,128]{4,3,2,1,0:T(8,128)S(1)} %get-tuple-element.51.part_ref, f32[1,7,8,128]{3,2,1,0:T(8,128)S(1)} %collective-permute-done.6.far_x_ref, f32[1,7,8,128]{3,2,1,0:T(8,128)S(1)} %collective-permute-done.7.near_x_ref, ...), custom_call_target="tpu_custom_call" | custom-call | tf_op jit(solution)/shard_map/second/pallas_call | solution.py:580
  64.9 15.9 %all_to_all.10.got_ref = f32[32,8,128]{2,1,0:T(8,128)S(1)} all-to-all(f32[32,8,128]{2,1,0:T(8,128)S(1)} %get-tuple-element.57), channel_id=1, replica_groups=mesh['slab'=16,'dom'=32] {'dom'}, dimensions={0} | all-to-all | bytes 262144 | tf_op jit(solution)/shard_map/all_to_all | solution.py:661
  80.8 0.7 middle.1
  81.5 5.2 %all-to-all-start.1 = ((f32[16,4,128]{2,1,0:T(4,128)}), f32[16,4,128]{2,1,0:T(4,128)S(1)}, u32[]{:S(2)}, u32[]{:S(2)}) async-start(f32[16,4,128]{2,1,0:T(4,128)} %get-tuple-element.63), calls=%async_computation.1 | async-start | bytes 65536 | tf_op jit(solution)/shard_map/all_to_all | solution.py:664
  86.7 9.3 %collective-permute-start.8 = (f32[1,7,8,128]{3,2,1,0:T(8,128)S(1)}, f32[1,7,8,128]{3,2,1,0:T(8,128)S(1)}, u32[]{:S(2)}, u32[]{:S(2)}) collective-permute-start(f32[1,7,8,128]{3,2,1,0:T(8,128)S(1)} %get-tuple-element.58), channel_id=1, source_target_pairs={{0,480},{32,64},{64,32},{96,128},{128,96},{160,192},{192,160},{224... | collective-permute-start | bytes 86024 | tf_op jit(solution)/shard_map/ppermute | solution.py:602
  96.0 1.9 %collective-permute-start.9 = (f32[1,7,8,128]{3,2,1,0:T(8,128)S(1)}, f32[1,7,8,128]{3,2,1,0:T(8,128)S(1)}, u32[]{:S(2)}, u32[]{:S(2)}) collective-permute-start(f32[1,7,8,128]{3,2,1,0:T(8,128)S(1)} %get-tuple-element.59), channel_id=1, source_target_pairs={{0,32},{32,0},{64,96},{96,64},{128,160},{160,128},{192,224},{224,1... | collective-permute-start | bytes 86024 | tf_op jit(solution)/shard_map/ppermute | solution.py:602
  97.9 0.0 collective-permute-done.8.far_x_ref
  97.9 2.7 %collective-permute-done.9.near_x_ref = f32[1,7,8,128]{3,2,1,0:T(8,128)S(1)} collective-permute-done((f32[1,7,8,128]{3,2,1,0:T(8,128)S(1)}, f32[1,7,8,128]{3,2,1,0:T(8,128)S(1)}, u32[]{:S(2)}, u32[]{:S(2)}) %collective-permute-start.9) | collective-permute-done | bytes 28704 | tf_op jit(solution)/shard_map/ppermute | solution.py:602
  100.6 0.0 all-to-all-done.1.dots_ref
  100.6 0.0 copy-done.1
  100.6 1.1 %finish.1 = (f32[218,128]{1,0:T(8,128)}, f32[218,128]{1,0:T(8,128)}) custom-call(f32[1,7,7,8,128]{4,3,2,1,0:T(8,128)S(1)} %get-tuple-element.56.part_ref, f32[1,7,8,128]{3,2,1,0:T(8,128)S(1)} %collective-permute-done.8.far_x_ref, f32[1,7,8,128]{3,2,1,0:T(8,128)S(1)} %collective-permute-done.9.near_x_ref, f32[7,8,128]{2,1,0:T(8,128)S(1)} %get-tuple-element.60.low_ref, ...), custom_call_target="tpu_custom_call" | custom-call | tf_op jit(solution)/shard_map/finish/pallas_call | solution.py:580
Async XLA Ops:
  4.2 19.2 %collective-permute-start = (f32[3,7,8,128]{3,2,1,0:T(8,128)S(1)}, f32[3,7,8,128]{3,2,1,0:T(8,128)S(1)}, u32[]{:S(2)}, u32[]{:S(2)}) collective-permute-start(f32[3,7,8,128]{3,2,1,0:T(8,128)S(1)} %get-tuple-element.35), channel_id=1, source_target_pairs={{0,480},{32,64},{64,32},{96,128},{128,96},{160,192},{192,160},{224... | collective-permute-start | bytes 258056 | tf_op jit(solution)/shard_map/ppermute | solution.py:602
  18.6 5.2 %collective-permute-start.1 = (f32[3,7,8,128]{3,2,1,0:T(8,128)S(1)}, f32[3,7,8,128]{3,2,1,0:T(8,128)S(1)}, u32[]{:S(2)}, u32[]{:S(2)}) collective-permute-start(f32[3,7,8,128]{3,2,1,0:T(8,128)S(1)} %get-tuple-element.36), channel_id=1, source_target_pairs={{0,32},{32,0},{64,96},{96,64},{128,160},{160,128},{192,224},{224,1... | collective-permute-start | bytes 258056 | tf_op jit(solution)/shard_map/ppermute | solution.py:602
  24.7 9.4 %collective-permute-start.2 = (f32[2,7,8,128]{3,2,1,0:T(8,128)S(1)}, f32[2,7,8,128]{3,2,1,0:T(8,128)S(1)}, u32[]{:S(2)}, u32[]{:S(2)}) collective-permute-start(f32[2,7,8,128]{3,2,1,0:T(8,128)S(1)} %get-tuple-element.40), channel_id=1, source_target_pairs={{0,31},{1,2},{2,1},{3,4},{4,3},{5,6},{6,5},{7,8},{8,7},{9,10},{10,... | collective-permute-start | bytes 172040 | tf_op jit(solution)/shard_map/ppermute | solution.py:602
  29.8 5.2 %collective-permute-start.3 = (f32[2,7,8,128]{3,2,1,0:T(8,128)S(1)}, f32[2,7,8,128]{3,2,1,0:T(8,128)S(1)}, u32[]{:S(2)}, u32[]{:S(2)}) collective-permute-start(f32[2,7,8,128]{3,2,1,0:T(8,128)S(1)} %get-tuple-element.41), channel_id=1, source_target_pairs={{0,1},{1,0},{2,3},{3,2},{4,5},{5,4},{6,7},{7,6},{8,9},{9,8},{10,11... | collective-permute-start | bytes 172040 | tf_op jit(solution)/shard_map/ppermute | solution.py:602
  36.4 11.5 %collective-permute-start.4 = (f32[2,7,8,128]{3,2,1,0:T(8,128)S(1)}, f32[2,7,8,128]{3,2,1,0:T(8,128)S(1)}, u32[]{:S(2)}, u32[]{:S(2)}) collective-permute-start(f32[2,7,8,128]{3,2,1,0:T(8,128)S(1)} %get-tuple-element.46), channel_id=1, source_target_pairs={{0,480},{32,64},{64,32},{96,128},{128,96},{160,192},{192,160},{224... | collective-permute-start | bytes 172040 | tf_op jit(solution)/shard_map/ppermute | solution.py:602
  42.6 5.2 %collective-permute-start.5 = (f32[2,7,8,128]{3,2,1,0:T(8,128)S(1)}, f32[2,7,8,128]{3,2,1,0:T(8,128)S(1)}, u32[]{:S(2)}, u32[]{:S(2)}) collective-permute-start(f32[2,7,8,128]{3,2,1,0:T(8,128)S(1)} %get-tuple-element.47), channel_id=1, source_target_pairs={{0,32},{32,0},{64,96},{96,64},{128,160},{160,128},{192,224},{224,1... | collective-permute-start | bytes 172040 | tf_op jit(solution)/shard_map/ppermute | solution.py:602
  47.8 14.5 %copy-start = (f32[224,128]{1,0:T(8,128)S(1)}, f32[224,128]{1,0:T(8,128)}, u32[]{:S(2)}) copy-start(f32[224,128]{1,0:T(8,128)} %constant.2.clone.shell_ref) | copy-start | bytes 344068
  51.4 10.9 %collective-permute-start.6 = (f32[1,7,8,128]{3,2,1,0:T(8,128)S(1)}, f32[1,7,8,128]{3,2,1,0:T(8,128)S(1)}, u32[]{:S(2)}, u32[]{:S(2)}) collective-permute-start(f32[1,7,8,128]{3,2,1,0:T(8,128)S(1)} %get-tuple-element.52), channel_id=1, source_target_pairs={{0,480},{32,64},{64,32},{96,128},{128,96},{160,192},{192,160},{224... | collective-permute-start | bytes 86024 | tf_op jit(solution)/shard_map/ppermute | solution.py:602
  57.6 4.7 %collective-permute-start.7 = (f32[1,7,8,128]{3,2,1,0:T(8,128)S(1)}, f32[1,7,8,128]{3,2,1,0:T(8,128)S(1)}, u32[]{:S(2)}, u32[]{:S(2)}) collective-permute-start(f32[1,7,8,128]{3,2,1,0:T(8,128)S(1)} %get-tuple-element.53), channel_id=1, source_target_pairs={{0,32},{32,0},{64,96},{96,64},{128,160},{160,128},{192,224},{224,1... | collective-permute-start | bytes 86024 | tf_op jit(solution)/shard_map/ppermute | solution.py:602
  62.3 38.3 %copy-start.1 = (s32[1,1,128]{2,1,0:T(1,128)S(1)}, s32[1,1,128]{2,1,0:T(1,128)}, u32[]{:S(2)}) copy-start(s32[1,1,128]{2,1,0:T(1,128)} %param.6) | copy-start | bytes 1540
  81.5 19.1 %all-to-all-start.1 = ((f32[16,4,128]{2,1,0:T(4,128)}), f32[16,4,128]{2,1,0:T(4,128)S(1)}, u32[]{:S(2)}, u32[]{:S(2)}) async-start(f32[16,4,128]{2,1,0:T(4,128)} %get-tuple-element.63), calls=%async_computation.1 | async-start | bytes 65536 | tf_op jit(solution)/shard_map/all_to_all | solution.py:664
  86.7 11.2 %collective-permute-start.8 = (f32[1,7,8,128]{3,2,1,0:T(8,128)S(1)}, f32[1,7,8,128]{3,2,1,0:T(8,128)S(1)}, u32[]{:S(2)}, u32[]{:S(2)}) collective-permute-start(f32[1,7,8,128]{3,2,1,0:T(8,128)S(1)} %get-tuple-element.58), channel_id=1, source_target_pairs={{0,480},{32,64},{64,32},{96,128},{128,96},{160,192},{192,160},{224... | collective-permute-start | bytes 86024 | tf_op jit(solution)/shard_map/ppermute | solution.py:602
  96.0 4.6 %collective-permute-start.9 = (f32[1,7,8,128]{3,2,1,0:T(8,128)S(1)}, f32[1,7,8,128]{3,2,1,0:T(8,128)S(1)}, u32[]{:S(2)}, u32[]{:S(2)}) collective-permute-start(f32[1,7,8,128]{3,2,1,0:T(8,128)S(1)} %get-tuple-element.59), channel_id=1, source_target_pairs={{0,32},{32,0},{64,96},{96,64},{128,160},{160,128},{192,224},{224,1... | collective-permute-start | bytes 86024 | tf_op jit(solution)/shard_map/ppermute | solution.py:602

commit v7 on v6

--- a/solution.py
+++ b/solution.py
@@ -382,7 +382,7 @@
     ]
     for copy in copies:
         copy.start()
-    for k in range(3):
+    for k in range(2):
         split_ref[224 * k + 208 : 224 * k + 224] = jnp.zeros((16, 256 * HALF), BF16)
     right_ref[...] = jnp.zeros(right_ref.shape, F32)
     for copy in copies:
@@ -393,14 +393,14 @@
         for side, side_ref in enumerate((left_ref, right_ref)):
             block = side_ref[pl.ds(c, MODES, stride=HALF), :]
             place = LANES * (2 * c + side)
-            for k, term in enumerate(terms(block)):
+            for k, term in enumerate(terms(block)[:2]):
                 split_ref[224 * k : 224 * k + MODES, place : place + LANES] = term
 
 
 def split_half(schur, half):
     return call(
         functools.partial(split_kernel, half),
-        [((672, 256 * HALF), BF16)],
+        [((448, 256 * HALF), BF16)],
         (schur,),
         [
             (MODES, HALF, MODES),
@@ -427,7 +427,7 @@
             for k, term in enumerate(terms(modes))
         ]
         low = jnp.concatenate([low, (three[0] + three[1] + three[2]).astype(BF16)], axis=1)
-        last_both, rows = jnp.concatenate([mine, classes[0:1]], axis=1), 672
+        last_both, rows = jnp.concatenate([mine, classes[0:1]], axis=1), 448
     zeros = jnp.zeros((32, 2 * LANES), BF16)
     for c in range(CLASSES):
         chosen, last_chosen = (
@@ -443,11 +443,11 @@
         total = total + jnp.dot(split_ref[...], right_ref[part], preferred_element_type=F32)
         small = small + jnp.dot(split_ref[0:rows], last_ref[part], preferred_element_type=F32)
     total = total[:, :LANES] + total[:, LANES:]
-    image_ref[...] = total[0:224] + (total[224:448] + (total[448:672] + small[0:224, :LANES]))
+    image_ref[...] = total[0:224] + (total[224:448] + small[0:224, :LANES])
     if ghost is None:
         return None
     extra = small[:, LANES:]
-    extra = extra[0:224] + (extra[224:448] + extra[448:672])
+    extra = extra[0:224] + extra[224:448]
     return extra + (pltpu.roll(extra, LANES - 32, 1) + pltpu.roll(extra, LANES - 64, 1))
 
 
@@ -495,7 +495,7 @@
 
 def second_apply_kernel(
     part_ref, far_x_ref, near_x_ref, split_0, split_1, class_ref, load_ref, first_ref, shell_ref,
-    power_ref, send_ref, out_ref, image_ref, full_ref, right_ref, last_ref,
+    power_ref, send_ref, out_ref, far_ref, near_ref, image_ref, full_ref, right_ref, last_ref,
 ):
     for a in range(7):
         sheet = add_streamwise(a, part_ref[0, a], far_x_ref[0], near_x_ref[0])
@@ -503,6 +503,7 @@
     gather_modes(full_ref, power_ref)
     multiply_blocks((split_0, split_1), class_ref, power_ref, image_ref, right_ref, last_ref)
     scatter_modes(image_ref, full_ref, out_ref)
+    emit_faces(out_ref, far_ref, near_ref, 0)
     load, power, shell = load_ref[...], power_ref[...], shell_ref[...]
     first, image = first_ref[...], image_ref[...]
     lane = lax.broadcasted_iota(jnp.int32, (1, LANES), 1)
@@ -523,34 +524,41 @@
     send_ref[lax.rem(mine + count - 1, count)] = jnp.where(node == 7, dots, down)
 
 
-def middle_kernel(part_ref, got_ref, far_ref, near_ref, low_ref, high_ref, sums_ref):
+def middle_kernel(got_ref, low_ref, high_ref, send_ref):
     node = lax.broadcasted_iota(jnp.int32, (8, LANES), 0)
+    _, by, _ = iotas((8, LANES))
     count = got_ref.shape[0]
     mine = lax.axis_index("dom")
     low = jnp.where(node < 7, got_ref[lax.rem(mine + count - 1, count)], 0.0)
     high = jnp.where(node < 7, got_ref[lax.rem(mine + 1, count)], 0.0)
-    faces = []
     for a in range(7):
         low_ref[a], high_ref[a] = lanes_from(low, a, 0), lanes_from(high, a, LANES - BZ)
-        if a in (0, 6):
-            faces.append(add_second(part_ref[0, a], low_ref[a], high_ref[a]))
-    even = even_place("slab", faces[0])
-    far_ref[0] = jnp.where(even, faces[0], faces[1])
-    near_ref[0] = jnp.where(even, faces[1], faces[0])
     total = jnp.sum(got_ref[...], axis=0)[7:8]
-    sums_ref[...] = jnp.broadcast_to(total[None], sums_ref.shape)
+    send_ref[...] = jnp.broadcast_to(jnp.where(node == 7, total, 0.0)[None], send_ref.shape)
+    slabs = send_ref.shape[0]
+    place = lax.axis_index("slab")
+    for a, step in ((6, 1), (0, slabs - 1)):
+        edges = jnp.where(by == 0, low_ref[a], jnp.where(by == BY - 1, high_ref[a], 0.0))
+        send_ref[lax.rem(place + step, slabs)] = jnp.where(node == 7, total, edges)
 
 
 def finish_kernel(
     part_ref, far_x_ref, near_x_ref, low_ref, high_ref, load_ref, power_ref, dots_ref, slot_ref,
     pressure_ref, residual_ref, full_ref, modes_ref,
 ):
+    node = lax.broadcasted_iota(jnp.int32, (8, LANES), 0)
+    slabs = dots_ref.shape[0]
+    place = lax.axis_index("slab")
     for a in range(7):
         sheet = add_streamwise(a, part_ref[0, a], far_x_ref[0], near_x_ref[0])
         sheet = add_second(sheet, low_ref[a], high_ref[a])
+        if a in (0, 6):
+            edges = dots_ref[lax.rem(place + (slabs - 1 if a == 0 else 1), slabs)]
+            edges = jnp.where(node < 7, edges, 0.0)
+            sheet = add_second(sheet, edges, edges)
         full_ref[56 * a : 56 * a + 56] = sheet.reshape(56, LANES)
     gather_modes(full_ref, modes_ref)
-    dots = jnp.sum(dots_ref[...], axis=0)[0:1]
+    dots = jnp.sum(dots_ref[...], axis=0)[7:8]
     square, energy, power_square, cross, power_energy = (dots[:, k : k + 1] for k in range(5))
     step = square / energy
     fresh = square - 2.0 * step * energy + step * step * power_square
@@ -648,24 +656,24 @@
         name="first",
     )
     slabs, doms = lax.axis_size("slab"), lax.axis_size("dom")
-    power, send, part = call(
+    power, send, part, far, near = call(
         second_apply_kernel,
-        [modes, (doms, 8, LANES), (1, *whole)],
+        [modes, (doms, 8, LANES), (1, *whole), (1, *face), (1, *face)],
         (part, *swap("slab", far, near), split_0, split_1, classes, load, first, shell),
         [modes, (392, LANES), *rights],
         name="second",
     )
-    far, near, low, high, sums = call(
-        middle_kernel,
-        [(1, *face), (1, *face), face, face, (slabs, 4, LANES)],
-        (part, lax.all_to_all(send, "dom", 0, 0)),
-        name="middle",
-    )
-    dots = lax.all_to_all(sums, "slab", 0, 0)
+    got = lax.all_to_all(send, "dom", 0, 0)
+    far_x, near_x = swap("slab", far, near)
+    got, near_x = lax.optimization_barrier((got, near_x))
+    low, high, send = call(
+        middle_kernel, [face, face, (slabs, 8, LANES)], (got,), name="middle"
+    )
+    dots = lax.all_to_all(send, "slab", 0, 0)
     return call(
         finish_kernel,
         [(MODES, LANES), (MODES, LANES)],
-        (part, *swap("slab", far, near), low, high, load, power, dots, slots),
+        (part, far_x, near_x, low, high, load, power, dots, slots),
         [(392, LANES), modes],
         name="finish",
     )

time: 102 us -> 99.6 us (0.976)
  blocking collectives: 15.9 us -> 0 us
  starting transfers between devices: 58.4 us -> 66.2 us
  waiting for transfers between devices: 7.12 us -> 14.1 us
  Pallas kernels: 19.5 us -> 17.8 us
    all_to_all x1 -> x0, blocking collectives: 15.9 us -> none  [per_device(): lax.all_to_all(send, 'dom', 0, 0)]
    all_to_all x1 -> x2, starting transfers between devices: 5.19 us -> 13.1 us  [the longest x1 7.87 us: per_device(): got = lax.all_to_all(send, 'dom', 0, 0)]
    all_to_all x1 -> x2, waiting for transfers between devices: 0.01 us -> 3.75 us  [the longest x1 3.75 us: per_device(): got = lax.all_to_all(send, 'dom', 0, 0)]
    ppermute x5, waiting for transfers between devices: 3.18 us -> 5.65 us  [swap(): lax.ppermute(far, axis, far_pairs)]
    pallas_call x9, Pallas kernels: 19.5 us -> 17.8 us  [call(): pl.pallas_call(kernel, out_shape=tuple((jax.ShapeDtypeStruct(*(o if isins...]
  transfers between devices with their start and end apart: 11 -> 12, of which waited for: 5 -> 7; matrix products, arithmetic and copies ran while one was open for 0% -> 0% of each run, Pallas kernels for 6% -> 5%
where the time goes in v7:
time: 99.6 us; the launch traced here: 99 us
  starting transfers between devices  66.2 us (66%)
  Pallas kernels  17.8 us (18%)
  waiting for transfers between devices  14.1 us (14%)
    ppermute x5, starting transfers between devices, swap(): lax.ppermute(far, axis, far_pairs)  41.2 us
    pallas_call x9, Pallas kernels, call(): pl.pallas_call(kernel, out_shape=tuple((jax.ShapeDtypeStruct(*(o if isins...  17.8 us
    ppermute x5, starting transfers between devices, swap(): lax.ppermute(near, axis, near_pairs)  12 us
    all_to_all x1, starting transfers between devices, per_device(): got = lax.all_to_all(send, 'dom', 0, 0)  7.87 us
    ppermute x5, waiting for transfers between devices, swap(): lax.ppermute(far, axis, far_pairs)  5.65 us
    all_to_all x1, starting transfers between devices, per_device(): dots = lax.all_to_all(send, 'slab', 0, 0)  5.21 us
    ppermute x5, waiting for transfers between devices, swap(): lax.ppermute(near, axis, near_pairs)  4.74 us
    all_to_all x1, waiting for transfers between devices, per_device(): got = lax.all_to_all(send, 'dom', 0, 0)  3.75 us
  transfers between devices with their start and end apart: 12, of which 7 were waited for; matrix products, arithmetic and copies ran while one was open for 0% of the time, Pallas kernels for 5%

profile of v7, /device:TPU:1, one launch (start us, length us, event | category | flops | bytes accessed | tf_op | source)
XLA Modules:
  0.0 99.0 jit_solution(8661819950115318065)
XLA Ops:
  0.6 3.6 %advect.1 = (f32[3,7,7,8,128]{4,3,2,1,0:T(8,128)S(1)}, f32[3,7,7,8,128]{4,3,2,1,0:T(8,128)S(1)}, f32[3,7,8,128]{3,2,1,0:T(8,128)S(1)}, f32[3,7,8,128]{3,2,1,0:T(8,128)S(1)}, f32[8,128]{1,0:T(8,128)S(1)}) custom-call(f32[3,343,128]{2,1,0:T(8,128)} %vel_hbm.1, s32[1,128]{1,0:T(1,128)} %bitcast.3, s32[1,128]{1,0:T(1,128)} %bitcast.7), custom_call_target="tpu_custom_call" | custom-call | tf_op jit(solution)/shard_map/advect/pallas_call | solution.py:588
  4.2 14.4 %collective-permute-start = (f32[3,7,8,128]{3,2,1,0:T(8,128)S(1)}, f32[3,7,8,128]{3,2,1,0:T(8,128)S(1)}, u32[]{:S(2)}, u32[]{:S(2)}) collective-permute-start(f32[3,7,8,128]{3,2,1,0:T(8,128)S(1)} %get-tuple-element.37), channel_id=1, source_target_pairs={{0,480},{32,64},{64,32},{96,128},{128,96},{160,192},{192,160},{224... | collective-permute-start | bytes 258056 | tf_op jit(solution)/shard_map/ppermute | solution.py:610
  18.6 1.9 %collective-permute-start.1 = (f32[3,7,8,128]{3,2,1,0:T(8,128)S(1)}, f32[3,7,8,128]{3,2,1,0:T(8,128)S(1)}, u32[]{:S(2)}, u32[]{:S(2)}) collective-permute-start(f32[3,7,8,128]{3,2,1,0:T(8,128)S(1)} %get-tuple-element.38), channel_id=1, source_target_pairs={{0,32},{32,0},{64,96},{96,64},{128,160},{160,128},{192,224},{224,1... | collective-permute-start | bytes 258056 | tf_op jit(solution)/shard_map/ppermute | solution.py:610
  20.5 2.4 %split.2.split_0 = bf16[448,2048]{1,0:T(8,128)(2,1)S(1)} custom-call(f32[218,16,218]{2,1,0:T(8,128)} %bitcast.5), custom_call_target="tpu_custom_call" | custom-call | tf_op jit(solution)/shard_map/split/pallas_call | solution.py:588
  22.9 0.0 collective-permute-done.far_x_ref
  22.9 0.9 collective-permute-done.1.near_x_ref
  23.8 0.9 source.1
  24.7 5.1 %collective-permute-start.2 = (f32[2,7,8,128]{3,2,1,0:T(8,128)S(1)}, f32[2,7,8,128]{3,2,1,0:T(8,128)S(1)}, u32[]{:S(2)}, u32[]{:S(2)}) collective-permute-start(f32[2,7,8,128]{3,2,1,0:T(8,128)S(1)} %get-tuple-element.42), channel_id=1, source_target_pairs={{0,31},{1,2},{2,1},{3,4},{4,3},{5,6},{6,5},{7,8},{8,7},{9,10},{10,... | collective-permute-start | bytes 172040 | tf_op jit(solution)/shard_map/ppermute | solution.py:610
  29.8 4.3 %collective-permute-start.3 = (f32[2,7,8,128]{3,2,1,0:T(8,128)S(1)}, f32[2,7,8,128]{3,2,1,0:T(8,128)S(1)}, u32[]{:S(2)}, u32[]{:S(2)}) collective-permute-start(f32[2,7,8,128]{3,2,1,0:T(8,128)S(1)} %get-tuple-element.43), channel_id=1, source_target_pairs={{0,1},{1,0},{2,3},{3,2},{4,5},{5,4},{6,7},{7,6},{8,9},{9,8},{10,11... | collective-permute-start | bytes 172040 | tf_op jit(solution)/shard_map/ppermute | solution.py:610
  34.2 0.0 collective-permute-done.2.far_y_ref
  34.2 0.9 collective-permute-done.3.near_y_ref
  35.0 1.3 %correct.1 = (f32[2,7,7,8,128]{4,3,2,1,0:T(8,128)S(1)}, f32[2,7,8,128]{3,2,1,0:T(8,128)S(1)}, f32[2,7,8,128]{3,2,1,0:T(8,128)S(1)}, f32[8,128]{1,0:T(8,128)S(1)}) custom-call(f32[1,7,7,8,128]{4,3,2,1,0:T(8,128)S(1)} %get-tuple-element.41.part_ref, f32[2,7,8,128]{3,2,1,0:T(8,128)S(1)} %collective-permute-done.2.far_y_ref, ...), custom_call_target="tpu_custom_call" | custom-call | tf_op jit(solution)/shard_map/correct/pallas_call | solution.py:588
  36.4 6.3 %collective-permute-start.4 = (f32[2,7,8,128]{3,2,1,0:T(8,128)S(1)}, f32[2,7,8,128]{3,2,1,0:T(8,128)S(1)}, u32[]{:S(2)}, u32[]{:S(2)}) collective-permute-start(f32[2,7,8,128]{3,2,1,0:T(8,128)S(1)} %get-tuple-element.48), channel_id=1, source_target_pairs={{0,480},{32,64},{64,32},{96,128},{128,96},{160,192},{192,160},{224... | collective-permute-start | bytes 172040 | tf_op jit(solution)/shard_map/ppermute | solution.py:610
  42.6 1.9 %collective-permute-start.5 = (f32[2,7,8,128]{3,2,1,0:T(8,128)S(1)}, f32[2,7,8,128]{3,2,1,0:T(8,128)S(1)}, u32[]{:S(2)}, u32[]{:S(2)}) collective-permute-start(f32[2,7,8,128]{3,2,1,0:T(8,128)S(1)} %get-tuple-element.49), channel_id=1, source_target_pairs={{0,32},{32,0},{64,96},{96,64},{128,160},{160,128},{192,224},{224,1... | collective-permute-start | bytes 172040 | tf_op jit(solution)/shard_map/ppermute | solution.py:610
  44.5 2.4 %split.3.split_1 = bf16[448,2048]{1,0:T(8,128)(2,1)S(1)} custom-call(f32[218,16,218]{2,1,0:T(8,128)} %bitcast.6), custom_call_target="tpu_custom_call" | custom-call | tf_op jit(solution)/shard_map/split/pallas_call | solution.py:588
  46.9 0.9 collective-permute-done.4.far_x_ref
  47.8 0.0 collective-permute-done.5.near_x_ref
  47.8 0.0 copy-start
  47.8 2.7 %first.1 = (f32[224,128]{1,0:T(8,128)S(1)}, f32[224,128]{1,0:T(8,128)S(1)}, f32[1,7,7,8,128]{4,3,2,1,0:T(8,128)S(1)}, f32[1,7,8,128]{3,2,1,0:T(8,128)S(1)}, f32[1,7,8,128]{3,2,1,0:T(8,128)S(1)}) custom-call(f32[2,7,7,8,128]{4,3,2,1,0:T(8,128)S(1)} %get-tuple-element.47.part_ref, f32[2,7,8,128]{3,2,1,0:T(8,128)S(1)} %collective-permute-done.4.far_x_ref, ...), custom_call_target="tpu_custom_call" | custom-call | tf_op jit(solution)/shard_map/first/pallas_call | solution.py:588
  50.5 6.2 %collective-permute-start.6 = (f32[1,7,8,128]{3,2,1,0:T(8,128)S(1)}, f32[1,7,8,128]{3,2,1,0:T(8,128)S(1)}, u32[]{:S(2)}, u32[]{:S(2)}) collective-permute-start(f32[1,7,8,128]{3,2,1,0:T(8,128)S(1)} %get-tuple-element.54), channel_id=1, source_target_pairs={{0,480},{32,64},{64,32},{96,128},{128,96},{160,192},{192,160},{224... | collective-permute-start | bytes 86024 | tf_op jit(solution)/shard_map/ppermute | solution.py:610
  56.7 1.9 %collective-permute-start.7 = (f32[1,7,8,128]{3,2,1,0:T(8,128)S(1)}, f32[1,7,8,128]{3,2,1,0:T(8,128)S(1)}, u32[]{:S(2)}, u32[]{:S(2)}) collective-permute-start(f32[1,7,8,128]{3,2,1,0:T(8,128)S(1)} %get-tuple-element.55), channel_id=1, source_target_pairs={{0,32},{32,0},{64,96},{96,64},{128,160},{160,128},{192,224},{224,1... | collective-permute-start | bytes 86024 | tf_op jit(solution)/shard_map/ppermute | solution.py:610
  58.6 2.8 %collective-permute-done.6.far_x_ref = f32[1,7,8,128]{3,2,1,0:T(8,128)S(1)} collective-permute-done((f32[1,7,8,128]{3,2,1,0:T(8,128)S(1)}, f32[1,7,8,128]{3,2,1,0:T(8,128)S(1)}, u32[]{:S(2)}, u32[]{:S(2)}) %collective-permute-start.6) | collective-permute-done | bytes 28704 | tf_op jit(solution)/shard_map/ppermute | solution.py:610
  61.4 0.0 collective-permute-done.7.near_x_ref
  61.4 0.0 copy-done
  61.4 0.0 copy-start.1
  61.4 2.7 %second.1 = (f32[224,128]{1,0:T(8,128)S(1)}, f32[32,8,128]{2,1,0:T(8,128)}, f32[1,7,7,8,128]{4,3,2,1,0:T(8,128)S(1)}, f32[1,7,8,128]{3,2,1,0:T(8,128)S(1)}, f32[1,7,8,128]{3,2,1,0:T(8,128)S(1)}) custom-call(f32[1,7,7,8,128]{4,3,2,1,0:T(8,128)S(1)} %get-tuple-element.53.part_ref, f32[1,7,8,128]{3,2,1,0:T(8,128)S(1)} %collective-permute-done.6.far_x_ref, ...), custom_call_target="tpu_custom_call" | custom-call | tf_op jit(solution)/shard_map/second/pallas_call | solution.py:588
  64.1 7.9 %all-to-all-start = ((f32[32,8,128]{2,1,0:T(8,128)}), f32[32,8,128]{2,1,0:T(8,128)S(1)}, u32[]{:S(2)}, u32[]{:S(2)}) async-start(f32[32,8,128]{2,1,0:T(8,128)} %get-tuple-element.60), calls=%async_computation | async-start | bytes 262144 | tf_op jit(solution)/shard_map/all_to_all | solution.py:666
  72.0 1.9 %collective-permute-start.9 = (f32[1,7,8,128]{3,2,1,0:T(8,128)S(1)}, f32[1,7,8,128]{3,2,1,0:T(8,128)S(1)}, u32[]{:S(2)}, u32[]{:S(2)}) collective-permute-start(f32[1,7,8,128]{3,2,1,0:T(8,128)S(1)} %get-tuple-element.61), channel_id=1, source_target_pairs={{0,32},{32,0},{64,96},{96,64},{128,160},{160,128},{192,224},{224,1... | collective-permute-start | bytes 86024 | tf_op jit(solution)/shard_map/ppermute | solution.py:610
  73.9 3.0 %collective-permute-done.9.near_x_ref = f32[1,7,8,128]{3,2,1,0:T(8,128)S(1)} collective-permute-done((f32[1,7,8,128]{3,2,1,0:T(8,128)S(1)}, f32[1,7,8,128]{3,2,1,0:T(8,128)S(1)}, u32[]{:S(2)}, u32[]{:S(2)}) %collective-permute-start.9) | collective-permute-done | bytes 28704 | tf_op jit(solution)/shard_map/ppermute | solution.py:610
  76.9 3.7 %all-to-all-done.got_ref = f32[32,8,128]{2,1,0:T(8,128)S(1)} async-done(((f32[32,8,128]{2,1,0:T(8,128)}), f32[32,8,128]{2,1,0:T(8,128)S(1)}, u32[]{:S(2)}, u32[]{:S(2)}) %all-to-all-start) | async-done | bytes 131104 | tf_op jit(solution)/shard_map/all_to_all | solution.py:666
  80.7 0.7 middle.1
  81.4 5.2 %all-to-all-start.1 = ((f32[16,8,128]{2,1,0:T(8,128)}), f32[16,8,128]{2,1,0:T(8,128)S(1)}, u32[]{:S(2)}, u32[]{:S(2)}) async-start(f32[16,8,128]{2,1,0:T(8,128)} %get-tuple-element.67), calls=%async_computation.1 | async-start | bytes 131072 | tf_op jit(solution)/shard_map/all_to_all | solution.py:672
  86.6 9.3 %collective-permute-start.8 = (f32[1,7,8,128]{3,2,1,0:T(8,128)S(1)}, f32[1,7,8,128]{3,2,1,0:T(8,128)S(1)}, u32[]{:S(2)}, u32[]{:S(2)}) collective-permute-start(f32[1,7,8,128]{3,2,1,0:T(8,128)S(1)} %get-tuple-element.59), channel_id=1, source_target_pairs={{0,480},{32,64},{64,32},{96,128},{128,96},{160,192},{192,160},{224... | collective-permute-start | bytes 86024 | tf_op jit(solution)/shard_map/ppermute | solution.py:610
  95.9 2.0 %collective-permute-done.8.far_x_ref = f32[1,7,8,128]{3,2,1,0:T(8,128)S(1)} collective-permute-done((f32[1,7,8,128]{3,2,1,0:T(8,128)S(1)}, f32[1,7,8,128]{3,2,1,0:T(8,128)S(1)}, u32[]{:S(2)}, u32[]{:S(2)}) %collective-permute-start.8) | collective-permute-done | bytes 28704 | tf_op jit(solution)/shard_map/ppermute | solution.py:610
  97.9 0.0 all-to-all-done.1.dots_ref
  97.9 0.0 copy-done.1
  97.9 1.1 %finish.1 = (f32[218,128]{1,0:T(8,128)}, f32[218,128]{1,0:T(8,128)}) custom-call(f32[1,7,7,8,128]{4,3,2,1,0:T(8,128)S(1)} %get-tuple-element.58.part_ref, f32[1,7,8,128]{3,2,1,0:T(8,128)S(1)} %collective-permute-done.8.far_x_ref, f32[1,7,8,128]{3,2,1,0:T(8,128)S(1)} %collective-permute-done.9.near_x_ref, f32[7,8,128]{2,1,0:T(8,128)S(1)} %get-tuple-element.64.low_ref, ...), custom_call_target="tpu_custom_call" | custom-call | tf_op jit(solution)/shard_map/finish/pallas_call | solution.py:588
Async XLA Ops:
  4.2 18.7 %collective-permute-start = (f32[3,7,8,128]{3,2,1,0:T(8,128)S(1)}, f32[3,7,8,128]{3,2,1,0:T(8,128)S(1)}, u32[]{:S(2)}, u32[]{:S(2)}) collective-permute-start(f32[3,7,8,128]{3,2,1,0:T(8,128)S(1)} %get-tuple-element.37), channel_id=1, source_target_pairs={{0,480},{32,64},{64,32},{96,128},{128,96},{160,192},{192,160},{224... | collective-permute-start | bytes 258056 | tf_op jit(solution)/shard_map/ppermute | solution.py:610
  18.6 5.2 %collective-permute-start.1 = (f32[3,7,8,128]{3,2,1,0:T(8,128)S(1)}, f32[3,7,8,128]{3,2,1,0:T(8,128)S(1)}, u32[]{:S(2)}, u32[]{:S(2)}) collective-permute-start(f32[3,7,8,128]{3,2,1,0:T(8,128)S(1)} %get-tuple-element.38), channel_id=1, source_target_pairs={{0,32},{32,0},{64,96},{96,64},{128,160},{160,128},{192,224},{224,1... | collective-permute-start | bytes 258056 | tf_op jit(solution)/shard_map/ppermute | solution.py:610
  24.7 9.4 %collective-permute-start.2 = (f32[2,7,8,128]{3,2,1,0:T(8,128)S(1)}, f32[2,7,8,128]{3,2,1,0:T(8,128)S(1)}, u32[]{:S(2)}, u32[]{:S(2)}) collective-permute-start(f32[2,7,8,128]{3,2,1,0:T(8,128)S(1)} %get-tuple-element.42), channel_id=1, source_target_pairs={{0,31},{1,2},{2,1},{3,4},{4,3},{5,6},{6,5},{7,8},{8,7},{9,10},{10,... | collective-permute-start | bytes 172040 | tf_op jit(solution)/shard_map/ppermute | solution.py:610
  29.8 5.2 %collective-permute-start.3 = (f32[2,7,8,128]{3,2,1,0:T(8,128)S(1)}, f32[2,7,8,128]{3,2,1,0:T(8,128)S(1)}, u32[]{:S(2)}, u32[]{:S(2)}) collective-permute-start(f32[2,7,8,128]{3,2,1,0:T(8,128)S(1)} %get-tuple-element.43), channel_id=1, source_target_pairs={{0,1},{1,0},{2,3},{3,2},{4,5},{5,4},{6,7},{7,6},{8,9},{9,8},{10,11... | collective-permute-start | bytes 172040 | tf_op jit(solution)/shard_map/ppermute | solution.py:610
  36.4 11.5 %collective-permute-start.4 = (f32[2,7,8,128]{3,2,1,0:T(8,128)S(1)}, f32[2,7,8,128]{3,2,1,0:T(8,128)S(1)}, u32[]{:S(2)}, u32[]{:S(2)}) collective-permute-start(f32[2,7,8,128]{3,2,1,0:T(8,128)S(1)} %get-tuple-element.48), channel_id=1, source_target_pairs={{0,480},{32,64},{64,32},{96,128},{128,96},{160,192},{192,160},{224... | collective-permute-start | bytes 172040 | tf_op jit(solution)/shard_map/ppermute | solution.py:610
  42.6 5.2 %collective-permute-start.5 = (f32[2,7,8,128]{3,2,1,0:T(8,128)S(1)}, f32[2,7,8,128]{3,2,1,0:T(8,128)S(1)}, u32[]{:S(2)}, u32[]{:S(2)}) collective-permute-start(f32[2,7,8,128]{3,2,1,0:T(8,128)S(1)} %get-tuple-element.49), channel_id=1, source_target_pairs={{0,32},{32,0},{64,96},{96,64},{128,160},{160,128},{192,224},{224,1... | collective-permute-start | bytes 172040 | tf_op jit(solution)/shard_map/ppermute | solution.py:610
  47.8 13.5 %copy-start = (f32[224,128]{1,0:T(8,128)S(1)}, f32[224,128]{1,0:T(8,128)}, u32[]{:S(2)}) copy-start(f32[224,128]{1,0:T(8,128)} %constant.2.clone.shell_ref) | copy-start | bytes 344068
  50.5 10.9 %collective-permute-start.6 = (f32[1,7,8,128]{3,2,1,0:T(8,128)S(1)}, f32[1,7,8,128]{3,2,1,0:T(8,128)S(1)}, u32[]{:S(2)}, u32[]{:S(2)}) collective-permute-start(f32[1,7,8,128]{3,2,1,0:T(8,128)S(1)} %get-tuple-element.54), channel_id=1, source_target_pairs={{0,480},{32,64},{64,32},{96,128},{128,96},{160,192},{192,160},{224... | collective-permute-start | bytes 86024 | tf_op jit(solution)/shard_map/ppermute | solution.py:610
  56.7 4.7 %collective-permute-start.7 = (f32[1,7,8,128]{3,2,1,0:T(8,128)S(1)}, f32[1,7,8,128]{3,2,1,0:T(8,128)S(1)}, u32[]{:S(2)}, u32[]{:S(2)}) collective-permute-start(f32[1,7,8,128]{3,2,1,0:T(8,128)S(1)} %get-tuple-element.55), channel_id=1, source_target_pairs={{0,32},{32,0},{64,96},{96,64},{128,160},{160,128},{192,224},{224,1... | collective-permute-start | bytes 86024 | tf_op jit(solution)/shard_map/ppermute | solution.py:610
  61.4 36.5 %copy-start.1 = (s32[1,1,128]{2,1,0:T(1,128)S(1)}, s32[1,1,128]{2,1,0:T(1,128)}, u32[]{:S(2)}) copy-start(s32[1,1,128]{2,1,0:T(1,128)} %param.6) | copy-start | bytes 1540
  64.1 16.5 %all-to-all-start = ((f32[32,8,128]{2,1,0:T(8,128)}), f32[32,8,128]{2,1,0:T(8,128)S(1)}, u32[]{:S(2)}, u32[]{:S(2)}) async-start(f32[32,8,128]{2,1,0:T(8,128)} %get-tuple-element.60), calls=%async_computation | async-start | bytes 262144 | tf_op jit(solution)/shard_map/all_to_all | solution.py:666
  72.0 4.9 %collective-permute-start.9 = (f32[1,7,8,128]{3,2,1,0:T(8,128)S(1)}, f32[1,7,8,128]{3,2,1,0:T(8,128)S(1)}, u32[]{:S(2)}, u32[]{:S(2)}) collective-permute-start(f32[1,7,8,128]{3,2,1,0:T(8,128)S(1)} %get-tuple-element.61), channel_id=1, source_target_pairs={{0,32},{32,0},{64,96},{96,64},{128,160},{160,128},{192,224},{224,1... | collective-permute-start | bytes 86024 | tf_op jit(solution)/shard_map/ppermute | solution.py:610
  81.4 16.5 %all-to-all-start.1 = ((f32[16,8,128]{2,1,0:T(8,128)}), f32[16,8,128]{2,1,0:T(8,128)S(1)}, u32[]{:S(2)}, u32[]{:S(2)}) async-start(f32[16,8,128]{2,1,0:T(8,128)} %get-tuple-element.67), calls=%async_computation.1 | async-start | bytes 131072 | tf_op jit(solution)/shard_map/all_to_all | solution.py:672
  86.6 11.3 %collective-permute-start.8 = (f32[1,7,8,128]{3,2,1,0:T(8,128)S(1)}, f32[1,7,8,128]{3,2,1,0:T(8,128)S(1)}, u32[]{:S(2)}, u32[]{:S(2)}) collective-permute-start(f32[1,7,8,128]{3,2,1,0:T(8,128)S(1)} %get-tuple-element.59), channel_id=1, source_target_pairs={{0,480},{32,64},{64,32},{96,128},{128,96},{160,192},{192,160},{224... | collective-permute-start | bytes 86024 | tf_op jit(solution)/shard_map/ppermute | solution.py:610

commit v8 on v7

--- a/solution.py
+++ b/solution.py
@@ -514,32 +514,41 @@
     for k, value in enumerate(values):
         dots = dots + jnp.where(lane == k, total_of(value), 0.0)
     node = lax.broadcasted_iota(jnp.int32, (8, LANES), 0)
-    count = send_ref.shape[0]
+    count = send_ref.shape[0] // 2
     mine = lax.axis_index("dom")
     alone = jnp.where(node == 7, dots, 0.0)
     send_ref[...] = jnp.broadcast_to(alone[None], send_ref.shape)
     up = pack_groups([out_ref[0, a, 6] for a in range(7)], LANES - BZ)
     down = pack_groups([out_ref[0, a, 0] for a in range(7)], 0)
-    send_ref[lax.rem(mine + 1, count)] = jnp.where(node == 7, dots, up)
-    send_ref[lax.rem(mine + count - 1, count)] = jnp.where(node == 7, dots, down)
+    for half in range(2):
+        send_ref[half * count + lax.rem(mine + 1, count)] = jnp.where(node == 7, dots, up)
+        send_ref[half * count + lax.rem(mine + count - 1, count)] = jnp.where(node == 7, dots, down)
 
 
 def middle_kernel(got_ref, low_ref, high_ref, send_ref):
     node = lax.broadcasted_iota(jnp.int32, (8, LANES), 0)
     _, by, _ = iotas((8, LANES))
-    count = got_ref.shape[0]
+    count, run = got_ref.shape[0] // 2, send_ref.shape[0]
     mine = lax.axis_index("dom")
-    low = jnp.where(node < 7, got_ref[lax.rem(mine + count - 1, count)], 0.0)
-    high = jnp.where(node < 7, got_ref[lax.rem(mine + 1, count)], 0.0)
+    slab = lax.axis_index("slab")
+    half, place = slab // run, lax.rem(slab, run)
+
+    def faces(which):
+        return tuple(
+            jnp.where(node < 7, got_ref[which * count + lax.rem(mine + step, count)], 0.0)
+            for step in (count - 1, 1)
+        )
+
+    low, high = faces(half)
     for a in range(7):
         low_ref[a], high_ref[a] = lanes_from(low, a, 0), lanes_from(high, a, LANES - BZ)
     total = jnp.sum(got_ref[...], axis=0)[7:8]
     send_ref[...] = jnp.broadcast_to(jnp.where(node == 7, total, 0.0)[None], send_ref.shape)
-    slabs = send_ref.shape[0]
-    place = lax.axis_index("slab")
-    for a, step in ((6, 1), (0, slabs - 1)):
-        edges = jnp.where(by == 0, low_ref[a], jnp.where(by == BY - 1, high_ref[a], 0.0))
-        send_ref[lax.rem(place + step, slabs)] = jnp.where(node == 7, total, edges)
+    for a, step, end in ((6, 1, run - 1), (0, run - 1, 0)):
+        low, high = faces(jnp.where(place == end, 1 - half, half))
+        low, high = lanes_from(low, a, 0), lanes_from(high, a, LANES - BZ)
+        edges = jnp.where(by == 0, low, jnp.where(by == BY - 1, high, 0.0))
+        send_ref[lax.rem(place + step, run)] = jnp.where(node == 7, total, edges)
 
 
 def finish_kernel(
@@ -547,13 +556,13 @@
     pressure_ref, residual_ref, full_ref, modes_ref,
 ):
     node = lax.broadcasted_iota(jnp.int32, (8, LANES), 0)
-    slabs = dots_ref.shape[0]
-    place = lax.axis_index("slab")
+    run = dots_ref.shape[0]
+    place = lax.rem(lax.axis_index("slab"), run)
     for a in range(7):
         sheet = add_streamwise(a, part_ref[0, a], far_x_ref[0], near_x_ref[0])
         sheet = add_second(sheet, low_ref[a], high_ref[a])
         if a in (0, 6):
-            edges = dots_ref[lax.rem(place + (slabs - 1 if a == 0 else 1), slabs)]
+            edges = dots_ref[lax.rem(place + (run - 1 if a == 0 else 1), run)]
             edges = jnp.where(node < 7, edges, 0.0)
             sheet = add_second(sheet, edges, edges)
         full_ref[56 * a : 56 * a + 56] = sheet.reshape(56, LANES)
@@ -655,21 +664,25 @@
         [(392, LANES), (392, LANES), modes, (2, *face), rights[0], rights[0]],
         name="first",
     )
-    slabs, doms = lax.axis_size("slab"), lax.axis_size("dom")
+    run, doms = lax.axis_size("slab") // 2, lax.axis_size("dom")
+    rings = [[doms * run * half + doms * k + d for k in range(run)] for half in range(2) for d in range(doms)]
+    sheets = [
+        [doms * (run * half + k) + d for half in range(2) for d in range(doms)] for k in range(run)
+    ]
     power, send, part, far, near = call(
         second_apply_kernel,
-        [modes, (doms, 8, LANES), (1, *whole), (1, *face), (1, *face)],
+        [modes, (2 * doms, 8, LANES), (1, *whole), (1, *face), (1, *face)],
         (part, *swap("slab", far, near), split_0, split_1, classes, load, first, shell),
         [modes, (392, LANES), *rights],
         name="second",
     )
-    got = lax.all_to_all(send, "dom", 0, 0)
+    got = lax.all_to_all(send, ("slab", "dom"), 0, 0, axis_index_groups=sheets)
     far_x, near_x = swap("slab", far, near)
-    got, near_x = lax.optimization_barrier((got, near_x))
+    got, far_x = lax.optimization_barrier((got, far_x))
     low, high, send = call(
-        middle_kernel, [face, face, (slabs, 8, LANES)], (got,), name="middle"
-    )
-    dots = lax.all_to_all(send, "slab", 0, 0)
+        middle_kernel, [face, face, (run, 8, LANES)], (got,), name="middle"
+    )
+    dots = lax.all_to_all(send, ("slab", "dom"), 0, 0, axis_index_groups=rings)
     return call(
         finish_kernel,
         [(MODES, LANES), (MODES, LANES)],

time: 99.6 us -> 100 us (level)
    all_to_all x2, waiting for transfers between devices: 3.75 us -> 5.48 us  [the longest x1 3.63 us: per_device(): got = lax.all_to_all(send, ('slab', 'dom'), 0, 0, axis_index_groups=sheets)]
    ppermute x5, starting transfers between devices: 12 us -> 13.4 us  [swap(): lax.ppermute(near, axis, near_pairs)]
    all_to_all x2, starting transfers between devices: 13.1 us -> 11.8 us  [the longest x1 8.42 us: per_device(): got = lax.all_to_all(send, ('slab', 'dom'), 0, 0, axis_index_groups=sheets)]
    ppermute x5, waiting for transfers between devices: 4.74 us -> 3.66 us  [swap(): lax.ppermute(near, axis, near_pairs)]
  transfers between devices with their start and end apart: 12 -> 12, of which waited for: 7 -> 8; matrix products, arithmetic and copies ran while one was open for 0% -> 0% of each run, Pallas kernels for 5% -> 5%
where the time goes in v8:
time: 100 us; the launch traced here: 99.4 us
  starting transfers between devices  66.3 us (66%)
  Pallas kernels  17.9 us (18%)
  waiting for transfers between devices  14.5 us (14%)
    ppermute x5, starting transfers between devices, swap(): lax.ppermute(far, axis, far_pairs)  41.1 us
    pallas_call x9, Pallas kernels, call(): pl.pallas_call(kernel, out_shape=tuple((jax.ShapeDtypeStruct(*(o if isins...  17.9 us
    ppermute x5, starting transfers between devices, swap(): lax.ppermute(near, axis, near_pairs)  13.4 us
    all_to_all x1, starting transfers between devices, per_device(): got = lax.all_to_all(send, ('slab', 'dom'), 0, 0, axis_index_groups=sheets)  8.42 us
    ppermute x5, waiting for transfers between devices, swap(): lax.ppermute(far, axis, far_pairs)  5.33 us
    ppermute x5, waiting for transfers between devices, swap(): lax.ppermute(near, axis, near_pairs)  3.66 us
    all_to_all x1, waiting for transfers between devices, per_device(): got = lax.all_to_all(send, ('slab', 'dom'), 0, 0, axis_index_groups=sheets)  3.63 us
    all_to_all x1, starting transfers between devices, per_device(): dots = lax.all_to_all(send, ('slab', 'dom'), 0, 0, axis_index_groups=rings)  3.38 us
  transfers between devices with their start and end apart: 12, of which 8 were waited for; matrix products, arithmetic and copies ran while one was open for 0% of the time, Pallas kernels for 5%

profile of v8, /device:TPU:1, one launch (start us, length us, event | category | flops | bytes accessed | tf_op | source)
XLA Modules:
  0.0 99.4 jit_solution(6964655913482681582)
XLA Ops:
  0.6 3.6 %advect.1 = (f32[3,7,7,8,128]{4,3,2,1,0:T(8,128)S(1)}, f32[3,7,7,8,128]{4,3,2,1,0:T(8,128)S(1)}, f32[3,7,8,128]{3,2,1,0:T(8,128)S(1)}, f32[3,7,8,128]{3,2,1,0:T(8,128)S(1)}, f32[8,128]{1,0:T(8,128)S(1)}) custom-call(f32[3,343,128]{2,1,0:T(8,128)} %vel_hbm.1, s32[1,128]{1,0:T(1,128)} %bitcast.3, s32[1,128]{1,0:T(1,128)} %bitcast.7), custom_call_target="tpu_custom_call" | custom-call | tf_op jit(solution)/shard_map/advect/pallas_call | solution.py:597
  4.2 14.4 %collective-permute-start = (f32[3,7,8,128]{3,2,1,0:T(8,128)S(1)}, f32[3,7,8,128]{3,2,1,0:T(8,128)S(1)}, u32[]{:S(2)}, u32[]{:S(2)}) collective-permute-start(f32[3,7,8,128]{3,2,1,0:T(8,128)S(1)} %get-tuple-element.37), channel_id=1, source_target_pairs={{0,480},{32,64},{64,32},{96,128},{128,96},{160,192},{192,160},{224... | collective-permute-start | bytes 258056 | tf_op jit(solution)/shard_map/ppermute | solution.py:619
  18.6 1.9 %collective-permute-start.1 = (f32[3,7,8,128]{3,2,1,0:T(8,128)S(1)}, f32[3,7,8,128]{3,2,1,0:T(8,128)S(1)}, u32[]{:S(2)}, u32[]{:S(2)}) collective-permute-start(f32[3,7,8,128]{3,2,1,0:T(8,128)S(1)} %get-tuple-element.38), channel_id=1, source_target_pairs={{0,32},{32,0},{64,96},{96,64},{128,160},{160,128},{192,224},{224,1... | collective-permute-start | bytes 258056 | tf_op jit(solution)/shard_map/ppermute | solution.py:619
  20.5 2.4 %split.2.split_0 = bf16[448,2048]{1,0:T(8,128)(2,1)S(1)} custom-call(f32[218,16,218]{2,1,0:T(8,128)} %bitcast.5), custom_call_target="tpu_custom_call" | custom-call | tf_op jit(solution)/shard_map/split/pallas_call | solution.py:597
  22.9 0.0 collective-permute-done.far_x_ref
  22.9 0.9 collective-permute-done.1.near_x_ref
  23.8 0.9 source.1
  24.7 5.1 %collective-permute-start.2 = (f32[2,7,8,128]{3,2,1,0:T(8,128)S(1)}, f32[2,7,8,128]{3,2,1,0:T(8,128)S(1)}, u32[]{:S(2)}, u32[]{:S(2)}) collective-permute-start(f32[2,7,8,128]{3,2,1,0:T(8,128)S(1)} %get-tuple-element.42), channel_id=1, source_target_pairs={{0,31},{1,2},{2,1},{3,4},{4,3},{5,6},{6,5},{7,8},{8,7},{9,10},{10,... | collective-permute-start | bytes 172040 | tf_op jit(solution)/shard_map/ppermute | solution.py:619
  29.8 4.3 %collective-permute-start.3 = (f32[2,7,8,128]{3,2,1,0:T(8,128)S(1)}, f32[2,7,8,128]{3,2,1,0:T(8,128)S(1)}, u32[]{:S(2)}, u32[]{:S(2)}) collective-permute-start(f32[2,7,8,128]{3,2,1,0:T(8,128)S(1)} %get-tuple-element.43), channel_id=1, source_target_pairs={{0,1},{1,0},{2,3},{3,2},{4,5},{5,4},{6,7},{7,6},{8,9},{9,8},{10,11... | collective-permute-start | bytes 172040 | tf_op jit(solution)/shard_map/ppermute | solution.py:619
  34.2 0.0 collective-permute-done.2.far_y_ref
  34.2 0.9 collective-permute-done.3.near_y_ref
  35.0 1.3 %correct.1 = (f32[2,7,7,8,128]{4,3,2,1,0:T(8,128)S(1)}, f32[2,7,8,128]{3,2,1,0:T(8,128)S(1)}, f32[2,7,8,128]{3,2,1,0:T(8,128)S(1)}, f32[8,128]{1,0:T(8,128)S(1)}) custom-call(f32[1,7,7,8,128]{4,3,2,1,0:T(8,128)S(1)} %get-tuple-element.41.part_ref, f32[2,7,8,128]{3,2,1,0:T(8,128)S(1)} %collective-permute-done.2.far_y_ref, ...), custom_call_target="tpu_custom_call" | custom-call | tf_op jit(solution)/shard_map/correct/pallas_call | solution.py:597
  36.4 6.3 %collective-permute-start.4 = (f32[2,7,8,128]{3,2,1,0:T(8,128)S(1)}, f32[2,7,8,128]{3,2,1,0:T(8,128)S(1)}, u32[]{:S(2)}, u32[]{:S(2)}) collective-permute-start(f32[2,7,8,128]{3,2,1,0:T(8,128)S(1)} %get-tuple-element.48), channel_id=1, source_target_pairs={{0,480},{32,64},{64,32},{96,128},{128,96},{160,192},{192,160},{224... | collective-permute-start | bytes 172040 | tf_op jit(solution)/shard_map/ppermute | solution.py:619
  42.6 1.9 %collective-permute-start.5 = (f32[2,7,8,128]{3,2,1,0:T(8,128)S(1)}, f32[2,7,8,128]{3,2,1,0:T(8,128)S(1)}, u32[]{:S(2)}, u32[]{:S(2)}) collective-permute-start(f32[2,7,8,128]{3,2,1,0:T(8,128)S(1)} %get-tuple-element.49), channel_id=1, source_target_pairs={{0,32},{32,0},{64,96},{96,64},{128,160},{160,128},{192,224},{224,1... | collective-permute-start | bytes 172040 | tf_op jit(solution)/shard_map/ppermute | solution.py:619
  44.5 2.4 %split.3.split_1 = bf16[448,2048]{1,0:T(8,128)(2,1)S(1)} custom-call(f32[218,16,218]{2,1,0:T(8,128)} %bitcast.6), custom_call_target="tpu_custom_call" | custom-call | tf_op jit(solution)/shard_map/split/pallas_call | solution.py:597
  46.9 0.9 collective-permute-done.4.far_x_ref
  47.8 0.0 collective-permute-done.5.near_x_ref
  47.8 0.0 copy-start
  47.8 2.7 %first.1 = (f32[224,128]{1,0:T(8,128)S(1)}, f32[224,128]{1,0:T(8,128)S(1)}, f32[1,7,7,8,128]{4,3,2,1,0:T(8,128)S(1)}, f32[1,7,8,128]{3,2,1,0:T(8,128)S(1)}, f32[1,7,8,128]{3,2,1,0:T(8,128)S(1)}) custom-call(f32[2,7,7,8,128]{4,3,2,1,0:T(8,128)S(1)} %get-tuple-element.47.part_ref, f32[2,7,8,128]{3,2,1,0:T(8,128)S(1)} %collective-permute-done.4.far_x_ref, ...), custom_call_target="tpu_custom_call" | custom-call | tf_op jit(solution)/shard_map/first/pallas_call | solution.py:597
  50.5 6.2 %collective-permute-start.6 = (f32[1,7,8,128]{3,2,1,0:T(8,128)S(1)}, f32[1,7,8,128]{3,2,1,0:T(8,128)S(1)}, u32[]{:S(2)}, u32[]{:S(2)}) collective-permute-start(f32[1,7,8,128]{3,2,1,0:T(8,128)S(1)} %get-tuple-element.54), channel_id=1, source_target_pairs={{0,480},{32,64},{64,32},{96,128},{128,96},{160,192},{192,160},{224... | collective-permute-start | bytes 86024 | tf_op jit(solution)/shard_map/ppermute | solution.py:619
  56.7 1.9 %collective-permute-start.7 = (f32[1,7,8,128]{3,2,1,0:T(8,128)S(1)}, f32[1,7,8,128]{3,2,1,0:T(8,128)S(1)}, u32[]{:S(2)}, u32[]{:S(2)}) collective-permute-start(f32[1,7,8,128]{3,2,1,0:T(8,128)S(1)} %get-tuple-element.55), channel_id=1, source_target_pairs={{0,32},{32,0},{64,96},{96,64},{128,160},{160,128},{192,224},{224,1... | collective-permute-start | bytes 86024 | tf_op jit(solution)/shard_map/ppermute | solution.py:619
  58.6 2.8 %collective-permute-done.6.far_x_ref = f32[1,7,8,128]{3,2,1,0:T(8,128)S(1)} collective-permute-done((f32[1,7,8,128]{3,2,1,0:T(8,128)S(1)}, f32[1,7,8,128]{3,2,1,0:T(8,128)S(1)}, u32[]{:S(2)}, u32[]{:S(2)}) %collective-permute-start.6) | collective-permute-done | bytes 28704 | tf_op jit(solution)/shard_map/ppermute | solution.py:619
  61.4 0.0 collective-permute-done.7.near_x_ref
  61.4 0.0 copy-done
  61.4 0.0 copy-start.1
  61.4 2.8 %second.1 = (f32[224,128]{1,0:T(8,128)S(1)}, f32[64,8,128]{2,1,0:T(8,128)}, f32[1,7,7,8,128]{4,3,2,1,0:T(8,128)S(1)}, f32[1,7,8,128]{3,2,1,0:T(8,128)S(1)}, f32[1,7,8,128]{3,2,1,0:T(8,128)S(1)}) custom-call(f32[1,7,7,8,128]{4,3,2,1,0:T(8,128)S(1)} %get-tuple-element.53.part_ref, f32[1,7,8,128]{3,2,1,0:T(8,128)S(1)} %collective-permute-done.6.far_x_ref, ...), custom_call_target="tpu_custom_call" | custom-call | tf_op jit(solution)/shard_map/second/pallas_call | solution.py:597
  64.2 8.4 %all-to-all-start = ((f32[64,8,128]{2,1,0:T(8,128)}), f32[64,8,128]{2,1,0:T(8,128)S(1)}, u32[]{:S(2)}, u32[]{:S(2)}) async-start(f32[64,8,128]{2,1,0:T(8,128)} %get-tuple-element.59), calls=%async_computation | async-start | bytes 524288 | tf_op jit(solution)/shard_map/all_to_all | solution.py:679
  72.6 9.2 %collective-permute-start.8 = (f32[1,7,8,128]{3,2,1,0:T(8,128)S(1)}, f32[1,7,8,128]{3,2,1,0:T(8,128)S(1)}, u32[]{:S(2)}, u32[]{:S(2)}) collective-permute-start(f32[1,7,8,128]{3,2,1,0:T(8,128)S(1)} %get-tuple-element.60), channel_id=1, source_target_pairs={{0,480},{32,64},{64,32},{96,128},{128,96},{160,192},{192,160},{224... | collective-permute-start | bytes 86024 | tf_op jit(solution)/shard_map/ppermute | solution.py:619
  81.8 1.7 %collective-permute-done.8.far_x_ref = f32[1,7,8,128]{3,2,1,0:T(8,128)S(1)} collective-permute-done((f32[1,7,8,128]{3,2,1,0:T(8,128)S(1)}, f32[1,7,8,128]{3,2,1,0:T(8,128)S(1)}, u32[]{:S(2)}, u32[]{:S(2)}) %collective-permute-start.8) | collective-permute-done | bytes 28704 | tf_op jit(solution)/shard_map/ppermute | solution.py:619
  83.5 3.6 %all-to-all-done.got_ref = f32[64,8,128]{2,1,0:T(8,128)S(1)} async-done(((f32[64,8,128]{2,1,0:T(8,128)}), f32[64,8,128]{2,1,0:T(8,128)S(1)}, u32[]{:S(2)}, u32[]{:S(2)}) %all-to-all-start) | async-done | bytes 262176 | tf_op jit(solution)/shard_map/all_to_all | solution.py:679
  87.1 0.7 middle.1
  87.8 3.4 %all-to-all-start.1 = ((f32[8,8,128]{2,1,0:T(8,128)}), f32[8,8,128]{2,1,0:T(8,128)S(1)}, u32[]{:S(2)}, u32[]{:S(2)}) async-start(f32[8,8,128]{2,1,0:T(8,128)} %get-tuple-element.67), calls=%async_computation.1 | async-start | bytes 65536 | tf_op jit(solution)/shard_map/all_to_all | solution.py:685
  91.2 3.4 %collective-permute-start.9 = (f32[1,7,8,128]{3,2,1,0:T(8,128)S(1)}, f32[1,7,8,128]{3,2,1,0:T(8,128)S(1)}, u32[]{:S(2)}, u32[]{:S(2)}) collective-permute-start(f32[1,7,8,128]{3,2,1,0:T(8,128)S(1)} %get-tuple-element.62), channel_id=1, source_target_pairs={{0,32},{32,0},{64,96},{96,64},{128,160},{160,128},{192,224},{224,1... | collective-permute-start | bytes 86024 | tf_op jit(solution)/shard_map/ppermute | solution.py:619
  94.6 1.9 %collective-permute-done.9.near_x_ref = f32[1,7,8,128]{3,2,1,0:T(8,128)S(1)} collective-permute-done((f32[1,7,8,128]{3,2,1,0:T(8,128)S(1)}, f32[1,7,8,128]{3,2,1,0:T(8,128)S(1)}, u32[]{:S(2)}, u32[]{:S(2)}) %collective-permute-start.9) | collective-permute-done | bytes 28704 | tf_op jit(solution)/shard_map/ppermute | solution.py:619
  96.5 1.9 %all-to-all-done.1.dots_ref = f32[8,8,128]{2,1,0:T(8,128)S(1)} async-done(((f32[8,8,128]{2,1,0:T(8,128)}), f32[8,8,128]{2,1,0:T(8,128)S(1)}, u32[]{:S(2)}, u32[]{:S(2)}) %all-to-all-start.1) | async-done | bytes 32800 | tf_op jit(solution)/shard_map/all_to_all | solution.py:685
  98.3 0.0 copy-done.1
  98.3 1.1 %finish.1 = (f32[218,128]{1,0:T(8,128)}, f32[218,128]{1,0:T(8,128)}) custom-call(f32[1,7,7,8,128]{4,3,2,1,0:T(8,128)S(1)} %get-tuple-element.58.part_ref, f32[1,7,8,128]{3,2,1,0:T(8,128)S(1)} %collective-permute-done.8.far_x_ref, f32[1,7,8,128]{3,2,1,0:T(8,128)S(1)} %collective-permute-done.9.near_x_ref, f32[7,8,128]{2,1,0:T(8,128)S(1)} %get-tuple-element.64.low_ref, ...), custom_call_target="tpu_custom_call" | custom-call | tf_op jit(solution)/shard_map/finish/pallas_call | solution.py:597
Async XLA Ops:
  4.2 18.7 %collective-permute-start = (f32[3,7,8,128]{3,2,1,0:T(8,128)S(1)}, f32[3,7,8,128]{3,2,1,0:T(8,128)S(1)}, u32[]{:S(2)}, u32[]{:S(2)}) collective-permute-start(f32[3,7,8,128]{3,2,1,0:T(8,128)S(1)} %get-tuple-element.37), channel_id=1, source_target_pairs={{0,480},{32,64},{64,32},{96,128},{128,96},{160,192},{192,160},{224... | collective-permute-start | bytes 258056 | tf_op jit(solution)/shard_map/ppermute | solution.py:619
  18.6 5.2 %collective-permute-start.1 = (f32[3,7,8,128]{3,2,1,0:T(8,128)S(1)}, f32[3,7,8,128]{3,2,1,0:T(8,128)S(1)}, u32[]{:S(2)}, u32[]{:S(2)}) collective-permute-start(f32[3,7,8,128]{3,2,1,0:T(8,128)S(1)} %get-tuple-element.38), channel_id=1, source_target_pairs={{0,32},{32,0},{64,96},{96,64},{128,160},{160,128},{192,224},{224,1... | collective-permute-start | bytes 258056 | tf_op jit(solution)/shard_map/ppermute | solution.py:619
  24.7 9.4 %collective-permute-start.2 = (f32[2,7,8,128]{3,2,1,0:T(8,128)S(1)}, f32[2,7,8,128]{3,2,1,0:T(8,128)S(1)}, u32[]{:S(2)}, u32[]{:S(2)}) collective-permute-start(f32[2,7,8,128]{3,2,1,0:T(8,128)S(1)} %get-tuple-element.42), channel_id=1, source_target_pairs={{0,31},{1,2},{2,1},{3,4},{4,3},{5,6},{6,5},{7,8},{8,7},{9,10},{10,... | collective-permute-start | bytes 172040 | tf_op jit(solution)/shard_map/ppermute | solution.py:619
  29.8 5.2 %collective-permute-start.3 = (f32[2,7,8,128]{3,2,1,0:T(8,128)S(1)}, f32[2,7,8,128]{3,2,1,0:T(8,128)S(1)}, u32[]{:S(2)}, u32[]{:S(2)}) collective-permute-start(f32[2,7,8,128]{3,2,1,0:T(8,128)S(1)} %get-tuple-element.43), channel_id=1, source_target_pairs={{0,1},{1,0},{2,3},{3,2},{4,5},{5,4},{6,7},{7,6},{8,9},{9,8},{10,11... | collective-permute-start | bytes 172040 | tf_op jit(solution)/shard_map/ppermute | solution.py:619
  36.4 11.5 %collective-permute-start.4 = (f32[2,7,8,128]{3,2,1,0:T(8,128)S(1)}, f32[2,7,8,128]{3,2,1,0:T(8,128)S(1)}, u32[]{:S(2)}, u32[]{:S(2)}) collective-permute-start(f32[2,7,8,128]{3,2,1,0:T(8,128)S(1)} %get-tuple-element.48), channel_id=1, source_target_pairs={{0,480},{32,64},{64,32},{96,128},{128,96},{160,192},{192,160},{224... | collective-permute-start | bytes 172040 | tf_op jit(solution)/shard_map/ppermute | solution.py:619
  42.6 5.2 %collective-permute-start.5 = (f32[2,7,8,128]{3,2,1,0:T(8,128)S(1)}, f32[2,7,8,128]{3,2,1,0:T(8,128)S(1)}, u32[]{:S(2)}, u32[]{:S(2)}) collective-permute-start(f32[2,7,8,128]{3,2,1,0:T(8,128)S(1)} %get-tuple-element.49), channel_id=1, source_target_pairs={{0,32},{32,0},{64,96},{96,64},{128,160},{160,128},{192,224},{224,1... | collective-permute-start | bytes 172040 | tf_op jit(solution)/shard_map/ppermute | solution.py:619
  47.8 13.5 %copy-start = (f32[224,128]{1,0:T(8,128)S(1)}, f32[224,128]{1,0:T(8,128)}, u32[]{:S(2)}) copy-start(f32[224,128]{1,0:T(8,128)} %constant.2.clone.shell_ref) | copy-start | bytes 344068
  50.5 10.9 %collective-permute-start.6 = (f32[1,7,8,128]{3,2,1,0:T(8,128)S(1)}, f32[1,7,8,128]{3,2,1,0:T(8,128)S(1)}, u32[]{:S(2)}, u32[]{:S(2)}) collective-permute-start(f32[1,7,8,128]{3,2,1,0:T(8,128)S(1)} %get-tuple-element.54), channel_id=1, source_target_pairs={{0,480},{32,64},{64,32},{96,128},{128,96},{160,192},{192,160},{224... | collective-permute-start | bytes 86024 | tf_op jit(solution)/shard_map/ppermute | solution.py:619
  56.7 4.7 %collective-permute-start.7 = (f32[1,7,8,128]{3,2,1,0:T(8,128)S(1)}, f32[1,7,8,128]{3,2,1,0:T(8,128)S(1)}, u32[]{:S(2)}, u32[]{:S(2)}) collective-permute-start(f32[1,7,8,128]{3,2,1,0:T(8,128)S(1)} %get-tuple-element.55), channel_id=1, source_target_pairs={{0,32},{32,0},{64,96},{96,64},{128,160},{160,128},{192,224},{224,1... | collective-permute-start | bytes 86024 | tf_op jit(solution)/shard_map/ppermute | solution.py:619
  61.4 36.9 %copy-start.1 = (s32[1,1,128]{2,1,0:T(1,128)S(1)}, s32[1,1,128]{2,1,0:T(1,128)}, u32[]{:S(2)}) copy-start(s32[1,1,128]{2,1,0:T(1,128)} %param.6) | copy-start | bytes 1540
  64.2 22.9 %all-to-all-start = ((f32[64,8,128]{2,1,0:T(8,128)}), f32[64,8,128]{2,1,0:T(8,128)S(1)}, u32[]{:S(2)}, u32[]{:S(2)}) async-start(f32[64,8,128]{2,1,0:T(8,128)} %get-tuple-element.59), calls=%async_computation | async-start | bytes 524288 | tf_op jit(solution)/shard_map/all_to_all | solution.py:679
  72.6 10.9 %collective-permute-start.8 = (f32[1,7,8,128]{3,2,1,0:T(8,128)S(1)}, f32[1,7,8,128]{3,2,1,0:T(8,128)S(1)}, u32[]{:S(2)}, u32[]{:S(2)}) collective-permute-start(f32[1,7,8,128]{3,2,1,0:T(8,128)S(1)} %get-tuple-element.60), channel_id=1, source_target_pairs={{0,480},{32,64},{64,32},{96,128},{128,96},{160,192},{192,160},{224... | collective-permute-start | bytes 86024 | tf_op jit(solution)/shard_map/ppermute | solution.py:619
  87.8 10.5 %all-to-all-start.1 = ((f32[8,8,128]{2,1,0:T(8,128)}), f32[8,8,128]{2,1,0:T(8,128)S(1)}, u32[]{:S(2)}, u32[]{:S(2)}) async-start(f32[8,8,128]{2,1,0:T(8,128)} %get-tuple-element.67), calls=%async_computation.1 | async-start | bytes 65536 | tf_op jit(solution)/shard_map/all_to_all | solution.py:685
  91.2 5.3 %collective-permute-start.9 = (f32[1,7,8,128]{3,2,1,0:T(8,128)S(1)}, f32[1,7,8,128]{3,2,1,0:T(8,128)S(1)}, u32[]{:S(2)}, u32[]{:S(2)}) collective-permute-start(f32[1,7,8,128]{3,2,1,0:T(8,128)S(1)} %get-tuple-element.62), channel_id=1, source_target_pairs={{0,32},{32,0},{64,96},{96,64},{128,160},{160,128},{192,224},{224,1... | collective-permute-start | bytes 86024 | tf_op jit(solution)/shard_map/ppermute | solution.py:619

commit v9 on v8

--- a/solution.py
+++ b/solution.py
@@ -678,7 +678,7 @@
     )
     got = lax.all_to_all(send, ("slab", "dom"), 0, 0, axis_index_groups=sheets)
     far_x, near_x = swap("slab", far, near)
-    got, far_x = lax.optimization_barrier((got, far_x))
+    got, near_x = lax.optimization_barrier((got, near_x))
     low, high, send = call(
         middle_kernel, [face, face, (run, 8, LANES)], (got,), name="middle"
     )

time: 100 us -> 102 us (1.020)
  waiting for transfers between devices: 14.5 us -> 22.1 us
  starting transfers between devices: 66.3 us -> 60.9 us
    all_to_all x1, waiting for transfers between devices: 3.63 us -> 8.34 us  [per_device(): got = lax.all_to_all(send, ('slab', 'dom'), 0, 0, axis_index_groups=sheets)]
    ppermute x5, starting transfers between devices: 41.1 us -> 37.1 us  [swap(): lax.ppermute(far, axis, far_pairs)]
    ppermute x5, waiting for transfers between devices: 5.33 us -> 9.06 us  [swap(): lax.ppermute(far, axis, far_pairs)]
    all_to_all x1, waiting for transfers between devices: 1.85 us -> 0.01 us  [per_device(): dots = lax.all_to_all(send, ('slab', 'dom'), 0, 0, axis_index_groups=rings)]
    ppermute x5, starting transfers between devices: 13.4 us -> 12 us  [swap(): lax.ppermute(near, axis, near_pairs)]
    ppermute x5, waiting for transfers between devices: 3.66 us -> 4.74 us  [swap(): lax.ppermute(near, axis, near_pairs)]
  transfers between devices with their start and end apart: 12 -> 12, of which waited for: 8 -> 7; matrix products, arithmetic and copies ran while one was open for 0% -> 0% of each run, Pallas kernels for 5% -> 5%
where the time goes in v9:
time: 102 us
  starting transfers between devices  60.9 us (60%)
  waiting for transfers between devices  22.1 us (22%)
  Pallas kernels  17.9 us (18%)
    ppermute x5, starting transfers between devices, swap(): lax.ppermute(far, axis, far_pairs)  37.1 us
    pallas_call x9, Pallas kernels, call(): pl.pallas_call(kernel, out_shape=tuple((jax.ShapeDtypeStruct(*(o if isins...  17.9 us
    ppermute x5, starting transfers between devices, swap(): lax.ppermute(near, axis, near_pairs)  12 us
    ppermute x5, waiting for transfers between devices, swap(): lax.ppermute(far, axis, far_pairs)  9.06 us
    all_to_all x1, starting transfers between devices, per_device(): got = lax.all_to_all(send, ('slab', 'dom'), 0, 0, axis_index_groups=sheets)  8.42 us
    all_to_all x1, waiting for transfers between devices, per_device(): got = lax.all_to_all(send, ('slab', 'dom'), 0, 0, axis_index_groups=sheets)  8.34 us
    ppermute x5, waiting for transfers between devices, swap(): lax.ppermute(near, axis, near_pairs)  4.74 us
    all_to_all x1, starting transfers between devices, per_device(): dots = lax.all_to_all(send, ('slab', 'dom'), 0, 0, axis_index_groups=rings)  3.38 us
  transfers between devices with their start and end apart: 12, of which 7 were waited for; matrix products, arithmetic and copies ran while one was open for 0% of the time, Pallas kernels for 5%

profile of v9, /device:TPU:1, one launch (start us, length us, event | category | flops | bytes accessed | tf_op | source)
XLA Modules:
  0.0 101.7 jit_solution(15645768925607520787)
XLA Ops:
  0.6 3.6 %advect.1 = (f32[3,7,7,8,128]{4,3,2,1,0:T(8,128)S(1)}, f32[3,7,7,8,128]{4,3,2,1,0:T(8,128)S(1)}, f32[3,7,8,128]{3,2,1,0:T(8,128)S(1)}, f32[3,7,8,128]{3,2,1,0:T(8,128)S(1)}, f32[8,128]{1,0:T(8,128)S(1)}) custom-call(f32[3,343,128]{2,1,0:T(8,128)} %vel_hbm.1, s32[1,128]{1,0:T(1,128)} %bitcast.3, s32[1,128]{1,0:T(1,128)} %bitcast.7), custom_call_target="tpu_custom_call" | custom-call | tf_op jit(solution)/shard_map/advect/pallas_call | solution.py:597
  4.2 14.4 %collective-permute-start = (f32[3,7,8,128]{3,2,1,0:T(8,128)S(1)}, f32[3,7,8,128]{3,2,1,0:T(8,128)S(1)}, u32[]{:S(2)}, u32[]{:S(2)}) collective-permute-start(f32[3,7,8,128]{3,2,1,0:T(8,128)S(1)} %get-tuple-element.37), channel_id=1, source_target_pairs={{0,480},{32,64},{64,32},{96,128},{128,96},{160,192},{192,160},{224... | collective-permute-start | bytes 258056 | tf_op jit(solution)/shard_map/ppermute | solution.py:619
  18.6 1.9 %collective-permute-start.1 = (f32[3,7,8,128]{3,2,1,0:T(8,128)S(1)}, f32[3,7,8,128]{3,2,1,0:T(8,128)S(1)}, u32[]{:S(2)}, u32[]{:S(2)}) collective-permute-start(f32[3,7,8,128]{3,2,1,0:T(8,128)S(1)} %get-tuple-element.38), channel_id=1, source_target_pairs={{0,32},{32,0},{64,96},{96,64},{128,160},{160,128},{192,224},{224,1... | collective-permute-start | bytes 258056 | tf_op jit(solution)/shard_map/ppermute | solution.py:619
  20.5 2.4 %split.2.split_0 = bf16[448,2048]{1,0:T(8,128)(2,1)S(1)} custom-call(f32[218,16,218]{2,1,0:T(8,128)} %bitcast.5), custom_call_target="tpu_custom_call" | custom-call | tf_op jit(solution)/shard_map/split/pallas_call | solution.py:597
  22.9 0.0 collective-permute-done.far_x_ref
  22.9 0.9 collective-permute-done.1.near_x_ref
  23.8 0.9 source.1
  24.7 5.1 %collective-permute-start.2 = (f32[2,7,8,128]{3,2,1,0:T(8,128)S(1)}, f32[2,7,8,128]{3,2,1,0:T(8,128)S(1)}, u32[]{:S(2)}, u32[]{:S(2)}) collective-permute-start(f32[2,7,8,128]{3,2,1,0:T(8,128)S(1)} %get-tuple-element.42), channel_id=1, source_target_pairs={{0,31},{1,2},{2,1},{3,4},{4,3},{5,6},{6,5},{7,8},{8,7},{9,10},{10,... | collective-permute-start | bytes 172040 | tf_op jit(solution)/shard_map/ppermute | solution.py:619
  29.8 4.3 %collective-permute-start.3 = (f32[2,7,8,128]{3,2,1,0:T(8,128)S(1)}, f32[2,7,8,128]{3,2,1,0:T(8,128)S(1)}, u32[]{:S(2)}, u32[]{:S(2)}) collective-permute-start(f32[2,7,8,128]{3,2,1,0:T(8,128)S(1)} %get-tuple-element.43), channel_id=1, source_target_pairs={{0,1},{1,0},{2,3},{3,2},{4,5},{5,4},{6,7},{7,6},{8,9},{9,8},{10,11... | collective-permute-start | bytes 172040 | tf_op jit(solution)/shard_map/ppermute | solution.py:619
  34.2 0.0 collective-permute-done.2.far_y_ref
  34.2 0.9 collective-permute-done.3.near_y_ref
  35.0 1.3 %correct.1 = (f32[2,7,7,8,128]{4,3,2,1,0:T(8,128)S(1)}, f32[2,7,8,128]{3,2,1,0:T(8,128)S(1)}, f32[2,7,8,128]{3,2,1,0:T(8,128)S(1)}, f32[8,128]{1,0:T(8,128)S(1)}) custom-call(f32[1,7,7,8,128]{4,3,2,1,0:T(8,128)S(1)} %get-tuple-element.41.part_ref, f32[2,7,8,128]{3,2,1,0:T(8,128)S(1)} %collective-permute-done.2.far_y_ref, ...), custom_call_target="tpu_custom_call" | custom-call | tf_op jit(solution)/shard_map/correct/pallas_call | solution.py:597
  36.4 6.3 %collective-permute-start.4 = (f32[2,7,8,128]{3,2,1,0:T(8,128)S(1)}, f32[2,7,8,128]{3,2,1,0:T(8,128)S(1)}, u32[]{:S(2)}, u32[]{:S(2)}) collective-permute-start(f32[2,7,8,128]{3,2,1,0:T(8,128)S(1)} %get-tuple-element.48), channel_id=1, source_target_pairs={{0,480},{32,64},{64,32},{96,128},{128,96},{160,192},{192,160},{224... | collective-permute-start | bytes 172040 | tf_op jit(solution)/shard_map/ppermute | solution.py:619
  42.6 1.9 %collective-permute-start.5 = (f32[2,7,8,128]{3,2,1,0:T(8,128)S(1)}, f32[2,7,8,128]{3,2,1,0:T(8,128)S(1)}, u32[]{:S(2)}, u32[]{:S(2)}) collective-permute-start(f32[2,7,8,128]{3,2,1,0:T(8,128)S(1)} %get-tuple-element.49), channel_id=1, source_target_pairs={{0,32},{32,0},{64,96},{96,64},{128,160},{160,128},{192,224},{224,1... | collective-permute-start | bytes 172040 | tf_op jit(solution)/shard_map/ppermute | solution.py:619
  44.5 2.4 %split.3.split_1 = bf16[448,2048]{1,0:T(8,128)(2,1)S(1)} custom-call(f32[218,16,218]{2,1,0:T(8,128)} %bitcast.6), custom_call_target="tpu_custom_call" | custom-call | tf_op jit(solution)/shard_map/split/pallas_call | solution.py:597
  46.9 0.9 collective-permute-done.4.far_x_ref
  47.8 0.0 collective-permute-done.5.near_x_ref
  47.8 0.0 copy-start
  47.8 2.7 %first.1 = (f32[224,128]{1,0:T(8,128)S(1)}, f32[224,128]{1,0:T(8,128)S(1)}, f32[1,7,7,8,128]{4,3,2,1,0:T(8,128)S(1)}, f32[1,7,8,128]{3,2,1,0:T(8,128)S(1)}, f32[1,7,8,128]{3,2,1,0:T(8,128)S(1)}) custom-call(f32[2,7,7,8,128]{4,3,2,1,0:T(8,128)S(1)} %get-tuple-element.47.part_ref, f32[2,7,8,128]{3,2,1,0:T(8,128)S(1)} %collective-permute-done.4.far_x_ref, ...), custom_call_target="tpu_custom_call" | custom-call | tf_op jit(solution)/shard_map/first/pallas_call | solution.py:597
  50.5 6.2 %collective-permute-start.6 = (f32[1,7,8,128]{3,2,1,0:T(8,128)S(1)}, f32[1,7,8,128]{3,2,1,0:T(8,128)S(1)}, u32[]{:S(2)}, u32[]{:S(2)}) collective-permute-start(f32[1,7,8,128]{3,2,1,0:T(8,128)S(1)} %get-tuple-element.54), channel_id=1, source_target_pairs={{0,480},{32,64},{64,32},{96,128},{128,96},{160,192},{192,160},{224... | collective-permute-start | bytes 86024 | tf_op jit(solution)/shard_map/ppermute | solution.py:619
  56.7 1.9 %collective-permute-start.7 = (f32[1,7,8,128]{3,2,1,0:T(8,128)S(1)}, f32[1,7,8,128]{3,2,1,0:T(8,128)S(1)}, u32[]{:S(2)}, u32[]{:S(2)}) collective-permute-start(f32[1,7,8,128]{3,2,1,0:T(8,128)S(1)} %get-tuple-element.55), channel_id=1, source_target_pairs={{0,32},{32,0},{64,96},{96,64},{128,160},{160,128},{192,224},{224,1... | collective-permute-start | bytes 86024 | tf_op jit(solution)/shard_map/ppermute | solution.py:619
  58.6 2.8 %collective-permute-done.6.far_x_ref = f32[1,7,8,128]{3,2,1,0:T(8,128)S(1)} collective-permute-done((f32[1,7,8,128]{3,2,1,0:T(8,128)S(1)}, f32[1,7,8,128]{3,2,1,0:T(8,128)S(1)}, u32[]{:S(2)}, u32[]{:S(2)}) %collective-permute-start.6) | collective-permute-done | bytes 28704 | tf_op jit(solution)/shard_map/ppermute | solution.py:619
  61.4 0.0 collective-permute-done.7.near_x_ref
  61.4 0.0 copy-done
  61.4 0.0 copy-start.1
  61.4 2.8 %second.1 = (f32[224,128]{1,0:T(8,128)S(1)}, f32[64,8,128]{2,1,0:T(8,128)}, f32[1,7,7,8,128]{4,3,2,1,0:T(8,128)S(1)}, f32[1,7,8,128]{3,2,1,0:T(8,128)S(1)}, f32[1,7,8,128]{3,2,1,0:T(8,128)S(1)}) custom-call(f32[1,7,7,8,128]{4,3,2,1,0:T(8,128)S(1)} %get-tuple-element.53.part_ref, f32[1,7,8,128]{3,2,1,0:T(8,128)S(1)} %collective-permute-done.6.far_x_ref, ...), custom_call_target="tpu_custom_call" | custom-call | tf_op jit(solution)/shard_map/second/pallas_call | solution.py:597
  64.2 8.4 %all-to-all-start = ((f32[64,8,128]{2,1,0:T(8,128)}), f32[64,8,128]{2,1,0:T(8,128)S(1)}, u32[]{:S(2)}, u32[]{:S(2)}) async-start(f32[64,8,128]{2,1,0:T(8,128)} %get-tuple-element.60), calls=%async_computation | async-start | bytes 524288 | tf_op jit(solution)/shard_map/all_to_all | solution.py:679
  72.6 1.9 %collective-permute-start.9 = (f32[1,7,8,128]{3,2,1,0:T(8,128)S(1)}, f32[1,7,8,128]{3,2,1,0:T(8,128)S(1)}, u32[]{:S(2)}, u32[]{:S(2)}) collective-permute-start(f32[1,7,8,128]{3,2,1,0:T(8,128)S(1)} %get-tuple-element.61), channel_id=1, source_target_pairs={{0,32},{32,0},{64,96},{96,64},{128,160},{160,128},{192,224},{224,1... | collective-permute-start | bytes 86024 | tf_op jit(solution)/shard_map/ppermute | solution.py:619
  74.5 3.0 %collective-permute-done.9.near_x_ref = f32[1,7,8,128]{3,2,1,0:T(8,128)S(1)} collective-permute-done((f32[1,7,8,128]{3,2,1,0:T(8,128)S(1)}, f32[1,7,8,128]{3,2,1,0:T(8,128)S(1)}, u32[]{:S(2)}, u32[]{:S(2)}) %collective-permute-start.9) | collective-permute-done | bytes 28704 | tf_op jit(solution)/shard_map/ppermute | solution.py:619
  77.5 8.3 %all-to-all-done.got_ref = f32[64,8,128]{2,1,0:T(8,128)S(1)} async-done(((f32[64,8,128]{2,1,0:T(8,128)}), f32[64,8,128]{2,1,0:T(8,128)S(1)}, u32[]{:S(2)}, u32[]{:S(2)}) %all-to-all-start) | async-done | bytes 262176 | tf_op jit(solution)/shard_map/all_to_all | solution.py:679
  85.9 0.7 middle.1
  86.6 3.4 %all-to-all-start.1 = ((f32[8,8,128]{2,1,0:T(8,128)}), f32[8,8,128]{2,1,0:T(8,128)S(1)}, u32[]{:S(2)}, u32[]{:S(2)}) async-start(f32[8,8,128]{2,1,0:T(8,128)} %get-tuple-element.67), calls=%async_computation.1 | async-start | bytes 65536 | tf_op jit(solution)/shard_map/all_to_all | solution.py:685
  90.0 5.2 %collective-permute-start.8 = (f32[1,7,8,128]{3,2,1,0:T(8,128)S(1)}, f32[1,7,8,128]{3,2,1,0:T(8,128)S(1)}, u32[]{:S(2)}, u32[]{:S(2)}) collective-permute-start(f32[1,7,8,128]{3,2,1,0:T(8,128)S(1)} %get-tuple-element.59), channel_id=1, source_target_pairs={{0,480},{32,64},{64,32},{96,128},{128,96},{160,192},{192,160},{224... | collective-permute-start | bytes 86024 | tf_op jit(solution)/shard_map/ppermute | solution.py:619
  95.2 5.4 %collective-permute-done.8.far_x_ref = f32[1,7,8,128]{3,2,1,0:T(8,128)S(1)} collective-permute-done((f32[1,7,8,128]{3,2,1,0:T(8,128)S(1)}, f32[1,7,8,128]{3,2,1,0:T(8,128)S(1)}, u32[]{:S(2)}, u32[]{:S(2)}) %collective-permute-start.8) | collective-permute-done | bytes 28704 | tf_op jit(solution)/shard_map/ppermute | solution.py:619
  100.6 0.0 all-to-all-done.1.dots_ref
  100.6 0.0 copy-done.1
  100.6 1.1 %finish.1 = (f32[218,128]{1,0:T(8,128)}, f32[218,128]{1,0:T(8,128)}) custom-call(f32[1,7,7,8,128]{4,3,2,1,0:T(8,128)S(1)} %get-tuple-element.58.part_ref, f32[1,7,8,128]{3,2,1,0:T(8,128)S(1)} %collective-permute-done.8.far_x_ref, f32[1,7,8,128]{3,2,1,0:T(8,128)S(1)} %collective-permute-done.9.near_x_ref, f32[7,8,128]{2,1,0:T(8,128)S(1)} %get-tuple-element.64.low_ref, ...), custom_call_target="tpu_custom_call" | custom-call | tf_op jit(solution)/shard_map/finish/pallas_call | solution.py:597
Async XLA Ops:
  4.2 18.7 %collective-permute-start = (f32[3,7,8,128]{3,2,1,0:T(8,128)S(1)}, f32[3,7,8,128]{3,2,1,0:T(8,128)S(1)}, u32[]{:S(2)}, u32[]{:S(2)}) collective-permute-start(f32[3,7,8,128]{3,2,1,0:T(8,128)S(1)} %get-tuple-element.37), channel_id=1, source_target_pairs={{0,480},{32,64},{64,32},{96,128},{128,96},{160,192},{192,160},{224... | collective-permute-start | bytes 258056 | tf_op jit(solution)/shard_map/ppermute | solution.py:619
  18.6 5.2 %collective-permute-start.1 = (f32[3,7,8,128]{3,2,1,0:T(8,128)S(1)}, f32[3,7,8,128]{3,2,1,0:T(8,128)S(1)}, u32[]{:S(2)}, u32[]{:S(2)}) collective-permute-start(f32[3,7,8,128]{3,2,1,0:T(8,128)S(1)} %get-tuple-element.38), channel_id=1, source_target_pairs={{0,32},{32,0},{64,96},{96,64},{128,160},{160,128},{192,224},{224,1... | collective-permute-start | bytes 258056 | tf_op jit(solution)/shard_map/ppermute | solution.py:619
  24.7 9.4 %collective-permute-start.2 = (f32[2,7,8,128]{3,2,1,0:T(8,128)S(1)}, f32[2,7,8,128]{3,2,1,0:T(8,128)S(1)}, u32[]{:S(2)}, u32[]{:S(2)}) collective-permute-start(f32[2,7,8,128]{3,2,1,0:T(8,128)S(1)} %get-tuple-element.42), channel_id=1, source_target_pairs={{0,31},{1,2},{2,1},{3,4},{4,3},{5,6},{6,5},{7,8},{8,7},{9,10},{10,... | collective-permute-start | bytes 172040 | tf_op jit(solution)/shard_map/ppermute | solution.py:619
  29.8 5.2 %collective-permute-start.3 = (f32[2,7,8,128]{3,2,1,0:T(8,128)S(1)}, f32[2,7,8,128]{3,2,1,0:T(8,128)S(1)}, u32[]{:S(2)}, u32[]{:S(2)}) collective-permute-start(f32[2,7,8,128]{3,2,1,0:T(8,128)S(1)} %get-tuple-element.43), channel_id=1, source_target_pairs={{0,1},{1,0},{2,3},{3,2},{4,5},{5,4},{6,7},{7,6},{8,9},{9,8},{10,11... | collective-permute-start | bytes 172040 | tf_op jit(solution)/shard_map/ppermute | solution.py:619
  36.4 11.5 %collective-permute-start.4 = (f32[2,7,8,128]{3,2,1,0:T(8,128)S(1)}, f32[2,7,8,128]{3,2,1,0:T(8,128)S(1)}, u32[]{:S(2)}, u32[]{:S(2)}) collective-permute-start(f32[2,7,8,128]{3,2,1,0:T(8,128)S(1)} %get-tuple-element.48), channel_id=1, source_target_pairs={{0,480},{32,64},{64,32},{96,128},{128,96},{160,192},{192,160},{224... | collective-permute-start | bytes 172040 | tf_op jit(solution)/shard_map/ppermute | solution.py:619
  42.6 5.2 %collective-permute-start.5 = (f32[2,7,8,128]{3,2,1,0:T(8,128)S(1)}, f32[2,7,8,128]{3,2,1,0:T(8,128)S(1)}, u32[]{:S(2)}, u32[]{:S(2)}) collective-permute-start(f32[2,7,8,128]{3,2,1,0:T(8,128)S(1)} %get-tuple-element.49), channel_id=1, source_target_pairs={{0,32},{32,0},{64,96},{96,64},{128,160},{160,128},{192,224},{224,1... | collective-permute-start | bytes 172040 | tf_op jit(solution)/shard_map/ppermute | solution.py:619
  47.8 13.5 %copy-start = (f32[224,128]{1,0:T(8,128)S(1)}, f32[224,128]{1,0:T(8,128)}, u32[]{:S(2)}) copy-start(f32[224,128]{1,0:T(8,128)} %constant.2.clone.shell_ref) | copy-start | bytes 344068
  50.5 10.9 %collective-permute-start.6 = (f32[1,7,8,128]{3,2,1,0:T(8,128)S(1)}, f32[1,7,8,128]{3,2,1,0:T(8,128)S(1)}, u32[]{:S(2)}, u32[]{:S(2)}) collective-permute-start(f32[1,7,8,128]{3,2,1,0:T(8,128)S(1)} %get-tuple-element.54), channel_id=1, source_target_pairs={{0,480},{32,64},{64,32},{96,128},{128,96},{160,192},{192,160},{224... | collective-permute-start | bytes 86024 | tf_op jit(solution)/shard_map/ppermute | solution.py:619
  56.7 4.7 %collective-permute-start.7 = (f32[1,7,8,128]{3,2,1,0:T(8,128)S(1)}, f32[1,7,8,128]{3,2,1,0:T(8,128)S(1)}, u32[]{:S(2)}, u32[]{:S(2)}) collective-permute-start(f32[1,7,8,128]{3,2,1,0:T(8,128)S(1)} %get-tuple-element.55), channel_id=1, source_target_pairs={{0,32},{32,0},{64,96},{96,64},{128,160},{160,128},{192,224},{224,1... | collective-permute-start | bytes 86024 | tf_op jit(solution)/shard_map/ppermute | solution.py:619
  61.4 39.2 %copy-start.1 = (s32[1,1,128]{2,1,0:T(1,128)S(1)}, s32[1,1,128]{2,1,0:T(1,128)}, u32[]{:S(2)}) copy-start(s32[1,1,128]{2,1,0:T(1,128)} %param.6) | copy-start | bytes 1540
  64.2 21.7 %all-to-all-start = ((f32[64,8,128]{2,1,0:T(8,128)}), f32[64,8,128]{2,1,0:T(8,128)S(1)}, u32[]{:S(2)}, u32[]{:S(2)}) async-start(f32[64,8,128]{2,1,0:T(8,128)} %get-tuple-element.60), calls=%async_computation | async-start | bytes 524288 | tf_op jit(solution)/shard_map/all_to_all | solution.py:679
  72.6 4.9 %collective-permute-start.9 = (f32[1,7,8,128]{3,2,1,0:T(8,128)S(1)}, f32[1,7,8,128]{3,2,1,0:T(8,128)S(1)}, u32[]{:S(2)}, u32[]{:S(2)}) collective-permute-start(f32[1,7,8,128]{3,2,1,0:T(8,128)S(1)} %get-tuple-element.61), channel_id=1, source_target_pairs={{0,32},{32,0},{64,96},{96,64},{128,160},{160,128},{192,224},{224,1... | collective-permute-start | bytes 86024 | tf_op jit(solution)/shard_map/ppermute | solution.py:619
  86.6 14.0 %all-to-all-start.1 = ((f32[8,8,128]{2,1,0:T(8,128)}), f32[8,8,128]{2,1,0:T(8,128)S(1)}, u32[]{:S(2)}, u32[]{:S(2)}) async-start(f32[8,8,128]{2,1,0:T(8,128)} %get-tuple-element.67), calls=%async_computation.1 | async-start | bytes 65536 | tf_op jit(solution)/shard_map/all_to_all | solution.py:685
  90.0 10.6 %collective-permute-start.8 = (f32[1,7,8,128]{3,2,1,0:T(8,128)S(1)}, f32[1,7,8,128]{3,2,1,0:T(8,128)S(1)}, u32[]{:S(2)}, u32[]{:S(2)}) collective-permute-start(f32[1,7,8,128]{3,2,1,0:T(8,128)S(1)} %get-tuple-element.59), channel_id=1, source_target_pairs={{0,480},{32,64},{64,32},{96,128},{128,96},{160,192},{192,160},{224... | collective-permute-start | bytes 86024 | tf_op jit(solution)/shard_map/ppermute | solution.py:619

commit v10 on v7

--- a/solution.py
+++ b/solution.py
@@ -154,11 +154,25 @@
     return pltpu.roll(packed, shift, 1) if shift else packed
 
 
-def derive_sheets(sheets, target):
-    total = float(DERIV[target, 0]) * sheets[0]
-    for source in range(1, 7):
-        total = total + float(DERIV[target, source]) * sheets[source]
-    return total
+def derive_line(sheets):
+    sums = [sheets[j] + sheets[6 - j] for j in range(3)] + [sheets[3]]
+    differences = [sheets[j] - sheets[6 - j] for j in range(3)]
+    odd, even = [], []
+    for i in range(4):
+        mirrored = [0.5 * (DERIV[i, j] - DERIV[6 - i, 6 - j]) for j in range(7)]
+        if i < 3:
+            weights = [0.5 * (mirrored[j] + mirrored[6 - j]) for j in range(3)] + [mirrored[3]]
+            total = float(weights[0]) * sums[0]
+            for j in range(1, 4):
+                total = total + float(weights[j]) * sums[j]
+            odd.append(total)
+        weights = [0.5 * (mirrored[j] - mirrored[6 - j]) for j in range(3)]
+        total = float(weights[0]) * differences[0]
+        for j in range(1, 3):
+            total = total + float(weights[j]) * differences[j]
+        even.append(total)
+    low = [even[i] + odd[i] for i in range(3)]
+    return [*low, even[3], *(even[i] - odd[i] for i in (2, 1, 0))]
 
 
 def derive_span(rolls, sheet):
@@ -224,16 +238,16 @@
                 brick_ref[i, a, b, 0:7, :] = stored[row : row + 7]
 
     def component(i, carry):
-        sheets = [brick_ref[i, a] for a in range(7)]
+        for b in range(7):
+            line = derive_line([brick_ref[i, a, b] for a in range(7)])
+            for a in range(7):
+                part_ref[i, a, b] = brick_ref[0, a, b] * line[a]
         for a in range(7):
-            along_a = derive_sheets(sheets, a)
-            sheet = sheets[a]
-            along_b = jnp.stack(
-                [derive_sheets([sheet[b] for b in range(7)], target) for target in range(7)], axis=0
-            )
+            sheet = brick_ref[i, a]
+            along_b = jnp.stack(derive_line([sheet[b] for b in range(7)]), axis=0)
             along_c = derive_span(rolls, sheet)
             advect = (
-                brick_ref[0, a] * along_a + brick_ref[1, a] * along_b + brick_ref[2, a] * along_c
+                part_ref[i, a] + brick_ref[1, a] * along_b + brick_ref[2, a] * along_c
             )
             part_ref[i, a] = join_local(advect)
         emit_faces(part_ref, far_ref, near_ref, i)
@@ -257,14 +271,14 @@
                 sheet[b] * (inverse * float(DELTA_T / (FACTOR[a] * FACTOR[b]))) for b in range(7)
             ]
             middle_ref[i, a] = brick_ref[i, a] - jnp.stack(scaled, axis=0)
-    sheets = [middle_ref[0, a] for a in range(7)]
-    for a in range(7):
-        along_a = derive_sheets(sheets, a)
+    for b in range(7):
+        line = derive_line([middle_ref[0, a, b] for a in range(7)])
+        for a in range(7):
+            out_ref[0, a, b] = line[a]
+    for a in range(7):
         second = middle_ref[1, a]
-        along_b = jnp.stack(
-            [derive_sheets([second[b] for b in range(7)], target) for target in range(7)], axis=0
-        )
-        diverge = along_a + along_b + derive_span(rolls, middle_ref[2, a])
+        along_b = jnp.stack(derive_line([second[b] for b in range(7)]), axis=0)
+        diverge = out_ref[0, a] + along_b + derive_span(rolls, middle_ref[2, a])
         source = [
             diverge[b] * (weights * float(-1.0 / DELTA_T * WEIGHTS[a] * WEIGHTS[b]))
             for b in range(7)
@@ -292,9 +306,8 @@
         for i in range(3):
             for a in range(7):
                 face[i][a] = face[i][a] * (inverse * float(-DELTA_T / (2.0 * FACTOR[a])))
-        across.append(
-            [derive_sheets(face[0], a) + derive_span(rolls, face[2][a][None])[0] for a in range(7)]
-        )
+        line = derive_line(face[0])
+        across.append([line[a] + derive_span(rolls, face[2][a][None])[0] for a in range(7)])
     sheets = []
     for a in range(7):
         rows = []
@@ -459,10 +472,6 @@
         out_ref[0, a] = join_local(full_ref[56 * a : 56 * a + 56].reshape(7, 8, LANES))
 
 
-def total_of(values):
-    return jnp.sum(jnp.sum(values, axis=0, keepdims=True), axis=1, keepdims=True)
-
-
 def first_apply_kernel(
     part_ref, far_x_ref, near_x_ref, split_0, split_1, class_ref, ghost_class_ref,
     load_ref, image_ref, out_ref, far_ref, near_ref,
@@ -506,14 +515,16 @@
     emit_faces(out_ref, far_ref, near_ref, 0)
     load, power, shell = load_ref[...], power_ref[...], shell_ref[...]
     first, image = first_ref[...], image_ref[...]
-    lane = lax.broadcasted_iota(jnp.int32, (1, LANES), 1)
-    dots = jnp.zeros((1, LANES), F32)
+    lane = lax.broadcasted_iota(jnp.int32, (8, LANES), 1)
+    node = lax.broadcasted_iota(jnp.int32, (8, LANES), 0)
+    columns = jnp.zeros((8, LANES), F32)
     values = (
         load * load * shell, load * first, power * power * shell, load * image, power * image
     )
     for k, value in enumerate(values):
-        dots = dots + jnp.where(lane == k, total_of(value), 0.0)
-    node = lax.broadcasted_iota(jnp.int32, (8, LANES), 0)
+        columns = jnp.where(node == k, jnp.sum(value, axis=0, keepdims=True), columns)
+    totals = jnp.sum(columns, axis=1, keepdims=True)
+    dots = jnp.sum(jnp.where(lane == node, totals, 0.0), axis=0, keepdims=True)
     count = send_ref.shape[0]
     mine = lax.axis_index("dom")
     alone = jnp.where(node == 7, dots, 0.0)

time: 99.6 us -> 99.5 us (level)
  no operation moved by 1% of the time
where the time goes in v10:
time: 99.5 us; the launch traced here: 99 us
  starting transfers between devices  66.2 us (67%)
  Pallas kernels  17.8 us (18%)
  waiting for transfers between devices  14.1 us (14%)
    ppermute x5, starting transfers between devices, swap(): lax.ppermute(far, axis, far_pairs)  41.2 us
    pallas_call x9, Pallas kernels, call(): pl.pallas_call(kernel, out_shape=tuple((jax.ShapeDtypeStruct(*(o if isins...  17.8 us
    ppermute x5, starting transfers between devices, swap(): lax.ppermute(near, axis, near_pairs)  12 us
    all_to_all x1, starting transfers between devices, per_device(): got = lax.all_to_all(send, 'dom', 0, 0)  7.87 us
    ppermute x5, waiting for transfers between devices, swap(): lax.ppermute(far, axis, far_pairs)  5.65 us
    all_to_all x1, starting transfers between devices, per_device(): dots = lax.all_to_all(send, 'slab', 0, 0)  5.2 us
    ppermute x5, waiting for transfers between devices, swap(): lax.ppermute(near, axis, near_pairs)  4.74 us
    all_to_all x1, waiting for transfers between devices, per_device(): got = lax.all_to_all(send, 'dom', 0, 0)  3.75 us
  transfers between devices with their start and end apart: 12, of which 7 were waited for; matrix products, arithmetic and copies ran while one was open for 0% of the time, Pallas kernels for 5%

profile of v10, /device:TPU:1, one launch (start us, length us, event | category | flops | bytes accessed | tf_op | source)
XLA Modules:
  0.0 99.0 jit_solution(11701567355170989456)
XLA Ops:
  0.6 3.6 %advect.1 = (f32[3,7,7,8,128]{4,3,2,1,0:T(8,128)S(1)}, f32[3,7,7,8,128]{4,3,2,1,0:T(8,128)S(1)}, f32[3,7,8,128]{3,2,1,0:T(8,128)S(1)}, f32[3,7,8,128]{3,2,1,0:T(8,128)S(1)}, f32[8,128]{1,0:T(8,128)S(1)}) custom-call(f32[3,343,128]{2,1,0:T(8,128)} %vel_hbm.1, s32[1,128]{1,0:T(1,128)} %bitcast.3, s32[1,128]{1,0:T(1,128)} %bitcast.7), custom_call_target="tpu_custom_call" | custom-call | tf_op jit(solution)/shard_map/advect/pallas_call | solution.py:599
  4.2 14.4 %collective-permute-start = (f32[3,7,8,128]{3,2,1,0:T(8,128)S(1)}, f32[3,7,8,128]{3,2,1,0:T(8,128)S(1)}, u32[]{:S(2)}, u32[]{:S(2)}) collective-permute-start(f32[3,7,8,128]{3,2,1,0:T(8,128)S(1)} %get-tuple-element.37), channel_id=1, source_target_pairs={{0,480},{32,64},{64,32},{96,128},{128,96},{160,192},{192,160},{224... | collective-permute-start | bytes 258056 | tf_op jit(solution)/shard_map/ppermute | solution.py:621
  18.6 1.9 %collective-permute-start.1 = (f32[3,7,8,128]{3,2,1,0:T(8,128)S(1)}, f32[3,7,8,128]{3,2,1,0:T(8,128)S(1)}, u32[]{:S(2)}, u32[]{:S(2)}) collective-permute-start(f32[3,7,8,128]{3,2,1,0:T(8,128)S(1)} %get-tuple-element.38), channel_id=1, source_target_pairs={{0,32},{32,0},{64,96},{96,64},{128,160},{160,128},{192,224},{224,1... | collective-permute-start | bytes 258056 | tf_op jit(solution)/shard_map/ppermute | solution.py:621
  20.5 2.4 %split.2.split_0 = bf16[448,2048]{1,0:T(8,128)(2,1)S(1)} custom-call(f32[218,16,218]{2,1,0:T(8,128)} %bitcast.5), custom_call_target="tpu_custom_call" | custom-call | tf_op jit(solution)/shard_map/split/pallas_call | solution.py:599
  22.9 0.0 collective-permute-done.far_x_ref
  22.9 0.9 collective-permute-done.1.near_x_ref
  23.8 0.9 source.1
  24.7 5.1 %collective-permute-start.2 = (f32[2,7,8,128]{3,2,1,0:T(8,128)S(1)}, f32[2,7,8,128]{3,2,1,0:T(8,128)S(1)}, u32[]{:S(2)}, u32[]{:S(2)}) collective-permute-start(f32[2,7,8,128]{3,2,1,0:T(8,128)S(1)} %get-tuple-element.42), channel_id=1, source_target_pairs={{0,31},{1,2},{2,1},{3,4},{4,3},{5,6},{6,5},{7,8},{8,7},{9,10},{10,... | collective-permute-start | bytes 172040 | tf_op jit(solution)/shard_map/ppermute | solution.py:621
  29.8 4.3 %collective-permute-start.3 = (f32[2,7,8,128]{3,2,1,0:T(8,128)S(1)}, f32[2,7,8,128]{3,2,1,0:T(8,128)S(1)}, u32[]{:S(2)}, u32[]{:S(2)}) collective-permute-start(f32[2,7,8,128]{3,2,1,0:T(8,128)S(1)} %get-tuple-element.43), channel_id=1, source_target_pairs={{0,1},{1,0},{2,3},{3,2},{4,5},{5,4},{6,7},{7,6},{8,9},{9,8},{10,11... | collective-permute-start | bytes 172040 | tf_op jit(solution)/shard_map/ppermute | solution.py:621
  34.1 0.0 collective-permute-done.2.far_y_ref
  34.1 0.9 collective-permute-done.3.near_y_ref
  35.0 1.3 %correct.1 = (f32[2,7,7,8,128]{4,3,2,1,0:T(8,128)S(1)}, f32[2,7,8,128]{3,2,1,0:T(8,128)S(1)}, f32[2,7,8,128]{3,2,1,0:T(8,128)S(1)}, f32[8,128]{1,0:T(8,128)S(1)}) custom-call(f32[1,7,7,8,128]{4,3,2,1,0:T(8,128)S(1)} %get-tuple-element.41.part_ref, f32[2,7,8,128]{3,2,1,0:T(8,128)S(1)} %collective-permute-done.2.far_y_ref, ...), custom_call_target="tpu_custom_call" | custom-call | tf_op jit(solution)/shard_map/correct/pallas_call | solution.py:599
  36.3 6.3 %collective-permute-start.4 = (f32[2,7,8,128]{3,2,1,0:T(8,128)S(1)}, f32[2,7,8,128]{3,2,1,0:T(8,128)S(1)}, u32[]{:S(2)}, u32[]{:S(2)}) collective-permute-start(f32[2,7,8,128]{3,2,1,0:T(8,128)S(1)} %get-tuple-element.48), channel_id=1, source_target_pairs={{0,480},{32,64},{64,32},{96,128},{128,96},{160,192},{192,160},{224... | collective-permute-start | bytes 172040 | tf_op jit(solution)/shard_map/ppermute | solution.py:621
  42.6 1.9 %collective-permute-start.5 = (f32[2,7,8,128]{3,2,1,0:T(8,128)S(1)}, f32[2,7,8,128]{3,2,1,0:T(8,128)S(1)}, u32[]{:S(2)}, u32[]{:S(2)}) collective-permute-start(f32[2,7,8,128]{3,2,1,0:T(8,128)S(1)} %get-tuple-element.49), channel_id=1, source_target_pairs={{0,32},{32,0},{64,96},{96,64},{128,160},{160,128},{192,224},{224,1... | collective-permute-start | bytes 172040 | tf_op jit(solution)/shard_map/ppermute | solution.py:621
  44.5 2.4 %split.3.split_1 = bf16[448,2048]{1,0:T(8,128)(2,1)S(1)} custom-call(f32[218,16,218]{2,1,0:T(8,128)} %bitcast.6), custom_call_target="tpu_custom_call" | custom-call | tf_op jit(solution)/shard_map/split/pallas_call | solution.py:599
  46.9 0.9 collective-permute-done.4.far_x_ref
  47.8 0.0 collective-permute-done.5.near_x_ref
  47.8 0.0 copy-start
  47.8 2.7 %first.1 = (f32[224,128]{1,0:T(8,128)S(1)}, f32[224,128]{1,0:T(8,128)S(1)}, f32[1,7,7,8,128]{4,3,2,1,0:T(8,128)S(1)}, f32[1,7,8,128]{3,2,1,0:T(8,128)S(1)}, f32[1,7,8,128]{3,2,1,0:T(8,128)S(1)}) custom-call(f32[2,7,7,8,128]{4,3,2,1,0:T(8,128)S(1)} %get-tuple-element.47.part_ref, f32[2,7,8,128]{3,2,1,0:T(8,128)S(1)} %collective-permute-done.4.far_x_ref, ...), custom_call_target="tpu_custom_call" | custom-call | tf_op jit(solution)/shard_map/first/pallas_call | solution.py:599
  50.5 6.2 %collective-permute-start.6 = (f32[1,7,8,128]{3,2,1,0:T(8,128)S(1)}, f32[1,7,8,128]{3,2,1,0:T(8,128)S(1)}, u32[]{:S(2)}, u32[]{:S(2)}) collective-permute-start(f32[1,7,8,128]{3,2,1,0:T(8,128)S(1)} %get-tuple-element.54), channel_id=1, source_target_pairs={{0,480},{32,64},{64,32},{96,128},{128,96},{160,192},{192,160},{224... | collective-permute-start | bytes 86024 | tf_op jit(solution)/shard_map/ppermute | solution.py:621
  56.7 1.9 %collective-permute-start.7 = (f32[1,7,8,128]{3,2,1,0:T(8,128)S(1)}, f32[1,7,8,128]{3,2,1,0:T(8,128)S(1)}, u32[]{:S(2)}, u32[]{:S(2)}) collective-permute-start(f32[1,7,8,128]{3,2,1,0:T(8,128)S(1)} %get-tuple-element.55), channel_id=1, source_target_pairs={{0,32},{32,0},{64,96},{96,64},{128,160},{160,128},{192,224},{224,1... | collective-permute-start | bytes 86024 | tf_op jit(solution)/shard_map/ppermute | solution.py:621
  58.6 2.8 %collective-permute-done.6.far_x_ref = f32[1,7,8,128]{3,2,1,0:T(8,128)S(1)} collective-permute-done((f32[1,7,8,128]{3,2,1,0:T(8,128)S(1)}, f32[1,7,8,128]{3,2,1,0:T(8,128)S(1)}, u32[]{:S(2)}, u32[]{:S(2)}) %collective-permute-start.6) | collective-permute-done | bytes 28704 | tf_op jit(solution)/shard_map/ppermute | solution.py:621
  61.4 0.0 collective-permute-done.7.near_x_ref
  61.4 0.0 copy-done
  61.4 0.0 copy-start.1
  61.4 2.7 %second.1 = (f32[224,128]{1,0:T(8,128)S(1)}, f32[32,8,128]{2,1,0:T(8,128)}, f32[1,7,7,8,128]{4,3,2,1,0:T(8,128)S(1)}, f32[1,7,8,128]{3,2,1,0:T(8,128)S(1)}, f32[1,7,8,128]{3,2,1,0:T(8,128)S(1)}) custom-call(f32[1,7,7,8,128]{4,3,2,1,0:T(8,128)S(1)} %get-tuple-element.53.part_ref, f32[1,7,8,128]{3,2,1,0:T(8,128)S(1)} %collective-permute-done.6.far_x_ref, ...), custom_call_target="tpu_custom_call" | custom-call | tf_op jit(solution)/shard_map/second/pallas_call | solution.py:599
  64.1 7.9 %all-to-all-start = ((f32[32,8,128]{2,1,0:T(8,128)}), f32[32,8,128]{2,1,0:T(8,128)S(1)}, u32[]{:S(2)}, u32[]{:S(2)}) async-start(f32[32,8,128]{2,1,0:T(8,128)} %get-tuple-element.60), calls=%async_computation | async-start | bytes 262144 | tf_op jit(solution)/shard_map/all_to_all | solution.py:677
  72.0 1.9 %collective-permute-start.9 = (f32[1,7,8,128]{3,2,1,0:T(8,128)S(1)}, f32[1,7,8,128]{3,2,1,0:T(8,128)S(1)}, u32[]{:S(2)}, u32[]{:S(2)}) collective-permute-start(f32[1,7,8,128]{3,2,1,0:T(8,128)S(1)} %get-tuple-element.61), channel_id=1, source_target_pairs={{0,32},{32,0},{64,96},{96,64},{128,160},{160,128},{192,224},{224,1... | collective-permute-start | bytes 86024 | tf_op jit(solution)/shard_map/ppermute | solution.py:621
  73.9 3.0 %collective-permute-done.9.near_x_ref = f32[1,7,8,128]{3,2,1,0:T(8,128)S(1)} collective-permute-done((f32[1,7,8,128]{3,2,1,0:T(8,128)S(1)}, f32[1,7,8,128]{3,2,1,0:T(8,128)S(1)}, u32[]{:S(2)}, u32[]{:S(2)}) %collective-permute-start.9) | collective-permute-done | bytes 28704 | tf_op jit(solution)/shard_map/ppermute | solution.py:621
  76.9 3.7 %all-to-all-done.got_ref = f32[32,8,128]{2,1,0:T(8,128)S(1)} async-done(((f32[32,8,128]{2,1,0:T(8,128)}), f32[32,8,128]{2,1,0:T(8,128)S(1)}, u32[]{:S(2)}, u32[]{:S(2)}) %all-to-all-start) | async-done | bytes 131104 | tf_op jit(solution)/shard_map/all_to_all | solution.py:677
  80.6 0.7 middle.1
  81.3 5.2 %all-to-all-start.1 = ((f32[16,8,128]{2,1,0:T(8,128)}), f32[16,8,128]{2,1,0:T(8,128)S(1)}, u32[]{:S(2)}, u32[]{:S(2)}) async-start(f32[16,8,128]{2,1,0:T(8,128)} %get-tuple-element.67), calls=%async_computation.1 | async-start | bytes 131072 | tf_op jit(solution)/shard_map/all_to_all | solution.py:683
  86.6 9.3 %collective-permute-start.8 = (f32[1,7,8,128]{3,2,1,0:T(8,128)S(1)}, f32[1,7,8,128]{3,2,1,0:T(8,128)S(1)}, u32[]{:S(2)}, u32[]{:S(2)}) collective-permute-start(f32[1,7,8,128]{3,2,1,0:T(8,128)S(1)} %get-tuple-element.59), channel_id=1, source_target_pairs={{0,480},{32,64},{64,32},{96,128},{128,96},{160,192},{192,160},{224... | collective-permute-start | bytes 86024 | tf_op jit(solution)/shard_map/ppermute | solution.py:621
  95.9 2.0 %collective-permute-done.8.far_x_ref = f32[1,7,8,128]{3,2,1,0:T(8,128)S(1)} collective-permute-done((f32[1,7,8,128]{3,2,1,0:T(8,128)S(1)}, f32[1,7,8,128]{3,2,1,0:T(8,128)S(1)}, u32[]{:S(2)}, u32[]{:S(2)}) %collective-permute-start.8) | collective-permute-done | bytes 28704 | tf_op jit(solution)/shard_map/ppermute | solution.py:621
  97.8 0.0 all-to-all-done.1.dots_ref
  97.8 0.0 copy-done.1
  97.8 1.1 %finish.1 = (f32[218,128]{1,0:T(8,128)}, f32[218,128]{1,0:T(8,128)}) custom-call(f32[1,7,7,8,128]{4,3,2,1,0:T(8,128)S(1)} %get-tuple-element.58.part_ref, f32[1,7,8,128]{3,2,1,0:T(8,128)S(1)} %collective-permute-done.8.far_x_ref, f32[1,7,8,128]{3,2,1,0:T(8,128)S(1)} %collective-permute-done.9.near_x_ref, f32[7,8,128]{2,1,0:T(8,128)S(1)} %get-tuple-element.64.low_ref, ...), custom_call_target="tpu_custom_call" | custom-call | tf_op jit(solution)/shard_map/finish/pallas_call | solution.py:599
Async XLA Ops:
  4.2 18.7 %collective-permute-start = (f32[3,7,8,128]{3,2,1,0:T(8,128)S(1)}, f32[3,7,8,128]{3,2,1,0:T(8,128)S(1)}, u32[]{:S(2)}, u32[]{:S(2)}) collective-permute-start(f32[3,7,8,128]{3,2,1,0:T(8,128)S(1)} %get-tuple-element.37), channel_id=1, source_target_pairs={{0,480},{32,64},{64,32},{96,128},{128,96},{160,192},{192,160},{224... | collective-permute-start | bytes 258056 | tf_op jit(solution)/shard_map/ppermute | solution.py:621
  18.6 5.2 %collective-permute-start.1 = (f32[3,7,8,128]{3,2,1,0:T(8,128)S(1)}, f32[3,7,8,128]{3,2,1,0:T(8,128)S(1)}, u32[]{:S(2)}, u32[]{:S(2)}) collective-permute-start(f32[3,7,8,128]{3,2,1,0:T(8,128)S(1)} %get-tuple-element.38), channel_id=1, source_target_pairs={{0,32},{32,0},{64,96},{96,64},{128,160},{160,128},{192,224},{224,1... | collective-permute-start | bytes 258056 | tf_op jit(solution)/shard_map/ppermute | solution.py:621
  24.7 9.4 %collective-permute-start.2 = (f32[2,7,8,128]{3,2,1,0:T(8,128)S(1)}, f32[2,7,8,128]{3,2,1,0:T(8,128)S(1)}, u32[]{:S(2)}, u32[]{:S(2)}) collective-permute-start(f32[2,7,8,128]{3,2,1,0:T(8,128)S(1)} %get-tuple-element.42), channel_id=1, source_target_pairs={{0,31},{1,2},{2,1},{3,4},{4,3},{5,6},{6,5},{7,8},{8,7},{9,10},{10,... | collective-permute-start | bytes 172040 | tf_op jit(solution)/shard_map/ppermute | solution.py:621
  29.8 5.2 %collective-permute-start.3 = (f32[2,7,8,128]{3,2,1,0:T(8,128)S(1)}, f32[2,7,8,128]{3,2,1,0:T(8,128)S(1)}, u32[]{:S(2)}, u32[]{:S(2)}) collective-permute-start(f32[2,7,8,128]{3,2,1,0:T(8,128)S(1)} %get-tuple-element.43), channel_id=1, source_target_pairs={{0,1},{1,0},{2,3},{3,2},{4,5},{5,4},{6,7},{7,6},{8,9},{9,8},{10,11... | collective-permute-start | bytes 172040 | tf_op jit(solution)/shard_map/ppermute | solution.py:621
  36.3 11.5 %collective-permute-start.4 = (f32[2,7,8,128]{3,2,1,0:T(8,128)S(1)}, f32[2,7,8,128]{3,2,1,0:T(8,128)S(1)}, u32[]{:S(2)}, u32[]{:S(2)}) collective-permute-start(f32[2,7,8,128]{3,2,1,0:T(8,128)S(1)} %get-tuple-element.48), channel_id=1, source_target_pairs={{0,480},{32,64},{64,32},{96,128},{128,96},{160,192},{192,160},{224... | collective-permute-start | bytes 172040 | tf_op jit(solution)/shard_map/ppermute | solution.py:621
  42.6 5.2 %collective-permute-start.5 = (f32[2,7,8,128]{3,2,1,0:T(8,128)S(1)}, f32[2,7,8,128]{3,2,1,0:T(8,128)S(1)}, u32[]{:S(2)}, u32[]{:S(2)}) collective-permute-start(f32[2,7,8,128]{3,2,1,0:T(8,128)S(1)} %get-tuple-element.49), channel_id=1, source_target_pairs={{0,32},{32,0},{64,96},{96,64},{128,160},{160,128},{192,224},{224,1... | collective-permute-start | bytes 172040 | tf_op jit(solution)/shard_map/ppermute | solution.py:621
  47.8 13.5 %copy-start = (f32[224,128]{1,0:T(8,128)S(1)}, f32[224,128]{1,0:T(8,128)}, u32[]{:S(2)}) copy-start(f32[224,128]{1,0:T(8,128)} %constant.2.clone.shell_ref) | copy-start | bytes 344068
  50.5 10.9 %collective-permute-start.6 = (f32[1,7,8,128]{3,2,1,0:T(8,128)S(1)}, f32[1,7,8,128]{3,2,1,0:T(8,128)S(1)}, u32[]{:S(2)}, u32[]{:S(2)}) collective-permute-start(f32[1,7,8,128]{3,2,1,0:T(8,128)S(1)} %get-tuple-element.54), channel_id=1, source_target_pairs={{0,480},{32,64},{64,32},{96,128},{128,96},{160,192},{192,160},{224... | collective-permute-start | bytes 86024 | tf_op jit(solution)/shard_map/ppermute | solution.py:621
  56.7 4.7 %collective-permute-start.7 = (f32[1,7,8,128]{3,2,1,0:T(8,128)S(1)}, f32[1,7,8,128]{3,2,1,0:T(8,128)S(1)}, u32[]{:S(2)}, u32[]{:S(2)}) collective-permute-start(f32[1,7,8,128]{3,2,1,0:T(8,128)S(1)} %get-tuple-element.55), channel_id=1, source_target_pairs={{0,32},{32,0},{64,96},{96,64},{128,160},{160,128},{192,224},{224,1... | collective-permute-start | bytes 86024 | tf_op jit(solution)/shard_map/ppermute | solution.py:621
  61.4 36.5 %copy-start.1 = (s32[1,1,128]{2,1,0:T(1,128)S(1)}, s32[1,1,128]{2,1,0:T(1,128)}, u32[]{:S(2)}) copy-start(s32[1,1,128]{2,1,0:T(1,128)} %param.6) | copy-start | bytes 1540
  64.1 16.5 %all-to-all-start = ((f32[32,8,128]{2,1,0:T(8,128)}), f32[32,8,128]{2,1,0:T(8,128)S(1)}, u32[]{:S(2)}, u32[]{:S(2)}) async-start(f32[32,8,128]{2,1,0:T(8,128)} %get-tuple-element.60), calls=%async_computation | async-start | bytes 262144 | tf_op jit(solution)/shard_map/all_to_all | solution.py:677
  72.0 4.9 %collective-permute-start.9 = (f32[1,7,8,128]{3,2,1,0:T(8,128)S(1)}, f32[1,7,8,128]{3,2,1,0:T(8,128)S(1)}, u32[]{:S(2)}, u32[]{:S(2)}) collective-permute-start(f32[1,7,8,128]{3,2,1,0:T(8,128)S(1)} %get-tuple-element.61), channel_id=1, source_target_pairs={{0,32},{32,0},{64,96},{96,64},{128,160},{160,128},{192,224},{224,1... | collective-permute-start | bytes 86024 | tf_op jit(solution)/shard_map/ppermute | solution.py:621
  81.3 16.5 %all-to-all-start.1 = ((f32[16,8,128]{2,1,0:T(8,128)}), f32[16,8,128]{2,1,0:T(8,128)S(1)}, u32[]{:S(2)}, u32[]{:S(2)}) async-start(f32[16,8,128]{2,1,0:T(8,128)} %get-tuple-element.67), calls=%async_computation.1 | async-start | bytes 131072 | tf_op jit(solution)/shard_map/all_to_all | solution.py:683
  86.6 11.3 %collective-permute-start.8 = (f32[1,7,8,128]{3,2,1,0:T(8,128)S(1)}, f32[1,7,8,128]{3,2,1,0:T(8,128)S(1)}, u32[]{:S(2)}, u32[]{:S(2)}) collective-permute-start(f32[1,7,8,128]{3,2,1,0:T(8,128)S(1)} %get-tuple-element.59), channel_id=1, source_target_pairs={{0,480},{32,64},{64,32},{96,128},{128,96},{160,192},{192,160},{224... | collective-permute-start | bytes 86024 | tf_op jit(solution)/shard_map/ppermute | solution.py:621

commit v11 on v10

--- a/solution.py
+++ b/solution.py
@@ -322,8 +322,23 @@
     return sheets
 
 
+def other_kernel(first_ref, last_ref, out_ref):
+    _, by, _ = iotas((8, LANES))
+    each = [(i, range(7)) for i in range(3)]
+    other = face_source(
+        span_rolls(), span_vector(WEIGHTS), span_vector(1.0 / FACTOR),
+        [
+            [jnp.where(by == 1, pltpu.roll(last_ref[i, a], 2 * BZ, 1), 0.0) for a in r]
+            for i, r in each
+        ],
+        [[jnp.where(by == 0, first_ref[i, a], 0.0) for a in r] for i, r in each],
+    )
+    for a in range(7):
+        out_ref[a] = join_span(other[a])
+
+
 def correct_kernel(
-    part_ref, far_y_ref, near_y_ref, first_ref, last_ref, out_ref, far_ref, near_ref, class_out
+    part_ref, far_y_ref, near_y_ref, other_ref, out_ref, far_ref, near_ref, class_out
 ):
     rolls = span_rolls()
     weights = span_vector(WEIGHTS)
@@ -342,15 +357,10 @@
         [[chosen(0, lanes_from(received[1][a][0], i, 0)) for a in r] for i, r in each],
         [[chosen(BY - 1, lanes_from(received[1][a][1], i, LANES - BZ)) for a in r] for i, r in each],
     )
-    other = face_source(
-        rolls, weights, inverse,
-        [[chosen(1, pltpu.roll(last_ref[i, a], 2 * BZ, 1)) for a in r] for i, r in each],
-        [[chosen(0, first_ref[i, a]) for a in r] for i, r in each],
-    )
     for a in range(7):
         mine = part_ref[0, a] + join_local(own[a])
         low, high = received[0][a]
-        theirs = join_span(other[a]) + jnp.stack(
+        theirs = other_ref[a] + jnp.stack(
             [
                 chosen(0, lanes_from(low, b, 0)) + chosen(1, lanes_from(high, b, BZ))
                 for b in range(7)
@@ -651,10 +661,11 @@
         [(3, *whole)],
         name="source",
     )
+    other = call(other_kernel, [whole], (first_side, last_side), name="other")[0]
     part, far, near, ghost_classes = call(
         correct_kernel,
         [(2, *whole), (2, *face), (2, *face), (8, LANES)],
-        (part, *swap("dom", far, near), first_side, last_side),
+        (part, *swap("dom", far, near), other),
         name="correct",
     )
     swapped = swap("slab", far, near)

time: 99.5 us -> 99.1 us (level)
    pallas_call x9 -> x10, Pallas kernels: 17.8 us -> 17.7 us  [call(): pl.pallas_call(kernel, out_shape=tuple((jax.ShapeDtypeStruct(*(o if isins...]
where the time goes in v11:
time: 99.1 us; the launch traced here: 98.5 us
  starting transfers between devices  66.2 us (67%)
  Pallas kernels  17.7 us (18%)
  waiting for transfers between devices  13.8 us (14%)
    ppermute x5, starting transfers between devices, swap(): lax.ppermute(far, axis, far_pairs)  41.2 us
    pallas_call x10, Pallas kernels, call(): pl.pallas_call(kernel, out_shape=tuple((jax.ShapeDtypeStruct(*(o if isins...  17.7 us
    ppermute x5, starting transfers between devices, swap(): lax.ppermute(near, axis, near_pairs)  12 us
    all_to_all x1, starting transfers between devices, per_device(): got = lax.all_to_all(send, 'dom', 0, 0)  7.87 us
    ppermute x5, waiting for transfers between devices, swap(): lax.ppermute(far, axis, far_pairs)  5.65 us
    all_to_all x1, starting transfers between devices, per_device(): dots = lax.all_to_all(send, 'slab', 0, 0)  5.21 us
    ppermute x5, waiting for transfers between devices, swap(): lax.ppermute(near, axis, near_pairs)  4.38 us
    all_to_all x1, waiting for transfers between devices, per_device(): got = lax.all_to_all(send, 'dom', 0, 0)  3.75 us
  transfers between devices with their start and end apart: 12, of which 7 were waited for; matrix products, arithmetic and copies ran while one was open for 0% of the time, Pallas kernels for 5%

profile of v11, /device:TPU:1, one launch (start us, length us, event | category | flops | bytes accessed | tf_op | source)
XLA Modules:
  0.0 98.5 jit_solution(2459823975384298888)
XLA Ops:
  0.6 3.6 %advect.1 = (f32[3,7,7,8,128]{4,3,2,1,0:T(8,128)S(1)}, f32[3,7,7,8,128]{4,3,2,1,0:T(8,128)S(1)}, f32[3,7,8,128]{3,2,1,0:T(8,128)S(1)}, f32[3,7,8,128]{3,2,1,0:T(8,128)S(1)}, f32[8,128]{1,0:T(8,128)S(1)}) custom-call(f32[3,343,128]{2,1,0:T(8,128)} %vel_hbm.1, s32[1,128]{1,0:T(1,128)} %bitcast.3, s32[1,128]{1,0:T(1,128)} %bitcast.7), custom_call_target="tpu_custom_call" | custom-call | tf_op jit(solution)/shard_map/advect/pallas_call | solution.py:609
  4.2 14.4 %collective-permute-start = (f32[3,7,8,128]{3,2,1,0:T(8,128)S(1)}, f32[3,7,8,128]{3,2,1,0:T(8,128)S(1)}, u32[]{:S(2)}, u32[]{:S(2)}) collective-permute-start(f32[3,7,8,128]{3,2,1,0:T(8,128)S(1)} %get-tuple-element.37), channel_id=1, source_target_pairs={{0,480},{32,64},{64,32},{96,128},{128,96},{160,192},{192,160},{224... | collective-permute-start | bytes 258056 | tf_op jit(solution)/shard_map/ppermute | solution.py:631
  18.6 1.9 %collective-permute-start.1 = (f32[3,7,8,128]{3,2,1,0:T(8,128)S(1)}, f32[3,7,8,128]{3,2,1,0:T(8,128)S(1)}, u32[]{:S(2)}, u32[]{:S(2)}) collective-permute-start(f32[3,7,8,128]{3,2,1,0:T(8,128)S(1)} %get-tuple-element.38), channel_id=1, source_target_pairs={{0,32},{32,0},{64,96},{96,64},{128,160},{160,128},{192,224},{224,1... | collective-permute-start | bytes 258056 | tf_op jit(solution)/shard_map/ppermute | solution.py:631
  20.5 2.4 %split.2.split_0 = bf16[448,2048]{1,0:T(8,128)(2,1)S(1)} custom-call(f32[218,16,218]{2,1,0:T(8,128)} %bitcast.5), custom_call_target="tpu_custom_call" | custom-call | tf_op jit(solution)/shard_map/split/pallas_call | solution.py:609
  22.9 0.0 collective-permute-done.far_x_ref
  22.9 0.9 collective-permute-done.1.near_x_ref
  23.8 0.9 source.1
  24.7 5.1 %collective-permute-start.2 = (f32[2,7,8,128]{3,2,1,0:T(8,128)S(1)}, f32[2,7,8,128]{3,2,1,0:T(8,128)S(1)}, u32[]{:S(2)}, u32[]{:S(2)}) collective-permute-start(f32[2,7,8,128]{3,2,1,0:T(8,128)S(1)} %get-tuple-element.42), channel_id=1, source_target_pairs={{0,31},{1,2},{2,1},{3,4},{4,3},{5,6},{6,5},{7,8},{8,7},{9,10},{10,... | collective-permute-start | bytes 172040 | tf_op jit(solution)/shard_map/ppermute | solution.py:631
  29.8 4.3 %collective-permute-start.3 = (f32[2,7,8,128]{3,2,1,0:T(8,128)S(1)}, f32[2,7,8,128]{3,2,1,0:T(8,128)S(1)}, u32[]{:S(2)}, u32[]{:S(2)}) collective-permute-start(f32[2,7,8,128]{3,2,1,0:T(8,128)S(1)} %get-tuple-element.43), channel_id=1, source_target_pairs={{0,1},{1,0},{2,3},{3,2},{4,5},{5,4},{6,7},{7,6},{8,9},{9,8},{10,11... | collective-permute-start | bytes 172040 | tf_op jit(solution)/shard_map/ppermute | solution.py:631
  34.1 0.4 other.1.other_ref
  34.5 0.0 collective-permute-done.2.far_y_ref
  34.5 0.5 collective-permute-done.3.near_y_ref
  35.0 0.9 correct.1
  35.9 6.3 %collective-permute-start.4 = (f32[2,7,8,128]{3,2,1,0:T(8,128)S(1)}, f32[2,7,8,128]{3,2,1,0:T(8,128)S(1)}, u32[]{:S(2)}, u32[]{:S(2)}) collective-permute-start(f32[2,7,8,128]{3,2,1,0:T(8,128)S(1)} %get-tuple-element.48), channel_id=1, source_target_pairs={{0,480},{32,64},{64,32},{96,128},{128,96},{160,192},{192,160},{224... | collective-permute-start | bytes 172040 | tf_op jit(solution)/shard_map/ppermute | solution.py:631
  42.2 1.9 %collective-permute-start.5 = (f32[2,7,8,128]{3,2,1,0:T(8,128)S(1)}, f32[2,7,8,128]{3,2,1,0:T(8,128)S(1)}, u32[]{:S(2)}, u32[]{:S(2)}) collective-permute-start(f32[2,7,8,128]{3,2,1,0:T(8,128)S(1)} %get-tuple-element.49), channel_id=1, source_target_pairs={{0,32},{32,0},{64,96},{96,64},{128,160},{160,128},{192,224},{224,1... | collective-permute-start | bytes 172040 | tf_op jit(solution)/shard_map/ppermute | solution.py:631
  44.1 2.4 %split.3.split_1 = bf16[448,2048]{1,0:T(8,128)(2,1)S(1)} custom-call(f32[218,16,218]{2,1,0:T(8,128)} %bitcast.6), custom_call_target="tpu_custom_call" | custom-call | tf_op jit(solution)/shard_map/split/pallas_call | solution.py:609
  46.5 0.9 collective-permute-done.4.far_x_ref
  47.4 0.0 collective-permute-done.5.near_x_ref
  47.4 0.0 copy-start
  47.4 2.7 %first.1 = (f32[224,128]{1,0:T(8,128)S(1)}, f32[224,128]{1,0:T(8,128)S(1)}, f32[1,7,7,8,128]{4,3,2,1,0:T(8,128)S(1)}, f32[1,7,8,128]{3,2,1,0:T(8,128)S(1)}, f32[1,7,8,128]{3,2,1,0:T(8,128)S(1)}) custom-call(f32[2,7,7,8,128]{4,3,2,1,0:T(8,128)S(1)} %get-tuple-element.47.part_ref, f32[2,7,8,128]{3,2,1,0:T(8,128)S(1)} %collective-permute-done.4.far_x_ref, ...), custom_call_target="tpu_custom_call" | custom-call | tf_op jit(solution)/shard_map/first/pallas_call | solution.py:609
  50.1 6.2 %collective-permute-start.6 = (f32[1,7,8,128]{3,2,1,0:T(8,128)S(1)}, f32[1,7,8,128]{3,2,1,0:T(8,128)S(1)}, u32[]{:S(2)}, u32[]{:S(2)}) collective-permute-start(f32[1,7,8,128]{3,2,1,0:T(8,128)S(1)} %get-tuple-element.54), channel_id=1, source_target_pairs={{0,480},{32,64},{64,32},{96,128},{128,96},{160,192},{192,160},{224... | collective-permute-start | bytes 86024 | tf_op jit(solution)/shard_map/ppermute | solution.py:631
  56.2 1.9 %collective-permute-start.7 = (f32[1,7,8,128]{3,2,1,0:T(8,128)S(1)}, f32[1,7,8,128]{3,2,1,0:T(8,128)S(1)}, u32[]{:S(2)}, u32[]{:S(2)}) collective-permute-start(f32[1,7,8,128]{3,2,1,0:T(8,128)S(1)} %get-tuple-element.55), channel_id=1, source_target_pairs={{0,32},{32,0},{64,96},{96,64},{128,160},{160,128},{192,224},{224,1... | collective-permute-start | bytes 86024 | tf_op jit(solution)/shard_map/ppermute | solution.py:631
  58.2 2.8 %collective-permute-done.6.far_x_ref = f32[1,7,8,128]{3,2,1,0:T(8,128)S(1)} collective-permute-done((f32[1,7,8,128]{3,2,1,0:T(8,128)S(1)}, f32[1,7,8,128]{3,2,1,0:T(8,128)S(1)}, u32[]{:S(2)}, u32[]{:S(2)}) %collective-permute-start.6) | collective-permute-done | bytes 28704 | tf_op jit(solution)/shard_map/ppermute | solution.py:631
  60.9 0.0 collective-permute-done.7.near_x_ref
  60.9 0.0 copy-done
  60.9 0.0 copy-start.1
  60.9 2.7 %second.1 = (f32[224,128]{1,0:T(8,128)S(1)}, f32[32,8,128]{2,1,0:T(8,128)}, f32[1,7,7,8,128]{4,3,2,1,0:T(8,128)S(1)}, f32[1,7,8,128]{3,2,1,0:T(8,128)S(1)}, f32[1,7,8,128]{3,2,1,0:T(8,128)S(1)}) custom-call(f32[1,7,7,8,128]{4,3,2,1,0:T(8,128)S(1)} %get-tuple-element.53.part_ref, f32[1,7,8,128]{3,2,1,0:T(8,128)S(1)} %collective-permute-done.6.far_x_ref, ...), custom_call_target="tpu_custom_call" | custom-call | tf_op jit(solution)/shard_map/second/pallas_call | solution.py:609
  63.7 7.9 %all-to-all-start = ((f32[32,8,128]{2,1,0:T(8,128)}), f32[32,8,128]{2,1,0:T(8,128)S(1)}, u32[]{:S(2)}, u32[]{:S(2)}) async-start(f32[32,8,128]{2,1,0:T(8,128)} %get-tuple-element.60), calls=%async_computation | async-start | bytes 262144 | tf_op jit(solution)/shard_map/all_to_all | solution.py:688
  71.5 1.9 %collective-permute-start.9 = (f32[1,7,8,128]{3,2,1,0:T(8,128)S(1)}, f32[1,7,8,128]{3,2,1,0:T(8,128)S(1)}, u32[]{:S(2)}, u32[]{:S(2)}) collective-permute-start(f32[1,7,8,128]{3,2,1,0:T(8,128)S(1)} %get-tuple-element.61), channel_id=1, source_target_pairs={{0,32},{32,0},{64,96},{96,64},{128,160},{160,128},{192,224},{224,1... | collective-permute-start | bytes 86024 | tf_op jit(solution)/shard_map/ppermute | solution.py:631
  73.5 3.0 %collective-permute-done.9.near_x_ref = f32[1,7,8,128]{3,2,1,0:T(8,128)S(1)} collective-permute-done((f32[1,7,8,128]{3,2,1,0:T(8,128)S(1)}, f32[1,7,8,128]{3,2,1,0:T(8,128)S(1)}, u32[]{:S(2)}, u32[]{:S(2)}) %collective-permute-start.9) | collective-permute-done | bytes 28704 | tf_op jit(solution)/shard_map/ppermute | solution.py:631
  76.4 3.7 %all-to-all-done.got_ref = f32[32,8,128]{2,1,0:T(8,128)S(1)} async-done(((f32[32,8,128]{2,1,0:T(8,128)}), f32[32,8,128]{2,1,0:T(8,128)S(1)}, u32[]{:S(2)}, u32[]{:S(2)}) %all-to-all-start) | async-done | bytes 131104 | tf_op jit(solution)/shard_map/all_to_all | solution.py:688
  80.2 0.7 middle.1
  80.9 5.2 %all-to-all-start.1 = ((f32[16,8,128]{2,1,0:T(8,128)}), f32[16,8,128]{2,1,0:T(8,128)S(1)}, u32[]{:S(2)}, u32[]{:S(2)}) async-start(f32[16,8,128]{2,1,0:T(8,128)} %get-tuple-element.67), calls=%async_computation.1 | async-start | bytes 131072 | tf_op jit(solution)/shard_map/all_to_all | solution.py:694
  86.1 9.3 %collective-permute-start.8 = (f32[1,7,8,128]{3,2,1,0:T(8,128)S(1)}, f32[1,7,8,128]{3,2,1,0:T(8,128)S(1)}, u32[]{:S(2)}, u32[]{:S(2)}) collective-permute-start(f32[1,7,8,128]{3,2,1,0:T(8,128)S(1)} %get-tuple-element.59), channel_id=1, source_target_pairs={{0,480},{32,64},{64,32},{96,128},{128,96},{160,192},{192,160},{224... | collective-permute-start | bytes 86024 | tf_op jit(solution)/shard_map/ppermute | solution.py:631
  95.4 2.0 %collective-permute-done.8.far_x_ref = f32[1,7,8,128]{3,2,1,0:T(8,128)S(1)} collective-permute-done((f32[1,7,8,128]{3,2,1,0:T(8,128)S(1)}, f32[1,7,8,128]{3,2,1,0:T(8,128)S(1)}, u32[]{:S(2)}, u32[]{:S(2)}) %collective-permute-start.8) | collective-permute-done | bytes 28704 | tf_op jit(solution)/shard_map/ppermute | solution.py:631
  97.4 0.0 all-to-all-done.1.dots_ref
  97.4 0.0 copy-done.1
  97.4 1.1 %finish.1 = (f32[218,128]{1,0:T(8,128)}, f32[218,128]{1,0:T(8,128)}) custom-call(f32[1,7,7,8,128]{4,3,2,1,0:T(8,128)S(1)} %get-tuple-element.58.part_ref, f32[1,7,8,128]{3,2,1,0:T(8,128)S(1)} %collective-permute-done.8.far_x_ref, f32[1,7,8,128]{3,2,1,0:T(8,128)S(1)} %collective-permute-done.9.near_x_ref, f32[7,8,128]{2,1,0:T(8,128)S(1)} %get-tuple-element.64.low_ref, ...), custom_call_target="tpu_custom_call" | custom-call | tf_op jit(solution)/shard_map/finish/pallas_call | solution.py:609
Async XLA Ops:
  4.2 18.7 %collective-permute-start = (f32[3,7,8,128]{3,2,1,0:T(8,128)S(1)}, f32[3,7,8,128]{3,2,1,0:T(8,128)S(1)}, u32[]{:S(2)}, u32[]{:S(2)}) collective-permute-start(f32[3,7,8,128]{3,2,1,0:T(8,128)S(1)} %get-tuple-element.37), channel_id=1, source_target_pairs={{0,480},{32,64},{64,32},{96,128},{128,96},{160,192},{192,160},{224... | collective-permute-start | bytes 258056 | tf_op jit(solution)/shard_map/ppermute | solution.py:631
  18.6 5.2 %collective-permute-start.1 = (f32[3,7,8,128]{3,2,1,0:T(8,128)S(1)}, f32[3,7,8,128]{3,2,1,0:T(8,128)S(1)}, u32[]{:S(2)}, u32[]{:S(2)}) collective-permute-start(f32[3,7,8,128]{3,2,1,0:T(8,128)S(1)} %get-tuple-element.38), channel_id=1, source_target_pairs={{0,32},{32,0},{64,96},{96,64},{128,160},{160,128},{192,224},{224,1... | collective-permute-start | bytes 258056 | tf_op jit(solution)/shard_map/ppermute | solution.py:631
  24.7 9.8 %collective-permute-start.2 = (f32[2,7,8,128]{3,2,1,0:T(8,128)S(1)}, f32[2,7,8,128]{3,2,1,0:T(8,128)S(1)}, u32[]{:S(2)}, u32[]{:S(2)}) collective-permute-start(f32[2,7,8,128]{3,2,1,0:T(8,128)S(1)} %get-tuple-element.42), channel_id=1, source_target_pairs={{0,31},{1,2},{2,1},{3,4},{4,3},{5,6},{6,5},{7,8},{8,7},{9,10},{10,... | collective-permute-start | bytes 172040 | tf_op jit(solution)/shard_map/ppermute | solution.py:631
  29.8 5.2 %collective-permute-start.3 = (f32[2,7,8,128]{3,2,1,0:T(8,128)S(1)}, f32[2,7,8,128]{3,2,1,0:T(8,128)S(1)}, u32[]{:S(2)}, u32[]{:S(2)}) collective-permute-start(f32[2,7,8,128]{3,2,1,0:T(8,128)S(1)} %get-tuple-element.43), channel_id=1, source_target_pairs={{0,1},{1,0},{2,3},{3,2},{4,5},{5,4},{6,7},{7,6},{8,9},{9,8},{10,11... | collective-permute-start | bytes 172040 | tf_op jit(solution)/shard_map/ppermute | solution.py:631
  35.9 11.5 %collective-permute-start.4 = (f32[2,7,8,128]{3,2,1,0:T(8,128)S(1)}, f32[2,7,8,128]{3,2,1,0:T(8,128)S(1)}, u32[]{:S(2)}, u32[]{:S(2)}) collective-permute-start(f32[2,7,8,128]{3,2,1,0:T(8,128)S(1)} %get-tuple-element.48), channel_id=1, source_target_pairs={{0,480},{32,64},{64,32},{96,128},{128,96},{160,192},{192,160},{224... | collective-permute-start | bytes 172040 | tf_op jit(solution)/shard_map/ppermute | solution.py:631
  42.2 5.2 %collective-permute-start.5 = (f32[2,7,8,128]{3,2,1,0:T(8,128)S(1)}, f32[2,7,8,128]{3,2,1,0:T(8,128)S(1)}, u32[]{:S(2)}, u32[]{:S(2)}) collective-permute-start(f32[2,7,8,128]{3,2,1,0:T(8,128)S(1)} %get-tuple-element.49), channel_id=1, source_target_pairs={{0,32},{32,0},{64,96},{96,64},{128,160},{160,128},{192,224},{224,1... | collective-permute-start | bytes 172040 | tf_op jit(solution)/shard_map/ppermute | solution.py:631
  47.4 13.5 %copy-start = (f32[224,128]{1,0:T(8,128)S(1)}, f32[224,128]{1,0:T(8,128)}, u32[]{:S(2)}) copy-start(f32[224,128]{1,0:T(8,128)} %constant.2.clone.shell_ref) | copy-start | bytes 344068
  50.1 10.9 %collective-permute-start.6 = (f32[1,7,8,128]{3,2,1,0:T(8,128)S(1)}, f32[1,7,8,128]{3,2,1,0:T(8,128)S(1)}, u32[]{:S(2)}, u32[]{:S(2)}) collective-permute-start(f32[1,7,8,128]{3,2,1,0:T(8,128)S(1)} %get-tuple-element.54), channel_id=1, source_target_pairs={{0,480},{32,64},{64,32},{96,128},{128,96},{160,192},{192,160},{224... | collective-permute-start | bytes 86024 | tf_op jit(solution)/shard_map/ppermute | solution.py:631
  56.2 4.7 %collective-permute-start.7 = (f32[1,7,8,128]{3,2,1,0:T(8,128)S(1)}, f32[1,7,8,128]{3,2,1,0:T(8,128)S(1)}, u32[]{:S(2)}, u32[]{:S(2)}) collective-permute-start(f32[1,7,8,128]{3,2,1,0:T(8,128)S(1)} %get-tuple-element.55), channel_id=1, source_target_pairs={{0,32},{32,0},{64,96},{96,64},{128,160},{160,128},{192,224},{224,1... | collective-permute-start | bytes 86024 | tf_op jit(solution)/shard_map/ppermute | solution.py:631
  60.9 36.5 %copy-start.1 = (s32[1,1,128]{2,1,0:T(1,128)S(1)}, s32[1,1,128]{2,1,0:T(1,128)}, u32[]{:S(2)}) copy-start(s32[1,1,128]{2,1,0:T(1,128)} %param.6) | copy-start | bytes 1540
  63.7 16.5 %all-to-all-start = ((f32[32,8,128]{2,1,0:T(8,128)}), f32[32,8,128]{2,1,0:T(8,128)S(1)}, u32[]{:S(2)}, u32[]{:S(2)}) async-start(f32[32,8,128]{2,1,0:T(8,128)} %get-tuple-element.60), calls=%async_computation | async-start | bytes 262144 | tf_op jit(solution)/shard_map/all_to_all | solution.py:688
  71.5 4.9 %collective-permute-start.9 = (f32[1,7,8,128]{3,2,1,0:T(8,128)S(1)}, f32[1,7,8,128]{3,2,1,0:T(8,128)S(1)}, u32[]{:S(2)}, u32[]{:S(2)}) collective-permute-start(f32[1,7,8,128]{3,2,1,0:T(8,128)S(1)} %get-tuple-element.61), channel_id=1, source_target_pairs={{0,32},{32,0},{64,96},{96,64},{128,160},{160,128},{192,224},{224,1... | collective-permute-start | bytes 86024 | tf_op jit(solution)/shard_map/ppermute | solution.py:631
  80.9 16.5 %all-to-all-start.1 = ((f32[16,8,128]{2,1,0:T(8,128)}), f32[16,8,128]{2,1,0:T(8,128)S(1)}, u32[]{:S(2)}, u32[]{:S(2)}) async-start(f32[16,8,128]{2,1,0:T(8,128)} %get-tuple-element.67), calls=%async_computation.1 | async-start | bytes 131072 | tf_op jit(solution)/shard_map/all_to_all | solution.py:694
  86.1 11.3 %collective-permute-start.8 = (f32[1,7,8,128]{3,2,1,0:T(8,128)S(1)}, f32[1,7,8,128]{3,2,1,0:T(8,128)S(1)}, u32[]{:S(2)}, u32[]{:S(2)}) collective-permute-start(f32[1,7,8,128]{3,2,1,0:T(8,128)S(1)} %get-tuple-element.59), channel_id=1, source_target_pairs={{0,480},{32,64},{64,32},{96,128},{128,96},{160,192},{192,160},{224... | collective-permute-start | bytes 86024 | tf_op jit(solution)/shard_map/ppermute | solution.py:631

commit v12 on v10

--- a/solution.py
+++ b/solution.py
@@ -429,8 +429,11 @@
     high, middle, low = terms(modes_ref[...])
     pair = jnp.concatenate([high, middle], axis=1)
     mine = class_ref[0:1, :]
-    both, last_both, rows = jnp.concatenate([mine, mine], axis=1), mine, 224
-    if ghost is not None:
+    both, rows = jnp.concatenate([mine, mine], axis=1), 224
+    last_both = both
+    if ghost is None:
+        low = jnp.concatenate([low, jnp.zeros(low.shape, BF16)], axis=1)
+    else:
         modes, classes = (
             x + pltpu.roll(x, 32, 1) + pltpu.roll(x, 64, 1) for x in (ghost[0], ghost[1])
         )
@@ -671,7 +674,7 @@
         second_apply_kernel,
         [modes, (doms, 8, LANES), (1, *whole), (1, *face), (1, *face)],
         (part, *swap("slab", far, near), split_0, split_1, classes, load, first, shell),
-        [modes, (392, LANES), *rights],
+        [modes, (392, LANES), rights[0], rights[0]],
         name="second",
     )
     got = lax.all_to_all(send, "dom", 0, 0)

time: 99.5 us -> 99.5 us (level)
  no operation moved by 1% of the time
where the time goes in v12:
time: 99.5 us; the launch traced here: 98.9 us
  starting transfers between devices  66.2 us (67%)
  Pallas kernels  17.7 us (18%)
  waiting for transfers between devices  14.1 us (14%)
    ppermute x5, starting transfers between devices, swap(): lax.ppermute(far, axis, far_pairs)  41.2 us
    pallas_call x9, Pallas kernels, call(): pl.pallas_call(kernel, out_shape=tuple((jax.ShapeDtypeStruct(*(o if isins...  17.7 us
    ppermute x5, starting transfers between devices, swap(): lax.ppermute(near, axis, near_pairs)  12 us
    all_to_all x1, starting transfers between devices, per_device(): got = lax.all_to_all(send, 'dom', 0, 0)  7.87 us
    ppermute x5, waiting for transfers between devices, swap(): lax.ppermute(far, axis, far_pairs)  5.65 us
    all_to_all x1, starting transfers between devices, per_device(): dots = lax.all_to_all(send, 'slab', 0, 0)  5.21 us
    ppermute x5, waiting for transfers between devices, swap(): lax.ppermute(near, axis, near_pairs)  4.74 us
    all_to_all x1, waiting for transfers between devices, per_device(): got = lax.all_to_all(send, 'dom', 0, 0)  3.75 us
  transfers between devices with their start and end apart: 12, of which 7 were waited for; matrix products, arithmetic and copies ran while one was open for 0% of the time, Pallas kernels for 5%

profile of v12, /device:TPU:1, one launch (start us, length us, event | category | flops | bytes accessed | tf_op | source)
XLA Modules:
  0.0 98.9 jit_solution(6828033779928166451)
XLA Ops:
  0.6 3.6 %advect.1 = (f32[3,7,7,8,128]{4,3,2,1,0:T(8,128)S(1)}, f32[3,7,7,8,128]{4,3,2,1,0:T(8,128)S(1)}, f32[3,7,8,128]{3,2,1,0:T(8,128)S(1)}, f32[3,7,8,128]{3,2,1,0:T(8,128)S(1)}, f32[8,128]{1,0:T(8,128)S(1)}) custom-call(f32[3,343,128]{2,1,0:T(8,128)} %vel_hbm.1, s32[1,128]{1,0:T(1,128)} %bitcast.3, s32[1,128]{1,0:T(1,128)} %bitcast.7), custom_call_target="tpu_custom_call" | custom-call | tf_op jit(solution)/shard_map/advect/pallas_call | solution.py:602
  4.2 14.4 %collective-permute-start = (f32[3,7,8,128]{3,2,1,0:T(8,128)S(1)}, f32[3,7,8,128]{3,2,1,0:T(8,128)S(1)}, u32[]{:S(2)}, u32[]{:S(2)}) collective-permute-start(f32[3,7,8,128]{3,2,1,0:T(8,128)S(1)} %get-tuple-element.37), channel_id=1, source_target_pairs={{0,480},{32,64},{64,32},{96,128},{128,96},{160,192},{192,160},{224... | collective-permute-start | bytes 258056 | tf_op jit(solution)/shard_map/ppermute | solution.py:624
  18.6 1.9 %collective-permute-start.1 = (f32[3,7,8,128]{3,2,1,0:T(8,128)S(1)}, f32[3,7,8,128]{3,2,1,0:T(8,128)S(1)}, u32[]{:S(2)}, u32[]{:S(2)}) collective-permute-start(f32[3,7,8,128]{3,2,1,0:T(8,128)S(1)} %get-tuple-element.38), channel_id=1, source_target_pairs={{0,32},{32,0},{64,96},{96,64},{128,160},{160,128},{192,224},{224,1... | collective-permute-start | bytes 258056 | tf_op jit(solution)/shard_map/ppermute | solution.py:624
  20.5 2.4 %split.2.split_0 = bf16[448,2048]{1,0:T(8,128)(2,1)S(1)} custom-call(f32[218,16,218]{2,1,0:T(8,128)} %bitcast.5), custom_call_target="tpu_custom_call" | custom-call | tf_op jit(solution)/shard_map/split/pallas_call | solution.py:602
  22.9 0.0 collective-permute-done.far_x_ref
  22.9 0.9 collective-permute-done.1.near_x_ref
  23.8 0.9 source.1
  24.7 5.1 %collective-permute-start.2 = (f32[2,7,8,128]{3,2,1,0:T(8,128)S(1)}, f32[2,7,8,128]{3,2,1,0:T(8,128)S(1)}, u32[]{:S(2)}, u32[]{:S(2)}) collective-permute-start(f32[2,7,8,128]{3,2,1,0:T(8,128)S(1)} %get-tuple-element.42), channel_id=1, source_target_pairs={{0,31},{1,2},{2,1},{3,4},{4,3},{5,6},{6,5},{7,8},{8,7},{9,10},{10,... | collective-permute-start | bytes 172040 | tf_op jit(solution)/shard_map/ppermute | solution.py:624
  29.8 4.3 %collective-permute-start.3 = (f32[2,7,8,128]{3,2,1,0:T(8,128)S(1)}, f32[2,7,8,128]{3,2,1,0:T(8,128)S(1)}, u32[]{:S(2)}, u32[]{:S(2)}) collective-permute-start(f32[2,7,8,128]{3,2,1,0:T(8,128)S(1)} %get-tuple-element.43), channel_id=1, source_target_pairs={{0,1},{1,0},{2,3},{3,2},{4,5},{5,4},{6,7},{7,6},{8,9},{9,8},{10,11... | collective-permute-start | bytes 172040 | tf_op jit(solution)/shard_map/ppermute | solution.py:624
  34.1 0.0 collective-permute-done.2.far_y_ref
  34.1 0.9 collective-permute-done.3.near_y_ref
  35.0 1.3 %correct.1 = (f32[2,7,7,8,128]{4,3,2,1,0:T(8,128)S(1)}, f32[2,7,8,128]{3,2,1,0:T(8,128)S(1)}, f32[2,7,8,128]{3,2,1,0:T(8,128)S(1)}, f32[8,128]{1,0:T(8,128)S(1)}) custom-call(f32[1,7,7,8,128]{4,3,2,1,0:T(8,128)S(1)} %get-tuple-element.41.part_ref, f32[2,7,8,128]{3,2,1,0:T(8,128)S(1)} %collective-permute-done.2.far_y_ref, ...), custom_call_target="tpu_custom_call" | custom-call | tf_op jit(solution)/shard_map/correct/pallas_call | solution.py:602
  36.3 6.3 %collective-permute-start.4 = (f32[2,7,8,128]{3,2,1,0:T(8,128)S(1)}, f32[2,7,8,128]{3,2,1,0:T(8,128)S(1)}, u32[]{:S(2)}, u32[]{:S(2)}) collective-permute-start(f32[2,7,8,128]{3,2,1,0:T(8,128)S(1)} %get-tuple-element.48), channel_id=1, source_target_pairs={{0,480},{32,64},{64,32},{96,128},{128,96},{160,192},{192,160},{224... | collective-permute-start | bytes 172040 | tf_op jit(solution)/shard_map/ppermute | solution.py:624
  42.6 1.9 %collective-permute-start.5 = (f32[2,7,8,128]{3,2,1,0:T(8,128)S(1)}, f32[2,7,8,128]{3,2,1,0:T(8,128)S(1)}, u32[]{:S(2)}, u32[]{:S(2)}) collective-permute-start(f32[2,7,8,128]{3,2,1,0:T(8,128)S(1)} %get-tuple-element.49), channel_id=1, source_target_pairs={{0,32},{32,0},{64,96},{96,64},{128,160},{160,128},{192,224},{224,1... | collective-permute-start | bytes 172040 | tf_op jit(solution)/shard_map/ppermute | solution.py:624
  44.5 2.4 %split.3.split_1 = bf16[448,2048]{1,0:T(8,128)(2,1)S(1)} custom-call(f32[218,16,218]{2,1,0:T(8,128)} %bitcast.6), custom_call_target="tpu_custom_call" | custom-call | tf_op jit(solution)/shard_map/split/pallas_call | solution.py:602
  46.9 0.9 collective-permute-done.4.far_x_ref
  47.8 0.0 collective-permute-done.5.near_x_ref
  47.8 0.0 copy-start
  47.8 2.7 %first.1 = (f32[224,128]{1,0:T(8,128)S(1)}, f32[224,128]{1,0:T(8,128)S(1)}, f32[1,7,7,8,128]{4,3,2,1,0:T(8,128)S(1)}, f32[1,7,8,128]{3,2,1,0:T(8,128)S(1)}, f32[1,7,8,128]{3,2,1,0:T(8,128)S(1)}) custom-call(f32[2,7,7,8,128]{4,3,2,1,0:T(8,128)S(1)} %get-tuple-element.47.part_ref, f32[2,7,8,128]{3,2,1,0:T(8,128)S(1)} %collective-permute-done.4.far_x_ref, ...), custom_call_target="tpu_custom_call" | custom-call | tf_op jit(solution)/shard_map/first/pallas_call | solution.py:602
  50.5 6.2 %collective-permute-start.6 = (f32[1,7,8,128]{3,2,1,0:T(8,128)S(1)}, f32[1,7,8,128]{3,2,1,0:T(8,128)S(1)}, u32[]{:S(2)}, u32[]{:S(2)}) collective-permute-start(f32[1,7,8,128]{3,2,1,0:T(8,128)S(1)} %get-tuple-element.54), channel_id=1, source_target_pairs={{0,480},{32,64},{64,32},{96,128},{128,96},{160,192},{192,160},{224... | collective-permute-start | bytes 86024 | tf_op jit(solution)/shard_map/ppermute | solution.py:624
  56.7 1.9 %collective-permute-start.7 = (f32[1,7,8,128]{3,2,1,0:T(8,128)S(1)}, f32[1,7,8,128]{3,2,1,0:T(8,128)S(1)}, u32[]{:S(2)}, u32[]{:S(2)}) collective-permute-start(f32[1,7,8,128]{3,2,1,0:T(8,128)S(1)} %get-tuple-element.55), channel_id=1, source_target_pairs={{0,32},{32,0},{64,96},{96,64},{128,160},{160,128},{192,224},{224,1... | collective-permute-start | bytes 86024 | tf_op jit(solution)/shard_map/ppermute | solution.py:624
  58.6 2.8 %collective-permute-done.6.far_x_ref = f32[1,7,8,128]{3,2,1,0:T(8,128)S(1)} collective-permute-done((f32[1,7,8,128]{3,2,1,0:T(8,128)S(1)}, f32[1,7,8,128]{3,2,1,0:T(8,128)S(1)}, u32[]{:S(2)}, u32[]{:S(2)}) %collective-permute-start.6) | collective-permute-done | bytes 28704 | tf_op jit(solution)/shard_map/ppermute | solution.py:624
  61.4 0.0 collective-permute-done.7.near_x_ref
  61.4 0.0 copy-done
  61.4 0.0 copy-start.1
  61.4 2.7 %second.1 = (f32[224,128]{1,0:T(8,128)S(1)}, f32[32,8,128]{2,1,0:T(8,128)}, f32[1,7,7,8,128]{4,3,2,1,0:T(8,128)S(1)}, f32[1,7,8,128]{3,2,1,0:T(8,128)S(1)}, f32[1,7,8,128]{3,2,1,0:T(8,128)S(1)}) custom-call(f32[1,7,7,8,128]{4,3,2,1,0:T(8,128)S(1)} %get-tuple-element.53.part_ref, f32[1,7,8,128]{3,2,1,0:T(8,128)S(1)} %collective-permute-done.6.far_x_ref, ...), custom_call_target="tpu_custom_call" | custom-call | tf_op jit(solution)/shard_map/second/pallas_call | solution.py:602
  64.1 7.9 %all-to-all-start = ((f32[32,8,128]{2,1,0:T(8,128)}), f32[32,8,128]{2,1,0:T(8,128)S(1)}, u32[]{:S(2)}, u32[]{:S(2)}) async-start(f32[32,8,128]{2,1,0:T(8,128)} %get-tuple-element.60), calls=%async_computation | async-start | bytes 262144 | tf_op jit(solution)/shard_map/all_to_all | solution.py:680
  71.9 1.9 %collective-permute-start.9 = (f32[1,7,8,128]{3,2,1,0:T(8,128)S(1)}, f32[1,7,8,128]{3,2,1,0:T(8,128)S(1)}, u32[]{:S(2)}, u32[]{:S(2)}) collective-permute-start(f32[1,7,8,128]{3,2,1,0:T(8,128)S(1)} %get-tuple-element.61), channel_id=1, source_target_pairs={{0,32},{32,0},{64,96},{96,64},{128,160},{160,128},{192,224},{224,1... | collective-permute-start | bytes 86024 | tf_op jit(solution)/shard_map/ppermute | solution.py:624
  73.9 3.0 %collective-permute-done.9.near_x_ref = f32[1,7,8,128]{3,2,1,0:T(8,128)S(1)} collective-permute-done((f32[1,7,8,128]{3,2,1,0:T(8,128)S(1)}, f32[1,7,8,128]{3,2,1,0:T(8,128)S(1)}, u32[]{:S(2)}, u32[]{:S(2)}) %collective-permute-start.9) | collective-permute-done | bytes 28704 | tf_op jit(solution)/shard_map/ppermute | solution.py:624
  76.8 3.7 %all-to-all-done.got_ref = f32[32,8,128]{2,1,0:T(8,128)S(1)} async-done(((f32[32,8,128]{2,1,0:T(8,128)}), f32[32,8,128]{2,1,0:T(8,128)S(1)}, u32[]{:S(2)}, u32[]{:S(2)}) %all-to-all-start) | async-done | bytes 131104 | tf_op jit(solution)/shard_map/all_to_all | solution.py:680
  80.6 0.7 middle.1
  81.3 5.2 %all-to-all-start.1 = ((f32[16,8,128]{2,1,0:T(8,128)}), f32[16,8,128]{2,1,0:T(8,128)S(1)}, u32[]{:S(2)}, u32[]{:S(2)}) async-start(f32[16,8,128]{2,1,0:T(8,128)} %get-tuple-element.67), calls=%async_computation.1 | async-start | bytes 131072 | tf_op jit(solution)/shard_map/all_to_all | solution.py:686
  86.5 9.3 %collective-permute-start.8 = (f32[1,7,8,128]{3,2,1,0:T(8,128)S(1)}, f32[1,7,8,128]{3,2,1,0:T(8,128)S(1)}, u32[]{:S(2)}, u32[]{:S(2)}) collective-permute-start(f32[1,7,8,128]{3,2,1,0:T(8,128)S(1)} %get-tuple-element.59), channel_id=1, source_target_pairs={{0,480},{32,64},{64,32},{96,128},{128,96},{160,192},{192,160},{224... | collective-permute-start | bytes 86024 | tf_op jit(solution)/shard_map/ppermute | solution.py:624
  95.8 2.0 %collective-permute-done.8.far_x_ref = f32[1,7,8,128]{3,2,1,0:T(8,128)S(1)} collective-permute-done((f32[1,7,8,128]{3,2,1,0:T(8,128)S(1)}, f32[1,7,8,128]{3,2,1,0:T(8,128)S(1)}, u32[]{:S(2)}, u32[]{:S(2)}) %collective-permute-start.8) | collective-permute-done | bytes 28704 | tf_op jit(solution)/shard_map/ppermute | solution.py:624
  97.8 0.0 all-to-all-done.1.dots_ref
  97.8 0.0 copy-done.1
  97.8 1.1 %finish.1 = (f32[218,128]{1,0:T(8,128)}, f32[218,128]{1,0:T(8,128)}) custom-call(f32[1,7,7,8,128]{4,3,2,1,0:T(8,128)S(1)} %get-tuple-element.58.part_ref, f32[1,7,8,128]{3,2,1,0:T(8,128)S(1)} %collective-permute-done.8.far_x_ref, f32[1,7,8,128]{3,2,1,0:T(8,128)S(1)} %collective-permute-done.9.near_x_ref, f32[7,8,128]{2,1,0:T(8,128)S(1)} %get-tuple-element.64.low_ref, ...), custom_call_target="tpu_custom_call" | custom-call | tf_op jit(solution)/shard_map/finish/pallas_call | solution.py:602
Async XLA Ops:
  4.2 18.7 %collective-permute-start = (f32[3,7,8,128]{3,2,1,0:T(8,128)S(1)}, f32[3,7,8,128]{3,2,1,0:T(8,128)S(1)}, u32[]{:S(2)}, u32[]{:S(2)}) collective-permute-start(f32[3,7,8,128]{3,2,1,0:T(8,128)S(1)} %get-tuple-element.37), channel_id=1, source_target_pairs={{0,480},{32,64},{64,32},{96,128},{128,96},{160,192},{192,160},{224... | collective-permute-start | bytes 258056 | tf_op jit(solution)/shard_map/ppermute | solution.py:624
  18.6 5.2 %collective-permute-start.1 = (f32[3,7,8,128]{3,2,1,0:T(8,128)S(1)}, f32[3,7,8,128]{3,2,1,0:T(8,128)S(1)}, u32[]{:S(2)}, u32[]{:S(2)}) collective-permute-start(f32[3,7,8,128]{3,2,1,0:T(8,128)S(1)} %get-tuple-element.38), channel_id=1, source_target_pairs={{0,32},{32,0},{64,96},{96,64},{128,160},{160,128},{192,224},{224,1... | collective-permute-start | bytes 258056 | tf_op jit(solution)/shard_map/ppermute | solution.py:624
  24.7 9.4 %collective-permute-start.2 = (f32[2,7,8,128]{3,2,1,0:T(8,128)S(1)}, f32[2,7,8,128]{3,2,1,0:T(8,128)S(1)}, u32[]{:S(2)}, u32[]{:S(2)}) collective-permute-start(f32[2,7,8,128]{3,2,1,0:T(8,128)S(1)} %get-tuple-element.42), channel_id=1, source_target_pairs={{0,31},{1,2},{2,1},{3,4},{4,3},{5,6},{6,5},{7,8},{8,7},{9,10},{10,... | collective-permute-start | bytes 172040 | tf_op jit(solution)/shard_map/ppermute | solution.py:624
  29.8 5.2 %collective-permute-start.3 = (f32[2,7,8,128]{3,2,1,0:T(8,128)S(1)}, f32[2,7,8,128]{3,2,1,0:T(8,128)S(1)}, u32[]{:S(2)}, u32[]{:S(2)}) collective-permute-start(f32[2,7,8,128]{3,2,1,0:T(8,128)S(1)} %get-tuple-element.43), channel_id=1, source_target_pairs={{0,1},{1,0},{2,3},{3,2},{4,5},{5,4},{6,7},{7,6},{8,9},{9,8},{10,11... | collective-permute-start | bytes 172040 | tf_op jit(solution)/shard_map/ppermute | solution.py:624
  36.3 11.5 %collective-permute-start.4 = (f32[2,7,8,128]{3,2,1,0:T(8,128)S(1)}, f32[2,7,8,128]{3,2,1,0:T(8,128)S(1)}, u32[]{:S(2)}, u32[]{:S(2)}) collective-permute-start(f32[2,7,8,128]{3,2,1,0:T(8,128)S(1)} %get-tuple-element.48), channel_id=1, source_target_pairs={{0,480},{32,64},{64,32},{96,128},{128,96},{160,192},{192,160},{224... | collective-permute-start | bytes 172040 | tf_op jit(solution)/shard_map/ppermute | solution.py:624
  42.6 5.2 %collective-permute-start.5 = (f32[2,7,8,128]{3,2,1,0:T(8,128)S(1)}, f32[2,7,8,128]{3,2,1,0:T(8,128)S(1)}, u32[]{:S(2)}, u32[]{:S(2)}) collective-permute-start(f32[2,7,8,128]{3,2,1,0:T(8,128)S(1)} %get-tuple-element.49), channel_id=1, source_target_pairs={{0,32},{32,0},{64,96},{96,64},{128,160},{160,128},{192,224},{224,1... | collective-permute-start | bytes 172040 | tf_op jit(solution)/shard_map/ppermute | solution.py:624
  47.8 13.5 %copy-start = (f32[224,128]{1,0:T(8,128)S(1)}, f32[224,128]{1,0:T(8,128)}, u32[]{:S(2)}) copy-start(f32[224,128]{1,0:T(8,128)} %constant.2.clone.shell_ref) | copy-start | bytes 344068
  50.5 10.9 %collective-permute-start.6 = (f32[1,7,8,128]{3,2,1,0:T(8,128)S(1)}, f32[1,7,8,128]{3,2,1,0:T(8,128)S(1)}, u32[]{:S(2)}, u32[]{:S(2)}) collective-permute-start(f32[1,7,8,128]{3,2,1,0:T(8,128)S(1)} %get-tuple-element.54), channel_id=1, source_target_pairs={{0,480},{32,64},{64,32},{96,128},{128,96},{160,192},{192,160},{224... | collective-permute-start | bytes 86024 | tf_op jit(solution)/shard_map/ppermute | solution.py:624
  56.7 4.7 %collective-permute-start.7 = (f32[1,7,8,128]{3,2,1,0:T(8,128)S(1)}, f32[1,7,8,128]{3,2,1,0:T(8,128)S(1)}, u32[]{:S(2)}, u32[]{:S(2)}) collective-permute-start(f32[1,7,8,128]{3,2,1,0:T(8,128)S(1)} %get-tuple-element.55), channel_id=1, source_target_pairs={{0,32},{32,0},{64,96},{96,64},{128,160},{160,128},{192,224},{224,1... | collective-permute-start | bytes 86024 | tf_op jit(solution)/shard_map/ppermute | solution.py:624
  61.4 36.4 %copy-start.1 = (s32[1,1,128]{2,1,0:T(1,128)S(1)}, s32[1,1,128]{2,1,0:T(1,128)}, u32[]{:S(2)}) copy-start(s32[1,1,128]{2,1,0:T(1,128)} %param.6) | copy-start | bytes 1540
  64.1 16.5 %all-to-all-start = ((f32[32,8,128]{2,1,0:T(8,128)}), f32[32,8,128]{2,1,0:T(8,128)S(1)}, u32[]{:S(2)}, u32[]{:S(2)}) async-start(f32[32,8,128]{2,1,0:T(8,128)} %get-tuple-element.60), calls=%async_computation | async-start | bytes 262144 | tf_op jit(solution)/shard_map/all_to_all | solution.py:680
  71.9 4.9 %collective-permute-start.9 = (f32[1,7,8,128]{3,2,1,0:T(8,128)S(1)}, f32[1,7,8,128]{3,2,1,0:T(8,128)S(1)}, u32[]{:S(2)}, u32[]{:S(2)}) collective-permute-start(f32[1,7,8,128]{3,2,1,0:T(8,128)S(1)} %get-tuple-element.61), channel_id=1, source_target_pairs={{0,32},{32,0},{64,96},{96,64},{128,160},{160,128},{192,224},{224,1... | collective-permute-start | bytes 86024 | tf_op jit(solution)/shard_map/ppermute | solution.py:624
  81.3 16.5 %all-to-all-start.1 = ((f32[16,8,128]{2,1,0:T(8,128)}), f32[16,8,128]{2,1,0:T(8,128)S(1)}, u32[]{:S(2)}, u32[]{:S(2)}) async-start(f32[16,8,128]{2,1,0:T(8,128)} %get-tuple-element.67), calls=%async_computation.1 | async-start | bytes 131072 | tf_op jit(solution)/shard_map/all_to_all | solution.py:686
  86.5 11.3 %collective-permute-start.8 = (f32[1,7,8,128]{3,2,1,0:T(8,128)S(1)}, f32[1,7,8,128]{3,2,1,0:T(8,128)S(1)}, u32[]{:S(2)}, u32[]{:S(2)}) collective-permute-start(f32[1,7,8,128]{3,2,1,0:T(8,128)S(1)} %get-tuple-element.59), channel_id=1, source_target_pairs={{0,480},{32,64},{64,32},{96,128},{128,96},{160,192},{192,160},{224... | collective-permute-start | bytes 86024 | tf_op jit(solution)/shard_map/ppermute | solution.py:624
